TPU v7x, 32 devices: a whole 2x2x4 slice. The times are simulated.
32 devices in a mesh: shard: 4 (over z), ctx: 4 (over x, core), tp: 2 (over y).
Axes of the slice: x: 2, y: 2, z: 4, core: 2. Of those that a mesh axis runs over, the one named last changes fastest.
Arguments:
- hidden_in: bfloat16 [2, 4, 1024, 2048], P(None, 'shard', 'ctx'), may hold values from -6 to 6
- attn_gain: bfloat16 [2048], P('shard'), may hold values from 0.099609375 to 1.8984375
- query_weight: bfloat16 [2048, 2048], P('shard', 'tp'), may hold values from -0.125 to 0.125
- key_weight: bfloat16 [2048, 2048], P('shard', 'tp'), may hold values from -0.125 to 0.125
- value_weight: bfloat16 [2048, 2048], P('shard', 'tp'), may hold values from -0.125 to 0.125
- conv_weight: bfloat16 [4, 3, 16, 128], P(None, None, 'tp', 'shard'), may hold values from -3 to 3
- beta_weight: bfloat16 [2048, 16], P('shard', 'tp'), may hold values from -0.125 to 0.125
- out_gain: bfloat16 [128], P('shard'), may hold values from 0.099609375 to 1.8984375
- out_weight: bfloat16 [2048, 2048], P('tp', 'shard'), may hold values from -0.125 to 0.125
- ffn_gain: bfloat16 [2048], P('shard'), may hold values from 0.099609375 to 1.8984375
- gate_weight: bfloat16 [2048, 5632], P('shard', 'tp'), may hold values from -0.125 to 0.125
- up_weight: bfloat16 [2048, 5632], P('shard', 'tp'), may hold values from -0.125 to 0.125
- down_weight: bfloat16 [5632, 2048], P('tp', 'shard'), may hold values from -0.078125 to 0.078125
- cotangent: bfloat16 [2, 4, 1024, 2048], P(None, 'shard', 'ctx'), may hold values from -6 to 6
- segment_ids: int32 [2, 4, 1024], P(None, 'shard', 'ctx'), may hold values from 0 to 3, never falling along the last dimension, each value on 1 to 512 neighbouring positions
Outputs:
- hidden_out: bfloat16 [2, 4, 1024, 2048], P(None, 'shard', 'ctx')
- grad_input: bfloat16 [2, 4, 1024, 2048], P(None, 'shard', 'ctx')
- grad_attn_gain: float32 [2048], P('shard')
- grad_query: float32 [2048, 2048], P('shard', 'tp')
- grad_key: float32 [2048, 2048], P('shard', 'tp')
- grad_value: float32 [2048, 2048], P('shard', 'tp')
- grad_conv: float32 [4, 3, 16, 128], P(None, None, 'tp', 'shard')
- grad_beta: float32 [2048, 16], P('shard', 'tp')
- grad_out_gain: float32 [128], P('shard')
- grad_out_weight: float32 [2048, 2048], P('tp', 'shard')
- grad_ffn_gain: float32 [2048], P('shard')
- grad_gate: float32 [2048, 5632], P('shard', 'tp')
- grad_up: float32 [2048, 5632], P('shard', 'tp')
- grad_down: float32 [5632, 2048], P('tp', 'shard')
Inputs may be any that keep to these rules, and one draw needn't show every extreme that they name: `segment_ids`: in each sequence of 1024 tokens the ids never fall from one token to the next, begin at 0, and each id covers one to 512 consecutive tokens; each id is one document.
All inputs are finite; a program needn't handle non-finite values.
Results may differ from a plain program's by a relative error of at most 0.023.
Values may be sent and summed in bfloat16 or wider, within the bound.
No kernel may reach another device: no remote copies, remote signals or barrier semaphores. Data moves between devices by JAX's collectives and lax.ppermute only.
A program may use at most 320 MiB of HBM per device.

v0:
```python
import jax
import jax.numpy as jnp
from jax import lax
from jax.sharding import PartitionSpec as P

BLOCK = 64


EPSILON = 1e-06
HIGHEST = lax.Precision.HIGHEST


def passed_along(value, axis, steps):
    count = lax.axis_size(axis)
    leading, last = (max(0, -steps), min(count, count - steps))
    return lax.ppermute(value, axis, [(source, source + steps) for source in range(leading, last)])


def carried_in(shard, axis, combine, identity):
    peers, mine = (lax.axis_size(axis), lax.axis_index(axis))
    everything = jax.tree.map(
        lambda part, kind: lax.all_gather(part.astype(kind), axis),
        shard,
        (jnp.bfloat16, jnp.bfloat16),
    )
    start = jax.tree.map(
        lambda part, zero: jnp.broadcast_to(jnp.asarray(zero, part.dtype), part.shape),
        shard,
        identity,
    )

    def carried_hop(k, before):
        reached = k < mine
        new = combine(
            before, jax.tree.map(lambda part, own: part[k].astype(own.dtype), everything, shard)
        )
        return jax.tree.map(lambda a, b: jnp.where(reached, a, b), new, before)

    return lax.fori_loop(0, peers, carried_hop, start)


def prefix(shard, axis, combine, identity):
    peers, mine = (lax.axis_size(axis), lax.axis_index(axis))
    everything = jax.tree.map(
        lambda part, kind: lax.all_gather(part.astype(kind), axis),
        shard,
        jax.tree.map(lambda a: jnp.bfloat16 if a.dtype == jnp.float32 else a.dtype, shard),
    )
    start = jax.tree.map(
        lambda part, zero: jnp.broadcast_to(jnp.asarray(zero, part.dtype), part.shape),
        shard,
        identity,
    )

    def prefix_hop(k, before):
        at = peers - 1 - k
        reached = at > mine
        new = combine(
            before, jax.tree.map(lambda part, own: part[at].astype(own.dtype), everything, shard)
        )
        return jax.tree.map(lambda a, b: jnp.where(reached, a, b), new, before)

    return lax.fori_loop(0, peers, prefix_hop, start)


def rms_scale(values, gain):
    return values * lax.rsqrt(jnp.mean(values * values, axis=-1, keepdims=True) + EPSILON) * gain


def unit_rows(values):
    return values * lax.rsqrt(jnp.sum(values * values, axis=-1, keepdims=True) + EPSILON)


def round_trip(values):
    return lax.optimization_barrier(values.astype(jnp.bfloat16)).astype(jnp.float32)


def precise(form, left, right):
    return jnp.einsum(form, left, right, precision=HIGHEST, preferred_element_type=jnp.float32)


def compose(earlier, later):
    first_map, first_bias = earlier
    second_map, second_bias = later
    return (
        precise("bhij,bhjk->bhik", first_map, second_map),
        precise("bhij,bhjk->bhik", first_bias, second_map) + second_bias,
    )


def to_blocks(values, count, size):
    shape = values.shape
    return values.reshape(shape[0], count, size, shape[2], shape[3]).transpose(1, 0, 3, 2, 4)


def from_blocks(values):
    moved = values.transpose(1, 0, 3, 2, 4)
    shape = moved.shape
    return moved.reshape(shape[0], shape[1] * shape[2], shape[3], shape[4])


def inverse_unit(strict, levels):
    unit = jnp.eye(strict.shape[-1], dtype=jnp.float32)
    result = unit - strict
    power = strict
    for level in range(levels - 1):
        power = precise("...ij,...jk->...ik", power, power)
        result = precise("...ij,...jk->...ik", result, unit + power)
    return result


def prepare(key_rows, value_rows, rates, same_doc, levels):
    gram = precise("nbhcd,nbhed->nbhce", key_rows, key_rows)
    strict = jnp.tril(gram * same_doc * rates[..., :, None], -1)
    solved = inverse_unit(strict, levels) * rates[..., None, :]
    return (
        precise("nbhce,nbhed->nbhcd", solved, key_rows),
        precise("nbhce,nbhed->nbhcd", solved, value_rows),
    )


def transitions(weight_rows, update_rows, key_rows, tail_rows, whole_rows, unit):
    moves = whole_rows[..., None] * (unit - precise("nbhcd,nbhce->nbhde", weight_rows, key_rows))
    adds = precise("nbhcv,nbhck->nbhvk", update_rows * tail_rows[..., None], key_rows)

    def transitions_advance(carry, item):
        current_map, current_bias = carry
        block_map, block_bias = item
        return (
            (
                precise("bhij,bhjk->bhik", current_map, block_map),
                precise("bhij,bhjk->bhik", current_bias, block_map) + block_bias,
            ),
            None,
        )

    shape = moves.shape[1:]
    initial = (jnp.broadcast_to(unit, shape), jnp.zeros(shape, jnp.float32))
    return lax.scan(transitions_advance, initial, (moves, adds))[0]


def outputs(
    queries,
    key_rows,
    weight_rows,
    update_rows,
    state,
    first_rows,
    tail_rows,
    masks,
    whole_rows,
    scale,
):

    def outputs_advance(carry, item):
        query_blk, key_blk, weight_blk, update_blk, first_blk, tail_blk, mask_blk, whole_blk = item
        fresh = update_blk - first_blk[..., None] * precise("bhcd,bhvd->bhcv", weight_blk, carry)
        inner = precise("bhcd,bhed->bhce", query_blk, key_blk) * mask_blk
        result = scale * (
            first_blk[..., None] * precise("bhcd,bhvd->bhcv", query_blk, carry)
            + precise("bhce,bhev->bhcv", inner, fresh)
        )
        carry = whole_blk[..., None] * carry + precise(
            "bhcv,bhck->bhvk", fresh * tail_blk[..., None], key_blk
        )
        return (carry, result)

    final_state, results = lax.scan(
        outputs_advance,
        state,
        (queries, key_rows, weight_rows, update_rows, first_rows, tail_rows, masks, whole_rows),
    )
    return (results, final_state)


def shards(
    hidden_in,
    attn_gain,
    query_weight,
    key_weight,
    value_weight,
    conv_weight,
    beta_weight,
    out_gain,
    out_weight,
    ffn_gain,
    gate_weight,
    up_weight,
    down_weight,
    cotangent,
    segment_ids,
):
    gathered = (
        lax.all_gather(attn_gain, "shard", axis=0, tiled=True),
        lax.all_gather(query_weight, "shard", axis=0, tiled=True),
        lax.all_gather(key_weight, "shard", axis=0, tiled=True),
        lax.all_gather(value_weight, "shard", axis=0, tiled=True),
        lax.all_gather(conv_weight, "shard", axis=3, tiled=True),
        lax.all_gather(beta_weight, "shard", axis=0, tiled=True),
        lax.all_gather(out_gain, "shard", axis=0, tiled=True),
        lax.all_gather(out_weight, "shard", axis=1, tiled=True),
        lax.all_gather(ffn_gain, "shard", axis=0, tiled=True),
        lax.all_gather(gate_weight, "shard", axis=0, tiled=True),
        lax.all_gather(up_weight, "shard", axis=0, tiled=True),
        lax.all_gather(down_weight, "shard", axis=1, tiled=True),
    )
    gain_in = gathered[0].astype(jnp.float32)
    joint_weight = jnp.concatenate([gathered[1], gathered[2], gathered[3]], axis=1)
    conv_full = gathered[4].astype(jnp.float32)
    rate_weight = gathered[5]
    gain_head = gathered[6].astype(jnp.float32)
    mixer_weight = gathered[7]
    gain_ffn = gathered[8].astype(jnp.float32)
    gate_full = gathered[9]
    up_full = gathered[10]
    down_full = gathered[11]
    micro_count, seq_local, tokens, width = hidden_in.shape
    seq_count = micro_count * seq_local
    taps, triple, heads_here, head_size = conv_full.shape
    local_width = heads_here * head_size
    conv_taps = conv_full.reshape(taps, 3 * local_width)
    margin = taps - 1
    block_size = BLOCK
    block_count = tokens // block_size
    levels = block_size.bit_length() - 1
    scale = head_size ** (-0.5)
    place = lax.axis_index("ctx") * tokens + jnp.arange(tokens, dtype=jnp.int32)
    lower_incl = jnp.tril(jnp.ones((block_size, block_size), jnp.float32))
    unit = jnp.eye(head_size, dtype=jnp.float32)
    state_shape = (seq_count, heads_here, head_size, head_size)
    neutral = (jnp.broadcast_to(unit, state_shape), jnp.zeros(state_shape, jnp.float32))
    hidden = hidden_in.reshape(seq_count, tokens, width).astype(jnp.float32)
    documents = segment_ids.reshape(seq_count, tokens)
    normed_in, norm_pull = jax.vjp(rms_scale, hidden, gain_in)
    normed_low = normed_in.astype(jnp.bfloat16)
    raw = jnp.einsum(
        "btd,de->bte", normed_low, joint_weight, preferred_element_type=jnp.float32
    ).astype(jnp.bfloat16)
    rate_logit = jnp.einsum(
        "btd,dh->bth", normed_low, rate_weight, preferred_element_type=jnp.float32
    )
    rates = jax.nn.sigmoid(rate_logit)
    prev_raw, prev_ids = passed_along(
        (raw[:, tokens - margin :], documents[:, tokens - margin :].astype(jnp.bfloat16)), "ctx", 1
    )
    doc_float = documents.astype(jnp.float32)
    ext_ids = jnp.concatenate([prev_ids.astype(jnp.float32), doc_float], axis=1)
    before = ext_ids[:, margin - 1 : margin - 1 + tokens]
    starts = jnp.where((place == 0)[None, :] | (before != doc_float), 1.0, 0.0).astype(jnp.float32)
    ext_raw = jnp.concatenate([prev_raw, raw], axis=1).astype(jnp.float32)
    links = [
        (ext_ids[:, tap_index : tap_index + tokens] == doc_float).astype(jnp.float32)
        for tap_index in range(taps)
    ]

    def conv_act(extended, tap_weights):
        total = jnp.zeros((seq_count, tokens, 3 * local_width), jnp.float32)
        for tap_index in range(taps):
            total = (
                total
                + tap_weights[tap_index]
                * extended[:, tap_index : tap_index + tokens]
                * links[tap_index][..., None]
            )
        active = jax.nn.silu(total)
        shape = (seq_count, tokens, heads_here, head_size)
        return (
            unit_rows(active[..., :local_width].reshape(shape)),
            unit_rows(active[..., local_width : 2 * local_width].reshape(shape)),
            active[..., 2 * local_width :].reshape(shape),
        )

    (query_act, key_act, value_act), conv_pull = jax.vjp(conv_act, ext_raw, conv_taps)
    query_blocks = to_blocks(round_trip(query_act), block_count, block_size)
    key_blocks = to_blocks(round_trip(key_act), block_count, block_size)
    value_blocks = to_blocks(round_trip(value_act), block_count, block_size)
    rate_blocks = rates.reshape(seq_count, block_count, block_size, heads_here).transpose(
        1, 0, 3, 2
    )
    start_blocks = starts.reshape(seq_count, block_count, block_size).transpose(1, 0, 2)
    groups = jnp.cumsum(start_blocks, axis=-1)
    first_rows = (groups == 0).astype(jnp.float32)[:, :, None, :]
    tail_rows = (groups == groups[..., -1:]).astype(jnp.float32)[:, :, None, :]
    whole_rows = first_rows[..., -1:]
    same_doc = (groups[..., :, None] == groups[..., None, :]).astype(jnp.float32)[:, :, None]
    masks = same_doc * lower_incl

    def run_prepare(key_rows, value_rows, rate_rows):
        return prepare(key_rows, value_rows, rate_rows, same_doc, levels)

    (weight_rows, update_rows), prep_pull = jax.vjp(
        run_prepare, key_blocks, value_blocks, rate_blocks
    )
    piece_map, piece_bias = transitions(
        weight_rows, update_rows, key_blocks, tail_rows, whole_rows, unit
    )
    prefix_map, incoming = carried_in((piece_map, piece_bias), "ctx", compose, neutral)

    def run_outputs(queries, key_rows, weights_in, updates_in, state):
        return outputs(
            queries,
            key_rows,
            weights_in,
            updates_in,
            state,
            first_rows,
            tail_rows,
            masks,
            whole_rows,
            scale,
        )

    (mixed_blocks, final_state), out_pull = jax.vjp(
        run_outputs, query_blocks, key_blocks, weight_rows, update_rows, incoming
    )
    mixed = from_blocks(mixed_blocks)
    head_normed, head_pull = jax.vjp(rms_scale, mixed, gain_head)
    head_low = head_normed.astype(jnp.bfloat16).reshape(seq_count, tokens, local_width)
    mixer_part = jnp.einsum(
        "bte,ed->btd", head_low, mixer_weight, preferred_element_type=jnp.float32
    )
    resid = hidden + lax.psum(mixer_part.astype(jnp.bfloat16), "tp").astype(jnp.float32)
    normed_ffn, ffn_pull = jax.vjp(rms_scale, resid, gain_ffn)
    ffn_low = normed_ffn.astype(jnp.bfloat16)
    gate = jnp.einsum("btd,df->btf", ffn_low, gate_full, preferred_element_type=jnp.float32)
    upward = jnp.einsum("btd,df->btf", ffn_low, up_full, preferred_element_type=jnp.float32)
    act_low = (jax.nn.silu(gate) * upward).astype(jnp.bfloat16)
    ffn_part = jnp.einsum("btf,fd->btd", act_low, down_full, preferred_element_type=jnp.float32)
    result_rows = (
        resid + lax.psum(ffn_part.astype(jnp.bfloat16), "tp").astype(jnp.float32)
    ).astype(jnp.bfloat16)
    grad_low = cotangent.reshape(seq_count, tokens, width)
    grad_out = grad_low.astype(jnp.float32)
    sum_down = jnp.einsum("btf,btd->fd", act_low, grad_low, preferred_element_type=jnp.float32)
    d_gate_in = round_trip(
        jnp.einsum("btd,fd->btf", grad_low, down_full, preferred_element_type=jnp.float32)
    )
    sigma = jax.nn.sigmoid(gate)
    d_gate = (d_gate_in * upward * sigma * (1.0 + gate * (1.0 - sigma))).astype(jnp.bfloat16)
    d_up = (d_gate_in * gate * sigma).astype(jnp.bfloat16)
    sum_gate = jnp.einsum("btd,btf->df", ffn_low, d_gate, preferred_element_type=jnp.float32)
    sum_up = jnp.einsum("btd,btf->df", ffn_low, d_up, preferred_element_type=jnp.float32)
    d_ffn = jnp.einsum(
        "btf,df->btd", d_gate, gate_full, preferred_element_type=jnp.float32
    ) + jnp.einsum("btf,df->btd", d_up, up_full, preferred_element_type=jnp.float32)
    d_ffn = lax.psum(d_ffn.astype(jnp.bfloat16), "tp").astype(jnp.float32)
    d_resid, sum_ffn_gain = ffn_pull(d_ffn)
    d_resid = grad_out + d_resid
    resid_low = d_resid.astype(jnp.bfloat16)
    sum_mixer = jnp.einsum("bte,btd->ed", head_low, resid_low, preferred_element_type=jnp.float32)
    d_head = round_trip(
        jnp.einsum("btd,ed->bte", resid_low, mixer_weight, preferred_element_type=jnp.float32)
    )
    d_mixed, d_gain_head = head_pull(d_head.reshape(seq_count, tokens, heads_here, head_size))
    d_mixed_blocks = to_blocks(d_mixed, block_count, block_size)
    dq_one, dk_one, dw_one, du_one, d_incoming = out_pull(
        (d_mixed_blocks, jnp.zeros_like(final_state))
    )
    suffix_map, d_final = prefix(
        (jnp.swapaxes(piece_map, -1, -2), d_incoming), "ctx", compose, neutral
    )
    dq_two, dk_two, dw_two, du_two, unused_state = out_pull((jnp.zeros_like(mixed_blocks), d_final))
    dk_three, dv_blocks, d_rates = prep_pull((dw_one + dw_two, du_one + du_two))
    d_query = round_trip(from_blocks(dq_one + dq_two))
    d_key = round_trip(from_blocks(dk_one + dk_two + dk_three))
    d_value = round_trip(from_blocks(dv_blocks))
    d_ext, sum_conv = conv_pull((d_query, d_key, d_value))
    back_edge = passed_along(d_ext[:, :margin].astype(jnp.bfloat16), "ctx", -1).astype(jnp.float32)
    d_raw = d_ext[:, margin:].at[:, tokens - margin :].add(back_edge)
    d_raw_low = d_raw.astype(jnp.bfloat16)
    d_rate_rows = d_rates.transpose(1, 0, 3, 2).reshape(seq_count, tokens, heads_here)
    d_logit = (d_rate_rows * rates * (1.0 - rates)).astype(jnp.bfloat16)
    sum_joint = jnp.einsum("btd,bte->de", normed_low, d_raw_low, preferred_element_type=jnp.float32)
    sum_rate = jnp.einsum("btd,bth->dh", normed_low, d_logit, preferred_element_type=jnp.float32)
    d_normed = jnp.einsum(
        "bte,de->btd", d_raw_low, joint_weight, preferred_element_type=jnp.float32
    ) + jnp.einsum("bth,dh->btd", d_logit, rate_weight, preferred_element_type=jnp.float32)
    d_normed, sum_head_gain = (
        lax.psum(d_normed.astype(jnp.bfloat16), "tp").astype(jnp.float32),
        lax.psum(d_gain_head.astype(jnp.bfloat16), "tp").astype(jnp.float32),
    )
    d_hidden, sum_attn_gain = norm_pull(d_normed)
    input_rows = (d_resid + d_hidden).astype(jnp.bfloat16)
    grad_query = sum_joint[:, :local_width]
    grad_key = sum_joint[:, local_width : 2 * local_width]
    grad_value = sum_joint[:, 2 * local_width :]
    grad_conv = sum_conv.reshape(taps, triple, heads_here, head_size)
    parts = (
        lax.psum_scatter(
            sum_attn_gain.astype(jnp.bfloat16), "shard", scatter_dimension=0, tiled=True
        ).astype(jnp.float32),
        lax.psum_scatter(
            grad_query.astype(jnp.bfloat16), "shard", scatter_dimension=0, tiled=True
        ).astype(jnp.float32),
        lax.psum_scatter(
            grad_key.astype(jnp.bfloat16), "shard", scatter_dimension=0, tiled=True
        ).astype(jnp.float32),
        lax.psum_scatter(
            grad_value.astype(jnp.bfloat16), "shard", scatter_dimension=0, tiled=True
        ).astype(jnp.float32),
        lax.psum_scatter(
            grad_conv.astype(jnp.bfloat16), "shard", scatter_dimension=3, tiled=True
        ).astype(jnp.float32),
        lax.psum_scatter(
            sum_rate.astype(jnp.bfloat16), "shard", scatter_dimension=0, tiled=True
        ).astype(jnp.float32),
        lax.psum_scatter(
            sum_head_gain.astype(jnp.bfloat16), "shard", scatter_dimension=0, tiled=True
        ).astype(jnp.float32),
        lax.psum_scatter(
            sum_mixer.astype(jnp.bfloat16), "shard", scatter_dimension=1, tiled=True
        ).astype(jnp.float32),
        lax.psum_scatter(
            sum_ffn_gain.astype(jnp.bfloat16), "shard", scatter_dimension=0, tiled=True
        ).astype(jnp.float32),
        lax.psum_scatter(
            sum_gate.astype(jnp.bfloat16), "shard", scatter_dimension=0, tiled=True
        ).astype(jnp.float32),
        lax.psum_scatter(
            sum_up.astype(jnp.bfloat16), "shard", scatter_dimension=0, tiled=True
        ).astype(jnp.float32),
        lax.psum_scatter(
            sum_down.astype(jnp.bfloat16), "shard", scatter_dimension=1, tiled=True
        ).astype(jnp.float32),
    )
    parts = (
        lax.psum(parts[0].astype(jnp.bfloat16), "ctx").astype(jnp.float32),
        lax.psum(parts[1].astype(jnp.bfloat16), "ctx").astype(jnp.float32),
        lax.psum(parts[2].astype(jnp.bfloat16), "ctx").astype(jnp.float32),
        lax.psum(parts[3].astype(jnp.bfloat16), "ctx").astype(jnp.float32),
        lax.psum(parts[4].astype(jnp.bfloat16), "ctx").astype(jnp.float32),
        lax.psum(parts[5].astype(jnp.bfloat16), "ctx").astype(jnp.float32),
        lax.psum(parts[6].astype(jnp.bfloat16), "ctx").astype(jnp.float32),
        lax.psum(parts[7].astype(jnp.bfloat16), "ctx").astype(jnp.float32),
        lax.psum(parts[8].astype(jnp.bfloat16), "ctx").astype(jnp.float32),
        lax.psum(parts[9].astype(jnp.bfloat16), "ctx").astype(jnp.float32),
        lax.psum(parts[10].astype(jnp.bfloat16), "ctx").astype(jnp.float32),
        lax.psum(parts[11].astype(jnp.bfloat16), "ctx").astype(jnp.float32),
    )
    out_shape = (micro_count, seq_local, tokens, width)
    return (
        result_rows.reshape(out_shape),
        input_rows.reshape(out_shape),
        parts[0],
        parts[1],
        parts[2],
        parts[3],
        parts[4],
        parts[5],
        parts[6],
        parts[7],
        parts[8],
        parts[9],
        parts[10],
        parts[11],
    )


def solution(mesh):
    return jax.shard_map(
        shards,
        mesh=mesh,
        in_specs=(
            P(None, "shard", "ctx", None),
            P("shard"),
            P("shard", "tp"),
            P("shard", "tp"),
            P("shard", "tp"),
            P(None, None, "tp", "shard"),
            P("shard", "tp"),
            P("shard"),
            P("tp", "shard"),
            P("shard"),
            P("shard", "tp"),
            P("shard", "tp"),
            P("tp", "shard"),
            P(None, "shard", "ctx", None),
            P(None, "shard", "ctx"),
        ),
        out_specs=(
            P(None, "shard", "ctx", None),
            P(None, "shard", "ctx", None),
            P("shard"),
            P("shard", "tp"),
            P("shard", "tp"),
            P("shard", "tp"),
            P(None, None, "tp", "shard"),
            P("shard", "tp"),
            P("shard"),
            P("tp", "shard"),
            P("shard"),
            P("shard", "tp"),
            P("shard", "tp"),
            P("tp", "shard"),
        ),
        check_vma=False,
    )
```

profile of v0, /device:TPU:0, one launch (start us, length us, event | category | flops | bytes accessed | tf_op | source)
XLA Modules:
  0.0 2995.5 jit_solution(13722143249631645663)
XLA Ops:
  12.0 12.9 all-gather.4
  25.1 19.3 all_gather.60
  44.7 13.3 all_gather.65
  63.0 36.9 %all-gather.18.cloned.1.call-done = bf16[2048,1024]{1,0:T(8,128)(2,1)} async-done(((bf16[512,1024]{1,0:T(8,128)(2,1)}), bf16[2048,1024]{1,0:T(8,128)(2,1)}) %all-gather.18.cloned.1.call-update) | async-done | bytes 4194320 | tf_op jit(solution)/shard_map/all_gather | solution.py:195
  99.8 80.9 %all-gather.20.cloned.1.call-done = bf16[2048,1024]{1,0:T(8,128)(2,1)} async-done(((bf16[512,1024]{1,0:T(8,128)(2,1)}), bf16[2048,1024]{1,0:T(8,128)(2,1)}) %all-gather.20.cloned.1.call-update) | async-done | bytes 4194320 | tf_op jit(solution)/shard_map/all_gather | solution.py:196
  180.7 80.9 %all-gather.22.cloned.1.call-done = bf16[2048,1024]{1,0:T(8,128)(2,1)} async-done(((bf16[512,1024]{1,0:T(8,128)(2,1)}), bf16[2048,1024]{1,0:T(8,128)(2,1)}) %all-gather.22.cloned.1.call-update) | async-done | bytes 4194320 | tf_op jit(solution)/shard_map/all_gather | solution.py:197
  261.6 13.1 fusion.192
  282.4 6.6 fusion.179
  296.6 5.2 fusion.342
  304.6 5.7 fusion.361
  313.4 5.7 fusion.362
  322.0 5.7 fusion.363
  330.6 5.8 fusion.364
  364.7 5.3 subtract_multiply_fusion.1
  370.1 26.7 while.127
  401.2 9.5 all-reduce.11
  420.7 24.0 all-gather.34.cloned.1.call-done
  444.7 22.4 while.128
  473.4 64.7 %while.125 = (s32[]{:T(128)}, f32[2,8,128,128]{3,2,1,0:T(8,128)S(1)}, f32[4,2,8,64,128]{4,3,2,1,0:T(8,128)}, f32[4,2,8,128,128]{4,3,2,1,0:T(8,128)}, f32[4,2,1,6...) while((s32[]{:T(128)}, ...), condition=%wide.region_9.10_spmd.clone, body=%wide.region_8.9_spmd.sunk.clone | while | flops 806813696 | bytes 25312004 | solution.py:168
  556.2 6.5 fusion.211
  564.9 11.9 all-gather.5
  576.8 49.0 %all-reduce.24.cloned.1.call-done = bf16[2,256,2048]{2,1,0:T(8,128)(2,1)} async-done(((bf16[2,256,2048]{2,1,0:T(8,128)(2,1)}), bf16[2,256,2048]{2,1,0:T(8,128)(2,1)}) %all-reduce.24.cloned.1.call-update) | async-done | bytes 2097168 | tf_op jit(solution)/shard_map/psum | solution.py:322
  631.6 196.9 %all-gather.30.cloned.1.call-done = bf16[2816,2048]{1,0:T(8,128)(2,1)} async-done(((bf16[2816,512]{1,0:T(8,128)(2,1)}), bf16[2816,2048]{1,0:T(8,128)(2,1)}) %all-gather.30.cloned.1.call-update) | async-done | bytes 11534352 | tf_op jit(solution)/shard_map/all_gather | solution.py:205
  828.5 12.1 fusion.189
  840.6 188.8 %all-gather.26.cloned.1.call-done = bf16[2048,2816]{1,0:T(8,128)(2,1)} async-done(((bf16[512,2816]{1,0:T(8,128)(2,1)}), bf16[2048,2816]{1,0:T(8,128)(2,1)}) %all-gather.26.cloned.1.call-update) | async-done | bytes 11534352 | tf_op jit(solution)/shard_map/all_gather | solution.py:203
  1029.4 12.5 fusion.173
  1041.9 188.3 %all-gather.28.cloned.1.call-done = bf16[2048,2816]{1,0:T(8,128)(2,1)} async-done(((bf16[512,2816]{1,0:T(8,128)(2,1)}), bf16[2048,2816]{1,0:T(8,128)(2,1)}) %all-gather.28.cloned.1.call-update) | async-done | bytes 11534352 | tf_op jit(solution)/shard_map/all_gather | solution.py:204
  1230.2 13.0 fusion.167
  1243.2 14.2 fusion.182
  1259.0 9.4 add_convert_fusion.1
  1270.6 59.1 %all-reduce.26.cloned.1.call-done = bf16[2,256,2048]{2,1,0:T(8,128)(2,1)} async-done(((bf16[2,256,2048]{2,1,0:T(8,128)(2,1)}), bf16[2,256,2048]{2,1,0:T(8,128)(2,1)}) %all-reduce.26.cloned.1.call-update) | async-done | bytes 2097168 | tf_op jit(solution)/shard_map/psum | solution.py:346
  1329.7 5.4 fusion.195
  1353.2 90.2 %while.129 = (s32[]{:T(128)}, f32[2,8,128,128]{3,2,1,0:T(8,128)S(1)}, f32[4,2,8,64,128]{4,2,3,0,1:T(8,128)}, f32[4,2,8,64,128]{4,3,2,1,0:T(8,128)}, f32[4,2,8,64...) while((s32[]{:T(128)}, ...), condition=%wide.region_18.19_spmd.clone.clone, body=%wide.region_17.18_spmd.clone.sunk.clone | while | flops 1613824128 | bytes 59621748 | solution.py:168
  1444.7 6.6 bitcast_convert_fusion.4
  1451.4 15.6 all-gather.38.cloned.1.call-done
  1467.0 22.3 while.130
  1497.1 81.7 %while.126 = (s32[]{:T(128)}, f32[2,8,128,128]{3,2,1,0:T(8,128)S(1)}, f32[4,2,8,64,128]{4,2,3,0,1:T(8,128)}, f32[4,2,8,64,128]{4,3,2,1,0:T(8,128)}, f32[4,2,8,64...) while((s32[]{:T(128)}, ...), condition=%wide.region_22.23_spmd.clone, body=%wide.region_21.22_spmd.sunk.clone | while | flops 1612513408 | bytes 47033120 | solution.py:168
  1578.9 6.5 fusion.277
  1667.2 8.2 fusion.280
  1699.6 16.7 multiply_reduce_fusion.3
  1716.4 5.9 multiply_multiply_fusion.3
  1722.2 7.8 pad_add_fusion
  1732.4 5.3 slice.148
  1740.3 9.1 bitcast_convert_fusion
  1749.4 4.8 fusion.356
  1755.4 11.4 bitcast_convert_fusion.3
  1766.9 12.9 bitcast_convert_fusion.2
  1779.9 11.1 bitcast_convert_fusion.1
  1791.1 11.0 fusion.208
  1806.6 12.4 add_convert_fusion
  1820.4 12.6 reduce-scatter.12.cloned.1.call-done
  1833.0 80.0 %reduce-scatter.14.cloned.1.call-done = bf16[512,1024]{1,0:T(8,128)(2,1)} async-done(((bf16[2048,1024]{1,0:T(8,128)(2,1)}), bf16[512,1024]{1,0:T(8,128)(2,1)}) %reduce-scatter.14.cloned.1.call-update) | async-done | bytes 1048592 | tf_op jit(solution)/shard_map/reduce_scatter | solution.py:395
  1913.0 80.1 %reduce-scatter.16.cloned.1.call-done = bf16[512,1024]{1,0:T(8,128)(2,1)} async-done(((bf16[2048,1024]{1,0:T(8,128)(2,1)}), bf16[512,1024]{1,0:T(8,128)(2,1)}) %reduce-scatter.16.cloned.1.call-update) | async-done | bytes 1048592 | tf_op jit(solution)/shard_map/reduce_scatter | solution.py:398
  1993.1 197.7 %reduce-scatter.22.cloned.1.call-done = bf16[512,2816]{1,0:T(8,128)(2,1)} async-done(((bf16[2048,2816]{1,0:T(8,128)(2,1)}), bf16[512,2816]{1,0:T(8,128)(2,1)}) %reduce-scatter.22.cloned.1.call-update) | async-done | bytes 2883600 | tf_op jit(solution)/shard_map/reduce_scatter | solution.py:416
  2190.8 198.4 %reduce-scatter.24.cloned.1.call-done = bf16[512,2816]{1,0:T(8,128)(2,1)} async-done(((bf16[2048,2816]{1,0:T(8,128)(2,1)}), bf16[512,2816]{1,0:T(8,128)(2,1)}) %reduce-scatter.24.cloned.1.call-update) | async-done | bytes 2883600 | tf_op jit(solution)/shard_map/reduce_scatter | solution.py:419
  2389.2 198.2 %reduce-scatter.26.cloned.1.call-done = bf16[2816,512]{1,0:T(8,128)(2,1)} async-done(((bf16[2816,2048]{1,0:T(8,128)(2,1)}), bf16[2816,512]{1,0:T(8,128)(2,1)}) %reduce-scatter.26.cloned.1.call-update) | async-done | bytes 2883600 | tf_op jit(solution)/shard_map/reduce_scatter | solution.py:422
  2590.8 19.4 reduce-scatter.28.cloned.1.call-done
  2611.2 109.2 %all-reduce.30.cloned.1.call-done = (bf16[2,256,2048]{2,1,0:T(8,128)(2,1)}, bf16[2,256,2048]{2,1,0:T(8,128)(2,1)}) async-done(((bf16[2,256,2048]{2,1,0:T(8,128)(2,1)}, bf16[2,256,2048]{2,1,0:T(8,128)(2,1)}), (bf16[2,256,2048]{2,1,0:T(8,128)(2,1)}, bf16[2,256,2048]{2,1,0:T(8,128)(2,1)})) %all-reduce.30.cloned.1.call-update) | async-done | bytes 4194320 | tf_op jit(solution)/shard_map/psum | solution.py:330
  2723.7 12.1 all-reduce.17
  2736.0 4.9 psum.136
  2742.2 11.7 all-reduce.15
  2756.9 8.0 fusion.219
  2764.9 206.0 %all-reduce.28.cloned.1.call-done = (bf16[512,1024]{1,0:T(8,128)(2,1)}, bf16[512,1024]{1,0:T(8,128)(2,1)}, bf16[512,1024]{1,0:T(8,128)(2,1)}, bf16[1024,512]{1,0...) async-done(((bf16[512,1024]{1,0:T(8,128)(2,1)}, bf16[512,1024]{1,0:T(8,128)(2,1)}, bf16[512,1024]{1,0:T(8,128)(2,1)}, ...) | async-done | bytes 12845072 | tf_op jit(solution)/shard_map/psum | solution.py:428
  2970.9 4.9 convert_element_type.452
  (810 shorter events, 588.8 us)
Async XLA Ops:
  7.2 17.8 copy-start.117
  7.2 37.4 %copy-start.126 = (bf16[512,8]{0,1:T(8,128)(2,1)S(1)}, bf16[512,8]{0,1:T(8,128)(2,1)}, u32[]{:S(2)}) copy-start(bf16[512,8]{0,1:T(8,128)(2,1)} %param.35) | copy-start | bytes 24580
  7.2 50.7 %copy-start.9 = (bf16[2,1,256,2048]{3,2,1,0:T(8,128)(2,1)S(1)}, bf16[2,1,256,2048]{3,2,1,0:T(8,128)(2,1)}, u32[]{:S(2)}) copy-start(bf16[2,1,256,2048]{3,2,1,0:T(8,128)(2,1)} %param.29) | copy-start | bytes 6291460
  7.2 92.6 %all-gather.18.cloned.1.call-start = ((), (), s32[]{:S(2)}) async-start(), calls=%async_computation.9 | async-start | bytes 5242880 | tf_op jit(solution)/shard_map/all_gather | solution.py:195
  8.0 172.8 %all-gather.20.cloned.1.call-start = ((), (), s32[]{:S(2)}) async-start(), calls=%async_computation.10 | async-start | bytes 5242880 | tf_op jit(solution)/shard_map/all_gather | solution.py:196
  8.7 252.9 %all-gather.22.cloned.1.call-start = ((), (), s32[]{:S(2)}) async-start(), calls=%async_computation.11 | async-start | bytes 5242880 | tf_op jit(solution)/shard_map/all_gather | solution.py:197
  9.4 411.3 %all-gather.32.cloned.1.call-start = ((), (), s32[]{:S(2)}) async-start(), calls=%async_computation.26 | async-start | bytes 2621440 | tf_op jit(solution)/shard_map/all_gather | solution.py:22
  9.6 51.1 %collective-permute-start = (bf16[2,3]{1,0:T(2,128)(2,1)S(1)}, bf16[2,3]{1,0:T(2,128)(2,1)S(1)}, u32[]{:S(2)}, u32[]{:S(2)}) collective-permute-start(bf16[2,3]{1,0:T(2,128)(2,1)S(1)} %slice.129), channel_id=1, source_target_pairs={{0,2},{2,4},{4,6},{1,3},{3,5},{5,7},{8,10},{10,12},{12,14},{9,11},... | collective-permute-start | bytes 44 | tf_op jit(solution)/shard_map/ppermute | solution.py:16
  24.9 236.7 %copy-start.100 = (f32[4,1,512]{2,1,0:T(1,128)}, f32[4,1,512]{2,1,0:T(1,128)S(1)}, u32[]{:S(2)}) copy-start(f32[4,1,512]{2,1,0:T(1,128)S(1)} %convert_element_type.461) | copy-start | bytes 24580
  58.5 203.2 %copy-start.118 = (f32[2,256]{1,0:T(2,128)}, f32[2,256]{1,0:T(2,128)S(1)}, u32[]{:S(2)}) copy-start(f32[2,256]{1,0:T(2,128)S(1)} %fusion.338) | copy-start | bytes 6148
  59.8 299.4 %copy-start.63 = (f32[2,4,64,8]{2,3,0,1:T(8,128)}, f32[2,4,64,8]{2,3,0,1:T(8,128)S(1)}, u32[]{:S(2)}) copy-start(f32[2,4,64,8]{2,3,0,1:T(8,128)S(1)} %copy.828) | copy-start | bytes 49156
  60.6 278.6 %copy-start.80 = (pred[64,64]{0,1:T(8,128)(4,1)}, pred[64,64]{0,1:T(8,128)(4,1)S(1)}, u32[]{:S(2)}) copy-start(pred[64,64]{0,1:T(8,128)(4,1)S(1)} %get-tuple-element.2091) | copy-start | bytes 12292
  60.6 293.6 %copy-start.65 = (f32[64,64]{0,1:T(8,128)}, f32[64,64]{0,1:T(8,128)S(1)}, u32[]{:S(2)}) copy-start(f32[64,64]{0,1:T(8,128)S(1)} %get-tuple-element.2092) | copy-start | bytes 49156
  60.7 221.7 %copy-start.92 = (f32[3072]{0:T(1024)}, f32[3072]{0:T(1024)S(1)}, u32[]{:S(2)}) copy-start(f32[3072]{0:T(1024)S(1)} %get-tuple-element.2072) | copy-start | bytes 36868
  60.7 221.7 %copy-start.94 = (f32[3072]{0:T(1024)}, f32[3072]{0:T(1024)S(1)}, u32[]{:S(2)}) copy-start(f32[3072]{0:T(1024)S(1)} %get-tuple-element.2073) | copy-start | bytes 36868
  60.7 221.7 %copy-start.96 = (f32[3072]{0:T(1024)}, f32[3072]{0:T(1024)S(1)}, u32[]{:S(2)}) copy-start(f32[3072]{0:T(1024)S(1)} %get-tuple-element.2074) | copy-start | bytes 36868
  60.7 221.7 %copy-start.98 = (f32[3072]{0:T(1024)}, f32[3072]{0:T(1024)S(1)}, u32[]{:S(2)}) copy-start(f32[3072]{0:T(1024)S(1)} %get-tuple-element.2075) | copy-start | bytes 36868
  62.2 220.2 %copy-start.109 = (f32[2,256]{1,0:T(2,128)}, f32[2,256]{1,0:T(2,128)S(1)}, u32[]{:S(2)}) copy-start(f32[2,256]{1,0:T(2,128)S(1)} %get-tuple-element.2079) | copy-start | bytes 6148
  62.2 220.2 %copy-start.111 = (f32[2,256]{1,0:T(2,128)}, f32[2,256]{1,0:T(2,128)S(1)}, u32[]{:S(2)}) copy-start(f32[2,256]{1,0:T(2,128)S(1)} %get-tuple-element.2080) | copy-start | bytes 6148
  62.2 220.2 %copy-start.113 = (f32[2,256]{1,0:T(2,128)}, f32[2,256]{1,0:T(2,128)S(1)}, u32[]{:S(2)}) copy-start(f32[2,256]{1,0:T(2,128)S(1)} %get-tuple-element.2081) | copy-start | bytes 6148
  62.2 220.2 %copy-start.115 = (f32[2,256]{1,0:T(2,128)}, f32[2,256]{1,0:T(2,128)S(1)}, u32[]{:S(2)}) copy-start(f32[2,256]{1,0:T(2,128)S(1)} %get-tuple-element.2082) | copy-start | bytes 6148
  63.0 276.3 %copy-start.34 = (f32[4,2,64,64]{2,3,1,0:T(8,128)}, f32[4,2,64,64]{2,3,1,0:T(8,128)S(1)}, u32[]{:S(2)}) copy-start(f32[4,2,64,64]{2,3,1,0:T(8,128)S(1)} %compare_convert_fusion) | copy-start | bytes 393220
  275.7 3.8 collective-permute-start.1
  295.9 115.1 %copy-start.15 = (bf16[2,256,8,128]{3,2,1,0:T(8,128)(2,1)}, bf16[2,256,8,128]{3,2,1,0:T(8,128)(2,1)S(1)}, u32[]{:S(2)}) copy-start(bf16[2,256,8,128]{3,2,1,0:T(8,128)(2,1)S(1)} %fusion.223) | copy-start | bytes 3145732
  296.6 42.7 %copy-start.13 = (f32[4,2,8,64,64]{3,4,2,1,0:T(8,128)}, f32[4,2,8,64,64]{3,4,2,1,0:T(8,128)S(1)}, u32[]{:S(2)}) copy-start(f32[4,2,8,64,64]{3,4,2,1,0:T(8,128)S(1)} %fusion.325) | copy-start | bytes 3145732
  336.3 17.9 copy-start.39
  339.2 20.0 copy-start.60
  397.8 12.9 copy-start.108
  397.8 46.9 %all-gather.34.cloned.1.call-start = ((), (), s32[]{:S(2)}) async-start(), calls=%async_computation.27 | async-start | bytes 2621440 | tf_op jit(solution)/shard_map/all_gather | solution.py:22
  398.9 157.3 %all-gather.24.cloned.1.call-start = ((), (), s32[]{:S(2)}) async-start(), calls=%async_computation.12 | async-start | bytes 5242880 | tf_op jit(solution)/shard_map/all_gather | solution.py:201
  399.5 226.2 %all-reduce.24.cloned.1.call-start = ((), (), s32[]{:S(2)}) async-start(), calls=%async_computation.13 | async-start | bytes 4194304 | tf_op jit(solution)/shard_map/psum | solution.py:322
  562.7 265.8 %all-gather.30.cloned.1.call-start = ((), (), s32[]{:S(2)}) async-start(), calls=%async_computation.16 | async-start | bytes 14417920 | tf_op jit(solution)/shard_map/all_gather | solution.py:205
  563.4 465.9 %all-gather.26.cloned.1.call-start = ((), (), s32[]{:S(2)}) async-start(), calls=%async_computation.14 | async-start | bytes 14417920 | tf_op jit(solution)/shard_map/all_gather | solution.py:203
  564.2 666.0 %all-gather.28.cloned.1.call-start = ((), (), s32[]{:S(2)}) async-start(), calls=%async_computation.15 | async-start | bytes 14417920 | tf_op jit(solution)/shard_map/all_gather | solution.py:204
  564.8 764.9 %all-reduce.26.cloned.1.call-start = ((), (), s32[]{:S(2)}) async-start(), calls=%async_computation.17 | async-start | bytes 4194304 | tf_op jit(solution)/shard_map/psum | solution.py:346
  576.7 758.4 %copy-start.83 = (f32[4,1,512]{2,1,0:T(1,128)}, f32[4,1,512]{2,1,0:T(1,128)S(1)}, u32[]{:S(2)}) copy-start(f32[4,1,512]{2,1,0:T(1,128)S(1)} %convert_element_type.462) | copy-start | bytes 24580
  628.8 706.3 %copy-start.104 = (f32[2,256]{1,0:T(2,128)}, f32[2,256]{1,0:T(2,128)S(1)}, u32[]{:S(2)}) copy-start(f32[2,256]{1,0:T(2,128)S(1)} %fusion.339) | copy-start | bytes 6148
  1230.2 13.0 copy-start.74
  1230.2 28.8 slice-start
  1230.2 28.8 slice-start.1
  1243.2 15.8 slice-start.2
  1268.4 183.0 %all-gather.36.cloned.1.call-start = ((), (), s32[]{:S(2)}) async-start(), calls=%async_computation.28 | async-start | bytes 2621440 | tf_op jit(solution)/shard_map/all_gather | solution.py:45
  1270.6 196.5 %all-gather.38.cloned.1.call-start = ((), (), s32[]{:S(2)}) async-start(), calls=%async_computation.29 | async-start | bytes 2621440 | tf_op jit(solution)/shard_map/all_gather | solution.py:45
  1444.3 376.1 %reduce-scatter.20.cloned.1.call-start = ((), (), s32[]{:S(2)}) async-start(), calls=%async_computation.22 | async-start | bytes 5242880 | tf_op jit(solution)/shard_map/reduce_scatter | solution.py:410
  1451.4 381.6 %reduce-scatter.12.cloned.1.call-start = ((), (), s32[]{:S(2)}) async-start(), calls=%async_computation.18 | async-start | bytes 5242880 | tf_op jit(solution)/shard_map/reduce_scatter | solution.py:392
  1497.1 81.7 %copy-start.64 = (f32[2,4,64,8]{2,3,0,1:T(8,128)S(1)}, f32[2,4,64,8]{2,3,0,1:T(8,128)}, u32[]{:S(2)}) copy-start(f32[2,4,64,8]{2,3,0,1:T(8,128)} %copy-done.63) | copy-start | bytes 49156
  1699.6 16.7 copy-start.93
  1699.6 16.7 copy-start.95
  1699.6 16.7 copy-start.97
  1699.6 16.7 copy-start.99
  1731.0 6.8 collective-permute-start.2
  1754.2 158.8 %reduce-scatter.14.cloned.1.call-start = ((), (), s32[]{:S(2)}) async-start(), calls=%async_computation.19 | async-start | bytes 5242880 | tf_op jit(solution)/shard_map/reduce_scatter | solution.py:395
  1754.8 238.3 %reduce-scatter.16.cloned.1.call-start = ((), (), s32[]{:S(2)}) async-start(), calls=%async_computation.20 | async-start | bytes 5242880 | tf_op jit(solution)/shard_map/reduce_scatter | solution.py:398
  1755.4 435.4 %reduce-scatter.22.cloned.1.call-start = ((), (), s32[]{:S(2)}) async-start(), calls=%async_computation.23 | async-start | bytes 14417920 | tf_op jit(solution)/shard_map/reduce_scatter | solution.py:416
  1766.9 622.3 %reduce-scatter.24.cloned.1.call-start = ((), (), s32[]{:S(2)}) async-start(), calls=%async_computation.24 | async-start | bytes 14417920 | tf_op jit(solution)/shard_map/reduce_scatter | solution.py:419
  1779.9 807.5 %reduce-scatter.26.cloned.1.call-start = ((), (), s32[]{:S(2)}) async-start(), calls=%async_computation.25 | async-start | bytes 14417920 | tf_op jit(solution)/shard_map/reduce_scatter | solution.py:422
  1791.0 819.2 %reduce-scatter.28.cloned.1.call-start = ((), (), s32[]{:S(2)}) async-start(), calls=%async_computation.30 | async-start | bytes 40960
  1806.5 913.9 %all-reduce.30.cloned.1.call-start = ((), (), s32[]{:S(2)}) async-start(), calls=%async_computation.32 | async-start | bytes 8388608 | tf_op jit(solution)/shard_map/psum | solution.py:330
  1819.0 923.2 %reduce-scatter.18.cloned.1.call-start = ((), (), s32[]{:S(2)}) async-start(), calls=%async_computation.21 | async-start | bytes 40960 | tf_op jit(solution)/shard_map/reduce_scatter | solution.py:404
  1820.3 1150.6 %all-reduce.28.cloned.1.call-start = ((), (), s32[]{:S(2)}) async-start(), calls=%async_computation.31 | async-start | bytes 25690112 | tf_op jit(solution)/shard_map/psum | solution.py:428
  2720.4 36.4 %copy-start.121 = (f32[2,256]{1,0:T(2,128)S(1)}, f32[2,256]{1,0:T(2,128)}, u32[]{:S(2)}) copy-start(f32[2,256]{1,0:T(2,128)} %copy-done.120) | copy-start | bytes 6148
  2720.4 36.4 %copy-start.84 = (f32[4,1,512]{2,1,0:T(1,128)S(1)}, f32[4,1,512]{2,1,0:T(1,128)}, u32[]{:S(2)}) copy-start(f32[4,1,512]{2,1,0:T(1,128)} %copy-done.83) | copy-start | bytes 24580
  2720.4 36.4 %copy-start.105 = (f32[2,256]{1,0:T(2,128)S(1)}, f32[2,256]{1,0:T(2,128)}, u32[]{:S(2)}) copy-start(f32[2,256]{1,0:T(2,128)} %copy-done.104) | copy-start | bytes 6148
  2720.4 36.4 %copy-start.123 = (f32[2,256]{1,0:T(2,128)S(1)}, f32[2,256]{1,0:T(2,128)}, u32[]{:S(2)}) copy-start(f32[2,256]{1,0:T(2,128)} %copy-done.122) | copy-start | bytes 6148
  (130 other events, 494.7 us)
Sparse Core Ops, SparseCore 0:
  9.6 90.1 all-gather.17
  101.4 79.2 all-gather.19
  182.3 79.2 all-gather.21
  398.0 22.7 all-gather.31
  422.1 22.5 all-gather.33
  446.2 80.7 all-gather.23
  562.8 62.8 all-reduce.23
  627.4 201.0 all-gather.29
  830.1 199.2 all-gather.25
  1030.9 199.2 all-gather.27
  1268.5 61.0 all-reduce.25
  1331.1 22.5 all-gather.35
  1444.4 22.5 all-gather.37
  1469.2 76.7 reduce-scatter.19
  1754.3 78.5 reduce-scatter.11
  1835.7 77.2 reduce-scatter.13
  1915.8 77.2 reduce-scatter.15
  1995.3 195.4 reduce-scatter.21
  2193.2 195.9 reduce-scatter.23
  2391.4 195.9 reduce-scatter.25
  2590.2 19.9 reduce-scatter.27
  2614.0 106.3 all-reduce.29
  2723.2 18.9 reduce-scatter.17
  2745.6 225.2 all-reduce.27
where the time goes:
time: 3010 us; the launch traced here: 3000 us
  waiting for transfers between devices  2030 us (67%)
  matrix products  567 us (19%)
  local copies, waits for them, and re-layouts  154 us (5%)
  other arithmetic  120 us (4%)
  blocking collectives  95.7 us (3%)
    dot_general x157, matrix products, precise(): jnp.einsum(form, left, right, precision=HIGHEST, preferred_element_type=j...  404 us
    psum x1, waiting for transfers between devices, shards(): lax.psum(parts[1].astype(jnp.bfloat16), 'ctx').astype(jnp.float32)  206 us
    reduce_scatter x1, waiting for transfers between devices, shards(): lax.psum_scatter(sum_up.astype(jnp.bfloat16), 'shard', scatter_dimension=...  198 us
    reduce_scatter x1, waiting for transfers between devices, shards(): lax.psum_scatter(sum_down.astype(jnp.bfloat16), 'shard', scatter_dimensio...  198 us
    reduce_scatter x1, waiting for transfers between devices, shards(): lax.psum_scatter(sum_gate.astype(jnp.bfloat16), 'shard', scatter_dimensio...  198 us
    all_gather x1, waiting for transfers between devices, shards(): lax.all_gather(down_weight, 'shard', axis=1, tiled=True)  197 us
    all_gather x1, waiting for transfers between devices, shards(): lax.all_gather(gate_weight, 'shard', axis=0, tiled=True)  189 us
    all_gather x1, waiting for transfers between devices, shards(): lax.all_gather(up_weight, 'shard', axis=0, tiled=True)  188 us
  transfers between devices with their start and end apart: 27, of which 21 were waited for; matrix products, arithmetic and copies ran while one was open for 21% of the time, Pallas kernels for 0%

commit v1 on v0

v1 whole, which is shorter than its diff:
```python
import functools

import jax
import jax.numpy as jnp
from jax import lax
from jax.experimental import pallas as pl
from jax.experimental.pallas import tpu as pltpu
from jax.sharding import Mesh
from jax.sharding import PartitionSpec as P

EPSILON = 1e-06
F32 = jnp.float32
BF16 = jnp.bfloat16
LANES = 128
HALO = 16
SWAP = [(0, 1), (1, 0)]


def mm(left, right, left_dim, right_dim):
    return lax.dot_general(
        left.astype(BF16),
        right.astype(BF16),
        (((left_dim,), (right_dim,)), ((), ())),
        preferred_element_type=F32,
    )


def nn(left, right):
    return mm(left, right, 1, 0)


def nt(left, right):
    return mm(left, right, 1, 1)


def tn(left, right):
    return mm(left, right, 0, 0)


def place_scalars():
    return jnp.stack([lax.axis_index("core"), lax.axis_index("cx")]).astype(jnp.int32)


def call(kernel, grid, in_specs, out_specs, out_shape, scratch=(), flops=0, moved=0):
    return pl.pallas_call(
        kernel,
        grid_spec=pltpu.PrefetchScalarGridSpec(
            num_scalar_prefetch=1,
            grid=grid,
            in_specs=in_specs,
            out_specs=out_specs,
            scratch_shapes=list(scratch),
        ),
        out_shape=out_shape,
        compiler_params=pltpu.CompilerParams(
            dimension_semantics=("arbitrary",) * len(grid), vmem_limit_bytes=48 << 20
        ),
        cost_estimate=pl.CostEstimate(flops=flops, transcendentals=0, bytes_accessed=moved),
    )


def split_rows(places, values, count):
    rows, width = values.shape
    half = width // (2 * count)
    if half % LANES:
        cut = values.reshape(rows, count, 2, half)
        cut = jnp.where(places[1] == 0, cut, cut[:, :, ::-1])
        return cut.transpose(2, 0, 1, 3).reshape(2, rows, width // 2)
    tile = max(t for t in range(16, 400, 16) if rows % t == 0)

    def kernel(where, source, target):
        for side in range(2):
            for shard in range(count):
                at = shard * 2 * half + (where[1] if side == 0 else 1 - where[1]) * half
                target[side, :, shard * half : (shard + 1) * half] = source[
                    :, pl.ds(pl.multiple_of(at, LANES), half)
                ]

    return call(
        kernel,
        (rows // tile,),
        [pl.BlockSpec((tile, width), lambda i, w: (i, 0))],
        pl.BlockSpec((2, tile, width // 2), lambda i, w: (0, i, 0)),
        jax.ShapeDtypeStruct((2, rows, width // 2), values.dtype),
        moved=2 * values.size * values.dtype.itemsize,
    )(places, values)


def join_rows(places, values, count):
    rows, width = values.shape[1], 2 * values.shape[2]
    half = width // (2 * count)
    if half % LANES:
        cut = values.reshape(2, rows, count, half).transpose(1, 2, 0, 3)
        cut = jnp.where(places[1] == 0, cut, cut[:, :, ::-1])
        return cut.reshape(rows, width)
    tile = max(t for t in range(16, 400, 16) if rows % t == 0)

    def kernel(where, source, target):
        for side in range(2):
            for shard in range(count):
                at = shard * 2 * half + (where[1] if side == 0 else 1 - where[1]) * half
                target[:, pl.ds(pl.multiple_of(at, LANES), half)] = source[
                    side, :, shard * half : (shard + 1) * half
                ]

    return call(
        kernel,
        (rows // tile,),
        [pl.BlockSpec((2, tile, width // 2), lambda i, w: (0, i, 0))],
        pl.BlockSpec((tile, width), lambda i, w: (i, 0)),
        jax.ShapeDtypeStruct((rows, width), values.dtype),
        moved=2 * values.size * values.dtype.itemsize,
    )(places, values)


def split_small(places, values, count):
    cut = values.reshape((count, 2, values.shape[0] // (2 * count)) + values.shape[1:])
    cut = jnp.where(places[1] == 0, cut, cut[:, ::-1])
    cut = jnp.swapaxes(cut, 0, 1)
    return cut.reshape((2, values.shape[0] // 2) + values.shape[1:])


def join_small(places, values, count):
    cut = values.reshape((2, count, values.shape[1] // count) + values.shape[2:])
    cut = jnp.swapaxes(cut, 0, 1)
    cut = jnp.where(places[1] == 0, cut, cut[:, ::-1])
    return cut.reshape((2 * values.shape[1],) + values.shape[2:])


def pack_heads(places, query, key, value, heads):
    half = query.shape[0] // 2

    def kernel(where, query_ref, key_ref, value_ref, out):
        out[:, :LANES] = query_ref[...]
        out[:, LANES : 2 * LANES] = key_ref[...]
        out[:, 2 * LANES :] = value_ref[...]

    spec = pl.BlockSpec((half, LANES), lambda h, w: (w[1], w[0] * heads + h))
    return call(
        kernel,
        (heads,),
        [spec] * 3,
        pl.BlockSpec((half, 3 * LANES), lambda h, w: (0, h)),
        jax.ShapeDtypeStruct((half, 3 * LANES * heads), query.dtype),
    )(places, query, key, value)


def own_block(places, weight):
    half, columns = weight.shape[0] // 2, weight.shape[1] // 2
    return lax.dynamic_slice(weight, (places[1] * half, places[0] * columns), (half, columns))


def own_block_turned(places, weight):
    rows, half = weight.shape[0] // 2, weight.shape[1] // 2
    return lax.dynamic_slice(weight, (places[0] * rows, places[1] * half), (rows, half)).T


def pieces_of(own):
    across = lax.ppermute(own, "cx", SWAP)
    return [own, across, lax.ppermute(own, "core", SWAP), lax.ppermute(across, "core", SWAP)]


def pick(where, core, cx, refs, store):
    which = 2 * jnp.bitwise_xor(where[0], core) + jnp.bitwise_xor(where[1], cx)
    for index in range(4):

        @pl.when(which == index)
        def _():
            store(refs[index][...].astype(F32))


def lay_heads(places, pieces, heads):
    half = pieces[0].shape[0]
    width = heads * LANES

    def kernel(where, a, b, c, d, *outs):
        def store(values):
            for head in range(heads):
                for index in range(3):
                    at = (head * 3 + index) * LANES
                    outs[index][:, head * LANES : (head + 1) * LANES] = values[:, at : at + LANES]

        pick(where, pl.program_id(1), pl.program_id(0), (a, b, c, d), store)

    return call(
        kernel,
        (2, 2),
        [pl.BlockSpec(pieces[0].shape, lambda i, j, w: (0, 0))] * 4,
        [pl.BlockSpec((half, width), lambda i, j, w: (i, j))] * 3,
        [jax.ShapeDtypeStruct((2 * half, 2 * width), F32)] * 3,
        moved=10 * pieces[0].size * 4,
    )(places, *pieces)


def lay_block(places, pieces):
    half, columns = pieces[0].shape

    def kernel(where, a, b, c, d, out):
        def store(values):
            out[...] = values

        pick(where, pl.program_id(1), pl.program_id(0), (a, b, c, d), store)

    return call(
        kernel,
        (2, 2),
        [pl.BlockSpec((half, columns), lambda i, j, w: (0, 0))] * 4,
        pl.BlockSpec((half, columns), lambda i, j, w: (i, j)),
        jax.ShapeDtypeStruct((2 * half, 2 * columns), F32),
        moved=6 * pieces[0].size * 4,
    )(places, *pieces)


def lay_block_turned(places, pieces):
    half, rows = pieces[0].shape

    def kernel(where, a, b, c, d, out):
        for side in range(2):

            def store(values):
                out[:, side * half : (side + 1) * half] = values.T

            pick(where, pl.program_id(0), side, (a, b, c, d), store)

    return call(
        kernel,
        (2,),
        [pl.BlockSpec((half, rows), lambda i, w: (0, 0))] * 4,
        pl.BlockSpec((rows, 2 * half), lambda i, w: (i, 0)),
        jax.ShapeDtypeStruct((2 * rows, 2 * half), F32),
        moved=6 * pieces[0].size * 4,
    )(places, *pieces)


def fill_ext(ext, index, halo, first, second, size):
    ext[index, :HALO, :] = halo[...].astype(F32)
    ext[index, HALO : HALO + size, :] = first[...].astype(F32)
    ext[index, HALO + size :, :] = second[...].astype(F32)


def links_of(ids, total):
    own = ids[0, HALO : HALO + total, :]
    return [
        (ids[0, HALO - 3 + tap : HALO - 3 + tap + total, :] == own).astype(F32) for tap in range(4)
    ]


def conv_of(ext, index, taps, links, total):
    result = None
    for tap in range(4):
        term = (
            taps[index, 0, tap : tap + 1, :]
            * ext[index, HALO - 3 + tap : HALO - 3 + tap + total, :]
            * links[tap]
        )
        result = term if result is None else result + term
    return result


def sigmoid(values):
    return 1.0 / (1.0 + jnp.exp(-values))


def column_of(values, head):
    lane = lax.broadcasted_iota(jnp.int32, values.shape, 1)
    return jnp.sum(jnp.where(lane == head, values, 0.0), axis=1, keepdims=True)


def marks(ids, rows, chunk, size):
    start = HALO + chunk * size
    column = ids[0, start : start + size, :]
    before = ids[0, start - 1 : start, :]
    last = ids[0, start + size - 1 : start + size, :]
    first = (column == before).astype(F32)
    tail = (column == last).astype(F32)
    whole = (last == before).astype(F32)
    same = column == rows[0, chunk : chunk + 1, :]
    row = lax.broadcasted_iota(jnp.int32, (size, size), 0)
    col = lax.broadcasted_iota(jnp.int32, (size, size), 1)
    return first, tail, whole, same & (row > col), same & (row >= col)


def inverse_unit(strict, size):
    row = lax.broadcasted_iota(jnp.int32, (size, size), 0)
    col = lax.broadcasted_iota(jnp.int32, (size, size), 1)
    mixed = jnp.bitwise_xor(row, col)
    result = jnp.where(row == col, 1.0, jnp.where(mixed == 1, -strict, 0.0))
    block = 2
    while block < size:
        part = jnp.where((mixed >= block) & (mixed < 2 * block), strict, 0.0).astype(BF16)
        low = result.astype(BF16)
        result = result - nn(low, nn(part, low))
        block *= 2
    return result


def forward_one(where, q0, k0, v0, q1, k1, v1, qh, kh, vh, taps, ids, rows, r0, r1, *rest, size):
    query, key, value, inverse, final, ext = rest
    head = pl.program_id(1)
    total = 2 * size
    for index, group in enumerate(((qh, q0, q1), (kh, k0, k1), (vh, v0, v1))):
        fill_ext(ext, index, *group, size)
    links = links_of(ids, total)
    out = []
    for index in range(3):
        conv = conv_of(ext, index, taps, links, total)
        act = conv * sigmoid(conv)
        if index < 2:
            act = act * lax.rsqrt(jnp.sum(act * act, axis=1, keepdims=True) + EPSILON)
        out.append(act.astype(BF16))
    for target, values in zip((query, key, value), out):
        target[0, 0] = values[:size]
        target[0, 1] = values[size:]
    state = None
    for chunk, rates in enumerate((r0, r1)):
        first, tail, whole, strict, _ = marks(ids, rows, chunk, size)
        rate = column_of(rates[...], head)
        keys = out[1][chunk * size : (chunk + 1) * size]
        fresh = out[2][chunk * size : (chunk + 1) * size].astype(F32)
        inv = inverse_unit(jnp.where(strict, rate * nt(keys, keys), 0.0), size).astype(BF16)
        inverse[0, 0, chunk] = inv
        if chunk:
            fresh = fresh - first * nt(keys, state)
        fresh = nn(inv, rate * fresh)
        added = tn(tail * fresh, keys)
        state = added if state is None else whole * state + added
    final[0, 0] = state.astype(BF16)


def forward_two(where, query, key, value, inverse, ids, rows, r0, r1, incoming, gain, *rest, size, scale):
    head_low, mixed_out, fresh_out, middle = rest
    head = pl.program_id(1)
    state = incoming[0, 0].astype(F32)
    for chunk, rates in enumerate((r0, r1)):
        first, tail, whole, _, lower = marks(ids, rows, chunk, size)
        rate = column_of(rates[...], head)
        keys, queries = key[0, chunk], query[0, chunk]
        if chunk:
            middle[0, 0] = state.astype(BF16)
        rest_rows = value[0, chunk].astype(F32) - first * nt(keys, state)
        fresh = nn(inverse[0, 0, chunk], rate * rest_rows)
        fresh_out[0, chunk] = fresh.astype(BF16)
        inner = jnp.where(lower, nt(queries, keys), 0.0)
        mixed = scale * (first * nt(queries, state) + nn(inner, fresh))
        mixed_out[0, chunk] = mixed
        normed = mixed * lax.rsqrt(jnp.mean(mixed * mixed, axis=1, keepdims=True) + EPSILON)
        slot = where[0] if chunk == 0 else 1 - where[0]
        head_low[slot, 0] = (normed * gain[...]).astype(BF16)
        if chunk == 0:
            state = whole * state + tn(tail * fresh, keys)


def backward_one(where, d_head, mixed, query, key, inverse, ids, rows, r0, r1, gain, *rest, size, scale):
    d_out, d_state_out, d_gain = rest
    head = pl.program_id(1)
    total = jnp.zeros((1, LANES), F32)
    d_state = None
    for chunk in (1, 0):
        first, tail, whole, _, lower = marks(ids, rows, chunk, size)
        rate = column_of((r0, r1)[chunk][...], head)
        keys, queries = key[0, chunk], query[0, chunk]
        slot = where[0] if chunk == 0 else 1 - where[0]
        grad = d_head[slot, 0].astype(F32)
        values = mixed[0, chunk]
        inv_rms = lax.rsqrt(jnp.mean(values * values, axis=1, keepdims=True) + EPSILON)
        normed = values * inv_rms
        total = total + jnp.sum(grad * normed, axis=0, keepdims=True)
        scaled = grad * gain[...]
        d_mixed = inv_rms * (scaled - normed * jnp.mean(scaled * normed, axis=1, keepdims=True))
        d_low = (scale * d_mixed).astype(BF16)
        d_out[0, chunk] = d_low
        inner = jnp.where(lower, nt(queries, keys), 0.0)
        d_fresh = tn(inner, d_low)
        if d_state is not None:
            d_fresh = d_fresh + tail * nt(keys, d_state)
        d_rest = rate * tn(inverse[0, 0, chunk], d_fresh)
        change = tn(first * d_low.astype(F32), queries) - tn(first * d_rest, keys)
        d_state = change if d_state is None else whole * d_state + change
    d_state_out[0, 0] = d_state.astype(BF16)
    d_gain[0, 0] = jnp.broadcast_to(total, (8, LANES))


def backward_two(where, q0, k0, v0, q1, k1, v1, qh, kh, vh, taps, ids, rows, r0, r1, *rest, size):
    query, key, value, inverse, fresh_in, d_in, incoming, middle, d_final = rest[:9]
    d_raw, d_edge, d_rates, d_taps = rest[9:13]
    ext, d_ext, d_rows = rest[13:]
    head = pl.program_id(1)
    total = 2 * size
    for index, group in enumerate(((qh, q0, q1), (kh, k0, k1), (vh, v0, v1))):
        fill_ext(ext, index, *group, size)
    d_state = d_final[0, 0].astype(F32)

    @pl.when(head == 0)
    def _():
        d_rates[...] = jnp.zeros_like(d_rates)

    for chunk in (1, 0):
        first, tail, whole, strict, lower = marks(ids, rows, chunk, size)
        rate = column_of((r0, r1)[chunk][...], head)
        keys, queries, fresh = key[0, chunk], query[0, chunk], fresh_in[0, chunk]
        inv, d_low = inverse[0, 0, chunk], d_in[0, chunk]
        state = (middle if chunk else incoming)[0, 0]
        d_mix = d_low.astype(F32)
        inner = jnp.where(lower, nt(queries, keys), 0.0)
        gram = jnp.where(strict, nt(keys, keys), 0.0)
        d_fresh = tn(inner, d_low) + tail * nt(keys, d_state)
        turned = tn(inv, d_fresh)
        d_rest = rate * turned
        rest_rows = value[0, chunk].astype(F32) - first * nt(keys, state)
        error = rest_rows - nn(gram, fresh)
        d_rate = jnp.sum(turned * error, axis=1, keepdims=True) * rate * (1.0 - rate)
        d_inner = jnp.where(lower, nt(d_low, fresh), 0.0)
        d_gram = rate * jnp.where(strict, -nt(turned, fresh), 0.0)
        d_query = first * nn(d_low, state) + nn(d_inner, keys)
        d_key = (
            tn(d_inner, queries)
            + tail * nn(fresh, d_state)
            - nn(first * d_rest, state)
            + nn(d_gram, keys)
            + tn(d_gram, keys)
        )
        for index, values in enumerate((d_query, d_key, d_rest)):
            d_rows[index, chunk * size : (chunk + 1) * size, :] = values
        lane = lax.broadcasted_iota(jnp.int32, (size, LANES), 1)
        d_rates[0, chunk] = d_rates[0, chunk] + jnp.where(lane == head, d_rate, 0.0)
        if chunk:
            d_state = (
                whole * d_state + tn(first * d_mix, queries) - tn(first * d_rest, keys)
            )
    links = links_of(ids, total)
    for index in range(3):
        conv = conv_of(ext, index, taps, links, total)
        sig = sigmoid(conv)
        d_act = d_rows[index].astype(BF16).astype(F32)
        if index < 2:
            act = conv * sig
            inv_norm = lax.rsqrt(jnp.sum(act * act, axis=1, keepdims=True) + EPSILON)
            unit = act * inv_norm
            d_act = (d_act - unit * jnp.sum(unit * d_act, axis=1, keepdims=True)) * inv_norm
        d_conv = d_act * sig * (1.0 + conv * (1.0 - sig))
        d_ext[...] = jnp.zeros_like(d_ext)
        for tap in range(4):
            window = slice(HALO - 3 + tap, HALO - 3 + tap + total)
            linked = d_conv * links[tap]
            d_taps[0, index, 0, tap : tap + 1, :] = jnp.sum(
                linked * ext[index, window, :], axis=0, keepdims=True
            )
            d_ext[window, :] = d_ext[window, :] + taps[index, 0, tap : tap + 1, :] * linked
        lanes = slice(index * LANES, (index + 1) * LANES)
        d_edge[0, :, lanes] = d_ext[:HALO, :].astype(BF16)
        d_raw[where[0], 0, :, lanes] = d_ext[HALO : HALO + size, :].astype(BF16)
        d_raw[1 - where[0], 0, :, lanes] = d_ext[HALO + size :, :].astype(BF16)


def mixer_calls(places, raw, rates, ids, rows, taps, gain, heads, seqs, size, scale):
    width = heads * LANES
    columns = 3 * width

    def raw_spec(chunk, part):
        def index(b, h, w):
            slot = w[0] if chunk == 0 else 1 - w[0]
            return (slot * seqs + b, 3 * h + part)

        return pl.BlockSpec((size, LANES), index)

    def rate_spec(chunk):
        def index(b, h, w):
            slot = w[0] if chunk == 0 else 1 - w[0]
            return (slot * seqs + b, 0)

        return pl.BlockSpec((size, LANES), index)

    halo_base = 2 * seqs * size // HALO

    def halo_spec(part):
        return pl.BlockSpec((HALO, LANES), lambda b, h, w: (halo_base + b, 3 * h + part))

    raw_specs = [raw_spec(c, p) for c in range(2) for p in range(3)] + [halo_spec(p) for p in range(3)]
    conv_specs = raw_specs + [
        pl.BlockSpec((3, 1, 4, LANES), lambda b, h, w: (0, h, 0, 0)),
        pl.BlockSpec((1, HALO + 2 * size, 1), lambda b, h, w: (b, 0, 0)),
        pl.BlockSpec((1, 2, size), lambda b, h, w: (b, 0, 0)),
        rate_spec(0),
        rate_spec(1),
    ]
    conv_args = (raw,) * 9 + (taps, ids, rows, rates, rates)
    id_specs, id_args = conv_specs[10:], conv_args[10:]
    act_spec = pl.BlockSpec((1, 2, size, LANES), lambda b, h, w: (b, 0, 0, h))
    act_shape = (seqs, 2, size, width)
    state_spec = pl.BlockSpec((1, 1, LANES, LANES), lambda b, h, w: (b, h, 0, 0))
    state_shape = jax.ShapeDtypeStruct((seqs, heads, LANES, LANES), BF16)
    inv_spec = pl.BlockSpec((1, 1, 2, size, size), lambda b, h, w: (b, h, 0, 0, 0))
    slot_spec = pl.BlockSpec((2, 1, size, LANES), lambda b, h, w: (0, b, 0, h))
    slot_shape = (2, seqs, size, width)
    gain_spec = pl.BlockSpec((1, LANES), lambda b, h, w: (0, 0))
    low = jax.ShapeDtypeStruct(act_shape, BF16)
    grid = (seqs, heads)
    steps = seqs * heads
    unit = 2 * size * size * LANES

    def one():
        return call(
            functools.partial(forward_one, size=size),
            grid,
            conv_specs,
            [act_spec] * 3 + [inv_spec, state_spec],
            [low] * 3
            + [jax.ShapeDtypeStruct((seqs, heads, 2, size, size), BF16), state_shape],
            [pltpu.VMEM((3, HALO + 2 * size, LANES), F32)],
            flops=steps * 64 * unit,
            moved=12 << 20,
        )(places, *conv_args)

    def two(query, key, value, inverse, incoming):
        return call(
            functools.partial(forward_two, size=size, scale=scale),
            grid,
            [act_spec] * 3 + [inv_spec] + id_specs + [state_spec, gain_spec],
            [slot_spec, act_spec, act_spec, state_spec],
            [
                jax.ShapeDtypeStruct(slot_shape, BF16),
                jax.ShapeDtypeStruct(act_shape, F32),
                low,
                state_shape,
            ],
            flops=steps * 10 * unit,
            moved=10 << 20,
        )(places, query, key, value, inverse, *id_args, incoming, gain)

    def three(d_head, mixed, query, key, inverse):
        return call(
            functools.partial(backward_one, size=size, scale=scale),
            grid,
            [slot_spec, act_spec, act_spec, act_spec, inv_spec] + id_specs + [gain_spec],
            [act_spec, state_spec, pl.BlockSpec((1, 1, 8, LANES), lambda b, h, w: (b, h, 0, 0))],
            [low, state_shape, jax.ShapeDtypeStruct((seqs, heads, 8, LANES), F32)],
            flops=steps * 16 * unit,
            moved=10 << 20,
        )(places, d_head, mixed, query, key, inverse, *id_args, gain)

    def four(query, key, value, inverse, fresh, d_low, incoming, middle, d_final):
        return call(
            functools.partial(backward_two, size=size),
            grid,
            conv_specs + [act_spec] * 3 + [inv_spec, act_spec, act_spec] + [state_spec] * 3,
            [
                pl.BlockSpec((2, 1, size, 3 * LANES), lambda b, h, w: (0, b, 0, h)),
                pl.BlockSpec((1, HALO, 3 * LANES), lambda b, h, w: (b, 0, h)),
                pl.BlockSpec((1, 2, size, LANES), lambda b, h, w: (b, 0, 0, 0)),
                pl.BlockSpec((1, 3, 1, 4, LANES), lambda b, h, w: (b, 0, h, 0, 0)),
            ],
            [
                jax.ShapeDtypeStruct((2, seqs, size, columns), BF16),
                jax.ShapeDtypeStruct((seqs, HALO, columns), BF16),
                jax.ShapeDtypeStruct((seqs, 2, size, LANES), F32),
                jax.ShapeDtypeStruct((seqs, 3, heads, 4, LANES), F32),
            ],
            [
                pltpu.VMEM((3, HALO + 2 * size, LANES), F32),
                pltpu.VMEM((HALO + 2 * size, LANES), F32),
                pltpu.VMEM((3, 2 * size, LANES), F32),
            ],
            flops=steps * 40 * unit,
            moved=20 << 20,
        )(
            places,
            *conv_args,
            query,
            key,
            value,
            inverse,
            fresh,
            d_low,
            incoming,
            middle,
            d_final,
        )

    return one, two, three, four


def dot_nn(left, right):
    return lax.dot_general(left, right, (((1,), (0,)), ((), ())), preferred_element_type=F32)


def dot_nt(left, right):
    return lax.dot_general(left, right, (((1,), (1,)), ((), ())), preferred_element_type=F32)


def dot_tn(left, right):
    return lax.dot_general(left, right, (((0,), (0,)), ((), ())), preferred_element_type=F32)


def rms_split(values, gain):
    mean = jnp.mean(values * values, axis=(0, 2), keepdims=True)
    return values * lax.rsqrt(mean + EPSILON) * gain


def sum_heads(mine, other):
    arrived = lax.ppermute(other.astype(BF16), "core", SWAP)
    part = (mine + arrived.astype(F32)).astype(BF16)
    return part.astype(F32) + lax.ppermute(part, "tp", SWAP).astype(F32)


def shards(
    hidden_in,
    attn_gain,
    query_weight,
    key_weight,
    value_weight,
    conv_weight,
    beta_weight,
    out_gain,
    out_weight,
    ffn_gain,
    gate_weight,
    up_weight,
    down_weight,
    cotangent,
    segment_ids,
):
    count = lax.axis_size("shard")
    places = place_scalars()
    core, cx = places[0], places[1]
    micro, local, size, width = hidden_in.shape
    seqs = micro * local
    own_rows = seqs * size
    heads_tp = conv_weight.shape[2]
    heads = heads_tp // 2
    scale = LANES ** (-0.5)

    pieces = [
        pack_heads(places, query_weight, key_weight, value_weight, heads),
        own_block_turned(places, out_weight),
        own_block(places, gate_weight),
        own_block(places, up_weight),
        own_block_turned(places, down_weight),
    ]
    full = []
    for piece in pieces:
        own = lax.all_gather(piece, "shard", axis=0, tiled=True)
        full.append((own, lax.ppermute(own, "cx", SWAP)))
    joint, outer, gates, ups, downs = full

    small = jnp.concatenate(
        [
            attn_gain,
            ffn_gain,
            out_gain,
            conv_weight.reshape(-1),
            beta_weight.reshape(-1),
        ]
    )
    small = lax.all_gather(small, "shard", axis=0)
    piece_d = attn_gain.shape[0]
    entry = out_gain.shape[0]
    at = 2 * piece_d + entry
    gain_in = split_small(places, small[:, :piece_d].reshape(-1), count).astype(F32)
    gain_ffn = split_small(places, small[:, piece_d : 2 * piece_d].reshape(-1), count).astype(F32)
    gain_head = small[:, 2 * piece_d : at].reshape(1, LANES).astype(F32)
    conv_size = conv_weight.size
    taps = small[:, at : at + conv_size].reshape(count, 4, 3, heads_tp, entry)
    taps = taps.transpose(2, 3, 1, 0, 4).reshape(3, heads_tp, 4, LANES)
    taps = lax.dynamic_slice_in_dim(taps, core * heads, heads, axis=1).astype(F32)
    beta = small[:, at + conv_size :].reshape(width, heads_tp)
    beta = lax.dynamic_slice_in_dim(beta, core * heads, heads, axis=1)
    beta = jnp.pad(beta, ((0, 0), (0, LANES - heads)))
    beta = split_small(places, beta, count)
    gain_in, gain_ffn = gain_in[:, None, :], gain_ffn[:, None, :]

    hidden_own = hidden_in.reshape(own_rows, width)
    hidden_other = lax.ppermute(hidden_own, "core", SWAP)
    grad_own = cotangent.reshape(own_rows, width)
    grad_all = split_rows(
        places, jnp.concatenate([grad_own, lax.ppermute(grad_own, "core", SWAP)]), count
    )
    ids_own = segment_ids.reshape(seqs, size)
    ids_other = lax.ppermute(ids_own, "core", SWAP)
    late = jnp.where(core == 1, hidden_own, hidden_other).reshape(seqs, size, width)[:, size - HALO :]
    early_ids = jnp.where(core == 0, ids_own, ids_other)
    late_ids = jnp.where(core == 1, ids_own, ids_other)
    halo = lax.ppermute(late, "cx", [(0, 1)]).reshape(seqs * HALO, width)
    halo_ids = lax.ppermute(late_ids[:, size - HALO :], "cx", [(0, 1)])
    halo_ids = jnp.where(cx == 0, -1, halo_ids)
    ids = jnp.concatenate([halo_ids, early_ids, late_ids], axis=1)[..., None]
    id_rows = jnp.stack([early_ids, late_ids], axis=1)
    hidden_all = split_rows(
        places, jnp.concatenate([hidden_own, hidden_other, halo]), count
    )

    normed_low = rms_split(hidden_all.astype(F32), gain_in).astype(BF16)
    raw = (dot_nn(normed_low[0], joint[0]) + dot_nn(normed_low[1], joint[1])).astype(BF16)
    rates = sigmoid(dot_nn(normed_low[0], beta[0]) + dot_nn(normed_low[1], beta[1]))
    one, two, three, four = mixer_calls(
        places, raw, rates, ids, id_rows, taps, gain_head, heads, seqs, size, scale
    )
    query, key, value, inverse, final = one()
    incoming = lax.ppermute(final, "cx", [(0, 1)])
    head_low, mixed, fresh, middle = two(query, key, value, inverse, incoming)

    head_rows = head_low.reshape(2 * own_rows, heads * LANES)

    def out_rows(rows):
        return jnp.stack([dot_nt(rows, outer[0]), dot_nt(rows, outer[1])])

    hidden_f32 = hidden_all[:, :own_rows].astype(F32)
    resid = hidden_f32 + sum_heads(out_rows(head_rows[:own_rows]), out_rows(head_rows[own_rows:]))
    normed_ffn, ffn_pull = jax.vjp(rms_split, resid, gain_ffn)
    ffn_own = normed_ffn.astype(BF16)
    ffn_low = jnp.concatenate([ffn_own, lax.ppermute(ffn_own, "core", SWAP)], axis=1)

    gate = dot_nn(ffn_low[0], gates[0]) + dot_nn(ffn_low[1], gates[1])
    up = dot_nn(ffn_low[0], ups[0]) + dot_nn(ffn_low[1], ups[1])
    sig = jax.nn.sigmoid(gate)
    act = (gate * sig * up).astype(BF16)

    def reduced(rows, grads):
        across = lax.ppermute(dot_tn(rows[1], grads).astype(BF16), "cx", SWAP)
        total = (dot_tn(rows[0], grads) + across.astype(F32)).astype(BF16)
        return lax.psum_scatter(total, "shard", scatter_dimension=0, tiled=True)

    grad_down = reduced(grad_all, act)
    d_act = (dot_nn(grad_all[0], downs[0]) + dot_nn(grad_all[1], downs[1])).astype(BF16).astype(F32)
    d_gate = (d_act * up * sig * (1.0 + gate * (1.0 - sig))).astype(BF16)
    d_up = (d_act * gate * sig).astype(BF16)
    grad_gate = reduced(ffn_low, d_gate)
    grad_up = reduced(ffn_low, d_up)

    def ffn_back(rows):
        return jnp.stack(
            [dot_nt(d_gate[rows], gates[i]) + dot_nt(d_up[rows], ups[i]) for i in range(2)]
        )

    first_rows, other_rows = slice(0, own_rows), slice(own_rows, 2 * own_rows)
    d_ffn = sum_heads(ffn_back(first_rows), ffn_back(other_rows))
    d_resid, sum_ffn_gain = ffn_pull(d_ffn)
    d_resid = grad_all[:, :own_rows].astype(F32) + d_resid
    resid_own = d_resid.astype(BF16)
    resid_low = jnp.concatenate([resid_own, lax.ppermute(resid_own, "core", SWAP)], axis=1)

    def down_rows(rows):
        return jnp.stack([dot_nt(act[rows], downs[0]), dot_nt(act[rows], downs[1])])

    result = resid + sum_heads(down_rows(first_rows), down_rows(other_rows))
    result_rows = join_rows(places, result.astype(BF16), count)

    d_head = (dot_nn(resid_low[0], outer[0]) + dot_nn(resid_low[1], outer[1])).astype(BF16)
    grad_outer = reduced(resid_low, head_rows)
    d_low, d_incoming, d_gain = three(
        d_head.reshape(head_low.shape), mixed, query, key, inverse
    )
    d_final = lax.ppermute(d_incoming, "cx", [(1, 0)])
    d_raw, d_edge, d_rates, d_taps = four(
        query, key, value, inverse, fresh, d_low, incoming, middle, d_final
    )
    d_edge = lax.ppermute(d_edge, "cx", [(1, 0)])
    window = (1 - core, 0, size - HALO, 0)
    edge_rows = lax.dynamic_slice(d_raw, window, (1,) + d_edge.shape)
    d_raw = lax.dynamic_update_slice(
        d_raw, (edge_rows.astype(F32) + d_edge.astype(F32)[None]).astype(BF16), window
    ).reshape(2 * own_rows, -1)
    d_logit = jnp.where(core == 0, d_rates, d_rates[:, ::-1]).transpose(1, 0, 2, 3)
    d_logit = d_logit.reshape(2 * own_rows, LANES).astype(BF16)
    normed_rows = normed_low[:, : 2 * own_rows]
    grad_joint = reduced(normed_rows, d_raw)
    sum_rate = jnp.stack([dot_tn(normed_rows[i], d_logit)[:, :heads] for i in range(2)])

    def normed_back(rows):
        return jnp.stack(
            [dot_nt(d_raw[rows], joint[i]) + dot_nt(d_logit[rows], beta[i]) for i in range(2)]
        )

    d_normed = sum_heads(normed_back(first_rows), normed_back(other_rows))
    _, norm_pull = jax.vjp(rms_split, hidden_f32, gain_in)
    d_hidden, sum_attn_gain = norm_pull(d_normed)
    input_rows = join_rows(places, (d_resid + d_hidden).astype(BF16), count)

    sum_taps = jnp.sum(d_taps, axis=0).transpose(2, 0, 1, 3)
    sum_taps = lax.dynamic_update_slice_in_dim(
        jnp.zeros((4, 3, heads_tp, LANES), F32), sum_taps, core * heads, axis=2
    )
    sum_rate = join_small(places, sum_rate, count)
    sum_rate = lax.dynamic_update_slice_in_dim(
        jnp.zeros((width, heads_tp), F32), sum_rate, core * heads, axis=1
    )
    sum_head_gain = jnp.sum(d_gain[:, :, 0, :], axis=(0, 1))
    sum_head_gain = lax.psum(sum_head_gain.astype(BF16), "tp").astype(F32)
    own = lax.axis_index("shard")
    packed = jnp.concatenate(
        [
            join_small(places, sum_attn_gain[:, 0], count),
            join_small(places, sum_ffn_gain[:, 0], count),
            sum_head_gain,
            sum_taps.reshape(-1),
            sum_rate.reshape(-1),
        ]
    ).astype(BF16)
    packed = lax.psum(packed, ("shard", "cx", "core")).astype(F32)
    ends = [width, 2 * width, 2 * width + LANES, 2 * width + LANES + sum_taps.size]
    grad_attn_gain = lax.dynamic_slice_in_dim(packed[: ends[0]], own * piece_d, piece_d)
    grad_ffn_gain = lax.dynamic_slice_in_dim(packed[ends[0] : ends[1]], own * piece_d, piece_d)
    grad_out_gain = lax.dynamic_slice_in_dim(packed[ends[1] : ends[2]], own * entry, entry)
    grad_conv = lax.dynamic_slice_in_dim(
        packed[ends[2] : ends[3]].reshape(4, 3, heads_tp, LANES), own * entry, entry, axis=3
    )
    grad_beta = lax.dynamic_slice_in_dim(
        packed[ends[3] :].reshape(width, heads_tp), own * piece_d, piece_d, axis=0
    )

    grad_query, grad_key, grad_value = lay_heads(places, pieces_of(grad_joint), heads)
    return (
        result_rows.reshape(hidden_in.shape),
        input_rows.reshape(hidden_in.shape),
        grad_attn_gain,
        grad_query,
        grad_key,
        grad_value,
        grad_conv,
        grad_beta,
        grad_out_gain,
        lay_block_turned(places, pieces_of(grad_outer)),
        grad_ffn_gain,
        lay_block(places, pieces_of(grad_gate)),
        lay_block(places, pieces_of(grad_up)),
        lay_block_turned(places, pieces_of(grad_down)),
    )


def solution(mesh):
    shard, ctx, tp = (mesh.shape[name] for name in ("shard", "ctx", "tp"))
    cores = Mesh(
        mesh.devices.reshape(shard, ctx // 2, 2, tp), ("shard", "cx", "core", "tp")
    )
    tokens = P(None, "shard", ("cx", "core"), None)
    outer = P("shard", "tp")
    turned = P("tp", "shard")
    conv = P(None, None, "tp", "shard")
    split = P("shard")
    return jax.shard_map(
        shards,
        mesh=cores,
        in_specs=(
            tokens,
            split,
            outer,
            outer,
            outer,
            conv,
            outer,
            split,
            turned,
            split,
            outer,
            outer,
            turned,
            tokens,
            P(None, "shard", ("cx", "core")),
        ),
        out_specs=(
            tokens,
            tokens,
            split,
            outer,
            outer,
            outer,
            conv,
            outer,
            split,
            turned,
            split,
            outer,
            outer,
            turned,
        ),
        check_vma=False,
    )
```

time: 3010 us -> 1170 us (0.39)
  waiting for transfers between devices: 2030 us -> 640 us
  matrix products: 567 us -> 170 us
  Pallas kernels: 0 us -> 151 us
  local copies, waits for them, and re-layouts: 154 us -> 49.3 us
  blocking collectives: 95.7 us -> 14.4 us
  other arithmetic: 120 us -> 75.3 us
  starting transfers between devices: 7.41 us -> 44.6 us
    reduce_scatter x8 -> x5, waiting for transfers between devices: 768 us -> 0.01 us  [reduced(): return lax.psum_scatter(total, 'shard', scatter_dimension=0, tiled=True)]
    all_gather x11 -> x5, waiting for transfers between devices: 815 us -> 86.4 us  [shards(): own = lax.all_gather(piece, 'shard', axis=0, tiled=True)]
    ppermute x3 -> x43, waiting for transfers between devices: 0.01 us -> 482 us  [the longest x5 194 us: reduced(): across = lax.ppermute(dot_tn(rows[1], grads).astype(BF16), 'cx', SWAP)]
    dot_general x175 -> x48, matrix products: 567 us -> 170 us  [the longest x24 64.2 us: dot_nt(): lax.dot_general(left, right, (((1,), (1,)), ((), ())), preferred_element_...]
    psum x4 -> x1, waiting for transfers between devices: 423 us -> 53.9 us  [shards(): packed = lax.psum(packed, ('shard', 'cx', 'core')).astype(F32)]
    pallas_call x0 -> x14, Pallas kernels: none -> 151 us  [the longest x1 55.6 us: one(): call(functools.partial(forward_one, size=size), grid, conv_specs, [act_sp...]
    all_gather x4 -> x0, blocking collectives: 57.4 us -> none  [the longest x1 19.3 us: shards(): lax.all_gather(conv_weight, 'shard', axis=3, tiled=True)]
    ppermute x3 -> x43, starting transfers between devices: 6.05 us -> 43.5 us  [the longest x5 6.99 us: shards(): full.append((own, lax.ppermute(own, 'cx', SWAP)))]
  transfers between devices with their start and end apart: 27 -> 55, of which waited for: 21 -> 22; matrix products, arithmetic and copies ran while one was open for 21% -> 21% of each run, Pallas kernels for 0% -> 13%
where the time goes in v1:
time: 1170 us; the launch traced here: 1160 us
  waiting for transfers between devices  640 us (55%)
  matrix products  170 us (15%)
  Pallas kernels  151 us (13%)
  other arithmetic  75.3 us (6%)
  local copies, waits for them, and re-layouts  49.3 us (4%)
  starting transfers between devices  44.6 us (4%)
  between operations  16.6 us (1%)
  blocking collectives  14.4 us (1%)
    ppermute x5, waiting for transfers between devices, reduced(): across = lax.ppermute(dot_tn(rows[1], grads).astype(BF16), 'cx', SWAP)  194 us
    ppermute x5, waiting for transfers between devices, shards(): full.append((own, lax.ppermute(own, 'cx', SWAP)))  158 us
    all_gather x5, waiting for transfers between devices, shards(): own = lax.all_gather(piece, 'shard', axis=0, tiled=True)  86.4 us
    ppermute x4, waiting for transfers between devices, sum_heads(): return part.astype(F32) + lax.ppermute(part, 'tp', SWAP).astype(F32)  84.5 us
    dot_general x24, matrix products, dot_nt(): lax.dot_general(left, right, (((1,), (1,)), ((), ())), preferred_element_...  64.2 us
    pallas_call x1, Pallas kernels, one(): call(functools.partial(forward_one, size=size), grid, conv_specs, [act_sp...  55.6 us
    dot_general x12, matrix products, dot_tn(): lax.dot_general(left, right, (((0,), (0,)), ((), ())), preferred_element_...  55.2 us
    psum x1, waiting for transfers between devices, shards(): packed = lax.psum(packed, ('shard', 'cx', 'core')).astype(F32)  53.9 us
  transfers between devices with their start and end apart: 55, of which 22 were waited for; matrix products, arithmetic and copies ran while one was open for 21% of the time, Pallas kernels for 13%

profile of v1, /device:TPU:0, one launch (start us, length us, event | category | flops | bytes accessed | tf_op | source)
XLA Modules:
  0.0 1161.4 jit_solution(1747539381253655156)
XLA Ops:
  27.4 4.5 collective-permute-start.4
  33.5 17.6 %all-reduce.7.cloned.1.call-done = bf16[32896]{0:T(1024)(128)(2,1)} async-done(((bf16[32896]{0:T(1024)(128)(2,1)}), bf16[32896]{0:T(1024)(128)(2,1)}) %all-reduce.7.cloned.1.call-update) | async-done | bytes 65808
  56.2 4.2 collective-permute-start.1
  60.8 22.7 %all-gather.9.cloned.1.call-done = bf16[1024,512]{0,1:T(8,128)(2,1)} async-done(((bf16[256,512]{0,1:T(8,128)(2,1)}), bf16[1024,512]{0,1:T(8,128)(2,1)}) %all-gather.9.cloned.1.call-update) | async-done | bytes 1048592 | tf_op jit(solution)/shard_map/all_gather | solution.py:641
  84.0 63.6 %all-gather.7.cloned.1.call-done = bf16[1024,1536]{1,0:T(8,128)(2,1)} async-done(((bf16[256,1536]{1,0:T(8,128)(2,1)}), bf16[1024,1536]{1,0:T(8,128)(2,1)}) %all-gather.7.cloned.1.call-update) | async-done | bytes 3145744 | tf_op jit(solution)/shard_map/all_gather | solution.py:641
  152.6 4.1 shard_map.254
  165.8 51.9 %collective-permute-done.2 = bf16[1024,1536]{1,0:T(8,128)(2,1)} collective-permute-done((bf16[1024,1536]{1,0:T(8,128)(2,1)}, bf16[1024,1536]{1,0:T(8,128)(2,1)}, u32[]{:S(2)}, u32[]{:S(2)}) %collective-permute-start.2) | collective-permute-done | bytes 3145760 | tf_op jit(solution)/shard_map/ppermute | solution.py:642
  217.7 6.8 fusion.3.q0.k0.v0.q1.k1.v1.qh.kh.vh
  224.5 55.6 %shard_map.256 = (bf16[2,2,256,512]{3,2,1,0:T(8,128)(2,1)S(1)}, bf16[2,2,256,512]{3,2,1,0:T(8,128)(2,1)S(1)}, bf16[2,2,256,512]{3,2,1,0:T(8,128)(2,1)S(1)}, bf16...) custom-call(s32[2]{0:T(128)S(1)} %pad_add_fusion.1.where, bf16[1056,1536]{1,0:T(8,128)(2,1)} %fusion.3.q0.k0.v0.q1.k1.v1.qh.kh.vh, ...), custom_call_target="tpu_custom_call" | custom-call | flops 8589934592 | bytes 12582912 | tf_op jit(solution)/shard_map/pallas_call | solution.py:502
  281.0 4.3 collective-permute-start.5
  285.4 4.0 collective-permute-done.5.incoming.rest_6_
  289.4 13.0 %shard_map.257 = (bf16[2,2,256,512]{3,2,1,0:T(8,128)(2,1)S(1)}, f32[2,2,256,512]{3,2,1,0:T(8,128)}, bf16[2,2,256,512]{3,2,1,0:T(8,128)(2,1)S(1)}, bf16[2,4,128,128]{3,2,1,0:T(8,128)(2,1)S(1)}) custom-call(s32[2]{0:T(128)S(1)} %pad_add_fusion.1.where, bf16[2,2,256,512]{3,2,1,0:T(8,128)(2,1)S(1)} %get-tuple-element.33.query.rest_0_, ...), custom_call_target="tpu_custom_call" | custom-call | flops 1342177280 | bytes 10485760 | tf_op jit(solution)/shard_map/pallas_call | solution.py:515
  311.6 4.5 fusion.16
  320.5 43.9 %collective-permute-done.8 = bf16[2,512,1024]{2,1,0:T(8,128)(2,1)} collective-permute-done((bf16[2,512,1024]{2,1,0:T(8,128)(2,1)}, bf16[2,512,1024]{2,1,0:T(8,128)(2,1)}, u32[]{:S(2)}, u32[]{:S(2)}) %collective-permute-start.8) | collective-permute-done | bytes 2097184 | tf_op jit(solution)/shard_map/ppermute | solution.py:602
  364.5 5.4 multiply_reduce_fusion.2
  374.9 4.8 pad_maximum_fusion.1.source
  379.8 4.1 shard_map.259
  387.4 5.6 add_convert_fusion.4
  395.4 50.2 %collective-permute-done.10 = bf16[1024,1408]{1,0:T(8,128)(2,1)} collective-permute-done((bf16[1024,1408]{1,0:T(8,128)(2,1)}, bf16[1024,1408]{1,0:T(8,128)(2,1)}, u32[]{:S(2)}, u32[]{:S(2)}) %collective-permute-start.10) | collective-permute-done | bytes 2883616 | tf_op jit(solution)/shard_map/ppermute | solution.py:642
  445.6 5.2 fusion.89
  450.9 56.1 %collective-permute-done.11 = bf16[1024,1408]{1,0:T(8,128)(2,1)S(1)} collective-permute-done((bf16[1024,1408]{1,0:T(8,128)(2,1)}, bf16[1024,1408]{1,0:T(8,128)(2,1)S(1)}, u32[]{:S(2)}, u32[]{:S(2)}) %collective-permute-start.11) | collective-permute-done | bytes 2883616 | tf_op jit(solution)/shard_map/ppermute | solution.py:642
  507.0 5.5 fusion.90
  516.1 9.3 fusion.6
  525.4 3.8 convolution_convert_fusion.2
  530.9 62.4 %collective-permute-done.31 = bf16[1024,1408]{1,0:T(8,128)(2,1)S(1)} collective-permute-done((bf16[1024,1408]{1,0:T(8,128)(2,1)S(1)}, bf16[1024,1408]{1,0:T(8,128)(2,1)S(1)}, u32[]{:S(2)}, u32[]{:S(2)}) %collective-permute-start.31) | collective-permute-done | bytes 2883616 | tf_op jit(solution)/shard_map/ppermute | solution.py:718
  593.4 4.9 add_convert_fusion.3
  598.6 6.1 convolution_convert_fusion.1
  609.8 3.8 fusion.42
  622.0 5.2 add_bitcast_fusion.2
  627.2 40.9 %collective-permute-done.35 = bf16[1024,1408]{1,0:T(8,128)(2,1)S(1)} collective-permute-done((bf16[1024,1408]{1,0:T(8,128)(2,1)S(1)}, bf16[1024,1408]{1,0:T(8,128)(2,1)S(1)}, u32[]{:S(2)}, u32[]{:S(2)}) %collective-permute-start.35) | collective-permute-done | bytes 2883616 | tf_op jit(solution)/shard_map/ppermute | solution.py:718
  668.1 5.3 add_convert_fusion.2
  673.4 4.9 add_bitcast_fusion.3
  682.7 3.8 convolution_convert_fusion
  687.6 39.8 %collective-permute-done.17 = bf16[2,512,1024]{2,1,0:T(8,128)(2,1)S(1)} collective-permute-done((bf16[2,512,1024]{2,1,0:T(8,128)(2,1)S(1)}, bf16[2,512,1024]{2,1,0:T(8,128)(2,1)S(1)}, u32[]{:S(2)}, u32[]{:S(2)}) %collective-permute-start.17) | collective-permute-done | bytes 2097184 | tf_op jit(solution)/shard_map/ppermute | solution.py:602
  727.4 4.0 multiply_reduce_fusion
  731.5 4.6 fusion.82
  736.1 13.2 %collective-permute-done.39 = bf16[1024,1408]{1,0:T(8,128)(2,1)S(1)} collective-permute-done((bf16[1024,1408]{1,0:T(8,128)(2,1)S(1)}, bf16[1024,1408]{1,0:T(8,128)(2,1)S(1)}, u32[]{:S(2)}, u32[]{:S(2)}) %collective-permute-start.39) | collective-permute-done | bytes 2883616 | tf_op jit(solution)/shard_map/ppermute | solution.py:718
  749.3 5.0 add_convert_fusion.1
  760.8 14.7 %shard_map.260 = (bf16[2,2,256,512]{3,2,1,0:T(8,128)(2,1)S(1)}, bf16[2,4,128,128]{3,2,1,0:T(8,128)(2,1)S(1)}, f32[2,4,8,128]{3,2,1,0:T(8,128)S(1)}) custom-call(s32[2]{0:T(128)S(1)} %pad_add_fusion.1.where, bf16[2,2,256,512]{3,2,1,0:T(8,128)(2,1)S(1)} %bitcast.215, f32[2,2,256,512]{3,2,1,0:T(8,128)} %get-tuple-element.40.mixed, ...), custom_call_target="tpu_custom_call" | custom-call | flops 2147483648 | bytes 10485760 | tf_op jit(solution)/shard_map/pallas_call | solution.py:531
  777.8 7.0 collective-permute-done.19.rest_8_
  784.8 31.3 %shard_map.261 = (bf16[2,2,256,1536]{3,2,1,0:T(8,128)(2,1)}, bf16[2,16,1536]{2,1,0:T(8,128)(2,1)S(1)}, f32[2,2,256,128]{3,2,1,0:T(8,128)S(1)}, f32[2,3,4,4,128]{4,3,2,1,0:T(4,128)S(1)}) custom-call(s32[2]{0:T(128)S(1)} %pad_add_fusion.1.where, bf16[1056,1536]{1,0:T(8,128)(2,1)} %fusion.3.q0.k0.v0.q1.k1.v1.qh.kh.vh, ...), custom_call_target="tpu_custom_call" | custom-call | flops 5368709120 | bytes 20971520 | tf_op jit(solution)/shard_map/pallas_call | solution.py:542
  818.1 5.2 collective-permute-done.20
  824.9 7.7 convolution_convert_fusion.3
  832.7 3.8 convolution_convert_fusion.4
  838.5 5.0 fusion.40
  843.5 77.0 %collective-permute-done.27 = bf16[1024,512]{1,0:T(8,128)(2,1)S(1)} collective-permute-done((bf16[1024,512]{1,0:T(8,128)(2,1)}, bf16[1024,512]{1,0:T(8,128)(2,1)S(1)}, u32[]{:S(2)}, u32[]{:S(2)}) %collective-permute-start.27) | collective-permute-done | bytes 1048608 | tf_op jit(solution)/shard_map/ppermute | solution.py:718
  920.6 3.8 add_convert_fusion.6
  928.3 7.1 add_convert_fusion
  935.9 4.3 fusion.93
  941.9 3.9 fusion.45
  956.5 5.1 add_bitcast_fusion
  963.7 5.0 fusion.19
  970.0 5.0 convolution_bitcast_fusion.2
  981.9 14.5 %collective-permute-done.36.b = bf16[256,1408]{1,0:T(8,128)(2,1)} collective-permute-done((bf16[256,1408]{1,0:T(8,128)(2,1)}, bf16[256,1408]{1,0:T(8,128)(2,1)}, u32[]{:S(2)}, u32[]{:S(2)}) %collective-permute-start.36) | collective-permute-done | bytes 720928 | tf_op jit(solution)/shard_map/ppermute | solution.py:159
  997.5 4.9 fusion.17
  1002.5 14.4 %psum.14 = bf16[128]{0:T(256)(128)(2,1)S(1)} all-reduce(bf16[128]{0:T(256)(128)(2,1)S(1)} %slice_reduce_fusion), channel_id=1, replica_groups=mesh['shard'=4,'cx'=2,'core'=2,'tp'=2] {'tp'}, use_global_device_ids=true, to_apply=%region_8.9 | all-reduce | flops 128 | bytes 512 | tf_op jit(solution)/shard_map/psum | solution.py:787
  1031.9 4.6 shard_map.265
  1036.5 4.8 shard_map.266
  1041.3 5.4 shard_map.267
  1047.2 5.2 fusion.15
  1056.4 10.1 collective-permute-done.24.b
  1068.5 13.4 %fusion.11 = (bf16[2,512,1024]{2,1,0:T(8,128)(2,1)S(1)}, bf16[2,512,1024]{2,1,0:T(8,128)(2,1)S(1)}) fusion(bf16[2,512,1024]{2,1,0:T(8,128)(2,1)} %collective-permute-done.22, f32[512]{0:T(512)S(1)} %multiply_multiply_fusion, f32[512]{0:T(512)S(1)} %fusion.77, f32[2,1024]{1,0:T(2,128)S(1)} %bitcast.254, bf16[2,1056,1024]{2,1,0:T(8,128)(2,1)} %copy-done.2, ...), kind=kLoop, calls=%fused_computation.33 | loop fusion | flops 39845888 | bytes 37773312 | tf_op jit(solution)/shard_map/convert_element_type | solution.py:776
  1086.2 53.9 %all-reduce.5.cloned.1.call-done = bf16[32896]{0:T(1024)(128)(2,1)} async-done(((bf16[32896]{0:T(1024)(128)(2,1)}), bf16[32896]{0:T(1024)(128)(2,1)}) %all-reduce.5.cloned.1.call-update) | async-done | bytes 65808 | tf_op jit(solution)/shard_map/psum | solution.py:798
  1148.8 5.6 shard_map.263
  (396 shorter events, 167.7 us)
Async XLA Ops:
  7.2 43.9 %all-reduce.7.cloned.1.call-start = ((), (), s32[]{:S(2)}) async-start(), calls=%async_computation.16 | async-start | bytes 135168
  14.4 69.1 %all-gather.9.cloned.1.call-start = ((), (), s32[]{:S(2)}) async-start(), calls=%async_computation.6 | async-start | bytes 1310720 | tf_op jit(solution)/shard_map/all_gather | solution.py:641
  16.2 131.4 %all-gather.7.cloned.1.call-start = ((), (), s32[]{:S(2)}) async-start(), calls=%async_computation.5 | async-start | bytes 3932160 | tf_op jit(solution)/shard_map/all_gather | solution.py:641
  22.1 295.7 %all-gather.15.cloned.1.call-start = ((), (), s32[]{:S(2)}) async-start(), calls=%async_computation.9 | async-start | bytes 3604480 | tf_op jit(solution)/shard_map/all_gather | solution.py:641
  23.1 297.4 %all-gather.11.cloned.1.call-start = ((), (), s32[]{:S(2)}) async-start(), calls=%async_computation.7 | async-start | bytes 3604480 | tf_op jit(solution)/shard_map/all_gather | solution.py:641
  23.1 30.4 %collective-permute-start = (bf16[512,2048]{1,0:T(8,128)(2,1)}, bf16[512,2048]{1,0:T(8,128)(2,1)}, u32[]{:S(2)}, u32[]{:S(2)}) collective-permute-start(bf16[512,2048]{1,0:T(8,128)(2,1)} %bitcast.218), channel_id=1, source_target_pairs={{0,2},{2,0},{1,3},{3,1},{4,6},{6,4},{5,7},{7,5},{8,10},{10,8},{9,1... | collective-permute-start | bytes 6291464 | tf_op jit(solution)/shard_map/ppermute | solution.py:672
  23.6 3.7 collective-permute-start.3
  25.9 346.6 %all-gather.13.cloned.1.call-start = ((), (), s32[]{:S(2)}) async-start(), calls=%async_computation.8 | async-start | bytes 3604480 | tf_op jit(solution)/shard_map/all_gather | solution.py:641
  27.4 5.8 collective-permute-start.4
  31.9 257.4 %copy-start.31 = (s32[2,2,256]{2,1,0:T(2,128)}, s32[2,2,256]{2,1,0:T(2,128)S(1)}, u32[]{:S(2)}) copy-start(s32[2,2,256]{2,1,0:T(2,128)S(1)} %pad_add_fusion.rows) | copy-start | bytes 12292
  53.5 105.4 %copy-start.45 = (bf16[1,4,256,128]{3,2,0,1:T(8,128)(2,1)}, bf16[1,4,256,128]{3,2,0,1:T(8,128)(2,1)S(1)}, u32[]{:S(2)}) copy-start(bf16[1,4,256,128]{3,2,0,1:T(8,128)(2,1)S(1)} %get-tuple-element.127) | copy-start | bytes 786436
  53.5 106.1 %copy-start.47 = (bf16[1,4,256,128]{3,2,0,1:T(8,128)(2,1)}, bf16[1,4,256,128]{3,2,0,1:T(8,128)(2,1)S(1)}, u32[]{:S(2)}) copy-start(bf16[1,4,256,128]{3,2,0,1:T(8,128)(2,1)S(1)} %get-tuple-element.126) | copy-start | bytes 786436
  56.2 92.9 %collective-permute-start.1 = (bf16[2,16,2048]{2,1,0:T(8,128)(2,1)}, bf16[2,16,2048]{2,1,0:T(8,128)(2,1)}, u32[]{:S(2)}, u32[]{:S(2)}) collective-permute-start(bf16[2,16,2048]{2,1,0:T(8,128)(2,1)} %slice.236), channel_id=1, source_target_pairs={{0,4},{1,5},{2,6},{3,7},{8,12},{9,13},{10,14},{11,15},{16,20},{17,... | collective-permute-start | bytes 393224 | tf_op jit(solution)/shard_map/ppermute | solution.py:682
  60.3 97.4 %copy-start.63 = (f32[4,2,256]{2,1,0:T(2,128)}, f32[4,2,256]{2,1,0:T(2,128)S(1)}, u32[]{:S(2)}) copy-start(f32[4,2,256]{2,1,0:T(2,128)S(1)} %fusion.72) | copy-start | bytes 24580
  60.8 163.7 %copy-start.29 = (f32[3,4,4,128]{3,2,1,0:T(4,128)}, f32[3,4,4,128]{3,2,1,0:T(4,128)S(1)}, u32[]{:S(2)}) copy-start(f32[3,4,4,128]{3,2,1,0:T(4,128)S(1)} %dynamic-slice_convert_fusion.taps) | copy-start | bytes 73732
  83.5 219.6 %collective-permute-start.6 = (bf16[1024,512]{0,1:T(8,128)(2,1)}, bf16[1024,512]{0,1:T(8,128)(2,1)}, u32[]{:S(2)}, u32[]{:S(2)}) collective-permute-start(bf16[1024,512]{0,1:T(8,128)(2,1)} %all-gather.9.cloned.1.call-done), channel_id=1, source_target_pairs={{0,4},{4,0},{1,5},{5,1},{2,6},{6,2},{3,7},{7,3},{8,12},{12,8},{9,1... | collective-permute-start | bytes 3145736 | tf_op jit(solution)/shard_map/ppermute | solution.py:642
  147.6 70.1 %collective-permute-start.2 = (bf16[1024,1536]{1,0:T(8,128)(2,1)}, bf16[1024,1536]{1,0:T(8,128)(2,1)}, u32[]{:S(2)}, u32[]{:S(2)}) collective-permute-start(bf16[1024,1536]{1,0:T(8,128)(2,1)} %all-gather.7.cloned.1.call-done), channel_id=1, source_target_pairs={{0,4},{4,0},{1,5},{5,1},{2,6},{6,2},{3,7},{7,3},{8,12},{12,8},{9,1... | collective-permute-start | bytes 9437192 | tf_op jit(solution)/shard_map/ppermute | solution.py:642
  281.0 8.3 collective-permute-start.5
  306.7 4.9 collective-permute-start.7
  308.7 652.9 %reduce-scatter.10.cloned.1.call-start = ((), (), s32[]{:S(2)}) async-start(), calls=%async_computation.13 | async-start | bytes 3604480 | tf_op jit(solution)/shard_map/reduce_scatter | solution.py:720
  316.1 48.4 %collective-permute-start.8 = (bf16[2,512,1024]{2,1,0:T(8,128)(2,1)}, bf16[2,512,1024]{2,1,0:T(8,128)(2,1)}, u32[]{:S(2)}, u32[]{:S(2)}) collective-permute-start(bf16[2,512,1024]{2,1,0:T(8,128)(2,1)} %fusion.16), channel_id=1, source_target_pairs={{0,1},{1,0},{2,3},{3,2},{4,5},{5,4},{6,7},{7,6},{8,9},{9,8},{10,11... | collective-permute-start | bytes 6291464 | tf_op jit(solution)/shard_map/ppermute | solution.py:602
  317.6 57.3 %collective-permute-start.15 = (bf16[512,2048]{1,0:T(8,128)(2,1)}, bf16[512,2048]{1,0:T(8,128)(2,1)}, u32[]{:S(2)}, u32[]{:S(2)}) collective-permute-start(bf16[512,2048]{1,0:T(8,128)(2,1)} %bitcast.35), channel_id=1, source_target_pairs={{0,2},{2,0},{1,3},{3,1},{4,6},{6,4},{5,7},{7,5},{8,10},{10,8},{9,1... | collective-permute-start | bytes 6291464 | tf_op jit(solution)/shard_map/ppermute | solution.py:675
  317.8 69.5 %collective-permute-start.12 = (bf16[1024,1408]{0,1:T(8,128)(2,1)}, bf16[1024,1408]{0,1:T(8,128)(2,1)}, u32[]{:S(2)}, u32[]{:S(2)}) collective-permute-start(bf16[1024,1408]{0,1:T(8,128)(2,1)} %all-gather.15.cloned.1.call-done), channel_id=1, source_target_pairs={{0,4},{4,0},{1,5},{5,1},{2,6},{6,2},{3,7},{7,3},{8,12},{12,8},{9,1... | collective-permute-start | bytes 8650760 | tf_op jit(solution)/shard_map/ppermute | solution.py:642
  320.4 125.2 %collective-permute-start.10 = (bf16[1024,1408]{1,0:T(8,128)(2,1)}, bf16[1024,1408]{1,0:T(8,128)(2,1)}, u32[]{:S(2)}, u32[]{:S(2)}) collective-permute-start(bf16[1024,1408]{1,0:T(8,128)(2,1)} %all-gather.11.cloned.1.call-done), channel_id=1, source_target_pairs={{0,4},{4,0},{1,5},{5,1},{2,6},{6,2},{3,7},{7,3},{8,12},{12,8},{9,1... | collective-permute-start | bytes 8650760 | tf_op jit(solution)/shard_map/ppermute | solution.py:642
  372.4 20.5 %collective-permute-start.9 = (bf16[2,512,1024]{2,1,0:T(8,128)(2,1)}, bf16[2,512,1024]{2,1,0:T(8,128)(2,1)}, u32[]{:S(2)}, u32[]{:S(2)}) collective-permute-start(bf16[2,512,1024]{2,1,0:T(8,128)(2,1)} %multiply_convert_fusion.1), channel_id=1, source_target_pairs={{0,2},{2,0},{1,3},{3,1},{4,6},{6,4},{5,7},{7,5},{8,10},{10,8},{9,1... | collective-permute-start | bytes 6291464 | tf_op jit(solution)/shard_map/ppermute | solution.py:710
  372.4 134.6 %collective-permute-start.11 = (bf16[1024,1408]{1,0:T(8,128)(2,1)}, bf16[1024,1408]{1,0:T(8,128)(2,1)S(1)}, u32[]{:S(2)}, u32[]{:S(2)}) collective-permute-start(bf16[1024,1408]{1,0:T(8,128)(2,1)} %all-gather.13.cloned.1.call-done), channel_id=1, source_target_pairs={{0,4},{4,0},{1,5},{5,1},{2,6},{6,2},{3,7},{7,3},{8,12},{12,8},{9,1... | collective-permute-start | bytes 8650760 | tf_op jit(solution)/shard_map/ppermute | solution.py:642
  395.4 129.9 %copy-start.53 = (bf16[1024,1024]{1,0:T(8,128)(2,1)}, bf16[1024,1024]{1,0:T(8,128)(2,1)S(1)}, u32[]{:S(2)}) copy-start(bf16[1024,1024]{1,0:T(8,128)(2,1)S(1)} %get-tuple-element.121) | copy-start | bytes 6291460
  395.4 198.0 %copy-start.51 = (bf16[1024,1024]{1,0:T(8,128)(2,1)}, bf16[1024,1024]{1,0:T(8,128)(2,1)S(1)}, u32[]{:S(2)}) copy-start(bf16[1024,1024]{1,0:T(8,128)(2,1)S(1)} %get-tuple-element.120) | copy-start | bytes 6291460
  529.1 64.2 %collective-permute-start.31 = (bf16[1024,1408]{1,0:T(8,128)(2,1)S(1)}, bf16[1024,1408]{1,0:T(8,128)(2,1)S(1)}, u32[]{:S(2)}, u32[]{:S(2)}) collective-permute-start(bf16[1024,1408]{1,0:T(8,128)(2,1)S(1)} %convolution_convert_fusion.2), channel_id=1, source_target_pairs={{0,4},{4,0},{1,5},{5,1},{2,6},{6,2},{3,7},{7,3},{8,12},{12,8},{9,1... | collective-permute-start | bytes 8650760 | tf_op jit(solution)/shard_map/ppermute | solution.py:718
  598.3 364.3 %reduce-scatter.12.cloned.1.call-start = ((), (), s32[]{:S(2)}) async-start(), calls=%async_computation.14 | async-start | bytes 3604480 | tf_op jit(solution)/shard_map/reduce_scatter | solution.py:720
  604.7 63.4 %collective-permute-start.35 = (bf16[1024,1408]{1,0:T(8,128)(2,1)S(1)}, bf16[1024,1408]{1,0:T(8,128)(2,1)S(1)}, u32[]{:S(2)}, u32[]{:S(2)}) collective-permute-start(bf16[1024,1408]{1,0:T(8,128)(2,1)S(1)} %convolution_convert_fusion.1), channel_id=1, source_target_pairs={{0,4},{4,0},{1,5},{5,1},{2,6},{6,2},{3,7},{7,3},{8,12},{12,8},{9,1... | collective-permute-start | bytes 8650760 | tf_op jit(solution)/shard_map/ppermute | solution.py:718
  617.0 61.3 %collective-permute-start.16 = (bf16[2,512,1024]{2,1,0:T(8,128)(2,1)}, bf16[2,512,1024]{2,1,0:T(8,128)(2,1)}, u32[]{:S(2)}, u32[]{:S(2)}) collective-permute-start(bf16[2,512,1024]{2,1,0:T(8,128)(2,1)} %pad_maximum_fusion.6), channel_id=1, source_target_pairs={{0,2},{2,0},{1,3},{3,1},{4,6},{6,4},{5,7},{7,5},{8,10},{10,8},{9,1... | collective-permute-start | bytes 6291464 | tf_op jit(solution)/shard_map/ppermute | solution.py:600
  673.3 304.9 %reduce-scatter.14.cloned.1.call-start = ((), (), s32[]{:S(2)}) async-start(), calls=%async_computation.15 | async-start | bytes 3604480 | tf_op jit(solution)/shard_map/reduce_scatter | solution.py:720
  681.6 45.9 %collective-permute-start.17 = (bf16[2,512,1024]{2,1,0:T(8,128)(2,1)S(1)}, bf16[2,512,1024]{2,1,0:T(8,128)(2,1)S(1)}, u32[]{:S(2)}, u32[]{:S(2)}) collective-permute-start(bf16[2,512,1024]{2,1,0:T(8,128)(2,1)S(1)} %fusion.18), channel_id=1, source_target_pairs={{0,1},{1,0},{2,3},{3,2},{4,5},{5,4},{6,7},{7,6},{8,9},{9,8},{10,11... | collective-permute-start | bytes 6291464 | tf_op jit(solution)/shard_map/ppermute | solution.py:602
  686.5 62.8 %collective-permute-start.39 = (bf16[1024,1408]{1,0:T(8,128)(2,1)S(1)}, bf16[1024,1408]{1,0:T(8,128)(2,1)S(1)}, u32[]{:S(2)}, u32[]{:S(2)}) collective-permute-start(bf16[1024,1408]{1,0:T(8,128)(2,1)S(1)} %convolution_convert_fusion), channel_id=1, source_target_pairs={{0,4},{4,0},{1,5},{5,1},{2,6},{6,2},{3,7},{7,3},{8,12},{12,8},{9,1... | collective-permute-start | bytes 8650760 | tf_op jit(solution)/shard_map/ppermute | solution.py:718
  736.1 18.2 %collective-permute-start.18 = (bf16[2,512,1024]{2,1,0:T(8,128)(2,1)}, bf16[2,512,1024]{2,1,0:T(8,128)(2,1)}, u32[]{:S(2)}, u32[]{:S(2)}) collective-permute-start(bf16[2,512,1024]{2,1,0:T(8,128)(2,1)} %fusion.82), channel_id=1, source_target_pairs={{0,2},{2,0},{1,3},{3,1},{4,6},{6,4},{5,7},{7,5},{8,10},{10,8},{9,1... | collective-permute-start | bytes 6291464 | tf_op jit(solution)/shard_map/ppermute | solution.py:739
  754.3 242.2 %reduce-scatter.8.cloned.1.call-start = ((), (), s32[]{:S(2)}) async-start(), calls=%async_computation.12 | async-start | bytes 1310720 | tf_op jit(solution)/shard_map/reduce_scatter | solution.py:720
  776.5 8.3 collective-permute-start.19
  816.9 6.5 collective-permute-start.20
  832.7 95.7 %collective-permute-start.23 = (bf16[1024,1536]{1,0:T(8,128)(2,1)}, bf16[1024,1536]{1,0:T(8,128)(2,1)}, u32[]{:S(2)}, u32[]{:S(2)}) collective-permute-start(bf16[1024,1536]{1,0:T(8,128)(2,1)} %convolution_convert_fusion.3), channel_id=1, source_target_pairs={{0,4},{4,0},{1,5},{5,1},{2,6},{6,2},{3,7},{7,3},{8,12},{12,8},{9,1... | collective-permute-start | bytes 9437192 | tf_op jit(solution)/shard_map/ppermute | solution.py:718
  836.5 84.1 %collective-permute-start.27 = (bf16[1024,512]{1,0:T(8,128)(2,1)}, bf16[1024,512]{1,0:T(8,128)(2,1)S(1)}, u32[]{:S(2)}, u32[]{:S(2)}) collective-permute-start(bf16[1024,512]{1,0:T(8,128)(2,1)} %convolution_convert_fusion.4), channel_id=1, source_target_pairs={{0,4},{4,0},{1,5},{5,1},{2,6},{6,2},{3,7},{7,3},{8,12},{12,8},{9,1... | collective-permute-start | bytes 3145736 | tf_op jit(solution)/shard_map/ppermute | solution.py:718
  843.5 80.9 %copy-start.25 = (f32[2,2,256,128]{3,2,1,0:T(8,128)S(1)}, f32[2,2,256,128]{3,2,1,0:T(8,128)}, u32[]{:S(2)}) copy-start(f32[2,2,256,128]{3,2,1,0:T(8,128)} %copy-done.24) | copy-start | bytes 1572868
  843.5 81.7 %copy-start.48 = (bf16[1,4,256,128]{3,2,0,1:T(8,128)(2,1)S(1)}, bf16[1,4,256,128]{3,2,0,1:T(8,128)(2,1)}, u32[]{:S(2)}) copy-start(bf16[1,4,256,128]{3,2,0,1:T(8,128)(2,1)} %copy-done.47) | copy-start | bytes 786436
  924.4 122.3 %reduce-scatter.6.cloned.1.call-start = ((), (), s32[]{:S(2)}) async-start(), calls=%async_computation.11 | async-start | bytes 3932160 | tf_op jit(solution)/shard_map/reduce_scatter | solution.py:720
  935.4 204.7 %all-reduce.5.cloned.1.call-start = ((), (), s32[]{:S(2)}) async-start(), calls=%async_computation.10 | async-start | bytes 135168 | tf_op jit(solution)/shard_map/psum | solution.py:798
  947.3 16.4 %collective-permute-start.21 = (bf16[2,512,1024]{2,1,0:T(8,128)(2,1)}, bf16[2,512,1024]{2,1,0:T(8,128)(2,1)}, u32[]{:S(2)}, u32[]{:S(2)}) collective-permute-start(bf16[2,512,1024]{2,1,0:T(8,128)(2,1)} %pad_maximum_fusion.7), channel_id=1, source_target_pairs={{0,2},{2,0},{1,3},{3,1},{4,6},{6,4},{5,7},{7,5},{8,10},{10,8},{9,1... | collective-permute-start | bytes 6291464 | tf_op jit(solution)/shard_map/ppermute | solution.py:600
  951.7 23.3 %collective-permute-start.13 = (bf16[2,512,1024]{2,1,0:T(8,128)(2,1)}, bf16[2,512,1024]{2,1,0:T(8,128)(2,1)}, u32[]{:S(2)}, u32[]{:S(2)}) collective-permute-start(bf16[2,512,1024]{2,1,0:T(8,128)(2,1)} %pad_maximum_fusion.5), channel_id=1, source_target_pairs={{0,2},{2,0},{1,3},{3,1},{4,6},{6,4},{5,7},{7,5},{8,10},{10,8},{9,1... | collective-permute-start | bytes 6291464 | tf_op jit(solution)/shard_map/ppermute | solution.py:600
  961.7 19.2 %collective-permute-start.32 = (bf16[256,1408]{1,0:T(8,128)(2,1)}, bf16[256,1408]{1,0:T(8,128)(2,1)S(1)}, u32[]{:S(2)}, u32[]{:S(2)}) collective-permute-start(bf16[256,1408]{1,0:T(8,128)(2,1)} %reduce-scatter.10.cloned.1.call-done.a), channel_id=1, source_target_pairs={{0,4},{4,0},{1,5},{5,1},{2,6},{6,2},{3,7},{7,3},{8,12},{12,8},{9,1... | collective-permute-start | bytes 2162696 | tf_op jit(solution)/shard_map/ppermute | solution.py:159
  962.6 19.3 %collective-permute-start.33 = (bf16[256,1408]{1,0:T(8,128)(2,1)}, bf16[256,1408]{1,0:T(8,128)(2,1)S(1)}, u32[]{:S(2)}, u32[]{:S(2)}) collective-permute-start(bf16[256,1408]{1,0:T(8,128)(2,1)} %reduce-scatter.10.cloned.1.call-done.a), channel_id=1, source_target_pairs={{0,2},{2,0},{1,3},{3,1},{4,6},{6,4},{5,7},{7,5},{8,10},{10,8},{9,1... | collective-permute-start | bytes 2162696 | tf_op jit(solution)/shard_map/ppermute | solution.py:160
  962.6 33.8 %collective-permute-start.36 = (bf16[256,1408]{1,0:T(8,128)(2,1)}, bf16[256,1408]{1,0:T(8,128)(2,1)}, u32[]{:S(2)}, u32[]{:S(2)}) collective-permute-start(bf16[256,1408]{1,0:T(8,128)(2,1)} %reduce-scatter.12.cloned.1.call-done.a), channel_id=1, source_target_pairs={{0,4},{4,0},{1,5},{5,1},{2,6},{6,2},{3,7},{7,3},{8,12},{12,8},{9,1... | collective-permute-start | bytes 2162696 | tf_op jit(solution)/shard_map/ppermute | solution.py:159
  968.7 78.5 %collective-permute-start.22 = (bf16[2,512,1024]{2,1,0:T(8,128)(2,1)}, bf16[2,512,1024]{2,1,0:T(8,128)(2,1)}, u32[]{:S(2)}, u32[]{:S(2)}) collective-permute-start(bf16[2,512,1024]{2,1,0:T(8,128)(2,1)} %fusion.19), channel_id=1, source_target_pairs={{0,1},{1,0},{2,3},{3,2},{4,5},{5,4},{6,7},{7,6},{8,9},{9,8},{10,11... | collective-permute-start | bytes 6291464 | tf_op jit(solution)/shard_map/ppermute | solution.py:602
  975.0 42.9 %collective-permute-start.37 = (bf16[256,1408]{1,0:T(8,128)(2,1)S(1)}, bf16[256,1408]{1,0:T(8,128)(2,1)S(1)}, u32[]{:S(2)}, u32[]{:S(2)}) collective-permute-start(bf16[256,1408]{1,0:T(8,128)(2,1)S(1)} %copy-done.18), channel_id=1, source_target_pairs={{0,2},{2,0},{1,3},{3,1},{4,6},{6,4},{5,7},{7,5},{8,10},{10,8},{9,1... | collective-permute-start | bytes 2162696 | tf_op jit(solution)/shard_map/ppermute | solution.py:160
  980.9 39.6 %collective-permute-start.40 = (bf16[256,1408]{1,0:T(8,128)(2,1)}, bf16[256,1408]{1,0:T(8,128)(2,1)}, u32[]{:S(2)}, u32[]{:S(2)}) collective-permute-start(bf16[256,1408]{1,0:T(8,128)(2,1)} %reduce-scatter.14.cloned.1.call-done.a), channel_id=1, source_target_pairs={{0,4},{4,0},{1,5},{5,1},{2,6},{6,2},{3,7},{7,3},{8,12},{12,8},{9,1... | collective-permute-start | bytes 2162696 | tf_op jit(solution)/shard_map/ppermute | solution.py:159
  981.9 40.4 %collective-permute-start.34 = (bf16[256,1408]{1,0:T(8,128)(2,1)S(1)}, bf16[256,1408]{1,0:T(8,128)(2,1)}, u32[]{:S(2)}, u32[]{:S(2)}) collective-permute-start(bf16[256,1408]{1,0:T(8,128)(2,1)S(1)} %collective-permute-done.32.b), channel_id=1, source_target_pairs={{0,2},{2,0},{1,3},{3,1},{4,6},{6,4},{5,7},{7,5},{8,10},{10,8},{9,1... | collective-permute-start | bytes 2162696 | tf_op jit(solution)/shard_map/ppermute | solution.py:160
  996.4 21.6 %collective-permute-start.28 = (bf16[256,512]{1,0:T(8,128)(2,1)}, bf16[256,512]{1,0:T(8,128)(2,1)S(1)}, u32[]{:S(2)}, u32[]{:S(2)}) collective-permute-start(bf16[256,512]{1,0:T(8,128)(2,1)} %reduce-scatter.8.cloned.1.call-done.a), channel_id=1, source_target_pairs={{0,4},{4,0},{1,5},{5,1},{2,6},{6,2},{3,7},{7,3},{8,12},{12,8},{9,1... | collective-permute-start | bytes 786440 | tf_op jit(solution)/shard_map/ppermute | solution.py:159
  1017.9 3.9 collective-permute-start.29
  1018.0 3.8 collective-permute-start.30
  1020.5 48.0 %collective-permute-start.14 = (bf16[2,512,1024]{2,1,0:T(8,128)(2,1)}, bf16[2,512,1024]{2,1,0:T(8,128)(2,1)}, u32[]{:S(2)}, u32[]{:S(2)}) collective-permute-start(bf16[2,512,1024]{2,1,0:T(8,128)(2,1)} %fusion.17), channel_id=1, source_target_pairs={{0,1},{1,0},{2,3},{3,2},{4,5},{5,4},{6,7},{7,6},{8,9},{9,8},{10,11... | collective-permute-start | bytes 6291464 | tf_op jit(solution)/shard_map/ppermute | solution.py:602
  1021.8 19.5 %collective-permute-start.41 = (bf16[256,1408]{1,0:T(8,128)(2,1)}, bf16[256,1408]{1,0:T(8,128)(2,1)}, u32[]{:S(2)}, u32[]{:S(2)}) collective-permute-start(bf16[256,1408]{1,0:T(8,128)(2,1)} %reduce-scatter.14.cloned.1.call-done.a), channel_id=1, source_target_pairs={{0,2},{2,0},{1,3},{3,1},{4,6},{6,4},{5,7},{7,5},{8,10},{10,8},{9,1... | collective-permute-start | bytes 2162696 | tf_op jit(solution)/shard_map/ppermute | solution.py:160
  1021.8 14.7 %collective-permute-start.38 = (bf16[256,1408]{1,0:T(8,128)(2,1)}, bf16[256,1408]{1,0:T(8,128)(2,1)}, u32[]{:S(2)}, u32[]{:S(2)}) collective-permute-start(bf16[256,1408]{1,0:T(8,128)(2,1)} %collective-permute-done.36.b), channel_id=1, source_target_pairs={{0,2},{2,0},{1,3},{3,1},{4,6},{6,4},{5,7},{7,5},{8,10},{10,8},{9,1... | collective-permute-start | bytes 2162696 | tf_op jit(solution)/shard_map/ppermute | solution.py:160
  1022.3 19.0 %collective-permute-start.42 = (bf16[256,1408]{1,0:T(8,128)(2,1)}, bf16[256,1408]{1,0:T(8,128)(2,1)}, u32[]{:S(2)}, u32[]{:S(2)}) collective-permute-start(bf16[256,1408]{1,0:T(8,128)(2,1)} %collective-permute-done.40.b), channel_id=1, source_target_pairs={{0,2},{2,0},{1,3},{3,1},{4,6},{6,4},{5,7},{7,5},{8,10},{10,8},{9,1... | collective-permute-start | bytes 2162696 | tf_op jit(solution)/shard_map/ppermute | solution.py:160
  1046.7 19.7 %collective-permute-start.24 = (bf16[256,1536]{1,0:T(8,128)(2,1)}, bf16[256,1536]{1,0:T(8,128)(2,1)}, u32[]{:S(2)}, u32[]{:S(2)}) collective-permute-start(bf16[256,1536]{1,0:T(8,128)(2,1)} %reduce-scatter.6.cloned.1.call-done.a), channel_id=1, source_target_pairs={{0,4},{4,0},{1,5},{5,1},{2,6},{6,2},{3,7},{7,3},{8,12},{12,8},{9,1... | collective-permute-start | bytes 2359304 | tf_op jit(solution)/shard_map/ppermute | solution.py:159
  1054.5 94.3 %collective-permute-start.25 = (bf16[256,1536]{1,0:T(8,128)(2,1)}, bf16[256,1536]{1,0:T(8,128)(2,1)}, u32[]{:S(2)}, u32[]{:S(2)}) collective-permute-start(bf16[256,1536]{1,0:T(8,128)(2,1)} %reduce-scatter.6.cloned.1.call-done.a), channel_id=1, source_target_pairs={{0,2},{2,0},{1,3},{3,1},{4,6},{6,4},{5,7},{7,5},{8,10},{10,8},{9,1... | collective-permute-start | bytes 2359304 | tf_op jit(solution)/shard_map/ppermute | solution.py:160
  1066.4 82.4 %collective-permute-start.26 = (bf16[256,1536]{1,0:T(8,128)(2,1)}, bf16[256,1536]{1,0:T(8,128)(2,1)}, u32[]{:S(2)}, u32[]{:S(2)}) collective-permute-start(bf16[256,1536]{1,0:T(8,128)(2,1)} %collective-permute-done.24.b), channel_id=1, source_target_pairs={{0,2},{2,0},{1,3},{3,1},{4,6},{6,4},{5,7},{7,5},{8,10},{10,8},{9,1... | collective-permute-start | bytes 2359304 | tf_op jit(solution)/shard_map/ppermute | solution.py:160
  (76 other events, 821.6 us)
Sparse Core Ops, SparseCore 0:
  14.5 36.5 all-reduce.6
  53.3 30.1 all-gather.8
  85.8 61.8 all-gather.6
  149.1 57.7 all-gather.14
  208.4 57.3 all-gather.10
  308.8 59.6 all-gather.12
  598.5 54.4 reduce-scatter.9
  673.5 54.1 reduce-scatter.11
  754.4 53.8 reduce-scatter.13
  924.5 24.8 reduce-scatter.7
  951.7 58.8 reduce-scatter.5
  1054.6 85.4 all-reduce.4

commit v2 on v1

v2 whole, which is shorter than its diff:
```python
import functools

import jax
import jax.numpy as jnp
from jax import lax
from jax.experimental import pallas as pl
from jax.experimental.pallas import tpu as pltpu
from jax.sharding import Mesh
from jax.sharding import PartitionSpec as P

EPSILON = 1e-06
F32 = jnp.float32
BF16 = jnp.bfloat16
LANES = 128
HALO = 16
SWAP = [(0, 1), (1, 0)]


def mm(left, right, left_dim, right_dim):
    return lax.dot_general(
        left.astype(BF16),
        right.astype(BF16),
        (((left_dim,), (right_dim,)), ((), ())),
        preferred_element_type=F32,
    )


def nn(left, right):
    return mm(left, right, 1, 0)


def nt(left, right):
    return mm(left, right, 1, 1)


def tn(left, right):
    return mm(left, right, 0, 0)


def place_scalars():
    return jnp.stack([lax.axis_index("core"), lax.axis_index("cx")]).astype(jnp.int32)


def call(kernel, grid, in_specs, out_specs, out_shape, scratch=(), aliases=None):
    return pl.pallas_call(
        kernel,
        grid_spec=pltpu.PrefetchScalarGridSpec(
            num_scalar_prefetch=1,
            grid=grid,
            in_specs=in_specs,
            out_specs=out_specs,
            scratch_shapes=list(scratch),
        ),
        out_shape=out_shape,
        input_output_aliases=aliases or {},
        compiler_params=pltpu.CompilerParams(
            dimension_semantics=("arbitrary",) * len(grid), vmem_limit_bytes=48 << 20
        ),
        cost_estimate=pl.CostEstimate(
            flops=1000, transcendentals=0, bytes_accessed=1000
        ),
    )


def split_rows(places, values, count):
    rows, width = values.shape
    half = width // (2 * count)
    if half % LANES:
        cut = values.reshape(rows, count, 2, half)
        cut = jnp.where(places[1] == 0, cut, cut[:, :, ::-1])
        return [cut[:, :, side].reshape(rows, width // 2) for side in range(2)]
    tile = max(t for t in range(16, 400, 16) if rows % t == 0)

    def kernel(where, source, *targets):
        for side in range(2):
            for shard in range(count):
                at = shard * 2 * half + (where[1] if side == 0 else 1 - where[1]) * half
                targets[side][:, shard * half : (shard + 1) * half] = source[
                    :, pl.ds(pl.multiple_of(at, LANES), half)
                ]

    return call(
        kernel,
        (rows // tile,),
        [pl.BlockSpec((tile, width), lambda i, w: (i, 0))],
        [pl.BlockSpec((tile, width // 2), lambda i, w: (i, 0))] * 2,
        [jax.ShapeDtypeStruct((rows, width // 2), values.dtype)] * 2,
    )(places, values)


def join_rows(places, values, count):
    rows, width = values[0].shape[0], 2 * values[0].shape[1]
    half = width // (2 * count)
    if half % LANES:
        cut = jnp.stack([part.reshape(rows, count, half) for part in values], axis=2)
        cut = jnp.where(places[1] == 0, cut, cut[:, :, ::-1])
        return cut.reshape(rows, width)
    tile = max(t for t in range(16, 400, 16) if rows % t == 0)

    def kernel(where, own, other, target):
        for side, source in enumerate((own, other)):
            for shard in range(count):
                at = shard * 2 * half + (where[1] if side == 0 else 1 - where[1]) * half
                target[:, pl.ds(pl.multiple_of(at, LANES), half)] = source[
                    :, shard * half : (shard + 1) * half
                ]

    return call(
        kernel,
        (rows // tile,),
        [pl.BlockSpec((tile, width // 2), lambda i, w: (i, 0))] * 2,
        pl.BlockSpec((tile, width), lambda i, w: (i, 0)),
        jax.ShapeDtypeStruct((rows, width), values[0].dtype),
    )(places, *values)


def split_small(places, values, count):
    cut = values.reshape((count, 2, values.shape[0] // (2 * count)) + values.shape[1:])
    cut = jnp.where(places[1] == 0, cut, cut[:, ::-1])
    cut = jnp.swapaxes(cut, 0, 1)
    return cut.reshape((2, values.shape[0] // 2) + values.shape[1:])


def join_small(places, values, count):
    cut = values.reshape((2, count, values.shape[1] // count) + values.shape[2:])
    cut = jnp.swapaxes(cut, 0, 1)
    cut = jnp.where(places[1] == 0, cut, cut[:, ::-1])
    return cut.reshape((2 * values.shape[1],) + values.shape[2:])


def pack_heads(places, query, key, value, heads, pair):
    half = query.shape[0] // 2

    def kernel(where, query_ref, key_ref, value_ref, out):
        out[:, :LANES] = query_ref[...]
        out[:, LANES : 2 * LANES] = key_ref[...]
        out[:, 2 * LANES :] = value_ref[...]

    spec = pl.BlockSpec((half, LANES), lambda h, w: (w[1], w[0] * heads + 2 * pair + h))
    return call(
        kernel,
        (2,),
        [spec] * 3,
        pl.BlockSpec((half, 3 * LANES), lambda h, w: (0, h)),
        jax.ShapeDtypeStruct((half, 6 * LANES), query.dtype),
    )(places, query, key, value)


def own_block(places, weight):
    half, columns = weight.shape[0] // 2, weight.shape[1] // 2
    return lax.dynamic_slice(weight, (places[1] * half, places[0] * columns), (half, columns))


def own_block_turned(places, weight):
    rows, half = weight.shape[0] // 2, weight.shape[1] // 2
    return lax.dynamic_slice(weight, (places[0] * rows, places[1] * half), (rows, half)).T


def pieces_of(own):
    across = lax.ppermute(own, "cx", SWAP)
    return [own, across, lax.ppermute(own, "core", SWAP), lax.ppermute(across, "core", SWAP)]


def pick(where, core, cx, refs, store):
    which = 2 * jnp.bitwise_xor(where[0], core) + jnp.bitwise_xor(where[1], cx)
    for index in range(4):

        @pl.when(which == index)
        def _():
            store(refs[index][...].astype(F32))


def lay_heads(places, pairs):
    half = pairs[0][0].shape[0]
    heads = 2 * len(pairs)
    width = heads * LANES

    def kernel(where, *refs):
        outs = refs[-3:]
        for pair in range(len(pairs)):

            def store(values):
                for inner in range(2):
                    head = 2 * pair + inner
                    for index in range(3):
                        at = (inner * 3 + index) * LANES
                        outs[index][:, head * LANES : (head + 1) * LANES] = values[
                            :, at : at + LANES
                        ]

            pick(
                where, pl.program_id(1), pl.program_id(0), refs[4 * pair : 4 * pair + 4], store
            )

    return call(
        kernel,
        (2, 2),
        [pl.BlockSpec(pairs[0][0].shape, lambda i, j, w: (0, 0))] * (4 * len(pairs)),
        [pl.BlockSpec((half, width), lambda i, j, w: (i, j))] * 3,
        [jax.ShapeDtypeStruct((2 * half, 2 * width), F32)] * 3,
    )(places, *(piece for pair in pairs for piece in pair))


def lay_block(places, pieces):
    half, columns = pieces[0].shape

    def kernel(where, a, b, c, d, out):
        def store(values):
            out[...] = values

        pick(where, pl.program_id(1), pl.program_id(0), (a, b, c, d), store)

    return call(
        kernel,
        (2, 2),
        [pl.BlockSpec((half, columns), lambda i, j, w: (0, 0))] * 4,
        pl.BlockSpec((half, columns), lambda i, j, w: (i, j)),
        jax.ShapeDtypeStruct((2 * half, 2 * columns), F32),
    )(places, *pieces)


def lay_block_turned(places, pieces):
    half, rows = pieces[0].shape

    def kernel(where, a, b, c, d, out):
        for side in range(2):

            def store(values):
                out[:, side * half : (side + 1) * half] = values.T

            pick(where, pl.program_id(0), side, (a, b, c, d), store)

    return call(
        kernel,
        (2,),
        [pl.BlockSpec((half, rows), lambda i, w: (0, 0))] * 4,
        pl.BlockSpec((rows, 2 * half), lambda i, w: (i, 0)),
        jax.ShapeDtypeStruct((2 * rows, 2 * half), F32),
    )(places, *pieces)


def fill_ext(ext, index, halo, first, second, size):
    ext[index, :HALO, :] = halo[...].astype(F32)
    ext[index, HALO : HALO + size, :] = first[...].astype(F32)
    ext[index, HALO + size :, :] = second[...].astype(F32)


def links_of(ids, total):
    own = ids[0, HALO : HALO + total, :]
    return [
        (ids[0, HALO - 3 + tap : HALO - 3 + tap + total, :] == own).astype(F32) for tap in range(4)
    ]


def conv_of(ext, index, taps, links, total):
    result = None
    for tap in range(4):
        term = (
            taps[index, 0, tap : tap + 1, :]
            * ext[index, HALO - 3 + tap : HALO - 3 + tap + total, :]
            * links[tap]
        )
        result = term if result is None else result + term
    return result


def sigmoid(values):
    return 1.0 / (1.0 + jnp.exp(-values))


def column_of(values, head):
    lane = lax.broadcasted_iota(jnp.int32, values.shape, 1)
    return jnp.sum(jnp.where(lane == head, values, 0.0), axis=1, keepdims=True)


def marks(ids, rows, chunk, size):
    start = HALO + chunk * size
    column = ids[0, start : start + size, :]
    before = ids[0, start - 1 : start, :]
    last = ids[0, start + size - 1 : start + size, :]
    first = (column == before).astype(F32)
    tail = (column == last).astype(F32)
    whole = (last == before).astype(F32)
    same = column == rows[0, chunk : chunk + 1, :]
    row = lax.broadcasted_iota(jnp.int32, (size, size), 0)
    col = lax.broadcasted_iota(jnp.int32, (size, size), 1)
    return first, tail, whole, same & (row > col), same & (row >= col)


def inverse_units(stricts, size):
    row = lax.broadcasted_iota(jnp.int32, (size, size), 0)
    col = lax.broadcasted_iota(jnp.int32, (size, size), 1)
    mixed = jnp.bitwise_xor(row, col)
    results = [
        jnp.where(row == col, 1.0, jnp.where(mixed == 1, -strict, 0.0)) for strict in stricts
    ]
    stricts = [strict.astype(BF16) for strict in stricts]
    block = 2
    while block < size:
        pair = (mixed >= block) & (mixed < 2 * block)
        lows = [result.astype(BF16) for result in results]
        parts = [jnp.where(pair, strict, 0.0) for strict in stricts]
        steps = [nn(part, low).astype(BF16) for part, low in zip(parts, lows)]
        results = [
            result - nn(low, step) for result, low, step in zip(results, lows, steps)
        ]
        block *= 2
    return [result.astype(BF16) for result in results]


def forward_one(where, q0, k0, v0, q1, k1, v1, qh, kh, vh, taps, ids, rows, r0, r1, *rest, size, base):
    query, key, value, inverse, final, ext = rest
    head = base + pl.program_id(1)
    total = 2 * size
    for index, group in enumerate(((qh, q0, q1), (kh, k0, k1), (vh, v0, v1))):
        fill_ext(ext, index, *group, size)
    links = links_of(ids, total)
    out = []
    for index in range(3):
        conv = conv_of(ext, index, taps, links, total)
        act = conv * sigmoid(conv)
        if index < 2:
            act = act * lax.rsqrt(jnp.sum(act * act, axis=1, keepdims=True) + EPSILON)
        out.append(act.astype(BF16))
    for target, values in zip((query, key, value), out):
        target[0, 0] = values[:size]
        target[0, 1] = values[size:]
    chunks = []
    for chunk, rates in enumerate((r0, r1)):
        first, tail, whole, strict, _ = marks(ids, rows, chunk, size)
        rate = column_of(rates[...], head)
        keys = out[1][chunk * size : (chunk + 1) * size]
        chunks.append((first, tail, whole, rate, keys, jnp.where(strict, rate * nt(keys, keys), 0.0)))
    inverses = inverse_units([item[-1] for item in chunks], size)
    state = None
    for chunk, (first, tail, whole, rate, keys, _) in enumerate(chunks):
        fresh = out[2][chunk * size : (chunk + 1) * size].astype(F32)
        inverse[0, 0, chunk] = inverses[chunk]
        if chunk:
            fresh = fresh - first * nt(keys, state)
        fresh = nn(inverses[chunk], rate * fresh)
        added = tn(tail * fresh, keys)
        state = added if state is None else whole * state + added
    final[0, 0] = state.astype(BF16)


def forward_two(where, query, key, value, inverse, ids, rows, r0, r1, incoming, gain, *rest, size, scale, base):
    head_low, mixed_out, fresh_out, middle = rest[-4:]
    head = base + pl.program_id(1)
    state = incoming[0, 0].astype(F32)
    for chunk, rates in enumerate((r0, r1)):
        first, tail, whole, _, lower = marks(ids, rows, chunk, size)
        rate = column_of(rates[...], head)
        keys, queries = key[0, chunk], query[0, chunk]
        if chunk:
            middle[0, 0] = state.astype(BF16)
        rest_rows = value[0, chunk].astype(F32) - first * nt(keys, state)
        fresh = nn(inverse[0, 0, chunk], rate * rest_rows)
        fresh_out[0, chunk] = fresh.astype(BF16)
        inner = jnp.where(lower, nt(queries, keys), 0.0)
        mixed = scale * (first * nt(queries, state) + nn(inner, fresh))
        mixed_out[0, chunk] = mixed
        normed = mixed * lax.rsqrt(jnp.mean(mixed * mixed, axis=1, keepdims=True) + EPSILON)
        slot = where[0] if chunk == 0 else 1 - where[0]
        head_low[slot, 0] = (normed * gain[...]).astype(BF16)
        if chunk == 0:
            state = whole * state + tn(tail * fresh, keys)


def backward_one(where, d_head, mixed, query, key, inverse, ids, rows, r0, r1, gain, *rest, size, scale, base):
    d_out, d_state_out, d_gain = rest
    head = base + pl.program_id(1)
    total = jnp.zeros((1, LANES), F32)
    d_state = None
    for chunk in (1, 0):
        first, tail, whole, _, lower = marks(ids, rows, chunk, size)
        rate = column_of((r0, r1)[chunk][...], head)
        keys, queries = key[0, chunk], query[0, chunk]
        slot = where[0] if chunk == 0 else 1 - where[0]
        grad = d_head[slot, 0].astype(F32)
        values = mixed[0, chunk]
        inv_rms = lax.rsqrt(jnp.mean(values * values, axis=1, keepdims=True) + EPSILON)
        normed = values * inv_rms
        total = total + jnp.sum(grad * normed, axis=0, keepdims=True)
        scaled = grad * gain[...]
        d_mixed = inv_rms * (scaled - normed * jnp.mean(scaled * normed, axis=1, keepdims=True))
        d_low = (scale * d_mixed).astype(BF16)
        d_out[0, chunk] = d_low
        inner = jnp.where(lower, nt(queries, keys), 0.0)
        d_fresh = tn(inner, d_low)
        if d_state is not None:
            d_fresh = d_fresh + tail * nt(keys, d_state)
        d_rest = rate * tn(inverse[0, 0, chunk], d_fresh)
        change = tn(first * d_low.astype(F32), queries) - tn(first * d_rest, keys)
        d_state = change if d_state is None else whole * d_state + change
    d_state_out[0, 0] = d_state.astype(BF16)
    d_gain[0, 0] = jnp.broadcast_to(total, (8, LANES))


def backward_two(where, q0, k0, v0, q1, k1, v1, qh, kh, vh, taps, ids, rows, r0, r1, *rest, size, base):
    query, key, value, inverse, fresh_in, d_in, incoming, middle, d_final = rest[:9]
    d_raw, d_edge, d_rates, d_taps = rest[9:13]
    ext, d_ext, d_rows = rest[13:]
    head = base + pl.program_id(1)
    total = 2 * size
    for index, group in enumerate(((qh, q0, q1), (kh, k0, k1), (vh, v0, v1))):
        fill_ext(ext, index, *group, size)
    d_state = d_final[0, 0].astype(F32)

    @pl.when(pl.program_id(1) == 0)
    def _():
        d_rates[...] = jnp.zeros_like(d_rates)

    for chunk in (1, 0):
        first, tail, whole, strict, lower = marks(ids, rows, chunk, size)
        rate = column_of((r0, r1)[chunk][...], head)
        keys, queries, fresh = key[0, chunk], query[0, chunk], fresh_in[0, chunk]
        inv, d_low = inverse[0, 0, chunk], d_in[0, chunk]
        state = (middle if chunk else incoming)[0, 0]
        d_mix = d_low.astype(F32)
        inner = jnp.where(lower, nt(queries, keys), 0.0)
        gram = jnp.where(strict, nt(keys, keys), 0.0)
        d_fresh = tn(inner, d_low) + tail * nt(keys, d_state)
        turned = tn(inv, d_fresh)
        d_rest = rate * turned
        rest_rows = value[0, chunk].astype(F32) - first * nt(keys, state)
        error = rest_rows - nn(gram, fresh)
        d_rate = jnp.sum(turned * error, axis=1, keepdims=True) * rate * (1.0 - rate)
        d_inner = jnp.where(lower, nt(d_low, fresh), 0.0)
        d_gram = rate * jnp.where(strict, -nt(turned, fresh), 0.0)
        d_query = first * nn(d_low, state) + nn(d_inner, keys)
        d_key = (
            tn(d_inner, queries)
            + tail * nn(fresh, d_state)
            - nn(first * d_rest, state)
            + nn(d_gram, keys)
            + tn(d_gram, keys)
        )
        for index, values in enumerate((d_query, d_key, d_rest)):
            d_rows[index, chunk * size : (chunk + 1) * size, :] = values
        lane = lax.broadcasted_iota(jnp.int32, (size, LANES), 1)
        d_rates[0, chunk] = d_rates[0, chunk] + jnp.where(lane == head, d_rate, 0.0)
        if chunk:
            d_state = (
                whole * d_state + tn(first * d_mix, queries) - tn(first * d_rest, keys)
            )
    links = links_of(ids, total)
    for index in range(3):
        conv = conv_of(ext, index, taps, links, total)
        sig = sigmoid(conv)
        d_act = d_rows[index].astype(BF16).astype(F32)
        if index < 2:
            act = conv * sig
            inv_norm = lax.rsqrt(jnp.sum(act * act, axis=1, keepdims=True) + EPSILON)
            unit = act * inv_norm
            d_act = (d_act - unit * jnp.sum(unit * d_act, axis=1, keepdims=True)) * inv_norm
        d_conv = d_act * sig * (1.0 + conv * (1.0 - sig))
        d_ext[...] = jnp.zeros_like(d_ext)
        for tap in range(4):
            window = slice(HALO - 3 + tap, HALO - 3 + tap + total)
            linked = d_conv * links[tap]
            d_taps[0, index, 0, tap : tap + 1, :] = jnp.sum(
                linked * ext[index, window, :], axis=0, keepdims=True
            )
            d_ext[window, :] = d_ext[window, :] + taps[index, 0, tap : tap + 1, :] * linked
        lanes = slice(index * LANES, (index + 1) * LANES)
        d_edge[0, :, lanes] = d_ext[:HALO, :].astype(BF16)
        d_raw[where[0], 0, :, lanes] = d_ext[HALO : HALO + size, :].astype(BF16)
        d_raw[1 - where[0], 0, :, lanes] = d_ext[HALO + size :, :].astype(BF16)


def mixer_calls(places, pair, raw, rates, ids, rows, taps, gain, heads, seqs, size, scale):
    base = 2 * pair

    def slot_of(chunk, w):
        return w[0] if chunk == 0 else 1 - w[0]

    def raw_spec(chunk, part):
        return pl.BlockSpec(
            (size, LANES), lambda b, h, w: (slot_of(chunk, w) * seqs + b, 3 * h + part)
        )

    def rate_spec(chunk):
        return pl.BlockSpec((size, LANES), lambda b, h, w: (slot_of(chunk, w) * seqs + b, 0))

    halo_base = 2 * seqs * size // HALO

    def halo_spec(part):
        return pl.BlockSpec((HALO, LANES), lambda b, h, w: (halo_base + b, 3 * h + part))

    conv_specs = (
        [raw_spec(c, p) for c in range(2) for p in range(3)]
        + [halo_spec(p) for p in range(3)]
        + [
            pl.BlockSpec((3, 1, 4, LANES), lambda b, h, w: (0, base + h, 0, 0)),
            pl.BlockSpec((1, HALO + 2 * size, 1), lambda b, h, w: (b, 0, 0)),
            pl.BlockSpec((1, 2, size), lambda b, h, w: (b, 0, 0)),
            rate_spec(0),
            rate_spec(1),
        ]
    )
    conv_args = (raw,) * 9 + (taps, ids, rows, rates, rates)
    id_specs, id_args = conv_specs[10:], conv_args[10:]
    act_spec = pl.BlockSpec((1, 2, size, LANES), lambda b, h, w: (b, 0, 0, h))
    act_shape = (seqs, 2, size, 2 * LANES)
    state_spec = pl.BlockSpec((1, 1, LANES, LANES), lambda b, h, w: (b, h, 0, 0))
    state_shape = jax.ShapeDtypeStruct((seqs, 2, LANES, LANES), BF16)
    inv_spec = pl.BlockSpec((1, 1, 2, size, size), lambda b, h, w: (b, h, 0, 0, 0))
    inv_shape = jax.ShapeDtypeStruct((seqs, 2, 2, size, size), BF16)
    slot_spec = pl.BlockSpec((2, 1, size, LANES), lambda b, h, w: (0, b, 0, base + h))
    slot_shape = jax.ShapeDtypeStruct((2, seqs, size, heads * LANES), BF16)
    gain_spec = pl.BlockSpec((1, LANES), lambda b, h, w: (0, 0))
    low = jax.ShapeDtypeStruct(act_shape, BF16)
    grid = (seqs, 2)

    def one():
        return call(
            functools.partial(forward_one, size=size, base=base),
            grid,
            conv_specs,
            [act_spec] * 3 + [inv_spec, state_spec],
            [low] * 3 + [inv_shape, state_shape],
            [pltpu.VMEM((3, HALO + 2 * size, LANES), F32)],
        )(places, *conv_args)

    def two(query, key, value, inverse, incoming, before=()):
        args = (query, key, value, inverse, *id_args, incoming, gain)
        return call(
            functools.partial(forward_two, size=size, scale=scale, base=base),
            grid,
            [act_spec] * 3
            + [inv_spec]
            + id_specs
            + [state_spec, gain_spec]
            + [pl.BlockSpec(memory_space=pl.ANY)] * len(before),
            [slot_spec, act_spec, act_spec, state_spec],
            [slot_shape, jax.ShapeDtypeStruct(act_shape, F32), low, state_shape],
            aliases={1 + len(args): 0} if before else None,
        )(places, *args, *before)

    def three(d_head, mixed, query, key, inverse):
        return call(
            functools.partial(backward_one, size=size, scale=scale, base=base),
            grid,
            [slot_spec, act_spec, act_spec, act_spec, inv_spec] + id_specs + [gain_spec],
            [act_spec, state_spec, pl.BlockSpec((1, 1, 8, LANES), lambda b, h, w: (b, h, 0, 0))],
            [low, state_shape, jax.ShapeDtypeStruct((seqs, 2, 8, LANES), F32)],
        )(places, d_head, mixed, query, key, inverse, *id_args, gain)

    def four(query, key, value, inverse, fresh, d_low, incoming, middle, d_final):
        return call(
            functools.partial(backward_two, size=size, base=base),
            grid,
            conv_specs + [act_spec] * 3 + [inv_spec, act_spec, act_spec] + [state_spec] * 3,
            [
                pl.BlockSpec((2, 1, size, 3 * LANES), lambda b, h, w: (0, b, 0, h)),
                pl.BlockSpec((1, HALO, 3 * LANES), lambda b, h, w: (b, 0, h)),
                pl.BlockSpec((1, 2, size, LANES), lambda b, h, w: (b, 0, 0, 0)),
                pl.BlockSpec((1, 3, 1, 4, LANES), lambda b, h, w: (b, 0, h, 0, 0)),
            ],
            [
                jax.ShapeDtypeStruct((2, seqs, size, 6 * LANES), BF16),
                jax.ShapeDtypeStruct((seqs, HALO, 6 * LANES), BF16),
                jax.ShapeDtypeStruct((seqs, 2, size, LANES), F32),
                jax.ShapeDtypeStruct((seqs, 3, 2, 4, LANES), F32),
            ],
            [
                pltpu.VMEM((3, HALO + 2 * size, LANES), F32),
                pltpu.VMEM((HALO + 2 * size, LANES), F32),
                pltpu.VMEM((3, 2 * size, LANES), F32),
            ],
        )(
            places,
            *conv_args,
            query,
            key,
            value,
            inverse,
            fresh,
            d_low,
            incoming,
            middle,
            d_final,
        )

    return one, two, three, four


def dot_nn(left, right):
    return lax.dot_general(left, right, (((1,), (0,)), ((), ())), preferred_element_type=F32)


def dot_nt(left, right):
    return lax.dot_general(left, right, (((1,), (1,)), ((), ())), preferred_element_type=F32)


def dot_tn(left, right):
    return lax.dot_general(left, right, (((0,), (0,)), ((), ())), preferred_element_type=F32)


def rms_split(values, gain):
    total = sum(jnp.sum(part * part, axis=1, keepdims=True) for part in values)
    factor = lax.rsqrt(total / (2 * values[0].shape[1]) + EPSILON)
    return [part * factor * own for part, own in zip(values, gain)]


def tie(value, *after):
    return lax.optimization_barrier((value, after))[0]


class Steps:
    def __init__(self):
        self.last = ()

    def wait(self, *values):
        self.last = (self.last, values)

    def __call__(self, fn, *args):
        traced, static = [], []
        for arg in args:
            leaves = jax.tree.leaves(arg)
            static.append(not leaves or not all(hasattr(leaf, "dtype") for leaf in leaves))
            if not static[-1]:
                traced.append(arg)
        traced = iter(tie(tuple(traced), self.last))
        result = fn(*(arg if fixed else next(traced) for arg, fixed in zip(args, static)))
        self.last = result
        return result


def across_cores(values):
    return [jnp.concatenate([part, lax.ppermute(part, "core", SWAP)]) for part in values]


def sum_cores(mine, other):
    arrived = [lax.ppermute(away.astype(BF16), "core", SWAP) for away in other]
    return [(own + more.astype(F32)).astype(BF16) for own, more in zip(mine, arrived)]


def sum_heads(mine, other):
    return [(part, lax.ppermute(part, "tp", SWAP)) for part in sum_cores(mine, other)]


def sum_over(values, axis, hop):
    partners = [(index, index ^ hop) for index in range(lax.axis_size(axis))]
    return (values.astype(F32) + lax.ppermute(values, axis, partners).astype(F32)).astype(BF16)


def add_pairs(pairs, values):
    return [base + (a.astype(F32) + b.astype(F32)) for (a, b), base in zip(pairs, values)]


def dots(dot, left, right):
    return dot(left[0], right[0]) + dot(left[1], right[1])


def shards(
    hidden_in,
    attn_gain,
    query_weight,
    key_weight,
    value_weight,
    conv_weight,
    beta_weight,
    out_gain,
    out_weight,
    ffn_gain,
    gate_weight,
    up_weight,
    down_weight,
    cotangent,
    segment_ids,
):
    count = lax.axis_size("shard")
    places = place_scalars()
    core, cx = places[0], places[1]
    micro, local, size, width = hidden_in.shape
    seqs = micro * local
    own_rows = seqs * size
    heads_tp = conv_weight.shape[2]
    heads = heads_tp // 2
    scale = LANES ** (-0.5)

    first_rows, other_rows = slice(0, own_rows), slice(own_rows, 2 * own_rows)

    small = jnp.concatenate(
        [
            attn_gain,
            ffn_gain,
            out_gain,
            conv_weight.reshape(-1),
            beta_weight.reshape(-1),
        ]
    )
    unpadded = small.size
    small = jnp.pad(small, (0, -unpadded % (16 * LANES))).reshape(-1, LANES)
    small = lax.all_gather(small, "shard", axis=0).reshape(count, -1)
    piece_d = attn_gain.shape[0]
    entry = out_gain.shape[0]
    at = 2 * piece_d + entry
    gain_in = split_small(places, small[:, :piece_d].reshape(-1), count).astype(F32)
    gain_ffn = split_small(places, small[:, piece_d : 2 * piece_d].reshape(-1), count).astype(F32)
    gain_head = small[:, 2 * piece_d : at].reshape(1, LANES).astype(F32)
    conv_size = conv_weight.size
    taps = small[:, at : at + conv_size].reshape(count, 4, 3, heads_tp, entry)
    taps = taps.transpose(2, 3, 1, 0, 4).reshape(3, heads_tp, 4, LANES)
    taps = lax.dynamic_slice_in_dim(taps, core * heads, heads, axis=1).astype(F32)
    beta = small[:, at + conv_size : unpadded].reshape(width, heads_tp)
    beta = lax.dynamic_slice_in_dim(beta, core * heads, heads, axis=1)
    beta = jnp.pad(beta, ((0, 0), (0, LANES - heads)))
    beta = split_small(places, beta, count)
    gain_in = [gain_in[side : side + 1] for side in range(2)]
    gain_ffn = [gain_ffn[side : side + 1] for side in range(2)]

    hidden_own = hidden_in.reshape(own_rows, width)
    hidden_other = lax.ppermute(hidden_own, "core", SWAP)
    grad_own = cotangent.reshape(own_rows, width)
    grad_all = split_rows(
        places, jnp.concatenate([grad_own, lax.ppermute(grad_own, "core", SWAP)]), count
    )
    ids_own = segment_ids.reshape(seqs, size)
    ids_other = lax.ppermute(ids_own, "core", SWAP)
    late = jnp.where(core == 1, hidden_own, hidden_other).reshape(seqs, size, width)[:, size - HALO :]
    early_ids = jnp.where(core == 0, ids_own, ids_other)
    late_ids = jnp.where(core == 1, ids_own, ids_other)
    halo = lax.ppermute(late, "cx", [(0, 1)]).reshape(seqs * HALO, width)
    halo_ids = lax.ppermute(late_ids[:, size - HALO :], "cx", [(0, 1)])
    halo_ids = jnp.where(cx == 0, -1, halo_ids)
    ids = jnp.concatenate([halo_ids, early_ids, late_ids], axis=1)[..., None]
    id_rows = jnp.stack([early_ids, late_ids], axis=1)
    hidden_all = split_rows(places, jnp.concatenate([hidden_own, hidden_other, halo]), count)

    hidden_wide = [part.astype(F32) for part in hidden_all]
    normed_low = [part.astype(BF16) for part in rms_split(hidden_wide, gain_in)]
    rates = sigmoid(dots(dot_nn, normed_low, beta))

    def gathered(piece):
        return lax.all_gather(piece, "shard", axis=0, tiled=True)

    def with_other(own, *after):
        return [own, lax.ppermute(tie(own, *after), "cx", SWAP)]

    pairs = range(heads // 2)
    weights = (query_weight, key_weight, value_weight)
    packs = [pack_heads(places, *weights, heads, pair) for pair in pairs]
    joint = []
    for piece in packs:
        joint.append(with_other(gathered(piece), *(part[1] for part in joint)))
    outer_own = gathered(tie(own_block_turned(places, out_weight), packs[-1]))
    gates_own = gathered(tie(own_block(places, gate_weight), hidden_all))
    ups_own = gathered(tie(own_block(places, up_weight), normed_low, rates))
    downs_own = gathered(tie(own_block_turned(places, down_weight), grad_all, joint[0][1]))
    outer = with_other(outer_own, joint[-1][1])

    raws = [dots(dot_nn, normed_low, part).astype(BF16) for part in joint]
    calls = [
        mixer_calls(
            places, pair, raws[pair], rates, ids, id_rows, taps, gain_head, heads, seqs, size, scale
        )
        for pair in pairs
    ]
    firsts = [one() for one, *_ in calls]
    incomings = [lax.ppermute(first[-1], "cx", [(0, 1)]) for first in firsts]
    seconds = []
    for pair in pairs:
        before = (seconds[-1][0],) if seconds else ()
        seconds.append(calls[pair][1](*firsts[pair][:4], incomings[pair], before))
    head_low = seconds[-1][0]

    head_rows = head_low.reshape(2 * own_rows, heads * LANES)

    def out_rows(rows):
        return [dot_nt(rows, part) for part in outer]

    hidden_f32 = [part[:own_rows].astype(F32) for part in hidden_all]
    mixer_pairs = sum_heads(out_rows(head_rows[:own_rows]), out_rows(head_rows[own_rows:]))
    gates = with_other(gates_own, outer[1], [pair[0] for pair in mixer_pairs])
    ups = with_other(ups_own, gates[1])
    downs = with_other(downs_own, ups[1])
    resid = add_pairs(mixer_pairs, hidden_f32)
    normed_ffn, ffn_pull = jax.vjp(rms_split, resid, gain_ffn)
    ffn_low = across_cores([part.astype(BF16) for part in normed_ffn])

    def across(part):
        return lax.ppermute(part, "cx", SWAP)

    def over_shard(total):
        return lax.psum_scatter(total, "shard", scatter_dimension=0, tiled=True)

    def grad_of(rows, grads):
        return dot_tn(rows, grads).astype(BF16)

    def grad_with(rows, grads, arrived):
        return (dot_tn(rows, grads) + arrived.astype(F32)).astype(BF16)

    steps = Steps()
    gate = steps(dots, dot_nn, ffn_low, gates)

    def activate(ffn_low, ups, gate):
        up = dots(dot_nn, ffn_low, ups)
        return up, (jax.nn.silu(gate) * up).astype(BF16)

    up, act = steps(activate, ffn_low, ups, gate)
    down_own = over_shard(steps(grad_of, grad_all[0], act))
    down_other = over_shard(steps(grad_of, grad_all[1], act))

    def ffn_grads(grad_all, downs, gate, up):
        d_act = dots(dot_nn, grad_all, downs).astype(BF16).astype(F32)
        sig = jax.nn.sigmoid(gate)
        d_gate = (d_act * up * sig * (1.0 + gate * (1.0 - sig))).astype(BF16)
        return d_gate, (d_act * gate * sig).astype(BF16)

    steps.wait(down_own)
    d_gate, d_up = steps(ffn_grads, grad_all, downs, gate, up)
    gate_sent = across(steps(grad_of, ffn_low[1], d_gate))

    def ffn_back(d_gate, d_up, gates, ups, rows):
        return [dot_nt(d_gate[rows], gates[i]) + dot_nt(d_up[rows], ups[i]) for i in range(2)]

    def away(fn, *args):
        values = steps(lambda *args: [part.astype(BF16) for part in fn(*args, other_rows)], *args)
        return [lax.ppermute(part, "core", SWAP) for part in values]

    def here(fn, arrived, *args):
        def total(arrived, *args):
            return [
                (own + more.astype(F32)).astype(BF16)
                for own, more in zip(fn(*args, first_rows), arrived)
            ]

        return steps(total, arrived, *args)

    def with_tp(parts):
        return [(part, lax.ppermute(part, "tp", SWAP)) for part in parts]

    args = (d_gate, d_up, gates, ups)
    arrived = away(ffn_back, *args)
    d_ffn_pairs = with_tp(here(ffn_back, arrived, *args))
    up_dot = steps(grad_of, ffn_low[1], d_up)

    def down_rows(act, downs, rows):
        return [dot_nt(act[rows], part) for part in downs]

    arrived = away(down_rows, act, downs)
    down_parts = here(down_rows, arrived, act, downs)
    gate_total = steps(grad_with, ffn_low[0], d_gate, gate_sent)
    steps.wait(down_other)
    grad_gate = over_shard(gate_total)

    def resid_back(d_ffn_pairs, grad_all):
        d_ffn = add_pairs(d_ffn_pairs, [jnp.zeros(part[0].shape, F32) for part in d_ffn_pairs])
        d_resid, sum_ffn_gain = ffn_pull(d_ffn)
        d_resid = [part[:own_rows].astype(F32) + more for part, more in zip(grad_all, d_resid)]
        return d_resid, sum_ffn_gain, [part.astype(BF16) for part in d_resid]

    d_resid, sum_ffn_gain, resid_own = steps(resid_back, d_ffn_pairs, grad_all)
    down_pairs = with_tp(tie(down_parts, resid_own))
    resid_other = [lax.ppermute(part, "core", SWAP) for part in resid_own]
    resid_low = steps(
        lambda own, other: [jnp.concatenate(parts) for parts in zip(own, other)],
        resid_own,
        resid_other,
    )
    outer_sent = across(steps(grad_of, resid_low[1], head_rows))
    d_head = steps(lambda rows, outer: dots(dot_nn, rows, outer).astype(BF16), resid_low, outer)
    d_head = d_head.reshape(head_low.shape)
    thirds = []
    for pair in pairs:
        thirds.append(
            steps(calls[pair][2], d_head, seconds[pair][1], *firsts[pair][:2], firsts[pair][3])
        )
    d_finals = [lax.ppermute(third[1], "cx", [(1, 0)]) for third in thirds]
    up_sent = across(tie(up_dot, d_finals, outer_sent))
    outer_total = steps(grad_with, resid_low[0], head_rows, outer_sent)
    grad_outer = over_shard(outer_total)

    def with_edge(d_raw, d_edge):
        window = (1 - core, 0, size - HALO, 0)
        edge_rows = lax.dynamic_slice(d_raw, window, (1,) + d_edge.shape)
        return lax.dynamic_update_slice(
            d_raw, (edge_rows.astype(F32) + d_edge.astype(F32)[None]).astype(BF16), window
        ).reshape(2 * own_rows, -1)

    def joint_step(d_raw, d_edge, rows):
        d_raw = with_edge(d_raw, d_edge)
        return d_raw, grad_of(rows, d_raw)

    normed_rows = [part[: 2 * own_rows] for part in normed_low]
    steps.wait(grad_gate)
    fourths, edges = [], []
    for pair in pairs:
        query, key, value, inverse, _ = firsts[pair]
        _, _, fresh, middle = seconds[pair]
        fourth = steps(
            calls[pair][3],
            query,
            key,
            value,
            inverse,
            fresh,
            thirds[pair][0],
            incomings[pair],
            middle,
            d_finals[pair],
        )
        edges.append(lax.ppermute(fourth[1], "cx", [(1, 0)]))
        fourths.append(fourth)
    steps.wait(grad_outer)
    d_raws, joint_sents = [], []
    for pair in pairs:
        d_raw, joint_dot = steps(joint_step, fourths[pair][0], edges[pair], normed_rows[1])
        d_raws.append(d_raw)
        joint_sents.append(across(joint_dot))
    up_total = steps(grad_with, ffn_low[0], d_up, up_sent)
    grad_up = over_shard(up_total)

    def logit_step(rates, rows):
        d_rates = sum(rates)
        d_logit = jnp.where(core == 0, d_rates, d_rates[:, ::-1]).transpose(1, 0, 2, 3)
        d_logit = d_logit.reshape(2 * own_rows, LANES).astype(BF16)
        return d_logit, jnp.stack([dot_tn(part, d_logit)[:, :heads] for part in rows])

    d_logit, sum_rate = steps(logit_step, [fourth[2] for fourth in fourths], normed_rows)

    def normed_back(d_raws, d_logit, joint, beta, rows):
        return [
            sum(dot_nt(d_raw[rows], part[i]) for d_raw, part in zip(d_raws, joint))
            + dot_nt(d_logit[rows], beta[i])
            for i in range(2)
        ]

    args = (d_raws, d_logit, joint, beta)
    arrived = away(normed_back, *args)
    d_normed_pairs = with_tp(here(normed_back, arrived, *args))
    result = steps(add_pairs, down_pairs, resid)
    result_rows = steps(
        lambda result: join_rows(places, [part.astype(BF16) for part in result], count), result
    )
    sum_head_gain = sum(jnp.sum(third[2][:, :, 0, :], axis=(0, 1)) for third in thirds)
    sum_head_gain = sum_over(sum_head_gain.astype(BF16), "tp", 1).astype(F32)
    grad_joint = [over_shard(steps(grad_with, normed_rows[0], d_raws[0], joint_sents[0]))]
    grad_down = steps(
        lambda own, other: (own.astype(F32) + other.astype(F32)).astype(BF16),
        down_own,
        across(tie(down_other, joint_sents[0])),
    )

    def input_back(d_normed_pairs, d_resid):
        d_normed = add_pairs(d_normed_pairs, [jnp.zeros(part.shape, F32) for part in d_resid])
        _, norm_pull = jax.vjp(rms_split, hidden_f32, gain_in)
        d_hidden, sum_attn_gain = norm_pull(d_normed)
        return sum_attn_gain, [(a + b).astype(BF16) for a, b in zip(d_resid, d_hidden)]

    steps.wait(grad_up)
    sum_attn_gain, input_halves = steps(input_back, d_normed_pairs, d_resid)
    grad_joint += [
        over_shard(steps(grad_with, normed_rows[0], d_raws[pair], joint_sents[pair]))
        for pair in pairs[1:]
    ]
    input_rows = steps(lambda halves: join_rows(places, halves, count), input_halves)
    out_down = lay_block_turned(places, pieces_of(grad_down))
    out_gate = lay_block(places, pieces_of(grad_gate))
    out_up = lay_block(places, pieces_of(grad_up))

    d_taps = jnp.concatenate([fourth[3] for fourth in fourths], axis=2)
    sum_taps = jnp.sum(d_taps, axis=0).transpose(2, 0, 1, 3)
    sum_rate = join_small(places, sum_rate, count)
    gains = jnp.concatenate(
        [
            join_small(places, jnp.concatenate(sum_attn_gain), count),
            join_small(places, jnp.concatenate(sum_ffn_gain), count),
            sum_head_gain,
        ]
    ).astype(BF16)
    gains = sum_over(gains, "core", 1)
    packed = jnp.concatenate(
        [gains, sum_taps.reshape(-1).astype(BF16), sum_rate.reshape(-1).astype(BF16)]
    )
    packed = sum_over(packed, "cx", 1)
    hop = 1
    while hop < count:
        packed = sum_over(packed, "shard", hop)
        hop *= 2
    own = lax.axis_index("shard")
    ends = [width, 2 * width, 2 * width + LANES, 2 * width + LANES + sum_taps.size]
    grad_attn_gain = lax.dynamic_slice_in_dim(packed[: ends[0]], own * piece_d, piece_d)
    grad_ffn_gain = lax.dynamic_slice_in_dim(packed[ends[0] : ends[1]], own * piece_d, piece_d)
    grad_out_gain = lax.dynamic_slice_in_dim(packed[ends[1] : ends[2]], own * entry, entry)
    own_conv = lax.dynamic_slice_in_dim(
        packed[ends[2] : ends[3]].reshape(4, 3, heads, LANES), own * entry, entry, axis=3
    )
    own_beta = lax.dynamic_slice_in_dim(
        packed[ends[3] :].reshape(width, heads), own * piece_d, piece_d, axis=0
    )

    def both_cores(values, axis):
        other = lax.ppermute(values, "core", SWAP)
        return jnp.where(
            core == 0,
            jnp.concatenate([values, other], axis=axis),
            jnp.concatenate([other, values], axis=axis),
        ).astype(F32)

    grad_out_weight = lay_block_turned(places, pieces_of(grad_outer))
    grad_query, grad_key, grad_value = lay_heads(places, [pieces_of(part) for part in grad_joint])
    return (
        result_rows.reshape(hidden_in.shape),
        input_rows.reshape(hidden_in.shape),
        grad_attn_gain.astype(F32),
        grad_query,
        grad_key,
        grad_value,
        both_cores(own_conv, 2),
        both_cores(own_beta, 1),
        grad_out_gain.astype(F32),
        grad_out_weight,
        grad_ffn_gain.astype(F32),
        out_gate,
        out_up,
        out_down,
    )


def solution(mesh):
    shard, ctx, tp = (mesh.shape[name] for name in ("shard", "ctx", "tp"))
    cores = Mesh(
        mesh.devices.reshape(shard, ctx // 2, 2, tp), ("shard", "cx", "core", "tp")
    )
    tokens = P(None, "shard", ("cx", "core"), None)
    outer = P("shard", "tp")
    turned = P("tp", "shard")
    conv = P(None, None, "tp", "shard")
    split = P("shard")
    return jax.shard_map(
        shards,
        mesh=cores,
        in_specs=(
            tokens,
            split,
            outer,
            outer,
            outer,
            conv,
            outer,
            split,
            turned,
            split,
            outer,
            outer,
            turned,
            tokens,
            P(None, "shard", ("cx", "core")),
        ),
        out_specs=(
            tokens,
            tokens,
            split,
            outer,
            outer,
            outer,
            conv,
            outer,
            split,
            turned,
            split,
            outer,
            outer,
            turned,
        ),
        check_vma=False,
    )
```

time: 1170 us -> 918 us (0.78)
  waiting for transfers between devices: 640 us -> 345 us
  local copies, waits for them, and re-layouts: 49.3 us -> 74.8 us
    ppermute x23 -> x45, waiting for transfers between devices: 452 us -> 268 us  [the longest x6 114 us: with_other(): return [own, lax.ppermute(tie(own, *after), 'cx', SWAP)]]
    all_gather x5 -> x6, waiting for transfers between devices: 86.4 us -> 14.3 us  [gathered(): return lax.all_gather(piece, 'shard', axis=0, tiled=True)]
    psum x1 -> x0, waiting for transfers between devices: 53.9 us -> none  [shards(): packed = lax.psum(packed, ('shard', 'cx', 'core')).astype(F32)]
    unnamed x182 -> x341, local copies, waits for them, and re-layouts: 21 us -> 54.6 us
    ppermute x5 -> x6, waiting for transfers between devices: 27.2 us -> 57.3 us  [pieces_of(): across = lax.ppermute(own, 'cx', SWAP)]
    unnamed x13, waiting for transfers between devices: 17.8 us -> 0.21 us
    all_gather x0 -> x1, blocking collectives: none -> 15.4 us  [shards(): small = lax.all_gather(small, 'shard', axis=0).reshape(count, -1)]
    psum x1 -> x0, blocking collectives: 14.4 us -> none  [shards(): sum_head_gain = lax.psum(sum_head_gain.astype(BF16), 'tp').astype(F32)]
  transfers between devices with their start and end apart: 55 -> 81, of which waited for: 22 -> 31; matrix products, arithmetic and copies ran while one was open for 21% -> 27% of each run, Pallas kernels for 13% -> 16%
where the time goes in v2:
time: 918 us; the launch traced here: 906 us
  waiting for transfers between devices  345 us (38%)
  matrix products  177 us (19%)
  Pallas kernels  150 us (16%)
  other arithmetic  75.7 us (8%)
  local copies, waits for them, and re-layouts  74.8 us (8%)
  starting transfers between devices  52 us (6%)
  between operations  16.1 us (2%)
  blocking collectives  15.4 us (2%)
    ppermute x6, waiting for transfers between devices, with_other(): return [own, lax.ppermute(tie(own, *after), 'cx', SWAP)]  114 us
    dot_general x28, matrix products, dot_nt(): lax.dot_general(left, right, (((1,), (1,)), ((), ())), preferred_element_...  70.3 us
    ppermute x6, waiting for transfers between devices, pieces_of(): across = lax.ppermute(own, 'cx', SWAP)  57.3 us
    dot_general x14, matrix products, dot_tn(): lax.dot_general(left, right, (((0,), (0,)), ((), ())), preferred_element_...  56.6 us
    unnamed x341, local copies, waits for them, and re-layouts  54.6 us
    ppermute x6, waiting for transfers between devices, across(): return lax.ppermute(part, 'cx', SWAP)  54.1 us
    dot_general x14, matrix products, dot_nn(): lax.dot_general(left, right, (((1,), (0,)), ((), ())), preferred_element_...  50.1 us
    pallas_call x2, Pallas kernels, four(): call(functools.partial(backward_two, size=size, base=base), grid, conv_sp...  44.9 us
  transfers between devices with their start and end apart: 81, of which 31 were waited for; matrix products, arithmetic and copies ran while one was open for 27% of the time, Pallas kernels for 16%

profile of v2, /device:TPU:0, one launch (start us, length us, event | category | flops | bytes accessed | tf_op | source)
XLA Modules:
  0.0 905.7 jit_solution(981548448792904632)
XLA Ops:
  21.4 15.4 %all_gather.21 = bf16[4,80,128]{2,1,0:T(8,128)(2,1)S(1)} all-gather(bf16[1,80,128]{2,1,0:T(8,128)(2,1)S(1)} %pad_bitcast_fusion), channel_id=1, replica_groups=mesh['shard'=4,'cx'=2,'core'=2,'tp'=2] {'shard'}, dimensions={0}, use_global_device_ids=true | all-gather | bytes 102400 | tf_op jit(solution)/shard_map/all_gather | solution.py:697
  53.3 3.6 pad_maximum_fusion.source
  57.9 3.8 shard_map.254
  70.2 4.6 fusion.10
  77.8 14.3 %all-gather.7.cloned.1.call-done = bf16[1024,768]{1,0:T(8,128)(2,1)} async-done(((bf16[256,768]{1,0:T(8,128)(2,1)}), bf16[1024,768]{1,0:T(8,128)(2,1)}) %all-gather.7.cloned.1.call-update) | async-done | bytes 1572880 | tf_op jit(solution)/shard_map/all_gather | solution.py:738
  92.1 7.4 collective-permute-done.2
  109.8 3.5 fusion.114
  113.3 19.9 %shard_map.258 = (bf16[2,2,256,256]{3,2,1,0:T(8,128)(2,1)S(1)}, bf16[2,2,256,256]{3,2,1,0:T(8,128)(2,1)S(1)}, bf16[2,2,256,256]{3,2,1,0:T(8,128)(2,1)S(1)}, bf16...) custom-call(s32[2]{0:T(128)S(1)} %pad_add_fusion.1.where, ...), custom_call_target="tpu_custom_call" | custom-call | flops 1000 | bytes 1000 | tf_op jit(solution)/shard_map/pallas_call | solution.py:517
  136.7 5.0 add_convert_fusion.4.q0.k0.v0.q1.k1.v1.qh.kh.vh
  141.7 4.4 collective-permute-start.7
  146.1 19.4 %shard_map.257 = (bf16[2,2,256,256]{3,2,1,0:T(8,128)(2,1)S(1)}, bf16[2,2,256,256]{3,2,1,0:T(8,128)(2,1)S(1)}, bf16[2,2,256,256]{3,2,1,0:T(8,128)(2,1)S(1)}, bf16...) custom-call(s32[2]{0:T(128)S(1)} %pad_add_fusion.1.where, ...), custom_call_target="tpu_custom_call" | custom-call | flops 1000 | bytes 1000 | tf_op jit(solution)/shard_map/pallas_call | solution.py:517
  175.2 7.2 shard_map.259
  184.0 7.0 shard_map.260
  207.7 24.2 %collective-permute-done.9 = bf16[512,1024]{1,0:T(8,128)(2,1)S(1)} collective-permute-done((bf16[512,1024]{1,0:T(8,128)(2,1)}, bf16[512,1024]{1,0:T(8,128)(2,1)S(1)}, u32[]{:S(2)}, u32[]{:S(2)}) %collective-permute-start.9) | collective-permute-done | bytes 1048608 | tf_op jit(solution)/shard_map/ppermute | solution.py:641
  234.7 18.7 %collective-permute-done.12 = bf16[512,1024]{1,0:T(8,128)(2,1)S(1)} collective-permute-done((bf16[512,1024]{1,0:T(8,128)(2,1)}, bf16[512,1024]{1,0:T(8,128)(2,1)S(1)}, u32[]{:S(2)}, u32[]{:S(2)}) %collective-permute-start.12) | collective-permute-done | bytes 1048608 | tf_op jit(solution)/shard_map/ppermute | solution.py:641
  258.0 12.4 %collective-permute-done.15 = bf16[1024,1408]{1,0:T(8,128)(2,1)} collective-permute-done((bf16[1024,1408]{1,0:T(8,128)(2,1)}, bf16[1024,1408]{1,0:T(8,128)(2,1)}, u32[]{:S(2)}, u32[]{:S(2)}) %collective-permute-start.15) | collective-permute-done | bytes 2883616 | tf_op jit(solution)/shard_map/ppermute | solution.py:741
  270.7 4.8 pad_maximum_fusion.1.source
  276.4 3.7 shard_map.261
  285.7 6.0 fusion.117
  291.8 3.5 convolution_add_fusion.1
  295.2 39.0 %collective-permute-done.16 = bf16[1024,1408]{1,0:T(8,128)(2,1)} collective-permute-done((bf16[1024,1408]{1,0:T(8,128)(2,1)}, bf16[1024,1408]{1,0:T(8,128)(2,1)}, u32[]{:S(2)}, u32[]{:S(2)}) %collective-permute-start.16) | collective-permute-done | bytes 2883616 | tf_op jit(solution)/shard_map/ppermute | solution.py:741
  334.2 5.2 fusion.118
  339.5 3.5 convolution_add_fusion
  347.1 5.2 convolution_convert_fusion.3
  353.0 7.5 convolution_convert_fusion.2
  360.5 54.9 %collective-permute-done.18 = bf16[1024,1408]{0,1:T(8,128)(2,1)} collective-permute-done((bf16[1024,1408]{0,1:T(8,128)(2,1)}, bf16[1024,1408]{0,1:T(8,128)(2,1)}, u32[]{:S(2)}, u32[]{:S(2)}) %collective-permute-start.18) | collective-permute-done | bytes 2883616 | tf_op jit(solution)/shard_map/ppermute | solution.py:741
  415.4 6.0 fusion.119
  421.5 4.2 add_convert_fusion.2
  428.6 4.9 convolution_convert_fusion.1
  438.2 3.6 fusion.45
  441.8 4.6 add_convert_fusion.17
  449.6 4.1 fusion.43
  453.7 3.9 fusion.41
  462.2 3.6 fusion.37
  468.9 5.1 convolution_convert_fusion
  475.9 3.6 convolution_convert_fusion.7
  486.6 4.7 add_convert_fusion.13
  491.3 20.6 %collective-permute-done.25 = bf16[1024,1408]{1,0:T(8,128)(2,1)S(1)} collective-permute-done((bf16[1024,1408]{1,0:T(8,128)(2,1)}, bf16[1024,1408]{1,0:T(8,128)(2,1)S(1)}, u32[]{:S(2)}, u32[]{:S(2)}) %collective-permute-start.25) | collective-permute-done | bytes 2883616 | tf_op jit(solution)/shard_map/ppermute | solution.py:785
  511.9 4.8 add_convert_fusion.1
  516.9 11.4 %collective-permute-done.24 = bf16[512,1024]{1,0:T(8,128)(2,1)} collective-permute-done((bf16[512,1024]{1,0:T(8,128)(2,1)}, bf16[512,1024]{1,0:T(8,128)(2,1)}, u32[]{:S(2)}, u32[]{:S(2)}) %collective-permute-start.24) | collective-permute-done | bytes 1048608 | tf_op jit(solution)/shard_map/ppermute | solution.py:834
  528.3 4.8 multiply_reduce_fusion.1
  533.2 5.3 fusion.104
  551.2 7.1 shard_map.262
  559.0 7.1 shard_map.263
  575.5 5.7 collective-permute-done.33.rest_8_
  588.3 28.4 %shard_map.264 = (bf16[2,2,256,768]{3,2,1,0:T(8,128)(2,1)}, bf16[2,16,768]{2,1,0:T(8,128)(2,1)S(1)}, f32[2,2,256,128]{3,2,1,0:T(8,128)S(1)}, f32[2,3,2,4,128]{4,3,2,1,0:T(4,128)S(1)}) custom-call(s32[2]{0:T(128)S(1)} %pad_add_fusion.1.where, bf16[1056,768]{1,0:T(8,128)(2,1)} %copy-done.3, bf16[1056,768]{1,0:T(8,128)(2,1)} %copy-done.3, ...), custom_call_target="tpu_custom_call" | custom-call | flops 1000 | bytes 1000 | tf_op jit(solution)/shard_map/pallas_call | solution.py:551
  625.7 16.5 %shard_map.265 = (bf16[2,2,256,768]{3,2,1,0:T(8,128)(2,1)}, bf16[2,16,768]{2,1,0:T(8,128)(2,1)S(1)}, f32[2,2,256,128]{3,2,1,0:T(8,128)S(1)}, f32[2,3,2,4,128]{4,3,2,1,0:T(4,128)S(1)}) custom-call(s32[2]{0:T(128)S(1)} %pad_add_fusion.1.where, bf16[1056,768]{1,0:T(8,128)(2,1)} %copy-done.2, bf16[1056,768]{1,0:T(8,128)(2,1)} %copy-done.2, ...), custom_call_target="tpu_custom_call" | custom-call | flops 1000 | bytes 1000 | tf_op jit(solution)/shard_map/pallas_call | solution.py:551
  644.4 3.7 collective-permute-done.32
  649.6 5.2 convolution_convert_fusion.5
  658.2 6.2 add_convert_fusion
  702.0 4.5 collective-permute-done.26
  706.9 22.1 %collective-permute-done.27 = bf16[512,1024]{1,0:T(8,128)(2,1)S(1)} collective-permute-done((bf16[512,1024]{1,0:T(8,128)(2,1)}, bf16[512,1024]{1,0:T(8,128)(2,1)S(1)}, u32[]{:S(2)}, u32[]{:S(2)}) %collective-permute-start.27) | collective-permute-done | bytes 1048608 | tf_op jit(solution)/shard_map/ppermute | solution.py:834
  732.2 19.7 %collective-permute-done.40 = bf16[1024,768]{1,0:T(8,128)(2,1)S(1)} collective-permute-done((bf16[1024,768]{1,0:T(8,128)(2,1)}, bf16[1024,768]{1,0:T(8,128)(2,1)S(1)}, u32[]{:S(2)}, u32[]{:S(2)}) %collective-permute-start.40) | collective-permute-done | bytes 1572896 | tf_op jit(solution)/shard_map/ppermute | solution.py:785
  757.9 10.8 %collective-permute-done.41 = bf16[256,1408]{1,0:T(8,128)(2,1)} collective-permute-done((bf16[256,1408]{1,0:T(8,128)(2,1)}, bf16[256,1408]{1,0:T(8,128)(2,1)}, u32[]{:S(2)}, u32[]{:S(2)}) %collective-permute-start.41) | collective-permute-done | bytes 720928 | tf_op jit(solution)/shard_map/ppermute | solution.py:785
  772.9 4.3 fusion.24
  777.2 4.5 fusion.20
  781.9 5.5 add_convert_fusion.5
  794.9 13.7 %collective-permute-done.59.b = bf16[256,1408]{1,0:T(8,128)(2,1)S(1)} collective-permute-done((bf16[256,1408]{1,0:T(8,128)(2,1)S(1)}, bf16[256,1408]{1,0:T(8,128)(2,1)S(1)}, u32[]{:S(2)}, u32[]{:S(2)}) %collective-permute-start.59) | collective-permute-done | bytes 720928 | tf_op jit(solution)/shard_map/ppermute | solution.py:160
  808.6 20.7 %collective-permute-done.56.b = bf16[256,512]{1,0:T(8,128)(2,1)S(1)} collective-permute-done((bf16[256,512]{1,0:T(8,128)(2,1)S(1)}, bf16[256,512]{1,0:T(8,128)(2,1)S(1)}, u32[]{:S(2)}, u32[]{:S(2)}) %collective-permute-start.56) | collective-permute-done | bytes 262176 | tf_op jit(solution)/shard_map/ppermute | solution.py:160
  837.4 4.8 shard_map.270
  842.1 5.4 shard_map.272
  855.1 20.1 %collective-permute-done.62.b = bf16[256,1408]{1,0:T(8,128)(2,1)S(1)} collective-permute-done((bf16[256,1408]{1,0:T(8,128)(2,1)S(1)}, bf16[256,1408]{1,0:T(8,128)(2,1)S(1)}, u32[]{:S(2)}, u32[]{:S(2)}) %collective-permute-start.62) | collective-permute-done | bytes 720928 | tf_op jit(solution)/shard_map/ppermute | solution.py:160
  888.7 4.8 shard_map.271
  893.6 5.4 shard_map.268
  (645 shorter events, 263.6 us)
Async XLA Ops:
  7.2 57.3 %all-gather.9.cloned.1.call-start = ((), (), s32[]{:S(2)}) async-start(), calls=%async_computation.8 | async-start | bytes 1966080 | tf_op jit(solution)/shard_map/all_gather | solution.py:738
  12.7 79.4 %all-gather.7.cloned.1.call-start = ((), (), s32[]{:S(2)}) async-start(), calls=%async_computation.7 | async-start | bytes 1966080 | tf_op jit(solution)/shard_map/all_gather | solution.py:738
  18.0 118.6 %all-gather.11.cloned.1.call-start = ((), (), s32[]{:S(2)}) async-start(), calls=%async_computation.9 | async-start | bytes 1310720 | tf_op jit(solution)/shard_map/all_gather | solution.py:738
  18.6 24.2 %collective-permute-start.4 = (s32[2,256]{1,0:T(2,128)}, s32[2,256]{1,0:T(2,128)}, u32[]{:S(2)}, u32[]{:S(2)}) collective-permute-start(s32[2,256]{1,0:T(2,128)} %bitcast.194), channel_id=1, source_target_pairs={{0,2},{2,0},{1,3},{3,1},{4,6},{6,4},{5,7},{7,5},{8,10},{10,8},{9,1... | collective-permute-start | bytes 6152 | tf_op jit(solution)/shard_map/ppermute | solution.py:722
  19.1 27.8 %collective-permute-start = (bf16[512,2048]{1,0:T(8,128)(2,1)}, bf16[512,2048]{1,0:T(8,128)(2,1)}, u32[]{:S(2)}, u32[]{:S(2)}) collective-permute-start(bf16[512,2048]{1,0:T(8,128)(2,1)} %bitcast.203), channel_id=1, source_target_pairs={{0,2},{2,0},{1,3},{3,1},{4,6},{6,4},{5,7},{7,5},{8,10},{10,8},{9,1... | collective-permute-start | bytes 6291464 | tf_op jit(solution)/shard_map/ppermute | solution.py:716
  20.8 184.8 %all-gather.15.cloned.1.call-start = ((), (), s32[]{:S(2)}) async-start(), calls=%async_computation.11 | async-start | bytes 3604480 | tf_op jit(solution)/shard_map/all_gather | solution.py:738
  64.4 35.0 %collective-permute-start.2 = (bf16[1024,768]{1,0:T(8,128)(2,1)}, bf16[1024,768]{1,0:T(8,128)(2,1)}, u32[]{:S(2)}, u32[]{:S(2)}) collective-permute-start(bf16[1024,768]{1,0:T(8,128)(2,1)} %all-gather.9.cloned.1.call-done), channel_id=1, source_target_pairs={{0,4},{4,0},{1,5},{5,1},{2,6},{6,2},{3,7},{7,3},{8,12},{12,8},{9,1... | collective-permute-start | bytes 4718600 | tf_op jit(solution)/shard_map/ppermute | solution.py:741
  70.2 187.8 %all-gather.13.cloned.1.call-start = ((), (), s32[]{:S(2)}) async-start(), calls=%async_computation.10 | async-start | bytes 3604480 | tf_op jit(solution)/shard_map/all_gather | solution.py:738
  99.5 37.1 %collective-permute-start.3 = (bf16[1024,768]{1,0:T(8,128)(2,1)}, bf16[1024,768]{1,0:T(8,128)(2,1)}, u32[]{:S(2)}, u32[]{:S(2)}) collective-permute-start(bf16[1024,768]{1,0:T(8,128)(2,1)} %all-gather.7.cloned.1.call-done), channel_id=1, source_target_pairs={{0,4},{4,0},{1,5},{5,1},{2,6},{6,2},{3,7},{7,3},{8,12},{12,8},{9,1... | collective-permute-start | bytes 4718600 | tf_op jit(solution)/shard_map/ppermute | solution.py:741
  136.6 60.5 %collective-permute-start.10 = (bf16[1024,512]{0,1:T(8,128)(2,1)}, bf16[1024,512]{0,1:T(8,128)(2,1)}, u32[]{:S(2)}, u32[]{:S(2)}) collective-permute-start(bf16[1024,512]{0,1:T(8,128)(2,1)} %all-gather.11.cloned.1.call-done), channel_id=1, source_target_pairs={{0,4},{4,0},{1,5},{5,1},{2,6},{6,2},{3,7},{7,3},{8,12},{12,8},{9,1... | collective-permute-start | bytes 3145736 | tf_op jit(solution)/shard_map/ppermute | solution.py:741
  141.7 29.3 %collective-permute-start.7 = (bf16[2,2,128,128]{3,2,1,0:T(8,128)(2,1)}, bf16[2,2,128,128]{3,2,1,0:T(8,128)(2,1)}, u32[]{:S(2)}, u32[]{:S(2)}) collective-permute-start(bf16[2,2,128,128]{3,2,1,0:T(8,128)(2,1)} %get-tuple-element.228), channel_id=1, source_target_pairs={{0,4},{1,5},{2,6},{3,7},{8,12},{9,13},{10,14},{11,15},{16,20},{17,... | collective-permute-start | bytes 393224 | tf_op jit(solution)/shard_map/ppermute | solution.py:763
  169.0 15.0 %collective-permute-start.6 = (bf16[2,2,128,128]{3,2,1,0:T(8,128)(2,1)}, bf16[2,2,128,128]{3,2,1,0:T(8,128)(2,1)}, u32[]{:S(2)}, u32[]{:S(2)}) collective-permute-start(bf16[2,2,128,128]{3,2,1,0:T(8,128)(2,1)} %get-tuple-element.223), channel_id=1, source_target_pairs={{0,4},{1,5},{2,6},{3,7},{8,12},{9,13},{10,14},{11,15},{16,20},{17,... | collective-permute-start | bytes 393224 | tf_op jit(solution)/shard_map/ppermute | solution.py:763
  196.9 155.4 %all-gather.17.cloned.1.call-start = ((), (), s32[]{:S(2)}) async-start(), calls=%async_computation.12 | async-start | bytes 3604480 | tf_op jit(solution)/shard_map/all_gather | solution.py:738
  205.6 64.7 %collective-permute-start.15 = (bf16[1024,1408]{1,0:T(8,128)(2,1)}, bf16[1024,1408]{1,0:T(8,128)(2,1)}, u32[]{:S(2)}, u32[]{:S(2)}) collective-permute-start(bf16[1024,1408]{1,0:T(8,128)(2,1)} %all-gather.15.cloned.1.call-done), channel_id=1, source_target_pairs={{0,4},{4,0},{1,5},{5,1},{2,6},{6,2},{3,7},{7,3},{8,12},{12,8},{9,1... | collective-permute-start | bytes 8650760 | tf_op jit(solution)/shard_map/ppermute | solution.py:741
  205.6 26.2 %collective-permute-start.9 = (bf16[512,1024]{1,0:T(8,128)(2,1)}, bf16[512,1024]{1,0:T(8,128)(2,1)S(1)}, u32[]{:S(2)}, u32[]{:S(2)}) collective-permute-start(bf16[512,1024]{1,0:T(8,128)(2,1)} %add_convert_fusion.20), channel_id=1, source_target_pairs={{0,1},{1,0},{2,3},{3,2},{4,5},{5,4},{6,7},{7,6},{8,9},{9,8},{10,11... | collective-permute-start | bytes 3145736 | tf_op jit(solution)/shard_map/ppermute | solution.py:641
  207.2 46.2 %collective-permute-start.12 = (bf16[512,1024]{1,0:T(8,128)(2,1)}, bf16[512,1024]{1,0:T(8,128)(2,1)S(1)}, u32[]{:S(2)}, u32[]{:S(2)}) collective-permute-start(bf16[512,1024]{1,0:T(8,128)(2,1)} %add_convert_fusion.19), channel_id=1, source_target_pairs={{0,1},{1,0},{2,3},{3,2},{4,5},{5,4},{6,7},{7,6},{8,9},{9,8},{10,11... | collective-permute-start | bytes 3145736 | tf_op jit(solution)/shard_map/ppermute | solution.py:641
  207.7 63.0 %collective-permute-start.17 = (bf16[512,2048]{1,0:T(8,128)(2,1)}, bf16[512,2048]{1,0:T(8,128)(2,1)}, u32[]{:S(2)}, u32[]{:S(2)}) collective-permute-start(bf16[512,2048]{1,0:T(8,128)(2,1)} %bitcast.219), channel_id=1, source_target_pairs={{0,2},{2,0},{1,3},{3,1},{4,6},{6,4},{5,7},{7,5},{8,10},{10,8},{9,1... | collective-permute-start | bytes 6291464 | tf_op jit(solution)/shard_map/ppermute | solution.py:719
  258.0 23.8 %collective-permute-start.14 = (bf16[512,1024]{1,0:T(8,128)(2,1)}, bf16[512,1024]{1,0:T(8,128)(2,1)}, u32[]{:S(2)}, u32[]{:S(2)}) collective-permute-start(bf16[512,1024]{1,0:T(8,128)(2,1)} %get-tuple-element.504), channel_id=1, source_target_pairs={{0,2},{2,0},{1,3},{3,1},{4,6},{6,4},{5,7},{7,5},{8,10},{10,8},{9,1... | collective-permute-start | bytes 3145736 | tf_op jit(solution)/shard_map/ppermute | solution.py:632
  270.4 63.9 %collective-permute-start.16 = (bf16[1024,1408]{1,0:T(8,128)(2,1)}, bf16[1024,1408]{1,0:T(8,128)(2,1)}, u32[]{:S(2)}, u32[]{:S(2)}) collective-permute-start(bf16[1024,1408]{1,0:T(8,128)(2,1)} %all-gather.13.cloned.1.call-done), channel_id=1, source_target_pairs={{0,4},{4,0},{1,5},{5,1},{2,6},{6,2},{3,7},{7,3},{8,12},{12,8},{9,1... | collective-permute-start | bytes 8650760 | tf_op jit(solution)/shard_map/ppermute | solution.py:741
  270.6 12.9 %collective-permute-start.13 = (bf16[512,1024]{1,0:T(8,128)(2,1)}, bf16[512,1024]{1,0:T(8,128)(2,1)}, u32[]{:S(2)}, u32[]{:S(2)}) collective-permute-start(bf16[512,1024]{1,0:T(8,128)(2,1)} %get-tuple-element.505), channel_id=1, source_target_pairs={{0,2},{2,0},{1,3},{3,1},{4,6},{6,4},{5,7},{7,5},{8,10},{10,8},{9,1... | collective-permute-start | bytes 3145736 | tf_op jit(solution)/shard_map/ppermute | solution.py:632
  281.4 133.9 %reduce-scatter.8.cloned.1.call-start = ((), (), s32[]{:S(2)}) async-start(), calls=%async_computation.13 | async-start | bytes 3604480 | tf_op jit(solution)/shard_map/reduce_scatter | solution.py:788
  352.3 164.6 %reduce-scatter.10.cloned.1.call-start = ((), (), s32[]{:S(2)}) async-start(), calls=%async_computation.14 | async-start | bytes 3604480 | tf_op jit(solution)/shard_map/reduce_scatter | solution.py:788
  352.3 63.0 %collective-permute-start.18 = (bf16[1024,1408]{0,1:T(8,128)(2,1)}, bf16[1024,1408]{0,1:T(8,128)(2,1)}, u32[]{:S(2)}, u32[]{:S(2)}) collective-permute-start(bf16[1024,1408]{0,1:T(8,128)(2,1)} %all-gather.17.cloned.1.call-done), channel_id=1, source_target_pairs={{0,4},{4,0},{1,5},{5,1},{2,6},{6,2},{3,7},{7,3},{8,12},{12,8},{9,1... | collective-permute-start | bytes 8650760 | tf_op jit(solution)/shard_map/ppermute | solution.py:741
  438.2 10.0 %collective-permute-start.19 = (bf16[512,1024]{1,0:T(8,128)(2,1)}, bf16[512,1024]{1,0:T(8,128)(2,1)}, u32[]{:S(2)}, u32[]{:S(2)}) collective-permute-start(bf16[512,1024]{1,0:T(8,128)(2,1)} %add_convert_fusion.18), channel_id=1, source_target_pairs={{0,2},{2,0},{1,3},{3,1},{4,6},{6,4},{5,7},{7,5},{8,10},{10,8},{9,1... | collective-permute-start | bytes 3145736 | tf_op jit(solution)/shard_map/ppermute | solution.py:822
  447.0 136.3 %reduce-scatter.12.cloned.1.call-start = ((), (), s32[]{:S(2)}) async-start(), calls=%async_computation.15 | async-start | bytes 3604480 | tf_op jit(solution)/shard_map/reduce_scatter | solution.py:788
  447.2 64.7 %collective-permute-start.25 = (bf16[1024,1408]{1,0:T(8,128)(2,1)}, bf16[1024,1408]{1,0:T(8,128)(2,1)S(1)}, u32[]{:S(2)}, u32[]{:S(2)}) collective-permute-start(bf16[1024,1408]{1,0:T(8,128)(2,1)} %convolution_convert_fusion.1), channel_id=1, source_target_pairs={{0,4},{4,0},{1,5},{5,1},{2,6},{6,2},{3,7},{7,3},{8,12},{12,8},{9,1... | collective-permute-start | bytes 8650760 | tf_op jit(solution)/shard_map/ppermute | solution.py:785
  480.1 36.8 %collective-permute-start.23 = (bf16[512,1024]{1,0:T(8,128)(2,1)}, bf16[512,1024]{1,0:T(8,128)(2,1)}, u32[]{:S(2)}, u32[]{:S(2)}) collective-permute-start(bf16[512,1024]{1,0:T(8,128)(2,1)} %add_convert_fusion.16), channel_id=1, source_target_pairs={{0,1},{1,0},{2,3},{3,2},{4,5},{5,4},{6,7},{7,6},{8,9},{9,8},{10,11... | collective-permute-start | bytes 3145736 | tf_op jit(solution)/shard_map/ppermute | solution.py:834
  481.8 46.5 %collective-permute-start.24 = (bf16[512,1024]{1,0:T(8,128)(2,1)}, bf16[512,1024]{1,0:T(8,128)(2,1)}, u32[]{:S(2)}, u32[]{:S(2)}) collective-permute-start(bf16[512,1024]{1,0:T(8,128)(2,1)} %add_convert_fusion.15), channel_id=1, source_target_pairs={{0,1},{1,0},{2,3},{3,2},{4,5},{5,4},{6,7},{7,6},{8,9},{9,8},{10,11... | collective-permute-start | bytes 3145736 | tf_op jit(solution)/shard_map/ppermute | solution.py:834
  516.8 127.6 %reduce-scatter.14.cloned.1.call-start = ((), (), s32[]{:S(2)}) async-start(), calls=%async_computation.16 | async-start | bytes 1310720 | tf_op jit(solution)/shard_map/reduce_scatter | solution.py:788
  545.4 25.3 %collective-permute-start.31 = (bf16[1024,512]{1,0:T(8,128)(2,1)S(1)}, bf16[1024,512]{1,0:T(8,128)(2,1)S(1)}, u32[]{:S(2)}, u32[]{:S(2)}) collective-permute-start(bf16[1024,512]{1,0:T(8,128)(2,1)S(1)} %convolution_convert_fusion.6), channel_id=1, source_target_pairs={{0,4},{4,0},{1,5},{5,1},{2,6},{6,2},{3,7},{7,3},{8,12},{12,8},{9,1... | collective-permute-start | bytes 3145736 | tf_op jit(solution)/shard_map/ppermute | solution.py:785
  572.9 200.0 %reduce-scatter.16.cloned.1.call-start = ((), (), s32[]{:S(2)}) async-start(), calls=%async_computation.17 | async-start | bytes 3604480 | tf_op jit(solution)/shard_map/reduce_scatter | solution.py:788
  572.9 8.3 collective-permute-start.33
  574.2 8.4 collective-permute-start.30
  583.3 74.6 %collective-permute-start.35 = (bf16[1024,1408]{1,0:T(8,128)(2,1)}, bf16[1024,1408]{1,0:T(8,128)(2,1)}, u32[]{:S(2)}, u32[]{:S(2)}) collective-permute-start(bf16[1024,1408]{1,0:T(8,128)(2,1)} %convolution_convert_fusion), channel_id=1, source_target_pairs={{0,4},{4,0},{1,5},{5,1},{2,6},{6,2},{3,7},{7,3},{8,12},{12,8},{9,1... | collective-permute-start | bytes 8650760 | tf_op jit(solution)/shard_map/ppermute | solution.py:785
  617.5 30.6 %collective-permute-start.32 = (bf16[2,16,768]{2,1,0:T(8,128)(2,1)S(1)}, bf16[2,16,768]{2,1,0:T(8,128)(2,1)}, u32[]{:S(2)}, u32[]{:S(2)}) collective-permute-start(bf16[2,16,768]{2,1,0:T(8,128)(2,1)S(1)} %get-tuple-element.340), channel_id=1, source_target_pairs={{4,0},{5,1},{6,2},{7,3},{12,8},{13,9},{14,10},{15,11},{20,16},{21,... | collective-permute-start | bytes 147464 | tf_op jit(solution)/shard_map/ppermute | solution.py:906
  643.1 11.7 %collective-permute-start.34 = (bf16[2,16,768]{2,1,0:T(8,128)(2,1)S(1)}, bf16[2,16,768]{2,1,0:T(8,128)(2,1)S(1)}, u32[]{:S(2)}, u32[]{:S(2)}) collective-permute-start(bf16[2,16,768]{2,1,0:T(8,128)(2,1)S(1)} %get-tuple-element.355), channel_id=1, source_target_pairs={{4,0},{5,1},{6,2},{7,3},{12,8},{13,9},{14,10},{15,11},{20,16},{21,... | collective-permute-start | bytes 147464 | tf_op jit(solution)/shard_map/ppermute | solution.py:906
  664.4 183.2 %reduce-scatter.18.cloned.1.call-start = ((), (), s32[]{:S(2)}) async-start(), calls=%async_computation.18 | async-start | bytes 1966080 | tf_op jit(solution)/shard_map/reduce_scatter | solution.py:788
  671.1 11.4 %collective-permute-start.36 = (bf16[512,1024]{1,0:T(8,128)(2,1)}, bf16[512,1024]{1,0:T(8,128)(2,1)}, u32[]{:S(2)}, u32[]{:S(2)}) collective-permute-start(bf16[512,1024]{1,0:T(8,128)(2,1)} %add_convert_fusion.10), channel_id=1, source_target_pairs={{0,2},{2,0},{1,3},{3,1},{4,6},{6,4},{5,7},{7,5},{8,10},{10,8},{9,1... | collective-permute-start | bytes 3145736 | tf_op jit(solution)/shard_map/ppermute | solution.py:822
  680.3 26.3 %collective-permute-start.26 = (bf16[512,1024]{1,0:T(8,128)(2,1)}, bf16[512,1024]{1,0:T(8,128)(2,1)S(1)}, u32[]{:S(2)}, u32[]{:S(2)}) collective-permute-start(bf16[512,1024]{1,0:T(8,128)(2,1)} %add_convert_fusion.14), channel_id=1, source_target_pairs={{0,1},{1,0},{2,3},{3,2},{4,5},{5,4},{6,7},{7,6},{8,9},{9,8},{10,11... | collective-permute-start | bytes 3145736 | tf_op jit(solution)/shard_map/ppermute | solution.py:834
  680.7 48.3 %collective-permute-start.27 = (bf16[512,1024]{1,0:T(8,128)(2,1)}, bf16[512,1024]{1,0:T(8,128)(2,1)S(1)}, u32[]{:S(2)}, u32[]{:S(2)}) collective-permute-start(bf16[512,1024]{1,0:T(8,128)(2,1)} %add_convert_fusion.13), channel_id=1, source_target_pairs={{0,1},{1,0},{2,3},{3,2},{4,5},{5,4},{6,7},{7,6},{8,9},{9,8},{10,11... | collective-permute-start | bytes 3145736 | tf_op jit(solution)/shard_map/ppermute | solution.py:834
  682.4 99.4 %collective-permute-start.42 = (bf16[1024,768]{1,0:T(8,128)(2,1)}, bf16[1024,768]{1,0:T(8,128)(2,1)}, u32[]{:S(2)}, u32[]{:S(2)}) collective-permute-start(bf16[1024,768]{1,0:T(8,128)(2,1)} %convolution_convert_fusion.4), channel_id=1, source_target_pairs={{0,4},{4,0},{1,5},{5,1},{2,6},{6,2},{3,7},{7,3},{8,12},{12,8},{9,1... | collective-permute-start | bytes 4718600 | tf_op jit(solution)/shard_map/ppermute | solution.py:785
  682.4 69.5 %collective-permute-start.40 = (bf16[1024,768]{1,0:T(8,128)(2,1)}, bf16[1024,768]{1,0:T(8,128)(2,1)S(1)}, u32[]{:S(2)}, u32[]{:S(2)}) collective-permute-start(bf16[1024,768]{1,0:T(8,128)(2,1)} %convolution_convert_fusion.5), channel_id=1, source_target_pairs={{0,4},{4,0},{1,5},{5,1},{2,6},{6,2},{3,7},{7,3},{8,12},{12,8},{9,1... | collective-permute-start | bytes 4718600 | tf_op jit(solution)/shard_map/ppermute | solution.py:785
  696.2 74.7 %collective-permute-start.39 = (bf16[512,1024]{1,0:T(8,128)(2,1)}, bf16[512,1024]{1,0:T(8,128)(2,1)}, u32[]{:S(2)}, u32[]{:S(2)}) collective-permute-start(bf16[512,1024]{1,0:T(8,128)(2,1)} %add_convert_fusion.7), channel_id=1, source_target_pairs={{0,1},{1,0},{2,3},{3,2},{4,5},{5,4},{6,7},{7,6},{8,9},{9,8},{10,11... | collective-permute-start | bytes 3145736 | tf_op jit(solution)/shard_map/ppermute | solution.py:834
  706.5 66.4 %collective-permute-start.38 = (bf16[512,1024]{1,0:T(8,128)(2,1)}, bf16[512,1024]{1,0:T(8,128)(2,1)}, u32[]{:S(2)}, u32[]{:S(2)}) collective-permute-start(bf16[512,1024]{1,0:T(8,128)(2,1)} %add_convert_fusion.8), channel_id=1, source_target_pairs={{0,1},{1,0},{2,3},{3,2},{4,5},{5,4},{6,7},{7,6},{8,9},{9,8},{10,11... | collective-permute-start | bytes 3145736 | tf_op jit(solution)/shard_map/ppermute | solution.py:834
  751.9 16.8 %collective-permute-start.41 = (bf16[256,1408]{1,0:T(8,128)(2,1)}, bf16[256,1408]{1,0:T(8,128)(2,1)}, u32[]{:S(2)}, u32[]{:S(2)}) collective-permute-start(bf16[256,1408]{1,0:T(8,128)(2,1)} %reduce-scatter.10.cloned.1.call-done), channel_id=1, source_target_pairs={{0,4},{4,0},{1,5},{5,1},{2,6},{6,2},{3,7},{7,3},{8,12},{12,8},{9,1... | collective-permute-start | bytes 2162696 | tf_op jit(solution)/shard_map/ppermute | solution.py:785
  755.2 98.9 %reduce-scatter.20.cloned.1.call-start = ((), (), s32[]{:S(2)}) async-start(), calls=%async_computation.19 | async-start | bytes 1966080 | tf_op jit(solution)/shard_map/reduce_scatter | solution.py:788
  788.9 19.7 %collective-permute-start.59 = (bf16[256,1408]{1,0:T(8,128)(2,1)S(1)}, bf16[256,1408]{1,0:T(8,128)(2,1)S(1)}, u32[]{:S(2)}, u32[]{:S(2)}) collective-permute-start(bf16[256,1408]{1,0:T(8,128)(2,1)S(1)} %copy-done.52), channel_id=1, source_target_pairs={{0,4},{4,0},{1,5},{5,1},{2,6},{6,2},{3,7},{7,3},{8,12},{12,8},{9,1... | collective-permute-start | bytes 2162696 | tf_op jit(solution)/shard_map/ppermute | solution.py:160
  790.9 38.4 %collective-permute-start.65 = (bf16[256,1408]{1,0:T(8,128)(2,1)}, bf16[256,1408]{1,0:T(8,128)(2,1)}, u32[]{:S(2)}, u32[]{:S(2)}) collective-permute-start(bf16[256,1408]{1,0:T(8,128)(2,1)} %add_convert_fusion.21.a), channel_id=1, source_target_pairs={{0,4},{4,0},{1,5},{5,1},{2,6},{6,2},{3,7},{7,3},{8,12},{12,8},{9,1... | collective-permute-start | bytes 2162696 | tf_op jit(solution)/shard_map/ppermute | solution.py:160
  791.0 38.3 %collective-permute-start.56 = (bf16[256,512]{1,0:T(8,128)(2,1)S(1)}, bf16[256,512]{1,0:T(8,128)(2,1)S(1)}, u32[]{:S(2)}, u32[]{:S(2)}) collective-permute-start(bf16[256,512]{1,0:T(8,128)(2,1)S(1)} %copy-done.78), channel_id=1, source_target_pairs={{0,4},{4,0},{1,5},{5,1},{2,6},{6,2},{3,7},{7,3},{8,12},{12,8},{9,1... | collective-permute-start | bytes 786440 | tf_op jit(solution)/shard_map/ppermute | solution.py:160
  793.2 36.6 %collective-permute-start.46 = (bf16[18560]{0:T(1024)(128)(2,1)S(1)}, bf16[18560]{0:T(1024)(128)(2,1)S(1)}, u32[]{:S(2)}, u32[]{:S(2)}) collective-permute-start(bf16[18560]{0:T(1024)(128)(2,1)S(1)} %add_convert_fusion.24), channel_id=1, source_target_pairs={{0,8},{8,0},{16,24},{24,16},{1,9},{9,1},{17,25},{25,17},{2,10},{10... | collective-permute-start | bytes 111368 | tf_op jit(solution)/shard_map/ppermute | solution.py:646
  794.9 40.3 %collective-permute-start.60 = (bf16[256,1408]{1,0:T(8,128)(2,1)S(1)}, bf16[256,1408]{1,0:T(8,128)(2,1)}, u32[]{:S(2)}, u32[]{:S(2)}) collective-permute-start(bf16[256,1408]{1,0:T(8,128)(2,1)S(1)} %copy-done.52), channel_id=1, source_target_pairs={{0,2},{2,0},{1,3},{3,1},{4,6},{6,4},{5,7},{7,5},{8,10},{10,8},{9,1... | collective-permute-start | bytes 2162696 | tf_op jit(solution)/shard_map/ppermute | solution.py:161
  808.6 26.5 %collective-permute-start.61 = (bf16[256,1408]{1,0:T(8,128)(2,1)S(1)}, bf16[256,1408]{1,0:T(8,128)(2,1)}, u32[]{:S(2)}, u32[]{:S(2)}) collective-permute-start(bf16[256,1408]{1,0:T(8,128)(2,1)S(1)} %collective-permute-done.59.b), channel_id=1, source_target_pairs={{0,2},{2,0},{1,3},{3,1},{4,6},{6,4},{5,7},{7,5},{8,10},{10,8},{9,1... | collective-permute-start | bytes 2162696 | tf_op jit(solution)/shard_map/ppermute | solution.py:161
  829.3 12.8 %collective-permute-start.66 = (bf16[256,1408]{1,0:T(8,128)(2,1)}, bf16[256,1408]{1,0:T(8,128)(2,1)}, u32[]{:S(2)}, u32[]{:S(2)}) collective-permute-start(bf16[256,1408]{1,0:T(8,128)(2,1)} %add_convert_fusion.21.a), channel_id=1, source_target_pairs={{0,2},{2,0},{1,3},{3,1},{4,6},{6,4},{5,7},{7,5},{8,10},{10,8},{9,1... | collective-permute-start | bytes 2162696 | tf_op jit(solution)/shard_map/ppermute | solution.py:161
  829.3 12.8 %collective-permute-start.67 = (bf16[256,1408]{1,0:T(8,128)(2,1)}, bf16[256,1408]{1,0:T(8,128)(2,1)}, u32[]{:S(2)}, u32[]{:S(2)}) collective-permute-start(bf16[256,1408]{1,0:T(8,128)(2,1)} %collective-permute-done.65.b), channel_id=1, source_target_pairs={{0,2},{2,0},{1,3},{3,1},{4,6},{6,4},{5,7},{7,5},{8,10},{10,8},{9,1... | collective-permute-start | bytes 2162696 | tf_op jit(solution)/shard_map/ppermute | solution.py:161
  832.2 21.8 %collective-permute-start.47 = (bf16[18560]{0:T(1024)(128)(2,1)S(1)}, bf16[18560]{0:T(1024)(128)(2,1)S(1)}, u32[]{:S(2)}, u32[]{:S(2)}) collective-permute-start(bf16[18560]{0:T(1024)(128)(2,1)S(1)} %add_convert_fusion.23), channel_id=1, source_target_pairs={{0,16},{8,24},{16,0},{24,8},{1,17},{9,25},{17,1},{25,9},{2,18},{10... | collective-permute-start | bytes 111368 | tf_op jit(solution)/shard_map/ppermute | solution.py:646
  847.6 29.5 %collective-permute-start.48 = (bf16[256,768]{1,0:T(8,128)(2,1)}, bf16[256,768]{1,0:T(8,128)(2,1)}, u32[]{:S(2)}, u32[]{:S(2)}) collective-permute-start(bf16[256,768]{1,0:T(8,128)(2,1)} %reduce-scatter.18.cloned.1.call-done.refs_0_), channel_id=1, source_target_pairs={{0,4},{4,0},{1,5},{5,1},{2,6},{6,2},{3,7},{7,3},{8,12},{12,8},{9,1... | collective-permute-start | bytes 1179656 | tf_op jit(solution)/shard_map/ppermute | solution.py:160
  853.0 25.7 %collective-permute-start.63 = (bf16[256,1408]{1,0:T(8,128)(2,1)S(1)}, bf16[256,1408]{1,0:T(8,128)(2,1)S(1)}, u32[]{:S(2)}, u32[]{:S(2)}) collective-permute-start(bf16[256,1408]{1,0:T(8,128)(2,1)S(1)} %copy-done.54), channel_id=1, source_target_pairs={{0,2},{2,0},{1,3},{3,1},{4,6},{6,4},{5,7},{7,5},{8,10},{10,8},{9,1... | collective-permute-start | bytes 2162696 | tf_op jit(solution)/shard_map/ppermute | solution.py:161
  853.0 22.3 %collective-permute-start.62 = (bf16[256,1408]{1,0:T(8,128)(2,1)S(1)}, bf16[256,1408]{1,0:T(8,128)(2,1)S(1)}, u32[]{:S(2)}, u32[]{:S(2)}) collective-permute-start(bf16[256,1408]{1,0:T(8,128)(2,1)S(1)} %copy-done.54), channel_id=1, source_target_pairs={{0,4},{4,0},{1,5},{5,1},{2,6},{6,2},{3,7},{7,3},{8,12},{12,8},{9,1... | collective-permute-start | bytes 2162696 | tf_op jit(solution)/shard_map/ppermute | solution.py:160
  854.1 28.5 %collective-permute-start.51 = (bf16[256,768]{1,0:T(8,128)(2,1)}, bf16[256,768]{1,0:T(8,128)(2,1)}, u32[]{:S(2)}, u32[]{:S(2)}) collective-permute-start(bf16[256,768]{1,0:T(8,128)(2,1)} %reduce-scatter.20.cloned.1.call-done.refs_4_), channel_id=1, source_target_pairs={{0,4},{4,0},{1,5},{5,1},{2,6},{6,2},{3,7},{7,3},{8,12},{12,8},{9,1... | collective-permute-start | bytes 1179656 | tf_op jit(solution)/shard_map/ppermute | solution.py:160
  875.2 10.1 %collective-permute-start.64 = (bf16[256,1408]{1,0:T(8,128)(2,1)S(1)}, bf16[256,1408]{1,0:T(8,128)(2,1)}, u32[]{:S(2)}, u32[]{:S(2)}) collective-permute-start(bf16[256,1408]{1,0:T(8,128)(2,1)S(1)} %collective-permute-done.62.b), channel_id=1, source_target_pairs={{0,2},{2,0},{1,3},{3,1},{4,6},{6,4},{5,7},{7,5},{8,10},{10,8},{9,1... | collective-permute-start | bytes 2162696 | tf_op jit(solution)/shard_map/ppermute | solution.py:161
  877.8 15.8 %collective-permute-start.49 = (bf16[256,768]{1,0:T(8,128)(2,1)S(1)}, bf16[256,768]{1,0:T(8,128)(2,1)}, u32[]{:S(2)}, u32[]{:S(2)}) collective-permute-start(bf16[256,768]{1,0:T(8,128)(2,1)S(1)} %copy-done.76), channel_id=1, source_target_pairs={{0,2},{2,0},{1,3},{3,1},{4,6},{6,4},{5,7},{7,5},{8,10},{10,8},{9,1... | collective-permute-start | bytes 1179656 | tf_op jit(solution)/shard_map/ppermute | solution.py:161
  878.5 15.1 %collective-permute-start.50 = (bf16[256,768]{1,0:T(8,128)(2,1)}, bf16[256,768]{1,0:T(8,128)(2,1)}, u32[]{:S(2)}, u32[]{:S(2)}) collective-permute-start(bf16[256,768]{1,0:T(8,128)(2,1)} %collective-permute-done.48.refs_1_), channel_id=1, source_target_pairs={{0,2},{2,0},{1,3},{3,1},{4,6},{6,4},{5,7},{7,5},{8,10},{10,8},{9,1... | collective-permute-start | bytes 1179656 | tf_op jit(solution)/shard_map/ppermute | solution.py:161
  879.5 14.1 %collective-permute-start.52 = (bf16[256,768]{1,0:T(8,128)(2,1)}, bf16[256,768]{1,0:T(8,128)(2,1)}, u32[]{:S(2)}, u32[]{:S(2)}) collective-permute-start(bf16[256,768]{1,0:T(8,128)(2,1)} %reduce-scatter.20.cloned.1.call-done.refs_4_), channel_id=1, source_target_pairs={{0,2},{2,0},{1,3},{3,1},{4,6},{6,4},{5,7},{7,5},{8,10},{10,8},{9,1... | collective-permute-start | bytes 1179656 | tf_op jit(solution)/shard_map/ppermute | solution.py:161
  882.6 10.9 %collective-permute-start.53 = (bf16[256,768]{1,0:T(8,128)(2,1)}, bf16[256,768]{1,0:T(8,128)(2,1)}, u32[]{:S(2)}, u32[]{:S(2)}) collective-permute-start(bf16[256,768]{1,0:T(8,128)(2,1)} %collective-permute-done.51.refs_5_), channel_id=1, source_target_pairs={{0,2},{2,0},{1,3},{3,1},{4,6},{6,4},{5,7},{7,5},{8,10},{10,8},{9,1... | collective-permute-start | bytes 1179656 | tf_op jit(solution)/shard_map/ppermute | solution.py:161
  (184 other events, 1523.6 us)
Sparse Core Ops, SparseCore 0:
  12.8 41.0 all-gather.8
  56.1 35.9 all-gather.6
  94.2 29.0 all-gather.10
  125.3 57.4 all-gather.14
  197.1 59.6 all-gather.12
  281.6 60.8 all-gather.16
  352.4 56.5 reduce-scatter.7
  447.1 56.8 reduce-scatter.9
  516.9 56.8 reduce-scatter.11
  575.9 26.9 reduce-scatter.13
  664.5 56.6 reduce-scatter.15
  755.4 36.9 reduce-scatter.17
  795.3 34.2 reduce-scatter.19

commit v3 on v2

v3 whole, which is shorter than its diff:
```python
import functools

import jax
import jax.numpy as jnp
from jax import lax
from jax.experimental import pallas as pl
from jax.experimental.pallas import tpu as pltpu
from jax.sharding import Mesh
from jax.sharding import PartitionSpec as P

EPSILON = 1e-06
F32 = jnp.float32
BF16 = jnp.bfloat16
LANES = 128
HALO = 16
SWAP = [(0, 1), (1, 0)]
LONG = 6 * 10**10


def mm(left, right, left_dim, right_dim):
    return lax.dot_general(
        left.astype(BF16),
        right.astype(BF16),
        (((left_dim,), (right_dim,)), ((), ())),
        preferred_element_type=F32,
    )


def nn(left, right):
    return mm(left, right, 1, 0)


def nt(left, right):
    return mm(left, right, 1, 1)


def tn(left, right):
    return mm(left, right, 0, 0)


def place_scalars():
    return jnp.stack([lax.axis_index("core"), lax.axis_index("cx")]).astype(jnp.int32)


def call(kernel, grid, in_specs, out_specs, out_shape, scratch=(), flops=1000):
    return pl.pallas_call(
        kernel,
        grid_spec=pltpu.PrefetchScalarGridSpec(
            num_scalar_prefetch=1,
            grid=grid,
            in_specs=in_specs,
            out_specs=out_specs,
            scratch_shapes=list(scratch),
        ),
        out_shape=out_shape,
        compiler_params=pltpu.CompilerParams(
            dimension_semantics=("arbitrary",) * len(grid), vmem_limit_bytes=48 << 20
        ),
        cost_estimate=pl.CostEstimate(flops=flops, transcendentals=0, bytes_accessed=1000),
    )


def pack_heads(places, query, key, value, heads):
    rows = query.shape[0]

    def kernel(where, query_ref, key_ref, value_ref, out):
        out[:, :LANES] = query_ref[...]
        out[:, LANES : 2 * LANES] = key_ref[...]
        out[:, 2 * LANES :] = value_ref[...]

    spec = pl.BlockSpec((rows, LANES), lambda h, w: (0, w[0] * heads + 2 * w[1] + h))
    return call(
        kernel,
        (2,),
        [spec] * 3,
        pl.BlockSpec((rows, 3 * LANES), lambda h, w: (0, h)),
        jax.ShapeDtypeStruct((rows, 6 * LANES), query.dtype),
    )(places, query, key, value)


def own_parts(units):
    wide = units // 2
    main = wide // (2 * LANES) * LANES
    return wide, main, wide - 2 * main


def own_units(places, weight, axis):
    wide, main, rest = own_parts(weight.shape[axis])
    first = lax.dynamic_slice_in_dim(weight, places[0] * wide + places[1] * main, main, axis)
    last = lax.dynamic_slice_in_dim(weight, places[0] * wide + 2 * main, rest, axis)
    low, high = jnp.split(last, 2, axis)
    return jnp.concatenate([first, jnp.where(places[1] == 0, low, high)], axis)


def own_heads(places, weight):
    rows = weight.shape[0] // 4
    return lax.dynamic_slice_in_dim(weight, (2 * places[0] + places[1]) * rows, rows, 0)


def pieces_of(own, *after):
    across = lax.ppermute(own, "cx", SWAP)
    late = tie(across, after)
    return [own, across, lax.ppermute(own, "core", SWAP), lax.ppermute(late, "core", SWAP)]


def pick(where, core, cx, refs, store):
    which = 2 * jnp.bitwise_xor(where[0], core) + jnp.bitwise_xor(where[1], cx)
    for index in range(4):

        @pl.when(which == index)
        def _():
            store(refs[index][...].astype(F32))


def lay_heads(places, heads):
    rows = heads[0][0].shape[0]

    def kernel(where, *refs):
        outs = refs[-3:]
        for head in range(2):

            def store(values):
                for index in range(3):
                    outs[index][:, head * LANES : (head + 1) * LANES] = values[
                        :, index * LANES : (index + 1) * LANES
                    ]

            pick(where, pl.program_id(0), pl.program_id(1), refs[4 * head : 4 * head + 4], store)

    return call(
        kernel,
        (2, 2),
        [pl.BlockSpec(heads[0][0].shape, lambda i, j, w: (0, 0))] * 8,
        [pl.BlockSpec((rows, 2 * LANES), lambda i, j, w: (0, 2 * i + j))] * 3,
        [jax.ShapeDtypeStruct((rows, 8 * LANES), F32)] * 3,
    )(places, *heads[0], *heads[1])


def lay_units(places, pieces):
    rows, units = pieces[0].shape
    wide, main, rest = own_parts(4 * units)
    half = rest // 2

    def kernel(where, a, b, c, d, out):
        for side in range(2):

            def store(values):
                out[:, side * main : (side + 1) * main] = values[:, :main]
                at = 2 * main + side * half
                out[:, at : at + half] = values[:, main:]

            pick(where, pl.program_id(0), side, (a, b, c, d), store)

    return call(
        kernel,
        (2,),
        [pl.BlockSpec((rows, units), lambda i, w: (0, 0))] * 4,
        pl.BlockSpec((rows, wide), lambda i, w: (0, i)),
        jax.ShapeDtypeStruct((rows, 2 * wide), F32),
    )(places, *pieces)


def lay_units_turned(places, pieces):
    rows, units = pieces[0].shape
    wide, main, rest = own_parts(4 * units)
    half = rest // 2

    def kernel(where, a, b, c, d, out):
        for side in range(2):

            def store(values):
                turned = values.T
                out[side * main : (side + 1) * main, :] = turned[:main]
                at = 2 * main + side * half
                out[at : at + half, :] = turned[main:]

            pick(where, pl.program_id(0), side, (a, b, c, d), store)

    return call(
        kernel,
        (2,),
        [pl.BlockSpec((rows, units), lambda i, w: (0, 0))] * 4,
        pl.BlockSpec((wide, rows), lambda i, w: (i, 0)),
        jax.ShapeDtypeStruct((2 * wide, rows), F32),
    )(places, *pieces)


def lay_heads_turned(places, pieces):
    rows, columns = pieces[0].shape

    def kernel(where, a, b, c, d, out):
        def store(values):
            out[...] = values.T

        pick(where, pl.program_id(0), pl.program_id(1), (a, b, c, d), store)

    return call(
        kernel,
        (2, 2),
        [pl.BlockSpec((rows, columns), lambda i, j, w: (0, 0))] * 4,
        pl.BlockSpec((columns, rows), lambda i, j, w: (2 * i + j, 0)),
        jax.ShapeDtypeStruct((4 * columns, rows), F32),
    )(places, *pieces)


def fill_ext(ext, index, halo, first, second, size):
    ext[index, :HALO, :] = halo[...].astype(F32)
    ext[index, HALO : HALO + size, :] = first[...].astype(F32)
    ext[index, HALO + size :, :] = second[...].astype(F32)


def links_of(ids, total):
    own = ids[0, HALO : HALO + total, :]
    return [
        (ids[0, HALO - 3 + tap : HALO - 3 + tap + total, :] == own).astype(F32) for tap in range(4)
    ]


def conv_of(ext, index, taps, links, total):
    result = None
    for tap in range(4):
        term = (
            taps[index, 0, tap : tap + 1, :]
            * ext[index, HALO - 3 + tap : HALO - 3 + tap + total, :]
            * links[tap]
        )
        result = term if result is None else result + term
    return result


def sigmoid(values):
    return 1.0 / (1.0 + jnp.exp(-values))


def first_head(where, own):
    return 2 * (where[1] if own else 1 - where[1])


def head_of(where, own):
    return first_head(where, own) + pl.program_id(1)


def column_of(values, head):
    lane = lax.broadcasted_iota(jnp.int32, values.shape, 1)
    return jnp.sum(jnp.where(lane == head, values, 0.0), axis=1, keepdims=True)


def marks(ids, rows, chunk, size):
    start = HALO + chunk * size
    column = ids[0, start : start + size, :]
    before = ids[0, start - 1 : start, :]
    last = ids[0, start + size - 1 : start + size, :]
    first = (column == before).astype(F32)
    tail = (column == last).astype(F32)
    whole = (last == before).astype(F32)
    same = column == rows[0, chunk : chunk + 1, :]
    row = lax.broadcasted_iota(jnp.int32, (size, size), 0)
    col = lax.broadcasted_iota(jnp.int32, (size, size), 1)
    return first, tail, whole, same & (row > col), same & (row >= col)


def inverse_units(stricts, size):
    row = lax.broadcasted_iota(jnp.int32, (size, size), 0)
    col = lax.broadcasted_iota(jnp.int32, (size, size), 1)
    mixed = jnp.bitwise_xor(row, col)
    results = [
        jnp.where(row == col, 1.0, jnp.where(mixed == 1, -strict, 0.0)) for strict in stricts
    ]
    stricts = [strict.astype(BF16) for strict in stricts]
    block = 2
    while block < size:
        pair = (mixed >= block) & (mixed < 2 * block)
        lows = [result.astype(BF16) for result in results]
        parts = [jnp.where(pair, strict, 0.0) for strict in stricts]
        steps = [nn(part, low).astype(BF16) for part, low in zip(parts, lows)]
        results = [
            result - nn(low, step) for result, low, step in zip(results, lows, steps)
        ]
        block *= 2
    return [result.astype(BF16) for result in results]


def forward_one(where, q0, k0, v0, q1, k1, v1, qh, kh, vh, taps, ids, rows, r0, r1, *rest, size, own):
    query, key, value, inverse, final, ext = rest
    head = head_of(where, own)
    total = 2 * size
    for index, group in enumerate(((qh, q0, q1), (kh, k0, k1), (vh, v0, v1))):
        fill_ext(ext, index, *group, size)
    links = links_of(ids, total)
    out = []
    for index in range(3):
        conv = conv_of(ext, index, taps, links, total)
        act = conv * sigmoid(conv)
        if index < 2:
            act = act * lax.rsqrt(jnp.sum(act * act, axis=1, keepdims=True) + EPSILON)
        out.append(act.astype(BF16))
    for target, values in zip((query, key, value), out):
        target[0, 0] = values[:size]
        target[0, 1] = values[size:]
    chunks = []
    for chunk, rates in enumerate((r0, r1)):
        first, tail, whole, strict, _ = marks(ids, rows, chunk, size)
        rate = column_of(rates[...], head)
        keys = out[1][chunk * size : (chunk + 1) * size]
        chunks.append((first, tail, whole, rate, keys, jnp.where(strict, rate * nt(keys, keys), 0.0)))
    inverses = inverse_units([item[-1] for item in chunks], size)
    state = None
    for chunk, (first, tail, whole, rate, keys, _) in enumerate(chunks):
        fresh = out[2][chunk * size : (chunk + 1) * size].astype(F32)
        inverse[0, 0, chunk] = inverses[chunk]
        if chunk:
            fresh = fresh - first * nt(keys, state)
        fresh = nn(inverses[chunk], rate * fresh)
        added = tn(tail * fresh, keys)
        state = added if state is None else whole * state + added
    final[0, 0] = state.astype(BF16)


def forward_two(where, query, key, value, inverse, ids, rows, r0, r1, incoming, gain, *rest, size, scale, own):
    head_low, mixed_out, fresh_out, middle = rest
    head = head_of(where, own)
    state = incoming[0, 0].astype(F32)
    for chunk, rates in enumerate((r0, r1)):
        first, tail, whole, _, lower = marks(ids, rows, chunk, size)
        rate = column_of(rates[...], head)
        keys, queries = key[0, chunk], query[0, chunk]
        if chunk:
            middle[0, 0] = state.astype(BF16)
        rest_rows = value[0, chunk].astype(F32) - first * nt(keys, state)
        fresh = nn(inverse[0, 0, chunk], rate * rest_rows)
        fresh_out[0, chunk] = fresh.astype(BF16)
        inner = jnp.where(lower, nt(queries, keys), 0.0)
        mixed = scale * (first * nt(queries, state) + nn(inner, fresh))
        mixed_out[0, chunk] = mixed
        normed = mixed * lax.rsqrt(jnp.mean(mixed * mixed, axis=1, keepdims=True) + EPSILON)
        slot = where[0] if chunk == 0 else 1 - where[0]
        head_low[slot, 0] = (normed * gain[...]).astype(BF16)
        if chunk == 0:
            state = whole * state + tn(tail * fresh, keys)


def backward_one(where, d_head, mixed, query, key, inverse, ids, rows, r0, r1, gain, *rest, size, scale, own):
    d_out, d_state_out, d_gain = rest
    head = head_of(where, own)
    total = jnp.zeros((1, LANES), F32)
    d_state = None
    for chunk in (1, 0):
        first, tail, whole, _, lower = marks(ids, rows, chunk, size)
        rate = column_of((r0, r1)[chunk][...], head)
        keys, queries = key[0, chunk], query[0, chunk]
        slot = where[0] if chunk == 0 else 1 - where[0]
        grad = d_head[slot, 0].astype(F32)
        values = mixed[0, chunk]
        inv_rms = lax.rsqrt(jnp.mean(values * values, axis=1, keepdims=True) + EPSILON)
        normed = values * inv_rms
        total = total + jnp.sum(grad * normed, axis=0, keepdims=True)
        scaled = grad * gain[...]
        d_mixed = inv_rms * (scaled - normed * jnp.mean(scaled * normed, axis=1, keepdims=True))
        d_low = (scale * d_mixed).astype(BF16)
        d_out[0, chunk] = d_low
        inner = jnp.where(lower, nt(queries, keys), 0.0)
        d_fresh = tn(inner, d_low)
        if d_state is not None:
            d_fresh = d_fresh + tail * nt(keys, d_state)
        d_rest = rate * tn(inverse[0, 0, chunk], d_fresh)
        change = tn(first * d_low.astype(F32), queries) - tn(first * d_rest, keys)
        d_state = change if d_state is None else whole * d_state + change
    d_state_out[0, 0] = d_state.astype(BF16)
    d_gain[0, 0] = jnp.broadcast_to(total, (8, LANES))


def backward_two(where, q0, k0, v0, q1, k1, v1, qh, kh, vh, taps, ids, rows, r0, r1, *rest, size, own):
    query, key, value, inverse, fresh_in, d_in, incoming, middle, d_final = rest[:9]
    d_raw, d_edge, d_rates, d_taps = rest[9:13]
    ext, d_ext, d_rows = rest[13:]
    head = head_of(where, own)
    total = 2 * size
    for index, group in enumerate(((qh, q0, q1), (kh, k0, k1), (vh, v0, v1))):
        fill_ext(ext, index, *group, size)
    d_state = d_final[0, 0].astype(F32)

    @pl.when(pl.program_id(1) == 0)
    def _():
        d_rates[...] = jnp.zeros_like(d_rates)

    for chunk in (1, 0):
        first, tail, whole, strict, lower = marks(ids, rows, chunk, size)
        rate = column_of((r0, r1)[chunk][...], head)
        keys, queries, fresh = key[0, chunk], query[0, chunk], fresh_in[0, chunk]
        inv, d_low = inverse[0, 0, chunk], d_in[0, chunk]
        state = (middle if chunk else incoming)[0, 0]
        d_mix = d_low.astype(F32)
        inner = jnp.where(lower, nt(queries, keys), 0.0)
        gram = jnp.where(strict, nt(keys, keys), 0.0)
        d_fresh = tn(inner, d_low) + tail * nt(keys, d_state)
        turned = tn(inv, d_fresh)
        d_rest = rate * turned
        rest_rows = value[0, chunk].astype(F32) - first * nt(keys, state)
        error = rest_rows - nn(gram, fresh)
        d_rate = jnp.sum(turned * error, axis=1, keepdims=True) * rate * (1.0 - rate)
        d_inner = jnp.where(lower, nt(d_low, fresh), 0.0)
        d_gram = rate * jnp.where(strict, -nt(turned, fresh), 0.0)
        d_query = first * nn(d_low, state) + nn(d_inner, keys)
        d_key = (
            tn(d_inner, queries)
            + tail * nn(fresh, d_state)
            - nn(first * d_rest, state)
            + nn(d_gram, keys)
            + tn(d_gram, keys)
        )
        for index, values in enumerate((d_query, d_key, d_rest)):
            d_rows[index, chunk * size : (chunk + 1) * size, :] = values
        lane = lax.broadcasted_iota(jnp.int32, (size, LANES), 1)
        d_rates[0, chunk] = d_rates[0, chunk] + jnp.where(lane == head, d_rate, 0.0)
        if chunk:
            d_state = (
                whole * d_state + tn(first * d_mix, queries) - tn(first * d_rest, keys)
            )
    links = links_of(ids, total)
    for index in range(3):
        conv = conv_of(ext, index, taps, links, total)
        sig = sigmoid(conv)
        d_act = d_rows[index].astype(BF16).astype(F32)
        if index < 2:
            act = conv * sig
            inv_norm = lax.rsqrt(jnp.sum(act * act, axis=1, keepdims=True) + EPSILON)
            unit = act * inv_norm
            d_act = (d_act - unit * jnp.sum(unit * d_act, axis=1, keepdims=True)) * inv_norm
        d_conv = d_act * sig * (1.0 + conv * (1.0 - sig))
        d_ext[...] = jnp.zeros_like(d_ext)
        for tap in range(4):
            window = slice(HALO - 3 + tap, HALO - 3 + tap + total)
            linked = d_conv * links[tap]
            d_taps[0, index, 0, tap : tap + 1, :] = jnp.sum(
                linked * ext[index, window, :], axis=0, keepdims=True
            )
            d_ext[window, :] = d_ext[window, :] + taps[index, 0, tap : tap + 1, :] * linked
        lanes = slice(index * LANES, (index + 1) * LANES)
        d_edge[0, :, lanes] = d_ext[:HALO, :].astype(BF16)
        d_raw[where[0], 0, :, lanes] = d_ext[HALO : HALO + size, :].astype(BF16)
        d_raw[1 - where[0], 0, :, lanes] = d_ext[HALO + size :, :].astype(BF16)


def mixer_calls(places, own, rates, ids, rows, taps, gain, seqs, size, scale):
    def slot_of(chunk, w):
        return w[0] if chunk == 0 else 1 - w[0]

    def raw_spec(chunk, part):
        return pl.BlockSpec(
            (size, LANES), lambda b, h, w: (slot_of(chunk, w) * seqs + b, 3 * h + part)
        )

    def rate_spec(chunk):
        return pl.BlockSpec((size, LANES), lambda b, h, w: (slot_of(chunk, w) * seqs + b, 0))

    halo_base = 2 * seqs * size // HALO

    def halo_spec(part):
        return pl.BlockSpec((HALO, LANES), lambda b, h, w: (halo_base + b, 3 * h + part))

    conv_specs = (
        [raw_spec(c, p) for c in range(2) for p in range(3)]
        + [halo_spec(p) for p in range(3)]
        + [
            pl.BlockSpec((3, 1, 4, LANES), lambda b, h, w: (0, first_head(w, own) + h, 0, 0)),
            pl.BlockSpec((1, HALO + 2 * size, 1), lambda b, h, w: (b, 0, 0)),
            pl.BlockSpec((1, 2, size), lambda b, h, w: (b, 0, 0)),
            rate_spec(0),
            rate_spec(1),
        ]
    )
    rest_args = (taps, ids, rows, rates, rates)
    id_specs, id_args = conv_specs[10:], rest_args[1:]
    act_spec = pl.BlockSpec((1, 2, size, LANES), lambda b, h, w: (b, 0, 0, h))
    act_shape = (seqs, 2, size, 2 * LANES)
    state_spec = pl.BlockSpec((1, 1, LANES, LANES), lambda b, h, w: (b, h, 0, 0))
    state_shape = jax.ShapeDtypeStruct((seqs, 2, LANES, LANES), BF16)
    inv_spec = pl.BlockSpec((1, 1, 2, size, size), lambda b, h, w: (b, h, 0, 0, 0))
    inv_shape = jax.ShapeDtypeStruct((seqs, 2, 2, size, size), BF16)
    slot_spec = pl.BlockSpec((2, 1, size, LANES), lambda b, h, w: (0, b, 0, h))
    slot_shape = jax.ShapeDtypeStruct((2, seqs, size, 2 * LANES), BF16)
    gain_spec = pl.BlockSpec((1, LANES), lambda b, h, w: (0, 0))
    low = jax.ShapeDtypeStruct(act_shape, BF16)
    grid = (seqs, 2)

    def one(raw):
        return call(
            functools.partial(forward_one, size=size, own=own),
            grid,
            conv_specs,
            [act_spec] * 3 + [inv_spec, state_spec],
            [low] * 3 + [inv_shape, state_shape],
            [pltpu.VMEM((3, HALO + 2 * size, LANES), F32)],
        )(places, *(raw,) * 9, *rest_args)

    def two(query, key, value, inverse, incoming):
        args = (query, key, value, inverse, *id_args, incoming, gain)
        return call(
            functools.partial(forward_two, size=size, scale=scale, own=own),
            grid,
            [act_spec] * 3
            + [inv_spec]
            + id_specs
            + [state_spec, gain_spec],
            [slot_spec, act_spec, act_spec, state_spec],
            [slot_shape, jax.ShapeDtypeStruct(act_shape, F32), low, state_shape],
        )(places, *args)

    def three(d_head, mixed, query, key, inverse):
        return call(
            functools.partial(backward_one, size=size, scale=scale, own=own),
            grid,
            [slot_spec, act_spec, act_spec, act_spec, inv_spec] + id_specs + [gain_spec],
            [act_spec, state_spec, pl.BlockSpec((1, 1, 8, LANES), lambda b, h, w: (b, h, 0, 0))],
            [low, state_shape, jax.ShapeDtypeStruct((seqs, 2, 8, LANES), F32)],
            flops=LONG,
        )(places, d_head, mixed, query, key, inverse, *id_args, gain)

    def four(raw, query, key, value, inverse, fresh, d_low, incoming, middle, d_final):
        return call(
            functools.partial(backward_two, size=size, own=own),
            grid,
            conv_specs + [act_spec] * 3 + [inv_spec, act_spec, act_spec] + [state_spec] * 3,
            [
                pl.BlockSpec((2, 1, size, 3 * LANES), lambda b, h, w: (0, b, 0, h)),
                pl.BlockSpec((1, HALO, 3 * LANES), lambda b, h, w: (b, 0, h)),
                pl.BlockSpec((1, 2, size, LANES), lambda b, h, w: (b, 0, 0, 0)),
                pl.BlockSpec((1, 3, 1, 4, LANES), lambda b, h, w: (b, 0, h, 0, 0)),
            ],
            [
                jax.ShapeDtypeStruct((2, seqs, size, 6 * LANES), BF16),
                jax.ShapeDtypeStruct((seqs, HALO, 6 * LANES), BF16),
                jax.ShapeDtypeStruct((seqs, 2, size, LANES), F32),
                jax.ShapeDtypeStruct((seqs, 3, 2, 4, LANES), F32),
            ],
            [
                pltpu.VMEM((3, HALO + 2 * size, LANES), F32),
                pltpu.VMEM((HALO + 2 * size, LANES), F32),
                pltpu.VMEM((3, 2 * size, LANES), F32),
            ],
            flops=LONG,
        )(
            places,
            *(raw,) * 9,
            *rest_args,
            query,
            key,
            value,
            inverse,
            fresh,
            d_low,
            incoming,
            middle,
            d_final,
        )

    return one, two, three, four


def tile_of(extent):
    return 512 if extent % 512 == 0 else extent


def rows_products(pairs, rows, block, add=None, out=BF16):
    columns = pairs[0][1].shape[0]
    tile = tile_of(columns)
    count = len(pairs)

    def kernel(*refs):
        total = None
        for index in range(count):
            part = nt(refs[index][...], refs[count + index][...])
            total = part if total is None else total + part
        if add is not None:
            total = total + refs[2 * count][...].astype(F32)
        refs[-1][...] = total.astype(out)

    lefts = [pl.BlockSpec((rows, left.shape[1]), lambda i: (block, 0)) for left, _ in pairs]
    rights = [pl.BlockSpec((tile, right.shape[1]), lambda i: (i, 0)) for _, right in pairs]
    spec = pl.BlockSpec((rows, tile), lambda i: (0, i))
    extra = () if add is None else (add,)
    return pl.pallas_call(
        kernel,
        grid=(columns // tile,),
        in_specs=lefts + rights + [spec] * len(extra),
        out_specs=spec,
        out_shape=jax.ShapeDtypeStruct((rows, columns), out),
        compiler_params=pltpu.CompilerParams(vmem_limit_bytes=48 << 20),
        cost_estimate=pl.CostEstimate(flops=1000, transcendentals=0, bytes_accessed=1000),
    )(*(left for left, _ in pairs), *(right for _, right in pairs), *extra)


def token_products(pairs, add=None):
    count = len(pairs)
    height, columns = pairs[0][0].shape[1], pairs[0][1].shape[1]
    tile = tile_of(height)

    def kernel(*refs):
        total = None
        for index in range(count):
            part = tn(refs[index][...], refs[count + index][...])
            total = part if total is None else total + part
        if add is not None:
            total = total + refs[2 * count][...].astype(F32)
        refs[-1][...] = total.astype(BF16)

    lefts = [
        pl.BlockSpec((rows, tile), lambda i, block=block: (block, i))
        for _, _, rows, block in pairs
    ]
    rights = [pl.BlockSpec((rows, columns), lambda i: (0, 0)) for _, _, rows, _ in pairs]
    spec = pl.BlockSpec((tile, columns), lambda i: (i, 0))
    extra = () if add is None else (add,)
    return pl.pallas_call(
        kernel,
        grid=(height // tile,),
        in_specs=lefts + rights + [spec] * len(extra),
        out_specs=spec,
        out_shape=jax.ShapeDtypeStruct((height, columns), BF16),
        compiler_params=pltpu.CompilerParams(vmem_limit_bytes=48 << 20),
        cost_estimate=pl.CostEstimate(flops=1000, transcendentals=0, bytes_accessed=1000),
    )(*(item[0] for item in pairs), *(item[1] for item in pairs), *extra)


def feed_forward(rows, grads, gates, ups, downs):
    tokens, width = rows.shape
    units = gates.shape[1]
    tile = 256 if tokens % 256 == 0 else tokens

    def kernel(rows_ref, grads_ref, gates_ref, ups_ref, downs_ref, act, d_gate, d_up):
        gate = nn(rows_ref[...], gates_ref[...])
        up = nn(rows_ref[...], ups_ref[...])
        d_act = nn(grads_ref[...], downs_ref[...]).astype(BF16).astype(F32)
        sig = sigmoid(gate)
        act[...] = (gate * sig * up).astype(BF16)
        d_gate[...] = (d_act * up * sig * (1.0 + gate * (1.0 - sig))).astype(BF16)
        d_up[...] = (d_act * gate * sig).astype(BF16)

    token_spec = pl.BlockSpec((tile, width), lambda i: (i, 0))
    weight_spec = pl.BlockSpec((width, units), lambda i: (0, 0))
    unit_spec = pl.BlockSpec((tile, units), lambda i: (i, 0))
    return pl.pallas_call(
        kernel,
        grid=(tokens // tile,),
        in_specs=[token_spec] * 2 + [weight_spec] * 3,
        out_specs=[unit_spec] * 3,
        out_shape=[jax.ShapeDtypeStruct((tokens, units), BF16)] * 3,
        compiler_params=pltpu.CompilerParams(vmem_limit_bytes=48 << 20),
        cost_estimate=pl.CostEstimate(flops=1000, transcendentals=0, bytes_accessed=1000),
    )(rows, grads, gates, ups, downs)


def dot_nn(left, right):
    return lax.dot_general(left, right, (((1,), (0,)), ((), ())), preferred_element_type=F32)


def dot_nt(left, right):
    return lax.dot_general(left, right, (((1,), (1,)), ((), ())), preferred_element_type=F32)


def dot_tn(left, right):
    return lax.dot_general(left, right, (((0,), (0,)), ((), ())), preferred_element_type=F32)


def rms(values, gain):
    return values * lax.rsqrt(jnp.mean(values * values, axis=1, keepdims=True) + EPSILON) * gain


def tie(value, *after):
    return lax.optimization_barrier((value, after))[0]


class Steps:
    def __init__(self):
        self.last = ()

    def wait(self, *values):
        self.last = (self.last, values)

    def __call__(self, fn, *args):
        traced, static = [], []
        for arg in args:
            leaves = jax.tree.leaves(arg)
            static.append(not leaves or not all(hasattr(leaf, "dtype") for leaf in leaves))
            if not static[-1]:
                traced.append(arg)
        traced = iter(tie(tuple(traced), self.last))
        result = fn(*(arg if fixed else next(traced) for arg, fixed in zip(args, static)))
        self.last = result
        return result


def sum_over(values, axis, hop):
    partners = [(index, index ^ hop) for index in range(lax.axis_size(axis))]
    return (values.astype(F32) + lax.ppermute(values, axis, partners).astype(F32)).astype(BF16)


def shards(
    hidden_in,
    attn_gain,
    query_weight,
    key_weight,
    value_weight,
    conv_weight,
    beta_weight,
    out_gain,
    out_weight,
    ffn_gain,
    gate_weight,
    up_weight,
    down_weight,
    cotangent,
    segment_ids,
):
    count = lax.axis_size("shard")
    places = place_scalars()
    core, cx = places[0], places[1]
    micro, local, size, width = hidden_in.shape
    seqs = micro * local
    own_rows = seqs * size
    heads_tp = conv_weight.shape[2]
    heads = heads_tp // 2
    scale = LANES ** (-0.5)
    first_rows, other_rows = slice(0, own_rows), slice(own_rows, 2 * own_rows)

    def gathered(piece):
        return lax.all_gather(piece, "shard", axis=0, tiled=True)

    def over_shard(total):
        return lax.psum_scatter(total, "shard", scatter_dimension=0, tiled=True)

    def across(part):
        return lax.ppermute(part, "cx", SWAP)

    def to_core(part):
        return lax.ppermute(part, "core", SWAP)

    def with_core(part):
        return jnp.concatenate([part, to_core(part)])

    pack = pack_heads(places, query_weight, key_weight, value_weight, heads)
    joint_own = gathered(pack)

    small = jnp.concatenate(
        [
            attn_gain,
            ffn_gain,
            out_gain,
            conv_weight.reshape(-1),
            beta_weight.reshape(-1),
        ]
    )
    unpadded = small.size
    small = jnp.pad(small, (0, -unpadded % (16 * LANES))).reshape(-1, LANES)
    small = lax.all_gather(small, "shard", axis=0).reshape(count, -1)
    piece_d = attn_gain.shape[0]
    entry = out_gain.shape[0]
    at = 2 * piece_d + entry
    gain_in = small[:, :piece_d].reshape(1, -1).astype(F32)
    gain_ffn = small[:, piece_d : 2 * piece_d].reshape(1, -1).astype(F32)
    gain_head = small[:, 2 * piece_d : at].reshape(1, LANES).astype(F32)
    conv_size = conv_weight.size
    taps = small[:, at : at + conv_size].reshape(count, 4, 3, heads_tp, entry)
    taps = taps.transpose(2, 3, 1, 0, 4).reshape(3, heads_tp, 4, LANES)
    taps = lax.dynamic_slice_in_dim(taps, core * heads, heads, axis=1).astype(F32)
    beta = small[:, at + conv_size : unpadded].reshape(width, heads_tp)
    beta = lax.dynamic_slice_in_dim(beta, core * heads, heads, axis=1)
    beta = jnp.pad(beta, ((0, 0), (0, LANES - heads)))

    hidden_own = hidden_in.reshape(own_rows, width)
    hidden_other = to_core(hidden_own)
    ids_own = segment_ids.reshape(seqs, size)
    ids_other = to_core(ids_own)
    late = jnp.where(core == 1, hidden_own, hidden_other).reshape(seqs, size, width)[:, size - HALO :]
    early_ids = jnp.where(core == 0, ids_own, ids_other)
    late_ids = jnp.where(core == 1, ids_own, ids_other)
    halo = lax.ppermute(late, "cx", [(0, 1)]).reshape(seqs * HALO, width)
    halo_ids = lax.ppermute(late_ids[:, size - HALO :], "cx", [(0, 1)])
    halo_ids = jnp.where(cx == 0, -1, halo_ids)
    ids = jnp.concatenate([halo_ids, early_ids, late_ids], axis=1)[..., None]
    id_rows = jnp.stack([early_ids, late_ids], axis=1)
    hidden_all = jnp.concatenate([hidden_own, hidden_other, halo])
    normed_low = rms(hidden_all.astype(F32), gain_in).astype(BF16)
    rates = sigmoid(dot_nn(normed_low, beta))
    grad_own = cotangent.reshape(own_rows, width)
    grad_near = with_core(grad_own)
    grad_far = with_core(across(grad_own))

    outer_own = gathered(tie(own_heads(places, out_weight).T, pack))
    gates = gathered(tie(own_units(places, gate_weight, 1), pack, hidden_all))
    ups = gathered(tie(own_units(places, up_weight, 1), normed_low, rates))
    downs = gathered(tie(own_units(places, down_weight, 0).T, grad_near, grad_far))
    joint_other = across(tie(joint_own, grad_far, ids, id_rows, normed_low))

    steps = Steps()
    shapes = (rates, ids, id_rows, taps, gain_head, seqs, size, scale)
    own_calls = mixer_calls(places, True, *shapes)
    other_calls = mixer_calls(places, False, *shapes)

    def project(rows, weight):
        return dot_nn(rows, weight).astype(BF16)

    raw_own = steps(project, normed_low, joint_own)
    first_own = steps(own_calls[0], raw_own)
    outer_other = across(tie(outer_own, joint_other, first_own[-1]))
    raw_other = steps(project, normed_low, joint_other)
    first_other = steps(other_calls[0], raw_other)
    in_other = lax.ppermute(first_own[-1], "cx", [(0, 1)])
    in_own = lax.ppermute(first_other[-1], "cx", [(0, 1)])
    head_other, mixed_other, fresh_other, middle_other = steps(
        other_calls[1], *first_other[:4], in_other
    )
    head_own, mixed_own, fresh_own, middle_own = steps(own_calls[1], *first_own[:4], in_own)
    slots = head_own.shape
    head_own, head_other = (part.reshape(2 * own_rows, -1) for part in (head_own, head_other))

    def products(block, lefts, rights, add=None, out=BF16):
        return rows_products(list(zip(lefts, rights)), own_rows, block, add, out)

    def away(*pairs):
        lefts, rights = zip(*pairs)
        return to_core(steps(lambda *args: products(1, *args), lefts, rights))

    def here(arrived, *pairs, out=BF16):
        lefts, rights = zip(*pairs)
        return steps(lambda *args: products(0, *args, out), lefts, rights, arrived)

    def with_tp(part):
        return part, lax.ppermute(part, "tp", SWAP)

    def pair_sum(pair):
        return pair[0].astype(F32) + pair[1].astype(F32)

    pairs = ((head_own, outer_own), (head_other, outer_other))
    mixer_pair = with_tp(here(away(*pairs), *pairs))
    hidden_f32 = hidden_own.astype(F32)

    def resid_step(pair, hidden):
        resid = hidden + pair_sum(pair)
        return resid, rms(resid, gain_ffn).astype(BF16)

    steps.wait(ups)
    resid, ffn_own = steps(resid_step, mixer_pair, hidden_f32)
    ffn_far_own = across(ffn_own)
    ffn_near = with_core(ffn_own)

    weights = (gates, ups, downs)
    act_near, d_gate_near, d_up_near = steps(feed_forward, ffn_near, grad_near, *weights)
    near = ((d_gate_near, gates), (d_up_near, ups))
    near_arrived = away(*near)
    down_near_arrived = away((act_near, downs))
    ffn_far = with_core(tie(ffn_far_own, down_near_arrived))
    act_far, d_gate_far, d_up_far = steps(feed_forward, ffn_far, grad_far, *weights)
    far = ((d_gate_far, gates), (d_up_far, ups))

    def both_grads(near, far, grads_near, grads_far):
        rows = near.shape[0]
        return token_products([(near, grads_near, rows, 0), (far, grads_far, rows, 0)])

    d_ffn_sent = across(here(away(*far), *far))
    grad_down = over_shard(steps(both_grads, grad_near, grad_far, act_near, act_far))
    d_ffn_near = here(near_arrived, *near, out=F32)
    down_far_arrived = away((act_far, downs))
    grad_gate = over_shard(steps(both_grads, ffn_near, ffn_far, d_gate_near, d_gate_far))

    def add_far(near, arrived):
        return (near + arrived.astype(F32)).astype(BF16)

    d_ffn_pair = with_tp(steps(add_far, d_ffn_near, d_ffn_sent))
    grad_up = over_shard(steps(both_grads, ffn_near, ffn_far, d_up_near, d_up_far))
    down_sent = across(here(down_far_arrived, (act_far, downs)))
    down_near = here(down_near_arrived, (act_near, downs), out=F32)

    def resid_back(pair, resid, grads):
        _, pull = jax.vjp(rms, resid, gain_ffn)
        d_resid, sum_ffn_gain = pull(pair_sum(pair))
        d_resid = grads.astype(F32) + d_resid
        return d_resid, sum_ffn_gain, d_resid.astype(BF16)

    d_resid, sum_ffn_gain, resid_own = steps(resid_back, d_ffn_pair, resid, grad_own)
    resid_other = to_core(resid_own)
    resid_low = steps(lambda own, other: jnp.concatenate([own, other]), resid_own, resid_other)

    def grad_of(rows, grads, *arrived):
        return token_products([(rows, grads, 2 * own_rows, 0)], *arrived)

    d_head_own = steps(project, resid_low, outer_own).reshape(slots)
    d_head_other = steps(project, resid_low, outer_other).reshape(slots)
    third_own = steps(own_calls[2], d_head_own, mixed_own, *first_own[:2], first_own[3])
    d_final_other = lax.ppermute(third_own[1], "cx", [(1, 0)])
    third_other = steps(other_calls[2], d_head_other, mixed_other, *first_other[:2], first_other[3])
    d_final_own = lax.ppermute(third_other[1], "cx", [(1, 0)])
    outer_sent = across(steps(grad_of, resid_low, head_other))
    down_pair = with_tp(steps(add_far, down_near, down_sent))
    steps.wait(d_final_own, d_final_other)
    fourth_other = steps(
        other_calls[3],
        raw_other,
        *first_other[:4],
        fresh_other,
        third_other[0],
        in_other,
        middle_other,
        d_final_other,
    )
    edge_own = lax.ppermute(fourth_other[1], "cx", [(1, 0)])
    normed_rows = normed_low[: 2 * own_rows]

    def joint_grad(half, d_raw, d_edge, *arrived):
        lanes = slice(half * 3 * LANES, (half + 1) * 3 * LANES)
        d_raw = d_raw.reshape(2 * own_rows, -1)[:, lanes]
        d_edge = d_edge.reshape(seqs * HALO, -1)[:, lanes]
        pairs = [(normed_low, d_raw, 2 * own_rows, 0)]
        pairs += [(normed_low, d_edge, seqs * HALO, 2 * own_rows // (seqs * HALO))]
        return token_products(pairs, *arrived)

    joint_dots = [
        steps(functools.partial(joint_grad, half), *fourth_other[:2]) for half in range(2)
    ]
    joint_sent = [across(joint_dots[0])]
    steps.wait(outer_sent)
    fourth_own = steps(
        own_calls[3],
        raw_own,
        *first_own[:4],
        fresh_own,
        third_own[0],
        in_own,
        middle_own,
        d_final_own,
    )
    edge_other = lax.ppermute(fourth_own[1], "cx", [(1, 0)])
    joint_sent.append(across(tie(joint_dots[1], edge_other)))
    grad_outer = over_shard(steps(grad_of, resid_low, head_own, outer_sent))
    grad_joint = [
        over_shard(steps(functools.partial(joint_grad, 0), *fourth_own[:2], joint_sent[0]))
    ]

    def with_edge(d_raw, d_edge):
        window = (1 - core, 0, size - HALO, 0)
        edge_rows = lax.dynamic_slice(d_raw, window, (1,) + d_edge.shape)
        return lax.dynamic_update_slice(
            d_raw, (edge_rows.astype(F32) + d_edge.astype(F32)[None]).astype(BF16), window
        ).reshape(2 * own_rows, -1)

    def logit_step(rates, rows):
        d_rates = sum(rates)
        d_logit = jnp.where(core == 0, d_rates, d_rates[:, ::-1]).transpose(1, 0, 2, 3)
        d_logit = d_logit.reshape(2 * own_rows, LANES).astype(BF16)
        return d_logit, dot_tn(rows, d_logit)[:, :heads]

    d_logit, sum_rate = steps(logit_step, [fourth_own[2], fourth_other[2]], normed_rows)
    d_raw_own = steps(with_edge, fourth_own[0], edge_own)
    d_raw_other = steps(with_edge, fourth_other[0], edge_other)

    pairs = ((d_raw_own, joint_own), (d_raw_other, joint_other), (d_logit, beta))
    d_normed_pair = with_tp(here(away(*pairs), *pairs))
    grad_joint.append(
        over_shard(steps(functools.partial(joint_grad, 1), *fourth_own[:2], joint_sent[1]))
    )
    sum_head_gain = sum(
        jnp.sum(third[2][:, :, 0, :], axis=(0, 1)) for third in (third_own, third_other)
    )
    sum_head_gain = sum_over(sum_head_gain.astype(BF16), "tp", 1).astype(F32)

    out_down = steps(lambda pieces: lay_units_turned(places, pieces), pieces_of(grad_down, d_normed_pair[0]))
    out_gate = steps(lambda pieces: lay_units(places, pieces), pieces_of(grad_gate, d_normed_pair[0]))
    out_up = steps(lambda pieces: lay_units(places, pieces), pieces_of(grad_up, d_normed_pair[0]))

    def input_back(pair, d_resid, hidden):
        _, pull = jax.vjp(rms, hidden, gain_in)
        d_hidden, sum_attn_gain = pull(pair_sum(pair))
        return sum_attn_gain, (d_resid + d_hidden).astype(BF16)

    sum_attn_gain, input_rows = steps(input_back, d_normed_pair, d_resid, hidden_f32)
    result_rows = steps(
        lambda pair, resid: (resid + pair_sum(pair)).astype(BF16), down_pair, resid
    )
    out_outer = steps(lambda pieces: lay_heads_turned(places, pieces), pieces_of(grad_outer))

    sum_taps = [jnp.sum(fourth[3], axis=0).transpose(2, 0, 1, 3) for fourth in (fourth_own, fourth_other)]
    sum_taps = jnp.where(
        cx == 0, jnp.concatenate(sum_taps, axis=2), jnp.concatenate(sum_taps[::-1], axis=2)
    )
    gains = jnp.concatenate([sum_attn_gain[0], sum_ffn_gain[0], sum_head_gain]).astype(BF16)
    gains = sum_over(gains, "core", 1)
    packed = jnp.concatenate(
        [gains, sum_taps.reshape(-1).astype(BF16), sum_rate.reshape(-1).astype(BF16)]
    )
    packed = sum_over(packed, "cx", 1)
    hop = 1
    while hop < count:
        packed = sum_over(packed, "shard", hop)
        hop *= 2
    own = lax.axis_index("shard")
    ends = [width, 2 * width, 2 * width + LANES, 2 * width + LANES + sum_taps.size]
    grad_attn_gain = lax.dynamic_slice_in_dim(packed[: ends[0]], own * piece_d, piece_d)
    grad_ffn_gain = lax.dynamic_slice_in_dim(packed[ends[0] : ends[1]], own * piece_d, piece_d)
    grad_out_gain = lax.dynamic_slice_in_dim(packed[ends[1] : ends[2]], own * entry, entry)
    own_conv = lax.dynamic_slice_in_dim(
        packed[ends[2] : ends[3]].reshape(4, 3, heads, LANES), own * entry, entry, axis=3
    )
    own_beta = lax.dynamic_slice_in_dim(
        packed[ends[3] :].reshape(width, heads), own * piece_d, piece_d, axis=0
    )

    def both_cores(values, axis):
        other = to_core(values)
        return jnp.where(
            core == 0,
            jnp.concatenate([values, other], axis=axis),
            jnp.concatenate([other, values], axis=axis),
        ).astype(F32)

    out_query, out_key, out_value = lay_heads(places, [pieces_of(part) for part in grad_joint])
    return (
        result_rows.reshape(hidden_in.shape),
        input_rows.reshape(hidden_in.shape),
        grad_attn_gain.astype(F32),
        out_query,
        out_key,
        out_value,
        both_cores(own_conv, 2),
        both_cores(own_beta, 1),
        grad_out_gain.astype(F32),
        out_outer,
        grad_ffn_gain.astype(F32),
        out_gate,
        out_up,
        out_down,
    )


def solution(mesh):
    shard, ctx, tp = (mesh.shape[name] for name in ("shard", "ctx", "tp"))
    cores = Mesh(
        mesh.devices.reshape(shard, ctx // 2, 2, tp), ("shard", "cx", "core", "tp")
    )
    tokens = P(None, "shard", ("cx", "core"), None)
    outer = P("shard", "tp")
    turned = P("tp", "shard")
    conv = P(None, None, "tp", "shard")
    split = P("shard")
    return jax.shard_map(
        shards,
        mesh=cores,
        in_specs=(
            tokens,
            split,
            outer,
            outer,
            outer,
            conv,
            outer,
            split,
            turned,
            split,
            outer,
            outer,
            turned,
            tokens,
            P(None, "shard", ("cx", "core")),
        ),
        out_specs=(
            tokens,
            tokens,
            split,
            outer,
            outer,
            outer,
            conv,
            outer,
            split,
            turned,
            split,
            outer,
            outer,
            turned,
        ),
        check_vma=False,
    )
```

time: 918 us -> 849 us (0.925)
  matrix products: 177 us -> 20.2 us
  Pallas kernels: 150 us -> 277 us
  waiting for transfers between devices: 345 us -> 266 us
  local copies, waits for them, and re-layouts: 74.8 us -> 120 us
    ppermute x43 -> x31, waiting for transfers between devices: 216 us -> 79.8 us  [the longest x4 53.8 us: with_tp(): return (part, lax.ppermute(part, 'tp', SWAP))]
    pallas_call x19 -> x37, Pallas kernels: 150 us -> 277 us  [the longest x12 70.4 us: rows_products(): pl.pallas_call(kernel, grid=(columns // tile,), in_specs=lefts + rights +...]
    dot_general x28 -> x0, matrix products: 70.3 us -> none  [dot_nt(): lax.dot_general(left, right, (((1,), (1,)), ((), ())), preferred_element_...]
    dot_general x14 -> x1, matrix products: 56.6 us -> 2.9 us  [dot_tn(): lax.dot_general(left, right, (((0,), (0,)), ((), ())), preferred_element_...]
    ppermute x5, waiting for transfers between devices: 0.27 us -> 45.8 us  [sum_over(): lax.ppermute(values, axis, partners).astype(F32)]
    ppermute x6 -> x9, waiting for transfers between devices: 54.1 us -> 88.8 us  [across(): return lax.ppermute(part, 'cx', SWAP)]
    dot_general x14 -> x5, matrix products: 50.1 us -> 17.3 us  [dot_nn(): lax.dot_general(left, right, (((1,), (0,)), ((), ())), preferred_element_...]
    ppermute x6, waiting for transfers between devices: 57.3 us -> 27.9 us  [pieces_of(): across = lax.ppermute(own, 'cx', SWAP)]
  transfers between devices with their start and end apart: 81 -> 70, of which waited for: 31 -> 27; matrix products, arithmetic and copies ran while one was open for 27% -> 18% of each run, Pallas kernels for 16% -> 28%
where the time goes in v3:
time: 849 us; the launch traced here: 839 us
  Pallas kernels  277 us (33%)
  waiting for transfers between devices  266 us (31%)
  local copies, waits for them, and re-layouts  120 us (14%)
  other arithmetic  71.7 us (8%)
  starting transfers between devices  54.6 us (6%)
  matrix products  20.2 us (2%)
  between operations  15.8 us (2%)
  blocking collectives  13.9 us (2%)
    ppermute x9, waiting for transfers between devices, across(): return lax.ppermute(part, 'cx', SWAP)  88.8 us
    pallas_call x12, Pallas kernels, rows_products(): pl.pallas_call(kernel, grid=(columns // tile,), in_specs=lefts + rights +...  70.4 us
    unnamed x247, local copies, waits for them, and re-layouts  69 us
    pallas_call x9, Pallas kernels, token_products(): pl.pallas_call(kernel, grid=(height // tile,), in_specs=lefts + rights +...  58 us
    ppermute x4, waiting for transfers between devices, with_tp(): return (part, lax.ppermute(part, 'tp', SWAP))  53.8 us
    ppermute x5, waiting for transfers between devices, sum_over(): lax.ppermute(values, axis, partners).astype(F32)  45.8 us
    pallas_call x2, Pallas kernels, one(): call(functools.partial(forward_one, size=size, own=own), grid, conv_specs...  37.7 us
    pallas_call x2, Pallas kernels, four(): call(functools.partial(backward_two, size=size, own=own), grid, conv_spec...  32.6 us
  transfers between devices with their start and end apart: 70, of which 27 were waited for; matrix products, arithmetic and copies ran while one was open for 18% of the time, Pallas kernels for 28%

profile of v3, /device:TPU:0, one launch (start us, length us, event | category | flops | bytes accessed | tf_op | source)
XLA Modules:
  0.0 839.3 jit_solution(9228762392454859345)
XLA Ops:
  17.6 13.9 %all_gather.18 = bf16[4,80,128]{2,1,0:T(8,128)(2,1)S(1)} all-gather(bf16[1,80,128]{2,1,0:T(8,128)(2,1)S(1)} %pad_bitcast_fusion), channel_id=1, replica_groups=mesh['shard'=4,'cx'=2,'core'=2,'tp'=2] {'shard'}, dimensions={0}, use_global_device_ids=true | all-gather | bytes 102400 | tf_op jit(solution)/shard_map/all_gather | solution.py:755
  42.3 20.3 %collective-permute-done.4 = bf16[512,2048]{1,0:T(8,128)(2,1)} collective-permute-done((bf16[512,2048]{1,0:T(8,128)(2,1)}, bf16[512,2048]{1,0:T(8,128)(2,1)}, u32[]{:S(2)}, u32[]{:S(2)}) %collective-permute-start.4) | collective-permute-done | bytes 2097184 | tf_op jit(solution)/shard_map/ppermute | solution.py:733
  72.7 4.4 collective-permute-start.3
  91.3 6.8 convolution_convert_fusion.1.q0.k0.v0.q1.k1.v1.qh.kh.vh
  98.0 18.8 %shard_map.255 = (bf16[2,2,256,256]{3,2,1,0:T(8,128)(2,1)S(1)}, bf16[2,2,256,256]{3,2,1,0:T(8,128)(2,1)S(1)}, bf16[2,2,256,256]{3,2,1,0:T(8,128)(2,1)S(1)}, bf16...) custom-call(s32[2]{0:T(128)S(1)} %pad_add_fusion.1.where, ...), custom_call_target="tpu_custom_call" | custom-call | flops 1000 | bytes 1000 | tf_op jit(solution)/shard_map/pallas_call | solution.py:487
  121.7 34.1 %collective-permute-done.6.refs_4_ = bf16[2048,768]{1,0:T(8,128)(2,1)} collective-permute-done((bf16[2048,768]{1,0:T(8,128)(2,1)}, bf16[2048,768]{1,0:T(8,128)(2,1)}, u32[]{:S(2)}, u32[]{:S(2)}) %collective-permute-start.6) | collective-permute-done | bytes 3145760 | tf_op jit(solution)/shard_map/ppermute | solution.py:733
  158.2 6.7 convolution_convert_fusion.q0.k0.v0.q1.k1.v1.qh.kh.vh
  165.0 18.8 %shard_map.256 = (bf16[2,2,256,256]{3,2,1,0:T(8,128)(2,1)S(1)}, bf16[2,2,256,256]{3,2,1,0:T(8,128)(2,1)S(1)}, bf16[2,2,256,256]{3,2,1,0:T(8,128)(2,1)S(1)}, bf16...) custom-call(s32[2]{0:T(128)S(1)} %pad_add_fusion.1.where, ...), custom_call_target="tpu_custom_call" | custom-call | flops 1000 | bytes 1000 | tf_op jit(solution)/shard_map/pallas_call | solution.py:487
  193.7 6.1 shard_map.257
  205.2 6.1 shard_map.258
  214.9 5.9 collective-permute-done.10.refs_4_
  222.1 4.6 shard_map.260
  231.9 4.8 pad_maximum_fusion.2.grads_ref.refs_0_
  237.3 4.2 bitcast_convert_fusion
  241.4 33.4 %collective-permute-done.11 = bf16[512,2048]{1,0:T(8,128)(2,1)} collective-permute-done((bf16[512,2048]{1,0:T(8,128)(2,1)}, bf16[512,2048]{1,0:T(8,128)(2,1)}, u32[]{:S(2)}, u32[]{:S(2)}) %collective-permute-start.11) | collective-permute-done | bytes 2097184 | tf_op jit(solution)/shard_map/ppermute | solution.py:829
  274.8 4.4 multiply_reduce_fusion.6
  283.0 4.4 collective-permute-done.12
  287.4 4.2 pad_maximum_fusion.1.rows_ref.refs_0_
  291.6 9.6 %all-gather.14.cloned.1.call-done.downs_ref.refs_1_ = bf16[2048,704]{1,0:T(8,128)(2,1)} async-done(((bf16[512,704]{1,0:T(8,128)(2,1)}), bf16[2048,704]{1,0:T(8,128)(2,1)}) %all-gather.14.cloned.1.call-update) | async-done | bytes 2883600 | tf_op jit(solution)/shard_map/all_gather | solution.py:727
  301.2 15.4 %shard_map.261 = (bf16[1024,704]{1,0:T(8,128)(2,1)S(1)}, bf16[1024,704]{1,0:T(8,128)(2,1)S(1)}, bf16[1024,704]{1,0:T(8,128)(2,1)S(1)}) custom-call(bf16[1024,2048]{1,0:T(8,128)(2,1)} %pad_maximum_fusion.1.rows_ref.refs_0_, bf16[1024,2048]{1,0:T(8,128)(2,1)} %pad_maximum_fusion.2.grads_ref.refs_0_, ...), custom_call_target="tpu_custom_call" | custom-call | flops 1000 | bytes 1000 | tf_op jit(solution)/shard_map/pallas_call | solution.py:642
  316.6 7.1 shard_map.262
  325.0 4.2 shard_map.263
  340.1 15.4 %shard_map.264 = (bf16[1024,704]{1,0:T(8,128)(2,1)S(1)}, bf16[1024,704]{1,0:T(8,128)(2,1)S(1)}, bf16[1024,704]{1,0:T(8,128)(2,1)S(1)}) custom-call(bf16[1024,2048]{1,0:T(8,128)(2,1)} %copy-done.99, bf16[1024,2048]{1,0:T(8,128)(2,1)} %constant_dynamic-update-slice_fusion.grads_ref.refs_1_, bf16[2048,704]{1,0:T(8,128)(2,1)} %all-gather.12.cloned.1.call-done.gates_ref.refs_2_, ...), custom_call_target="tpu_custom_call" | custom-call | flops 1000 | bytes 1000 | tf_op jit(solution)/shard_map/pallas_call | solution.py:642
  355.6 7.1 shard_map.265
  362.9 4.0 collective-permute-done.18.refs_4_
  368.2 6.3 shard_map.266
  375.9 9.8 %shard_map.267 = bf16[2048,704]{1,0:T(8,128)(2,1)} custom-call(bf16[1024,2048]{1,0:T(8,128)(2,1)} %pad_maximum_fusion.2.grads_ref.refs_0_, bf16[1024,2048]{1,0:T(8,128)(2,1)} %constant_dynamic-update-slice_fusion.grads_ref.refs_1_, bf16[1024,704]{1,0:T(8,128)(2,1)S(1)} %get-tuple-element.354.refs_0_.refs_2_, ...), custom_call_target="tpu_custom_call" | custom-call | flops 1000 | bytes 1000 | tf_op jit(solution)/shard_map/pallas_call | solution.py:614
  393.3 7.3 shard_map.268
  400.7 5.3 shard_map.269
  406.2 9.9 %shard_map.270 = bf16[2048,704]{1,0:T(8,128)(2,1)} custom-call(bf16[1024,2048]{1,0:T(8,128)(2,1)} %pad_maximum_fusion.1.rows_ref.refs_0_, bf16[1024,2048]{1,0:T(8,128)(2,1)} %copy-done.99, bf16[1024,704]{1,0:T(8,128)(2,1)S(1)} %copy-done.21, bf16[1024,704]{1,0:T(8,128)(2,1)S(1)} %copy-done.16), custom_call_target="tpu_custom_call" | custom-call | flops 1000 | bytes 1000 | tf_op jit(solution)/shard_map/pallas_call | solution.py:614
  416.1 18.3 %collective-permute-done.20 = bf16[512,2048]{1,0:T(8,128)(2,1)} collective-permute-done((bf16[512,2048]{1,0:T(8,128)(2,1)}, bf16[512,2048]{1,0:T(8,128)(2,1)}, u32[]{:S(2)}, u32[]{:S(2)}) %collective-permute-start.20) | collective-permute-done | bytes 2097184 | tf_op jit(solution)/shard_map/ppermute | solution.py:733
  434.4 5.0 add_convert_fusion.2
  443.7 9.9 %shard_map.271 = bf16[2048,704]{1,0:T(8,128)(2,1)} custom-call(bf16[1024,2048]{1,0:T(8,128)(2,1)} %pad_maximum_fusion.1.rows_ref.refs_0_, bf16[1024,2048]{1,0:T(8,128)(2,1)} %copy-done.99, bf16[1024,704]{1,0:T(8,128)(2,1)S(1)} %copy-done.19, bf16[1024,704]{1,0:T(8,128)(2,1)S(1)} %copy-done.14), custom_call_target="tpu_custom_call" | custom-call | flops 1000 | bytes 1000 | tf_op jit(solution)/shard_map/pallas_call | solution.py:614
  455.0 5.6 shard_map.272
  460.6 5.7 shard_map.273
  466.3 20.4 %collective-permute-done.22 = bf16[512,2048]{1,0:T(8,128)(2,1)} collective-permute-done((bf16[512,2048]{1,0:T(8,128)(2,1)}, bf16[512,2048]{1,0:T(8,128)(2,1)}, u32[]{:S(2)}, u32[]{:S(2)}) %collective-permute-start.22) | collective-permute-done | bytes 2097184 | tf_op jit(solution)/shard_map/ppermute | solution.py:829
  487.1 4.3 multiply_reduce_fusion
  491.4 5.5 fusion.25
  509.1 7.1 shard_map.274
  517.6 7.1 shard_map.275
  531.5 14.1 %collective-permute-done.21 = bf16[512,2048]{1,0:T(8,128)(2,1)} collective-permute-done((bf16[512,2048]{1,0:T(8,128)(2,1)}, bf16[512,2048]{1,0:T(8,128)(2,1)}, u32[]{:S(2)}, u32[]{:S(2)}) %collective-permute-start.21) | collective-permute-done | bytes 2097184 | tf_op jit(solution)/shard_map/ppermute | solution.py:733
  545.7 4.9 add_convert_fusion.1
  551.2 16.4 %shard_map.277 = (bf16[2,2,256,768]{3,2,1,0:T(8,128)(2,1)}, bf16[2,16,768]{2,1,0:T(8,128)(2,1)S(1)}, f32[2,2,256,128]{3,2,1,0:T(8,128)S(1)}, f32[2,3,2,4,128]{4,3,2,1,0:T(4,128)S(1)}) custom-call(s32[2]{0:T(128)S(1)} %pad_add_fusion.1.where, bf16[1056,768]{1,0:T(8,128)(2,1)} %copy-done.3, bf16[1056,768]{1,0:T(8,128)(2,1)} %copy-done.3, ...), custom_call_target="tpu_custom_call" | custom-call | flops 60000002048 | bytes 1000 | tf_op jit(solution)/shard_map/pallas_call | solution.py:520
  569.0 6.2 shard_map.278
  576.2 5.1 shard_map.279
  582.6 16.3 %shard_map.280 = (bf16[2,2,256,768]{3,2,1,0:T(8,128)(2,1)}, bf16[2,16,768]{2,1,0:T(8,128)(2,1)S(1)}, f32[2,2,256,128]{3,2,1,0:T(8,128)S(1)}, f32[2,3,2,4,128]{4,3,2,1,0:T(4,128)S(1)}) custom-call(s32[2]{0:T(128)S(1)} %pad_add_fusion.1.where, bf16[1056,768]{1,0:T(8,128)(2,1)} %copy-done.2, bf16[1056,768]{1,0:T(8,128)(2,1)} %copy-done.2, ...), custom_call_target="tpu_custom_call" | custom-call | flops 60000002048 | bytes 1000 | tf_op jit(solution)/shard_map/pallas_call | solution.py:520
  599.6 4.0 shard_map.281
  604.9 5.0 slice.120
  612.8 5.4 shard_map.282
  624.0 8.4 shard_map.283
  644.7 6.7 shard_map.284
  655.9 42.8 %collective-permute-done.43 = bf16[128]{0:T(256)(128)(2,1)S(1)} collective-permute-done((bf16[128]{0:T(256)(128)(2,1)S(1)}, bf16[128]{0:T(256)(128)(2,1)S(1)}, u32[]{:S(2)}, u32[]{:S(2)}) %collective-permute-start.43) | collective-permute-done | bytes 288 | tf_op jit(solution)/shard_map/ppermute | solution.py:695
  702.0 15.6 %collective-permute-done.33 = bf16[512,704]{0,1:T(8,128)(2,1)} collective-permute-done((bf16[512,704]{0,1:T(8,128)(2,1)}, bf16[512,704]{0,1:T(8,128)(2,1)}, u32[]{:S(2)}, u32[]{:S(2)}) %collective-permute-start.33) | collective-permute-done | bytes 720928 | tf_op jit(solution)/shard_map/ppermute | solution.py:101
  719.5 5.4 shard_map.285
  735.4 3.7 shard_map.286
  751.8 3.3 shard_map.287
  765.4 3.5 shard_map.288
  772.8 3.2 multiply_reduce_fusion.1
  784.5 6.9 fusion.5
  792.9 4.8 add_convert_fusion
  797.7 3.8 shard_map.290
  801.5 10.7 %reduce-scatter.15.cloned.1.call-done.refs_4_ = bf16[512,384]{1,0:T(8,128)(2,1)} async-done(((bf16[2048,384]{1,0:T(8,128)(2,1)}), bf16[512,384]{1,0:T(8,128)(2,1)}) %reduce-scatter.15.cloned.1.call-update) | async-done | bytes 393232 | tf_op jit(solution)/shard_map/reduce_scatter | solution.py:730
  815.6 7.5 collective-permute-done.51.refs_5_
  827.8 4.7 shard_map.289
  (496 shorter events, 222.6 us)
Async XLA Ops:
  7.2 77.6 %all-gather.6.cloned.1.call-start = ((), (), s32[]{:S(2)}) async-start(), calls=%async_computation.6 | async-start | bytes 3932160 | tf_op jit(solution)/shard_map/all_gather | solution.py:727
  12.9 142.8 %all-gather.8.cloned.1.call-start = ((), (), s32[]{:S(2)}) async-start(), calls=%async_computation.7 | async-start | bytes 1310720 | tf_op jit(solution)/shard_map/all_gather | solution.py:727
  13.0 24.5 %collective-permute-start = (bf16[512,2048]{1,0:T(8,128)(2,1)S(1)}, bf16[512,2048]{1,0:T(8,128)(2,1)}, u32[]{:S(2)}, u32[]{:S(2)}) collective-permute-start(bf16[512,2048]{1,0:T(8,128)(2,1)S(1)} %bitcast.102), channel_id=1, source_target_pairs={{0,2},{2,0},{1,3},{3,1},{4,6},{6,4},{5,7},{7,5},{8,10},{10,8},{9,1... | collective-permute-start | bytes 6291464 | tf_op jit(solution)/shard_map/ppermute | solution.py:736
  13.5 49.1 %collective-permute-start.4 = (bf16[512,2048]{1,0:T(8,128)(2,1)}, bf16[512,2048]{1,0:T(8,128)(2,1)}, u32[]{:S(2)}, u32[]{:S(2)}) collective-permute-start(bf16[512,2048]{1,0:T(8,128)(2,1)} %bitcast.9), channel_id=1, source_target_pairs={{0,4},{4,0},{1,5},{5,1},{2,6},{6,2},{3,7},{7,3},{8,12},{12,8},{9,1... | collective-permute-start | bytes 6291464 | tf_op jit(solution)/shard_map/ppermute | solution.py:733
  17.0 224.5 %all-gather.10.cloned.1.call-start = ((), (), s32[]{:S(2)}) async-start(), calls=%async_computation.8 | async-start | bytes 3932160 | tf_op jit(solution)/shard_map/all_gather | solution.py:727
  39.3 25.3 %collective-permute-start.1 = (bf16[2,16,2048]{2,1,0:T(8,128)(2,1)S(1)}, bf16[2,16,2048]{2,1,0:T(8,128)(2,1)S(1)}, u32[]{:S(2)}, u32[]{:S(2)}) collective-permute-start(bf16[2,16,2048]{2,1,0:T(8,128)(2,1)S(1)} %slice.109), channel_id=1, source_target_pairs={{0,4},{1,5},{2,6},{3,7},{8,12},{9,13},{10,14},{11,15},{16,20},{17,... | collective-permute-start | bytes 393224 | tf_op jit(solution)/shard_map/ppermute | solution.py:777
  62.6 19.0 %collective-permute-start.5 = (bf16[512,2048]{1,0:T(8,128)(2,1)}, bf16[512,2048]{1,0:T(8,128)(2,1)}, u32[]{:S(2)}, u32[]{:S(2)}) collective-permute-start(bf16[512,2048]{1,0:T(8,128)(2,1)} %collective-permute-done.4), channel_id=1, source_target_pairs={{0,2},{2,0},{1,3},{3,1},{4,6},{6,4},{5,7},{7,5},{8,10},{10,8},{9,1... | collective-permute-start | bytes 6291464 | tf_op jit(solution)/shard_map/ppermute | solution.py:736
  71.4 220.2 %all-gather.12.cloned.1.call-start = ((), (), s32[]{:S(2)}) async-start(), calls=%async_computation.9 | async-start | bytes 3932160 | tf_op jit(solution)/shard_map/all_gather | solution.py:727
  72.7 5.7 collective-permute-start.3
  84.8 70.9 %collective-permute-start.6 = (bf16[2048,768]{1,0:T(8,128)(2,1)}, bf16[2048,768]{1,0:T(8,128)(2,1)}, u32[]{:S(2)}, u32[]{:S(2)}) collective-permute-start(bf16[2048,768]{1,0:T(8,128)(2,1)} %all-gather.6.cloned.1.call-done.refs_3_), channel_id=1, source_target_pairs={{0,4},{4,0},{1,5},{5,1},{2,6},{6,2},{3,7},{7,3},{8,12},{12,8},{9,1... | collective-permute-start | bytes 9437192 | tf_op jit(solution)/shard_map/ppermute | solution.py:733
  91.0 210.2 %all-gather.14.cloned.1.call-start = ((), (), s32[]{:S(2)}) async-start(), calls=%async_computation.10 | async-start | bytes 3932160 | tf_op jit(solution)/shard_map/all_gather | solution.py:727
  119.5 69.9 %collective-permute-start.8 = (bf16[2,2,128,128]{3,2,1,0:T(8,128)(2,1)S(1)}, bf16[2,2,128,128]{3,2,1,0:T(8,128)(2,1)S(1)}, u32[]{:S(2)}, u32[]{:S(2)}) collective-permute-start(bf16[2,2,128,128]{3,2,1,0:T(8,128)(2,1)S(1)} %get-tuple-element.254), channel_id=1, source_target_pairs={{0,4},{1,5},{2,6},{3,7},{8,12},{9,13},{10,14},{11,15},{16,20},{17,... | collective-permute-start | bytes 393224 | tf_op jit(solution)/shard_map/ppermute | solution.py:808
  155.7 56.6 %collective-permute-start.9 = (bf16[2048,256]{1,0:T(8,128)(2,1)}, bf16[2048,256]{1,0:T(8,128)(2,1)S(1)}, u32[]{:S(2)}, u32[]{:S(2)}) collective-permute-start(bf16[2048,256]{1,0:T(8,128)(2,1)} %all-gather.8.cloned.1.call-done.refs_2_), channel_id=1, source_target_pairs={{0,4},{4,0},{1,5},{5,1},{2,6},{6,2},{3,7},{7,3},{8,12},{12,8},{9,1... | collective-permute-start | bytes 3145736 | tf_op jit(solution)/shard_map/ppermute | solution.py:733
  187.3 14.3 %collective-permute-start.7 = (bf16[2,2,128,128]{3,2,1,0:T(8,128)(2,1)S(1)}, bf16[2,2,128,128]{3,2,1,0:T(8,128)(2,1)S(1)}, u32[]{:S(2)}, u32[]{:S(2)}) collective-permute-start(bf16[2,2,128,128]{3,2,1,0:T(8,128)(2,1)S(1)} %get-tuple-element.258), channel_id=1, source_target_pairs={{0,4},{1,5},{2,6},{3,7},{8,12},{9,13},{10,14},{11,15},{16,20},{17,... | collective-permute-start | bytes 393224 | tf_op jit(solution)/shard_map/ppermute | solution.py:809
  214.4 6.4 collective-permute-start.10
  214.4 17.5 %collective-permute-start.13 = (bf16[512,2048]{1,0:T(8,128)(2,1)}, bf16[512,2048]{1,0:T(8,128)(2,1)}, u32[]{:S(2)}, u32[]{:S(2)}) collective-permute-start(bf16[512,2048]{1,0:T(8,128)(2,1)} %bitcast.9), channel_id=1, source_target_pairs={{0,2},{2,0},{1,3},{3,1},{4,6},{6,4},{5,7},{7,5},{8,10},{10,8},{9,1... | collective-permute-start | bytes 6291464 | tf_op jit(solution)/shard_map/ppermute | solution.py:736
  226.8 48.1 %collective-permute-start.11 = (bf16[512,2048]{1,0:T(8,128)(2,1)}, bf16[512,2048]{1,0:T(8,128)(2,1)}, u32[]{:S(2)}, u32[]{:S(2)}) collective-permute-start(bf16[512,2048]{1,0:T(8,128)(2,1)} %shard_map.260), channel_id=1, source_target_pairs={{0,1},{1,0},{2,3},{3,2},{4,5},{5,4},{6,7},{7,6},{8,9},{9,8},{10,11... | collective-permute-start | bytes 6291464 | tf_op jit(solution)/shard_map/ppermute | solution.py:829
  236.7 398.5 %reduce-scatter.11.cloned.1.call-start = ((), (), s32[]{:S(2)}) async-start(), calls=%async_computation.13 | async-start | bytes 3932160 | tf_op jit(solution)/shard_map/reduce_scatter | solution.py:730
  283.0 4.4 collective-permute-start.12
  283.0 48.4 %collective-permute-start.15 = (bf16[512,2048]{1,0:T(8,128)(2,1)}, bf16[512,2048]{1,0:T(8,128)(2,1)}, u32[]{:S(2)}, u32[]{:S(2)}) collective-permute-start(bf16[512,2048]{1,0:T(8,128)(2,1)} %multiply_convert_fusion), channel_id=1, source_target_pairs={{0,4},{4,0},{1,5},{5,1},{2,6},{6,2},{3,7},{7,3},{8,12},{12,8},{9,1... | collective-permute-start | bytes 6291464 | tf_op jit(solution)/shard_map/ppermute | solution.py:733
  329.3 4.2 collective-permute-start.14
  333.5 4.4 collective-permute-start.16
  385.7 251.8 %reduce-scatter.9.cloned.1.call-start = ((), (), s32[]{:S(2)}) async-start(), calls=%async_computation.12 | async-start | bytes 3932160 | tf_op jit(solution)/shard_map/reduce_scatter | solution.py:730
  385.9 4.4 collective-permute-start.17
  386.1 48.2 %collective-permute-start.20 = (bf16[512,2048]{1,0:T(8,128)(2,1)}, bf16[512,2048]{1,0:T(8,128)(2,1)}, u32[]{:S(2)}, u32[]{:S(2)}) collective-permute-start(bf16[512,2048]{1,0:T(8,128)(2,1)} %copy-done.49), channel_id=1, source_target_pairs={{0,4},{4,0},{1,5},{5,1},{2,6},{6,2},{3,7},{7,3},{8,12},{12,8},{9,1... | collective-permute-start | bytes 6291464 | tf_op jit(solution)/shard_map/ppermute | solution.py:733
  406.0 47.6 %collective-permute-start.19 = (bf16[512,2048]{1,0:T(8,128)(2,1)}, bf16[512,2048]{1,0:T(8,128)(2,1)}, u32[]{:S(2)}, u32[]{:S(2)}) collective-permute-start(bf16[512,2048]{1,0:T(8,128)(2,1)} %shard_map.269), channel_id=1, source_target_pairs={{0,2},{2,0},{1,3},{3,1},{4,6},{6,4},{5,7},{7,5},{8,10},{10,8},{9,1... | collective-permute-start | bytes 6291464 | tf_op jit(solution)/shard_map/ppermute | solution.py:736
  439.3 47.4 %collective-permute-start.22 = (bf16[512,2048]{1,0:T(8,128)(2,1)}, bf16[512,2048]{1,0:T(8,128)(2,1)}, u32[]{:S(2)}, u32[]{:S(2)}) collective-permute-start(bf16[512,2048]{1,0:T(8,128)(2,1)} %add_convert_fusion.2), channel_id=1, source_target_pairs={{0,1},{1,0},{2,3},{3,2},{4,5},{5,4},{6,7},{7,6},{8,9},{9,8},{10,11... | collective-permute-start | bytes 6291464 | tf_op jit(solution)/shard_map/ppermute | solution.py:829
  440.8 212.8 %reduce-scatter.7.cloned.1.call-start = ((), (), s32[]{:S(2)}) async-start(), calls=%async_computation.11 | async-start | bytes 3932160 | tf_op jit(solution)/shard_map/reduce_scatter | solution.py:730
  496.9 4.5 collective-permute-start.23
  496.9 48.7 %collective-permute-start.21 = (bf16[512,2048]{1,0:T(8,128)(2,1)}, bf16[512,2048]{1,0:T(8,128)(2,1)}, u32[]{:S(2)}, u32[]{:S(2)}) collective-permute-start(bf16[512,2048]{1,0:T(8,128)(2,1)} %shard_map.272), channel_id=1, source_target_pairs={{0,4},{4,0},{1,5},{5,1},{2,6},{6,2},{3,7},{7,3},{8,12},{12,8},{9,1... | collective-permute-start | bytes 6291464 | tf_op jit(solution)/shard_map/ppermute | solution.py:733
  498.4 242.1 %reduce-scatter.17.cloned.1.call-start = ((), (), s32[]{:S(2)}) async-start(), calls=%async_computation.16 | async-start | bytes 1310720 | tf_op jit(solution)/shard_map/reduce_scatter | solution.py:730
  516.2 34.9 %collective-permute-start.26 = (bf16[2,2,128,128]{3,2,1,0:T(8,128)(2,1)S(1)}, bf16[2,2,128,128]{3,2,1,0:T(8,128)(2,1)S(1)}, u32[]{:S(2)}, u32[]{:S(2)}) collective-permute-start(bf16[2,2,128,128]{3,2,1,0:T(8,128)(2,1)S(1)} %get-tuple-element.373), channel_id=1, source_target_pairs={{4,0},{5,1},{6,2},{7,3},{12,8},{13,9},{14,10},{15,11},{20,16},{21,... | collective-permute-start | bytes 393224 | tf_op jit(solution)/shard_map/ppermute | solution.py:890
  524.7 26.4 %collective-permute-start.25 = (bf16[2,2,128,128]{3,2,1,0:T(8,128)(2,1)S(1)}, bf16[2,2,128,128]{3,2,1,0:T(8,128)(2,1)S(1)}, u32[]{:S(2)}, u32[]{:S(2)}) collective-permute-start(bf16[2,2,128,128]{3,2,1,0:T(8,128)(2,1)S(1)} %get-tuple-element.381), channel_id=1, source_target_pairs={{4,0},{5,1},{6,2},{7,3},{12,8},{13,9},{14,10},{15,11},{20,16},{21,... | collective-permute-start | bytes 393224 | tf_op jit(solution)/shard_map/ppermute | solution.py:892
  528.8 53.7 %collective-permute-start.27 = (bf16[2048,256]{1,0:T(8,128)(2,1)S(1)}, bf16[2048,256]{1,0:T(8,128)(2,1)S(1)}, u32[]{:S(2)}, u32[]{:S(2)}) collective-permute-start(bf16[2048,256]{1,0:T(8,128)(2,1)S(1)} %shard_map.276), channel_id=1, source_target_pairs={{0,4},{4,0},{1,5},{5,1},{2,6},{6,2},{3,7},{7,3},{8,12},{12,8},{9,1... | collective-permute-start | bytes 3145736 | tf_op jit(solution)/shard_map/ppermute | solution.py:733
  575.3 37.4 %collective-permute-start.29 = (bf16[2048,384]{1,0:T(8,128)(2,1)}, bf16[2048,384]{1,0:T(8,128)(2,1)}, u32[]{:S(2)}, u32[]{:S(2)}) collective-permute-start(bf16[2048,384]{1,0:T(8,128)(2,1)} %shard_map.278), channel_id=1, source_target_pairs={{0,4},{4,0},{1,5},{5,1},{2,6},{6,2},{3,7},{7,3},{8,12},{12,8},{9,1... | collective-permute-start | bytes 4718600 | tf_op jit(solution)/shard_map/ppermute | solution.py:733
  604.7 164.3 %reduce-scatter.13.cloned.1.call-start = ((), (), s32[]{:S(2)}) async-start(), calls=%async_computation.14 | async-start | bytes 1966080 | tf_op jit(solution)/shard_map/reduce_scatter | solution.py:730
  609.9 13.8 %collective-permute-start.28 = (bf16[2,16,768]{2,1,0:T(8,128)(2,1)S(1)}, bf16[2,16,768]{2,1,0:T(8,128)(2,1)S(1)}, u32[]{:S(2)}, u32[]{:S(2)}) collective-permute-start(bf16[2,16,768]{2,1,0:T(8,128)(2,1)S(1)} %get-tuple-element.404), channel_id=1, source_target_pairs={{4,0},{5,1},{6,2},{7,3},{12,8},{13,9},{14,10},{15,11},{20,16},{21,... | collective-permute-start | bytes 147464 | tf_op jit(solution)/shard_map/ppermute | solution.py:906
  611.2 12.7 %collective-permute-start.30 = (bf16[2,16,768]{2,1,0:T(8,128)(2,1)S(1)}, bf16[2,16,768]{2,1,0:T(8,128)(2,1)S(1)}, u32[]{:S(2)}, u32[]{:S(2)}) collective-permute-start(bf16[2,16,768]{2,1,0:T(8,128)(2,1)S(1)} %get-tuple-element.450), channel_id=1, source_target_pairs={{4,0},{5,1},{6,2},{7,3},{12,8},{13,9},{14,10},{15,11},{20,16},{21,... | collective-permute-start | bytes 147464 | tf_op jit(solution)/shard_map/ppermute | solution.py:932
  632.3 9.6 %collective-permute-start.31 = (bf16[512,2048]{1,0:T(8,128)(2,1)}, bf16[512,2048]{1,0:T(8,128)(2,1)}, u32[]{:S(2)}, u32[]{:S(2)}) collective-permute-start(bf16[512,2048]{1,0:T(8,128)(2,1)} %shard_map.283), channel_id=1, source_target_pairs={{0,2},{2,0},{1,3},{3,1},{4,6},{6,4},{5,7},{7,5},{8,10},{10,8},{9,1... | collective-permute-start | bytes 6291464 | tf_op jit(solution)/shard_map/ppermute | solution.py:736
  632.4 179.8 %reduce-scatter.15.cloned.1.call-start = ((), (), s32[]{:S(2)}) async-start(), calls=%async_computation.15 | async-start | bytes 1966080 | tf_op jit(solution)/shard_map/reduce_scatter | solution.py:730
  632.5 85.1 %collective-permute-start.42 = (bf16[2048,384]{1,0:T(8,128)(2,1)}, bf16[2048,384]{1,0:T(8,128)(2,1)}, u32[]{:S(2)}, u32[]{:S(2)}) collective-permute-start(bf16[2048,384]{1,0:T(8,128)(2,1)} %copy-done.50), channel_id=1, source_target_pairs={{0,4},{4,0},{1,5},{5,1},{2,6},{6,2},{3,7},{7,3},{8,12},{12,8},{9,1... | collective-permute-start | bytes 4718600 | tf_op jit(solution)/shard_map/ppermute | solution.py:733
  637.5 61.3 %collective-permute-start.39 = (bf16[512,704]{0,1:T(8,128)(2,1)}, bf16[512,704]{0,1:T(8,128)(2,1)}, u32[]{:S(2)}, u32[]{:S(2)}) collective-permute-start(bf16[512,704]{0,1:T(8,128)(2,1)} %copy.120), channel_id=1, source_target_pairs={{0,4},{4,0},{1,5},{5,1},{2,6},{6,2},{3,7},{7,3},{8,12},{12,8},{9,1... | collective-permute-start | bytes 2162696 | tf_op jit(solution)/shard_map/ppermute | solution.py:101
  639.9 61.6 %collective-permute-start.36 = (bf16[512,704]{0,1:T(8,128)(2,1)}, bf16[512,704]{0,1:T(8,128)(2,1)}, u32[]{:S(2)}, u32[]{:S(2)}) collective-permute-start(bf16[512,704]{0,1:T(8,128)(2,1)} %copy.118), channel_id=1, source_target_pairs={{0,4},{4,0},{1,5},{5,1},{2,6},{6,2},{3,7},{7,3},{8,12},{12,8},{9,1... | collective-permute-start | bytes 2162696 | tf_op jit(solution)/shard_map/ppermute | solution.py:101
  651.4 118.6 %collective-permute-start.32 = (bf16[512,2048]{1,0:T(8,128)(2,1)S(1)}, bf16[512,2048]{1,0:T(8,128)(2,1)}, u32[]{:S(2)}, u32[]{:S(2)}) collective-permute-start(bf16[512,2048]{1,0:T(8,128)(2,1)S(1)} %shard_map.284), channel_id=1, source_target_pairs={{0,1},{1,0},{2,3},{3,2},{4,5},{5,4},{6,7},{7,6},{8,9},{9,8},{10,11... | collective-permute-start | bytes 6291464 | tf_op jit(solution)/shard_map/ppermute | solution.py:829
  653.0 45.7 %collective-permute-start.43 = (bf16[128]{0:T(256)(128)(2,1)S(1)}, bf16[128]{0:T(256)(128)(2,1)S(1)}, u32[]{:S(2)}, u32[]{:S(2)}) collective-permute-start(bf16[128]{0:T(256)(128)(2,1)S(1)} %add_convert_fusion.8), channel_id=1, source_target_pairs={{0,1},{1,0},{2,3},{3,2},{4,5},{5,4},{6,7},{7,6},{8,9},{9,8},{10,11... | collective-permute-start | bytes 776 | tf_op jit(solution)/shard_map/ppermute | solution.py:695
  698.8 18.9 %collective-permute-start.33 = (bf16[512,704]{0,1:T(8,128)(2,1)}, bf16[512,704]{0,1:T(8,128)(2,1)}, u32[]{:S(2)}, u32[]{:S(2)}) collective-permute-start(bf16[512,704]{0,1:T(8,128)(2,1)} %copy.116), channel_id=1, source_target_pairs={{0,4},{4,0},{1,5},{5,1},{2,6},{6,2},{3,7},{7,3},{8,12},{12,8},{9,1... | collective-permute-start | bytes 2162696 | tf_op jit(solution)/shard_map/ppermute | solution.py:101
  701.5 16.7 %collective-permute-start.41 = (bf16[512,704]{0,1:T(8,128)(2,1)}, bf16[512,704]{0,1:T(8,128)(2,1)}, u32[]{:S(2)}, u32[]{:S(2)}) collective-permute-start(bf16[512,704]{0,1:T(8,128)(2,1)} %collective-permute-done.39), channel_id=1, source_target_pairs={{0,2},{2,0},{1,3},{3,1},{4,6},{6,4},{5,7},{7,5},{8,10},{10,8},{9,1... | collective-permute-start | bytes 2162696 | tf_op jit(solution)/shard_map/ppermute | solution.py:103
  701.5 37.6 %collective-permute-start.37 = (bf16[512,704]{0,1:T(8,128)(2,1)}, bf16[512,704]{0,1:T(8,128)(2,1)}, u32[]{:S(2)}, u32[]{:S(2)}) collective-permute-start(bf16[512,704]{0,1:T(8,128)(2,1)} %copy.118), channel_id=1, source_target_pairs={{0,2},{2,0},{1,3},{3,1},{4,6},{6,4},{5,7},{7,5},{8,10},{10,8},{9,1... | collective-permute-start | bytes 2162696 | tf_op jit(solution)/shard_map/ppermute | solution.py:103
  717.6 22.9 %collective-permute-start.38 = (bf16[512,704]{0,1:T(8,128)(2,1)}, bf16[512,704]{0,1:T(8,128)(2,1)}, u32[]{:S(2)}, u32[]{:S(2)}) collective-permute-start(bf16[512,704]{0,1:T(8,128)(2,1)} %collective-permute-done.36), channel_id=1, source_target_pairs={{0,2},{2,0},{1,3},{3,1},{4,6},{6,4},{5,7},{7,5},{8,10},{10,8},{9,1... | collective-permute-start | bytes 2162696 | tf_op jit(solution)/shard_map/ppermute | solution.py:103
  717.6 37.5 %collective-permute-start.34 = (bf16[512,704]{0,1:T(8,128)(2,1)}, bf16[512,704]{0,1:T(8,128)(2,1)}, u32[]{:S(2)}, u32[]{:S(2)}) collective-permute-start(bf16[512,704]{0,1:T(8,128)(2,1)} %copy.116), channel_id=1, source_target_pairs={{0,2},{2,0},{1,3},{3,1},{4,6},{6,4},{5,7},{7,5},{8,10},{10,8},{9,1... | collective-permute-start | bytes 2162696 | tf_op jit(solution)/shard_map/ppermute | solution.py:103
  718.1 37.0 %collective-permute-start.35 = (bf16[512,704]{0,1:T(8,128)(2,1)}, bf16[512,704]{0,1:T(8,128)(2,1)}, u32[]{:S(2)}, u32[]{:S(2)}) collective-permute-start(bf16[512,704]{0,1:T(8,128)(2,1)} %collective-permute-done.33), channel_id=1, source_target_pairs={{0,2},{2,0},{1,3},{3,1},{4,6},{6,4},{5,7},{7,5},{8,10},{10,8},{9,1... | collective-permute-start | bytes 2162696 | tf_op jit(solution)/shard_map/ppermute | solution.py:103
  739.1 52.3 %collective-permute-start.24 = (bf16[512,2048]{1,0:T(8,128)(2,1)}, bf16[512,2048]{1,0:T(8,128)(2,1)}, u32[]{:S(2)}, u32[]{:S(2)}) collective-permute-start(bf16[512,2048]{1,0:T(8,128)(2,1)} %add_convert_fusion.1), channel_id=1, source_target_pairs={{0,1},{1,0},{2,3},{3,2},{4,5},{5,4},{6,7},{7,6},{8,9},{9,8},{10,11... | collective-permute-start | bytes 6291464 | tf_op jit(solution)/shard_map/ppermute | solution.py:829
  740.6 37.3 %collective-permute-start.56 = (bf16[512,256]{1,0:T(8,128)(2,1)}, bf16[512,256]{1,0:T(8,128)(2,1)}, u32[]{:S(2)}, u32[]{:S(2)}) collective-permute-start(bf16[512,256]{1,0:T(8,128)(2,1)} %reduce-scatter.17.cloned.1.call-done.a), channel_id=1, source_target_pairs={{0,4},{4,0},{1,5},{5,1},{2,6},{6,2},{3,7},{7,3},{8,12},{12,8},{9,1... | collective-permute-start | bytes 786440 | tf_op jit(solution)/shard_map/ppermute | solution.py:101
  769.0 11.3 %collective-permute-start.48 = (bf16[512,384]{1,0:T(8,128)(2,1)}, bf16[512,384]{1,0:T(8,128)(2,1)}, u32[]{:S(2)}, u32[]{:S(2)}) collective-permute-start(bf16[512,384]{1,0:T(8,128)(2,1)} %reduce-scatter.13.cloned.1.call-done.refs_0_), channel_id=1, source_target_pairs={{0,4},{4,0},{1,5},{5,1},{2,6},{6,2},{3,7},{7,3},{8,12},{12,8},{9,1... | collective-permute-start | bytes 1179656 | tf_op jit(solution)/shard_map/ppermute | solution.py:101
  776.1 4.2 collective-permute-start.44
  777.3 20.4 %collective-permute-start.57 = (bf16[512,256]{1,0:T(8,128)(2,1)}, bf16[512,256]{1,0:T(8,128)(2,1)}, u32[]{:S(2)}, u32[]{:S(2)}) collective-permute-start(bf16[512,256]{1,0:T(8,128)(2,1)} %reduce-scatter.17.cloned.1.call-done.a), channel_id=1, source_target_pairs={{0,2},{2,0},{1,3},{3,1},{4,6},{6,4},{5,7},{7,5},{8,10},{10,8},{9,1... | collective-permute-start | bytes 786440 | tf_op jit(solution)/shard_map/ppermute | solution.py:103
  777.9 19.8 %collective-permute-start.58 = (bf16[512,256]{1,0:T(8,128)(2,1)}, bf16[512,256]{1,0:T(8,128)(2,1)}, u32[]{:S(2)}, u32[]{:S(2)}) collective-permute-start(bf16[512,256]{1,0:T(8,128)(2,1)} %collective-permute-done.56.b), channel_id=1, source_target_pairs={{0,2},{2,0},{1,3},{3,1},{4,6},{6,4},{5,7},{7,5},{8,10},{10,8},{9,1... | collective-permute-start | bytes 786440 | tf_op jit(solution)/shard_map/ppermute | solution.py:103
  780.3 46.4 %collective-permute-start.49 = (bf16[512,384]{1,0:T(8,128)(2,1)S(1)}, bf16[512,384]{1,0:T(8,128)(2,1)}, u32[]{:S(2)}, u32[]{:S(2)}) collective-permute-start(bf16[512,384]{1,0:T(8,128)(2,1)S(1)} %copy-done.80), channel_id=1, source_target_pairs={{0,2},{2,0},{1,3},{3,1},{4,6},{6,4},{5,7},{7,5},{8,10},{10,8},{9,1... | collective-permute-start | bytes 1179656 | tf_op jit(solution)/shard_map/ppermute | solution.py:103
  784.4 7.0 collective-permute-start.46
  791.4 35.4 %collective-permute-start.50 = (bf16[512,384]{1,0:T(8,128)(2,1)}, bf16[512,384]{1,0:T(8,128)(2,1)S(1)}, u32[]{:S(2)}, u32[]{:S(2)}) collective-permute-start(bf16[512,384]{1,0:T(8,128)(2,1)} %collective-permute-done.48.refs_1_), channel_id=1, source_target_pairs={{0,2},{2,0},{1,3},{3,1},{4,6},{6,4},{5,7},{7,5},{8,10},{10,8},{9,1... | collective-permute-start | bytes 1179656 | tf_op jit(solution)/shard_map/ppermute | solution.py:103
  791.4 10.1 %collective-permute-start.47 = (bf16[18560]{0:T(1024)(128)(2,1)S(1)}, bf16[18560]{0:T(1024)(128)(2,1)S(1)}, u32[]{:S(2)}, u32[]{:S(2)}) collective-permute-start(bf16[18560]{0:T(1024)(128)(2,1)S(1)} %add_convert_fusion.4), channel_id=1, source_target_pairs={{0,16},{8,24},{16,0},{24,8},{1,17},{9,25},{17,1},{25,9},{2,18},{10... | collective-permute-start | bytes 111368 | tf_op jit(solution)/shard_map/ppermute | solution.py:695
  812.2 10.9 %collective-permute-start.51 = (bf16[512,384]{1,0:T(8,128)(2,1)}, bf16[512,384]{1,0:T(8,128)(2,1)S(1)}, u32[]{:S(2)}, u32[]{:S(2)}) collective-permute-start(bf16[512,384]{1,0:T(8,128)(2,1)} %reduce-scatter.15.cloned.1.call-done.refs_4_), channel_id=1, source_target_pairs={{0,4},{4,0},{1,5},{5,1},{2,6},{6,2},{3,7},{7,3},{8,12},{12,8},{9,1... | collective-permute-start | bytes 1179656 | tf_op jit(solution)/shard_map/ppermute | solution.py:101
  814.9 9.5 %collective-permute-start.54 = (bf16[4,3,4,32]{3,2,1,0:T(4,128)(2,1)S(1)}, bf16[4,3,4,32]{3,2,1,0:T(4,128)(2,1)S(1)}, u32[]{:S(2)}, u32[]{:S(2)}) collective-permute-start(bf16[4,3,4,32]{3,2,1,0:T(4,128)(2,1)S(1)} %constant_dynamic-slice_fusion.1), channel_id=1, source_target_pairs={{0,2},{2,0},{1,3},{3,1},{4,6},{6,4},{5,7},{7,5},{8,10},{10,8},{9,1... | collective-permute-start | bytes 9224 | tf_op jit(solution)/shard_map/ppermute | solution.py:736
  815.0 11.7 %collective-permute-start.52 = (bf16[512,384]{1,0:T(8,128)(2,1)}, bf16[512,384]{1,0:T(8,128)(2,1)S(1)}, u32[]{:S(2)}, u32[]{:S(2)}) collective-permute-start(bf16[512,384]{1,0:T(8,128)(2,1)} %reduce-scatter.15.cloned.1.call-done.refs_4_), channel_id=1, source_target_pairs={{0,2},{2,0},{1,3},{3,1},{4,6},{6,4},{5,7},{7,5},{8,10},{10,8},{9,1... | collective-permute-start | bytes 1179656 | tf_op jit(solution)/shard_map/ppermute | solution.py:103
  (123 other events, 939.5 us)
Sparse Core Ops, SparseCore 0:
  13.1 66.6 all-gather.5
  81.9 26.2 all-gather.7
  110.4 62.9 all-gather.9
  175.4 62.1 all-gather.11
  239.0 62.1 all-gather.13
  385.8 58.8 reduce-scatter.10
  447.1 60.2 reduce-scatter.8
  509.7 60.2 reduce-scatter.6
  604.8 25.5 reduce-scatter.16
  633.3 34.4 reduce-scatter.12
  778.1 34.0 reduce-scatter.14

commit v4 on v3

--- a/solution.py
+++ b/solution.py
@@ -136,8 +136,8 @@
     )(places, *heads[0], *heads[1])
 
 
-def lay_units(places, pieces):
-    rows, units = pieces[0].shape
+def lay_units(places, pieces, turn, flops=1000):
+    units, rows = pieces[0].shape
     wide, main, rest = own_parts(4 * units)
     half = rest // 2
 
@@ -145,43 +145,25 @@
         for side in range(2):
 
             def store(values):
-                out[:, side * main : (side + 1) * main] = values[:, :main]
                 at = 2 * main + side * half
-                out[:, at : at + half] = values[:, main:]
+                if turn:
+                    values = values.T
+                    out[:, side * main : (side + 1) * main] = values[:, :main]
+                    out[:, at : at + half] = values[:, main:]
+                else:
+                    out[side * main : (side + 1) * main, :] = values[:main]
+                    out[at : at + half, :] = values[main:]
 
             pick(where, pl.program_id(0), side, (a, b, c, d), store)
 
+    shape = (rows, wide) if turn else (wide, rows)
     return call(
         kernel,
         (2,),
-        [pl.BlockSpec((rows, units), lambda i, w: (0, 0))] * 4,
-        pl.BlockSpec((rows, wide), lambda i, w: (0, i)),
-        jax.ShapeDtypeStruct((rows, 2 * wide), F32),
-    )(places, *pieces)
-
-
-def lay_units_turned(places, pieces):
-    rows, units = pieces[0].shape
-    wide, main, rest = own_parts(4 * units)
-    half = rest // 2
-
-    def kernel(where, a, b, c, d, out):
-        for side in range(2):
-
-            def store(values):
-                turned = values.T
-                out[side * main : (side + 1) * main, :] = turned[:main]
-                at = 2 * main + side * half
-                out[at : at + half, :] = turned[main:]
-
-            pick(where, pl.program_id(0), side, (a, b, c, d), store)
-
-    return call(
-        kernel,
-        (2,),
-        [pl.BlockSpec((rows, units), lambda i, w: (0, 0))] * 4,
-        pl.BlockSpec((wide, rows), lambda i, w: (i, 0)),
-        jax.ShapeDtypeStruct((2 * wide, rows), F32),
+        [pl.BlockSpec((units, rows), lambda i, w: (0, 0))] * 4,
+        pl.BlockSpec(shape, (lambda i, w: (0, i)) if turn else (lambda i, w: (i, 0))),
+        jax.ShapeDtypeStruct((rows, 2 * wide) if turn else (2 * wide, rows), F32),
+        flops=flops,
     )(places, *pieces)
 
 
@@ -513,7 +495,7 @@
             [slot_spec, act_spec, act_spec, act_spec, inv_spec] + id_specs + [gain_spec],
             [act_spec, state_spec, pl.BlockSpec((1, 1, 8, LANES), lambda b, h, w: (b, h, 0, 0))],
             [low, state_shape, jax.ShapeDtypeStruct((seqs, 2, 8, LANES), F32)],
-            flops=LONG,
+            flops=int(26 * 1.1e9),
         )(places, d_head, mixed, query, key, inverse, *id_args, gain)
 
     def four(raw, query, key, value, inverse, fresh, d_low, incoming, middle, d_final):
@@ -538,7 +520,7 @@
                 pltpu.VMEM((HALO + 2 * size, LANES), F32),
                 pltpu.VMEM((3, 2 * size, LANES), F32),
             ],
-            flops=LONG,
+            flops=int(26 * 1.1e9),
         )(
             places,
             *(raw,) * 9,
@@ -561,7 +543,7 @@
     return 512 if extent % 512 == 0 else extent
 
 
-def rows_products(pairs, rows, block, add=None, out=BF16):
+def rows_products(pairs, rows, block, add=None, out=BF16, flops=1000):
     columns = pairs[0][1].shape[0]
     tile = tile_of(columns)
     count = len(pairs)
@@ -586,11 +568,11 @@
         out_specs=spec,
         out_shape=jax.ShapeDtypeStruct((rows, columns), out),
         compiler_params=pltpu.CompilerParams(vmem_limit_bytes=48 << 20),
-        cost_estimate=pl.CostEstimate(flops=1000, transcendentals=0, bytes_accessed=1000),
+        cost_estimate=pl.CostEstimate(flops=flops, transcendentals=0, bytes_accessed=1000),
     )(*(left for left, _ in pairs), *(right for _, right in pairs), *extra)
 
 
-def token_products(pairs, add=None):
+def token_products(pairs, add=None, flops=1000):
     count = len(pairs)
     height, columns = pairs[0][0].shape[1], pairs[0][1].shape[1]
     tile = tile_of(height)
@@ -618,7 +600,7 @@
         out_specs=spec,
         out_shape=jax.ShapeDtypeStruct((height, columns), BF16),
         compiler_params=pltpu.CompilerParams(vmem_limit_bytes=48 << 20),
-        cost_estimate=pl.CostEstimate(flops=1000, transcendentals=0, bytes_accessed=1000),
+        cost_estimate=pl.CostEstimate(flops=flops, transcendentals=0, bytes_accessed=1000),
     )(*(item[0] for item in pairs), *(item[1] for item in pairs), *extra)
 
 
@@ -814,12 +796,12 @@
     slots = head_own.shape
     head_own, head_other = (part.reshape(2 * own_rows, -1) for part in (head_own, head_other))
 
-    def products(block, lefts, rights, add=None, out=BF16):
-        return rows_products(list(zip(lefts, rights)), own_rows, block, add, out)
-
-    def away(*pairs):
+    def products(block, lefts, rights, add=None, out=BF16, flops=1000):
+        return rows_products(list(zip(lefts, rights)), own_rows, block, add, out, flops)
+
+    def away(*pairs, flops=1000):
         lefts, rights = zip(*pairs)
-        return to_core(steps(lambda *args: products(1, *args), lefts, rights))
+        return to_core(steps(lambda *args: products(1, *args, flops=flops), lefts, rights))
 
     def here(arrived, *pairs, out=BF16):
         lefts, rights = zip(*pairs)
@@ -881,18 +863,26 @@
     resid_other = to_core(resid_own)
     resid_low = steps(lambda own, other: jnp.concatenate([own, other]), resid_own, resid_other)
 
-    def grad_of(rows, grads, *arrived):
-        return token_products([(rows, grads, 2 * own_rows, 0)], *arrived)
+    def grad_of(rows, grads, *arrived, flops=1000):
+        return token_products([(rows, grads, 2 * own_rows, 0)], *arrived, flops=flops)
 
     d_head_own = steps(project, resid_low, outer_own).reshape(slots)
     d_head_other = steps(project, resid_low, outer_other).reshape(slots)
+    steps.wait(grad_down)
     third_own = steps(own_calls[2], d_head_own, mixed_own, *first_own[:2], first_own[3])
     d_final_other = lax.ppermute(third_own[1], "cx", [(1, 0)])
     third_other = steps(other_calls[2], d_head_other, mixed_other, *first_other[:2], first_other[3])
     d_final_own = lax.ppermute(third_other[1], "cx", [(1, 0)])
     outer_sent = across(steps(grad_of, resid_low, head_other))
     down_pair = with_tp(steps(add_far, down_near, down_sent))
-    steps.wait(d_final_own, d_final_other)
+    sum_head_gain = steps(
+        lambda *parts: sum(jnp.sum(part[:, :, 0, :], axis=(0, 1)) for part in parts).astype(BF16),
+        third_own[2],
+        third_other[2],
+    )
+    sum_head_gain = sum_over(sum_head_gain, "tp", 1)
+    steps.wait(d_final_own, d_final_other, sum_head_gain)
+    steps.wait(grad_gate)
     fourth_other = steps(
         other_calls[3],
         raw_other,
@@ -906,19 +896,22 @@
     edge_own = lax.ppermute(fourth_other[1], "cx", [(1, 0)])
     normed_rows = normed_low[: 2 * own_rows]
 
-    def joint_grad(half, d_raw, d_edge, *arrived):
+    def joint_grad(half, d_raw, d_edge, *arrived, flops=1000):
         lanes = slice(half * 3 * LANES, (half + 1) * 3 * LANES)
         d_raw = d_raw.reshape(2 * own_rows, -1)[:, lanes]
         d_edge = d_edge.reshape(seqs * HALO, -1)[:, lanes]
         pairs = [(normed_low, d_raw, 2 * own_rows, 0)]
         pairs += [(normed_low, d_edge, seqs * HALO, 2 * own_rows // (seqs * HALO))]
-        return token_products(pairs, *arrived)
-
+        return token_products(pairs, *arrived, flops=flops)
+
+    out_down = steps(
+        lambda pieces: lay_units(places, pieces, False, 1000), pieces_of(grad_down.T, fourth_other[1])
+    )
     joint_dots = [
         steps(functools.partial(joint_grad, half), *fourth_other[:2]) for half in range(2)
     ]
     joint_sent = [across(joint_dots[0])]
-    steps.wait(outer_sent)
+    steps.wait(outer_sent, grad_up)
     fourth_own = steps(
         own_calls[3],
         raw_own,
@@ -930,12 +923,11 @@
         d_final_own,
     )
     edge_other = lax.ppermute(fourth_own[1], "cx", [(1, 0)])
+    result_rows = steps(
+        lambda pair, resid: (resid + pair_sum(pair)).astype(BF16), down_pair, resid
+    )
+    steps.wait(joint_sent[0])
     joint_sent.append(across(tie(joint_dots[1], edge_other)))
-    grad_outer = over_shard(steps(grad_of, resid_low, head_own, outer_sent))
-    grad_joint = [
-        over_shard(steps(functools.partial(joint_grad, 0), *fourth_own[:2], joint_sent[0]))
-    ]
-
     def with_edge(d_raw, d_edge):
         window = (1 - core, 0, size - HALO, 0)
         edge_rows = lax.dynamic_slice(d_raw, window, (1,) + d_edge.shape)
@@ -954,18 +946,17 @@
     d_raw_other = steps(with_edge, fourth_other[0], edge_other)
 
     pairs = ((d_raw_own, joint_own), (d_raw_other, joint_other), (d_logit, beta))
-    d_normed_pair = with_tp(here(away(*pairs), *pairs))
-    grad_joint.append(
-        over_shard(steps(functools.partial(joint_grad, 1), *fourth_own[:2], joint_sent[1]))
-    )
-    sum_head_gain = sum(
-        jnp.sum(third[2][:, :, 0, :], axis=(0, 1)) for third in (third_own, third_other)
-    )
-    sum_head_gain = sum_over(sum_head_gain.astype(BF16), "tp", 1).astype(F32)
-
-    out_down = steps(lambda pieces: lay_units_turned(places, pieces), pieces_of(grad_down, d_normed_pair[0]))
-    out_gate = steps(lambda pieces: lay_units(places, pieces), pieces_of(grad_gate, d_normed_pair[0]))
-    out_up = steps(lambda pieces: lay_units(places, pieces), pieces_of(grad_up, d_normed_pair[0]))
+    d_normed_pair = with_tp(here(away(*pairs, flops=LONG), *pairs))
+    grad_outer = over_shard(steps(functools.partial(grad_of, flops=LONG), resid_low, head_own, outer_sent))
+    grad_joint = [
+        over_shard(steps(functools.partial(joint_grad, 0), *fourth_own[:2], joint_sent[0]))
+    ]
+    joint_total = steps(functools.partial(joint_grad, 1), *fourth_own[:2], joint_sent[1])
+    grad_joint.append(over_shard(joint_total))
+    steps.wait(grad_joint[0])
+    out_gate = steps(
+        lambda pieces: lay_units(places, pieces, True, 1000), pieces_of(grad_gate.T, fourth_own[1])
+    )
 
     def input_back(pair, d_resid, hidden):
         _, pull = jax.vjp(rms, hidden, gain_in)
@@ -973,8 +964,8 @@
         return sum_attn_gain, (d_resid + d_hidden).astype(BF16)
 
     sum_attn_gain, input_rows = steps(input_back, d_normed_pair, d_resid, hidden_f32)
-    result_rows = steps(
-        lambda pair, resid: (resid + pair_sum(pair)).astype(BF16), down_pair, resid
+    out_up = steps(
+        lambda pieces: lay_units(places, pieces, True, LONG), pieces_of(grad_up.T, sum_attn_gain)
     )
     out_outer = steps(lambda pieces: lay_heads_turned(places, pieces), pieces_of(grad_outer))
 
@@ -982,8 +973,8 @@
     sum_taps = jnp.where(
         cx == 0, jnp.concatenate(sum_taps, axis=2), jnp.concatenate(sum_taps[::-1], axis=2)
     )
-    gains = jnp.concatenate([sum_attn_gain[0], sum_ffn_gain[0], sum_head_gain]).astype(BF16)
-    gains = sum_over(gains, "core", 1)
+    gains = jnp.concatenate([sum_attn_gain[0], sum_ffn_gain[0]]).astype(BF16)
+    gains = sum_over(jnp.concatenate([gains, sum_head_gain]), "core", 1)
     packed = jnp.concatenate(
         [gains, sum_taps.reshape(-1).astype(BF16), sum_rate.reshape(-1).astype(BF16)]
     )

time: 849 us -> 839 us (0.988)
    ppermute x5, waiting for transfers between devices: 45.8 us -> 6.43 us  [sum_over(): lax.ppermute(values, axis, partners).astype(F32)]
    ppermute x6, waiting for transfers between devices: 27.9 us -> 65.5 us  [pieces_of(): across = lax.ppermute(own, 'cx', SWAP)]
    optimization_barrier x9 -> x0, local copies, waits for them, and re-layouts: 19.6 us -> none  [tie(): return lax.optimization_barrier((value, after))[0]]
    pallas_call x0 -> x3, local copies, waits for them, and re-layouts: none -> 14 us  [token_products(): pl.pallas_call(kernel, grid=(height // tile,), in_specs=lefts + rights +...]
    ppermute x1, waiting for transfers between devices: 0.57 us -> 14 us  [shards(): d_final_own = lax.ppermute(third_other[1], 'cx', [(1, 0)])]
    unnamed x247 -> x275, local copies, waits for them, and re-layouts: 69 us -> 76.8 us
  transfers between devices with their start and end apart: 70 -> 70, of which waited for: 27 -> 28; matrix products, arithmetic and copies ran while one was open for 18% -> 15% of each run, Pallas kernels for 28% -> 26%
where the time goes in v4:
time: 839 us; the launch traced here: 830 us
  Pallas kernels  282 us (34%)
  waiting for transfers between devices  268 us (32%)
  local copies, waits for them, and re-layouts  112 us (13%)
  other arithmetic  64.6 us (8%)
  starting transfers between devices  54.3 us (6%)
  matrix products  19.7 us (2%)
  between operations  15.7 us (2%)
  blocking collectives  13.9 us (2%)
    ppermute x9, waiting for transfers between devices, across(): return lax.ppermute(part, 'cx', SWAP)  85.5 us
    unnamed x275, local copies, waits for them, and re-layouts  76.8 us
    pallas_call x12, Pallas kernels, rows_products(): pl.pallas_call(kernel, grid=(columns // tile,), in_specs=lefts + rights +...  69.1 us
    ppermute x6, waiting for transfers between devices, pieces_of(): across = lax.ppermute(own, 'cx', SWAP)  65.5 us
    pallas_call x9, Pallas kernels, token_products(): pl.pallas_call(kernel, grid=(height // tile,), in_specs=lefts + rights +...  59.2 us
    ppermute x4, waiting for transfers between devices, with_tp(): return (part, lax.ppermute(part, 'tp', SWAP))  50.3 us
    pallas_call x2, Pallas kernels, one(): call(functools.partial(forward_one, size=size, own=own), grid, conv_specs...  37.7 us
    pallas_call x2, Pallas kernels, four(): call(functools.partial(backward_two, size=size, own=own), grid, conv_spec...  33 us
  transfers between devices with their start and end apart: 70, of which 28 were waited for; matrix products, arithmetic and copies ran while one was open for 15% of the time, Pallas kernels for 26%

profile of v4, /device:TPU:0, one launch (start us, length us, event | category | flops | bytes accessed | tf_op | source)
XLA Modules:
  0.0 830.1 jit_solution(2301983656243976231)
XLA Ops:
  17.6 13.9 %all_gather.18 = bf16[4,80,128]{2,1,0:T(8,128)(2,1)S(1)} all-gather(bf16[1,80,128]{2,1,0:T(8,128)(2,1)S(1)} %pad_bitcast_fusion), channel_id=1, replica_groups=mesh['shard'=4,'cx'=2,'core'=2,'tp'=2] {'shard'}, dimensions={0}, use_global_device_ids=true | all-gather | bytes 102400 | tf_op jit(solution)/shard_map/all_gather | solution.py:737
  42.3 20.3 %collective-permute-done.4 = bf16[512,2048]{1,0:T(8,128)(2,1)} collective-permute-done((bf16[512,2048]{1,0:T(8,128)(2,1)}, bf16[512,2048]{1,0:T(8,128)(2,1)}, u32[]{:S(2)}, u32[]{:S(2)}) %collective-permute-start.4) | collective-permute-done | bytes 2097184 | tf_op jit(solution)/shard_map/ppermute | solution.py:715
  72.7 4.4 collective-permute-start.3
  91.3 6.8 convolution_convert_fusion.1.q0.k0.v0.q1.k1.v1.qh.kh.vh
  98.1 18.8 %shard_map.255 = (bf16[2,2,256,256]{3,2,1,0:T(8,128)(2,1)S(1)}, bf16[2,2,256,256]{3,2,1,0:T(8,128)(2,1)S(1)}, bf16[2,2,256,256]{3,2,1,0:T(8,128)(2,1)S(1)}, bf16...) custom-call(s32[2]{0:T(128)S(1)} %pad_add_fusion.1.where, ...), custom_call_target="tpu_custom_call" | custom-call | flops 1000 | bytes 1000 | tf_op jit(solution)/shard_map/pallas_call | solution.py:469
  121.8 34.0 %collective-permute-done.6.refs_4_ = bf16[2048,768]{1,0:T(8,128)(2,1)} collective-permute-done((bf16[2048,768]{1,0:T(8,128)(2,1)}, bf16[2048,768]{1,0:T(8,128)(2,1)}, u32[]{:S(2)}, u32[]{:S(2)}) %collective-permute-start.6) | collective-permute-done | bytes 3145760 | tf_op jit(solution)/shard_map/ppermute | solution.py:715
  158.3 6.7 convolution_convert_fusion.q0.k0.v0.q1.k1.v1.qh.kh.vh
  165.0 18.9 %shard_map.256 = (bf16[2,2,256,256]{3,2,1,0:T(8,128)(2,1)S(1)}, bf16[2,2,256,256]{3,2,1,0:T(8,128)(2,1)S(1)}, bf16[2,2,256,256]{3,2,1,0:T(8,128)(2,1)S(1)}, bf16...) custom-call(s32[2]{0:T(128)S(1)} %pad_add_fusion.1.where, ...), custom_call_target="tpu_custom_call" | custom-call | flops 1000 | bytes 1000 | tf_op jit(solution)/shard_map/pallas_call | solution.py:469
  193.8 6.1 shard_map.257
  205.2 6.1 shard_map.258
  215.1 5.9 collective-permute-done.10.refs_4_
  222.3 4.6 shard_map.260
  232.1 4.8 pad_maximum_fusion.2.grads_ref.refs_0_
  237.5 4.2 bitcast_convert_fusion
  241.7 33.3 %collective-permute-done.11 = bf16[512,2048]{1,0:T(8,128)(2,1)} collective-permute-done((bf16[512,2048]{1,0:T(8,128)(2,1)}, bf16[512,2048]{1,0:T(8,128)(2,1)}, u32[]{:S(2)}, u32[]{:S(2)}) %collective-permute-start.11) | collective-permute-done | bytes 2097184 | tf_op jit(solution)/shard_map/ppermute | solution.py:811
  275.0 4.4 multiply_reduce_fusion.6
  283.1 4.4 collective-permute-done.12
  287.5 4.2 pad_maximum_fusion.1.rows_ref.refs_0_
  291.7 9.5 %all-gather.14.cloned.1.call-done.downs_ref.refs_1_ = bf16[2048,704]{1,0:T(8,128)(2,1)} async-done(((bf16[512,704]{1,0:T(8,128)(2,1)}), bf16[2048,704]{1,0:T(8,128)(2,1)}) %all-gather.14.cloned.1.call-update) | async-done | bytes 2883600 | tf_op jit(solution)/shard_map/all_gather | solution.py:709
  301.2 15.4 %shard_map.261 = (bf16[1024,704]{1,0:T(8,128)(2,1)S(1)}, bf16[1024,704]{1,0:T(8,128)(2,1)S(1)}, bf16[1024,704]{1,0:T(8,128)(2,1)S(1)}) custom-call(bf16[1024,2048]{1,0:T(8,128)(2,1)} %pad_maximum_fusion.1.rows_ref.refs_0_, bf16[1024,2048]{1,0:T(8,128)(2,1)} %pad_maximum_fusion.2.grads_ref.refs_0_, ...), custom_call_target="tpu_custom_call" | custom-call | flops 1000 | bytes 1000 | tf_op jit(solution)/shard_map/pallas_call | solution.py:624
  316.6 7.1 shard_map.262
  325.0 4.2 shard_map.263
  340.2 15.4 %shard_map.264 = (bf16[1024,704]{1,0:T(8,128)(2,1)S(1)}, bf16[1024,704]{1,0:T(8,128)(2,1)S(1)}, bf16[1024,704]{1,0:T(8,128)(2,1)S(1)}) custom-call(bf16[1024,2048]{1,0:T(8,128)(2,1)} %copy-done.112, bf16[1024,2048]{1,0:T(8,128)(2,1)} %constant_dynamic-update-slice_fusion.grads_ref.refs_1_, bf16[2048,704]{1,0:T(8,128)(2,1)} %all-gather.12.cloned.1.call-done.gates_ref.refs_2_, ...), custom_call_target="tpu_custom_call" | custom-call | flops 1000 | bytes 1000 | tf_op jit(solution)/shard_map/pallas_call | solution.py:624
  355.6 7.1 shard_map.265
  362.9 4.0 collective-permute-done.18.refs_4_
  368.3 6.3 shard_map.266
  376.0 9.8 %shard_map.267 = bf16[2048,704]{1,0:T(8,128)(2,1)} custom-call(bf16[1024,2048]{1,0:T(8,128)(2,1)} %pad_maximum_fusion.2.grads_ref.refs_0_, bf16[1024,2048]{1,0:T(8,128)(2,1)} %constant_dynamic-update-slice_fusion.grads_ref.refs_1_, bf16[1024,704]{1,0:T(8,128)(2,1)S(1)} %get-tuple-element.356.refs_0_.refs_2_, ...), custom_call_target="tpu_custom_call" | custom-call | flops 1000 | bytes 1000 | tf_op jit(solution)/shard_map/pallas_call | solution.py:596
  385.8 4.7 copy.105
  398.1 7.4 shard_map.268
  405.5 5.3 shard_map.269
  411.0 10.0 %shard_map.270 = bf16[2048,704]{1,0:T(8,128)(2,1)} custom-call(bf16[1024,2048]{1,0:T(8,128)(2,1)} %pad_maximum_fusion.1.rows_ref.refs_0_, bf16[1024,2048]{1,0:T(8,128)(2,1)} %copy-done.112, bf16[1024,704]{1,0:T(8,128)(2,1)S(1)} %copy-done.15, bf16[1024,704]{1,0:T(8,128)(2,1)S(1)} %copy-done.10), custom_call_target="tpu_custom_call" | custom-call | flops 1000 | bytes 1000 | tf_op jit(solution)/shard_map/pallas_call | solution.py:596
  421.0 18.0 %collective-permute-done.20 = bf16[512,2048]{1,0:T(8,128)(2,1)S(1)} collective-permute-done((bf16[512,2048]{1,0:T(8,128)(2,1)}, bf16[512,2048]{1,0:T(8,128)(2,1)S(1)}, u32[]{:S(2)}, u32[]{:S(2)}) %collective-permute-start.20) | collective-permute-done | bytes 2097184 | tf_op jit(solution)/shard_map/ppermute | solution.py:715
  442.5 4.7 copy.108
  450.1 10.0 %shard_map.271 = bf16[2048,704]{1,0:T(8,128)(2,1)} custom-call(bf16[1024,2048]{1,0:T(8,128)(2,1)} %pad_maximum_fusion.1.rows_ref.refs_0_, bf16[1024,2048]{1,0:T(8,128)(2,1)} %copy-done.112, bf16[1024,704]{1,0:T(8,128)(2,1)S(1)} %copy-done.13, bf16[1024,704]{1,0:T(8,128)(2,1)S(1)} %copy-done.8), custom_call_target="tpu_custom_call" | custom-call | flops 1000 | bytes 1000 | tf_op jit(solution)/shard_map/pallas_call | solution.py:596
  460.1 5.7 shard_map.272
  465.8 5.7 shard_map.273
  471.5 17.1 %collective-permute-done.22 = bf16[512,2048]{1,0:T(8,128)(2,1)} collective-permute-done((bf16[512,2048]{1,0:T(8,128)(2,1)}, bf16[512,2048]{1,0:T(8,128)(2,1)}, u32[]{:S(2)}, u32[]{:S(2)}) %collective-permute-start.22) | collective-permute-done | bytes 2097184 | tf_op jit(solution)/shard_map/ppermute | solution.py:811
  488.9 4.2 multiply_reduce_fusion
  493.1 5.5 fusion.25
  500.1 4.6 copy.110
  516.2 7.1 shard_map.274
  524.3 7.8 shard_map.275
  536.0 11.0 %collective-permute-done.21 = bf16[512,2048]{1,0:T(8,128)(2,1)} collective-permute-done((bf16[512,2048]{1,0:T(8,128)(2,1)}, bf16[512,2048]{1,0:T(8,128)(2,1)}, u32[]{:S(2)}, u32[]{:S(2)}) %collective-permute-start.21) | collective-permute-done | bytes 2097184 | tf_op jit(solution)/shard_map/ppermute | solution.py:715
  560.1 14.0 %collective-permute-done.25.rest_8_ = bf16[2,2,128,128]{3,2,1,0:T(8,128)(2,1)S(1)} collective-permute-done((bf16[2,2,128,128]{3,2,1,0:T(8,128)(2,1)}, bf16[2,2,128,128]{3,2,1,0:T(8,128)(2,1)S(1)}, u32[]{:S(2)}, u32[]{:S(2)}) %collective-permute-start.25) | collective-permute-done | bytes 131104 | tf_op jit(solution)/shard_map/ppermute | solution.py:875
  582.2 16.4 %shard_map.277 = (bf16[2,2,256,768]{3,2,1,0:T(8,128)(2,1)}, bf16[2,16,768]{2,1,0:T(8,128)(2,1)S(1)}, f32[2,2,256,128]{3,2,1,0:T(8,128)S(1)}, f32[2,3,2,4,128]{4,3,2,1,0:T(4,128)S(1)}) custom-call(s32[2]{0:T(128)S(1)} %pad_add_fusion.1.where, bf16[1056,768]{1,0:T(8,128)(2,1)} %copy-done.3, bf16[1056,768]{1,0:T(8,128)(2,1)} %copy-done.3, ...), custom_call_target="tpu_custom_call" | custom-call | flops 28600000512 | bytes 1000 | tf_op jit(solution)/shard_map/pallas_call | solution.py:502
  603.9 4.6 shard_map.278
  610.4 6.0 shard_map.279
  619.2 5.1 shard_map.280
  632.0 16.6 %shard_map.281 = (bf16[2,2,256,768]{3,2,1,0:T(8,128)(2,1)}, bf16[2,16,768]{2,1,0:T(8,128)(2,1)S(1)}, f32[2,2,256,128]{3,2,1,0:T(8,128)S(1)}, f32[2,3,2,4,128]{4,3,2,1,0:T(4,128)S(1)}) custom-call(s32[2]{0:T(128)S(1)} %pad_add_fusion.1.where, bf16[1056,768]{1,0:T(8,128)(2,1)} %copy-done.2, bf16[1056,768]{1,0:T(8,128)(2,1)} %copy-done.2, ...), custom_call_target="tpu_custom_call" | custom-call | flops 28600000512 | bytes 1000 | tf_op jit(solution)/shard_map/pallas_call | solution.py:502
  649.9 4.8 add_convert_fusion
  656.3 6.9 shard_map.282
  663.3 4.1 collective-permute-done.35.refs_6_
  670.2 6.7 shard_map.283
  676.9 4.1 shard_map.284
  683.2 5.4 shard_map.285
  694.7 50.2 %collective-permute-done.37.b = bf16[704,512]{1,0:T(8,128)(2,1)} collective-permute-done((bf16[704,512]{1,0:T(8,128)(2,1)}, bf16[704,512]{1,0:T(8,128)(2,1)}, u32[]{:S(2)}, u32[]{:S(2)}) %collective-permute-start.37) | collective-permute-done | bytes 720928 | tf_op jit(solution)/shard_map/ppermute | solution.py:101
  747.9 5.6 shard_map.286
  755.8 5.6 shard_map.287
  768.8 7.1 collective-permute-done.53.b
  776.4 6.1 collective-permute-done.43
  782.6 6.8 fusion.5
  800.6 8.2 collective-permute-done.48.refs_5_
  810.6 5.5 shard_map.289
  819.7 3.6 shard_map.288
  (517 shorter events, 211.3 us)
Async XLA Ops:
  7.2 77.6 %all-gather.6.cloned.1.call-start = ((), (), s32[]{:S(2)}) async-start(), calls=%async_computation.6 | async-start | bytes 3932160 | tf_op jit(solution)/shard_map/all_gather | solution.py:709
  12.9 142.8 %all-gather.8.cloned.1.call-start = ((), (), s32[]{:S(2)}) async-start(), calls=%async_computation.7 | async-start | bytes 1310720 | tf_op jit(solution)/shard_map/all_gather | solution.py:709
  13.0 24.4 %collective-permute-start = (bf16[512,2048]{1,0:T(8,128)(2,1)S(1)}, bf16[512,2048]{1,0:T(8,128)(2,1)}, u32[]{:S(2)}, u32[]{:S(2)}) collective-permute-start(bf16[512,2048]{1,0:T(8,128)(2,1)S(1)} %bitcast.112), channel_id=1, source_target_pairs={{0,2},{2,0},{1,3},{3,1},{4,6},{6,4},{5,7},{7,5},{8,10},{10,8},{9,1... | collective-permute-start | bytes 6291464 | tf_op jit(solution)/shard_map/ppermute | solution.py:718
  13.5 49.1 %collective-permute-start.4 = (bf16[512,2048]{1,0:T(8,128)(2,1)}, bf16[512,2048]{1,0:T(8,128)(2,1)}, u32[]{:S(2)}, u32[]{:S(2)}) collective-permute-start(bf16[512,2048]{1,0:T(8,128)(2,1)} %bitcast.9), channel_id=1, source_target_pairs={{0,4},{4,0},{1,5},{5,1},{2,6},{6,2},{3,7},{7,3},{8,12},{12,8},{9,1... | collective-permute-start | bytes 6291464 | tf_op jit(solution)/shard_map/ppermute | solution.py:715
  17.0 224.7 %all-gather.10.cloned.1.call-start = ((), (), s32[]{:S(2)}) async-start(), calls=%async_computation.8 | async-start | bytes 3932160 | tf_op jit(solution)/shard_map/all_gather | solution.py:709
  39.3 25.3 %collective-permute-start.1 = (bf16[2,16,2048]{2,1,0:T(8,128)(2,1)S(1)}, bf16[2,16,2048]{2,1,0:T(8,128)(2,1)S(1)}, u32[]{:S(2)}, u32[]{:S(2)}) collective-permute-start(bf16[2,16,2048]{2,1,0:T(8,128)(2,1)S(1)} %slice.109), channel_id=1, source_target_pairs={{0,4},{1,5},{2,6},{3,7},{8,12},{9,13},{10,14},{11,15},{16,20},{17,... | collective-permute-start | bytes 393224 | tf_op jit(solution)/shard_map/ppermute | solution.py:759
  62.6 19.1 %collective-permute-start.5 = (bf16[512,2048]{1,0:T(8,128)(2,1)}, bf16[512,2048]{1,0:T(8,128)(2,1)}, u32[]{:S(2)}, u32[]{:S(2)}) collective-permute-start(bf16[512,2048]{1,0:T(8,128)(2,1)} %collective-permute-done.4), channel_id=1, source_target_pairs={{0,2},{2,0},{1,3},{3,1},{4,6},{6,4},{5,7},{7,5},{8,10},{10,8},{9,1... | collective-permute-start | bytes 6291464 | tf_op jit(solution)/shard_map/ppermute | solution.py:718
  71.4 220.3 %all-gather.12.cloned.1.call-start = ((), (), s32[]{:S(2)}) async-start(), calls=%async_computation.9 | async-start | bytes 3932160 | tf_op jit(solution)/shard_map/all_gather | solution.py:709
  72.7 5.7 collective-permute-start.3
  84.8 70.9 %collective-permute-start.6 = (bf16[2048,768]{1,0:T(8,128)(2,1)}, bf16[2048,768]{1,0:T(8,128)(2,1)}, u32[]{:S(2)}, u32[]{:S(2)}) collective-permute-start(bf16[2048,768]{1,0:T(8,128)(2,1)} %all-gather.6.cloned.1.call-done.refs_3_), channel_id=1, source_target_pairs={{0,4},{4,0},{1,5},{5,1},{2,6},{6,2},{3,7},{7,3},{8,12},{12,8},{9,1... | collective-permute-start | bytes 9437192 | tf_op jit(solution)/shard_map/ppermute | solution.py:715
  91.0 210.1 %all-gather.14.cloned.1.call-start = ((), (), s32[]{:S(2)}) async-start(), calls=%async_computation.10 | async-start | bytes 3932160 | tf_op jit(solution)/shard_map/all_gather | solution.py:709
  119.6 69.8 %collective-permute-start.8 = (bf16[2,2,128,128]{3,2,1,0:T(8,128)(2,1)S(1)}, bf16[2,2,128,128]{3,2,1,0:T(8,128)(2,1)S(1)}, u32[]{:S(2)}, u32[]{:S(2)}) collective-permute-start(bf16[2,2,128,128]{3,2,1,0:T(8,128)(2,1)S(1)} %get-tuple-element.256), channel_id=1, source_target_pairs={{0,4},{1,5},{2,6},{3,7},{8,12},{9,13},{10,14},{11,15},{16,20},{17,... | collective-permute-start | bytes 393224 | tf_op jit(solution)/shard_map/ppermute | solution.py:790
  155.8 56.7 %collective-permute-start.9 = (bf16[2048,256]{1,0:T(8,128)(2,1)}, bf16[2048,256]{1,0:T(8,128)(2,1)S(1)}, u32[]{:S(2)}, u32[]{:S(2)}) collective-permute-start(bf16[2048,256]{1,0:T(8,128)(2,1)} %all-gather.8.cloned.1.call-done.refs_2_), channel_id=1, source_target_pairs={{0,4},{4,0},{1,5},{5,1},{2,6},{6,2},{3,7},{7,3},{8,12},{12,8},{9,1... | collective-permute-start | bytes 3145736 | tf_op jit(solution)/shard_map/ppermute | solution.py:715
  187.3 14.3 %collective-permute-start.7 = (bf16[2,2,128,128]{3,2,1,0:T(8,128)(2,1)S(1)}, bf16[2,2,128,128]{3,2,1,0:T(8,128)(2,1)S(1)}, u32[]{:S(2)}, u32[]{:S(2)}) collective-permute-start(bf16[2,2,128,128]{3,2,1,0:T(8,128)(2,1)S(1)} %get-tuple-element.260), channel_id=1, source_target_pairs={{0,4},{1,5},{2,6},{3,7},{8,12},{9,13},{10,14},{11,15},{16,20},{17,... | collective-permute-start | bytes 393224 | tf_op jit(solution)/shard_map/ppermute | solution.py:791
  214.5 6.4 collective-permute-start.10
  214.6 17.6 %collective-permute-start.13 = (bf16[512,2048]{1,0:T(8,128)(2,1)}, bf16[512,2048]{1,0:T(8,128)(2,1)}, u32[]{:S(2)}, u32[]{:S(2)}) collective-permute-start(bf16[512,2048]{1,0:T(8,128)(2,1)} %bitcast.9), channel_id=1, source_target_pairs={{0,2},{2,0},{1,3},{3,1},{4,6},{6,4},{5,7},{7,5},{8,10},{10,8},{9,1... | collective-permute-start | bytes 6291464 | tf_op jit(solution)/shard_map/ppermute | solution.py:718
  226.9 48.1 %collective-permute-start.11 = (bf16[512,2048]{1,0:T(8,128)(2,1)}, bf16[512,2048]{1,0:T(8,128)(2,1)}, u32[]{:S(2)}, u32[]{:S(2)}) collective-permute-start(bf16[512,2048]{1,0:T(8,128)(2,1)} %shard_map.260), channel_id=1, source_target_pairs={{0,1},{1,0},{2,3},{3,2},{4,5},{5,4},{6,7},{7,6},{8,9},{9,8},{10,11... | collective-permute-start | bytes 6291464 | tf_op jit(solution)/shard_map/ppermute | solution.py:811
  237.0 275.9 %reduce-scatter.7.cloned.1.call-start = ((), (), s32[]{:S(2)}) async-start(), calls=%async_computation.11 | async-start | bytes 3604480 | tf_op jit(solution)/shard_map/reduce_scatter | solution.py:712
  283.1 4.4 collective-permute-start.12
  283.1 48.4 %collective-permute-start.15 = (bf16[512,2048]{1,0:T(8,128)(2,1)}, bf16[512,2048]{1,0:T(8,128)(2,1)}, u32[]{:S(2)}, u32[]{:S(2)}) collective-permute-start(bf16[512,2048]{1,0:T(8,128)(2,1)} %multiply_convert_fusion), channel_id=1, source_target_pairs={{0,4},{4,0},{1,5},{5,1},{2,6},{6,2},{3,7},{7,3},{8,12},{12,8},{9,1... | collective-permute-start | bytes 6291464 | tf_op jit(solution)/shard_map/ppermute | solution.py:715
  329.3 4.2 collective-permute-start.14
  333.5 4.4 collective-permute-start.16
  362.7 4.2 collective-permute-start.18
  390.5 169.6 %reduce-scatter.9.cloned.1.call-start = ((), (), s32[]{:S(2)}) async-start(), calls=%async_computation.12 | async-start | bytes 3604480 | tf_op jit(solution)/shard_map/reduce_scatter | solution.py:712
  390.7 4.4 collective-permute-start.17
  390.9 48.1 %collective-permute-start.20 = (bf16[512,2048]{1,0:T(8,128)(2,1)}, bf16[512,2048]{1,0:T(8,128)(2,1)S(1)}, u32[]{:S(2)}, u32[]{:S(2)}) collective-permute-start(bf16[512,2048]{1,0:T(8,128)(2,1)} %copy-done.35), channel_id=1, source_target_pairs={{0,4},{4,0},{1,5},{5,1},{2,6},{6,2},{3,7},{7,3},{8,12},{12,8},{9,1... | collective-permute-start | bytes 6291464 | tf_op jit(solution)/shard_map/ppermute | solution.py:715
  410.8 49.3 %collective-permute-start.19 = (bf16[512,2048]{1,0:T(8,128)(2,1)}, bf16[512,2048]{1,0:T(8,128)(2,1)}, u32[]{:S(2)}, u32[]{:S(2)}) collective-permute-start(bf16[512,2048]{1,0:T(8,128)(2,1)} %shard_map.269), channel_id=1, source_target_pairs={{0,2},{2,0},{1,3},{3,1},{4,6},{6,4},{5,7},{7,5},{8,10},{10,8},{9,1... | collective-permute-start | bytes 6291464 | tf_op jit(solution)/shard_map/ppermute | solution.py:718
  441.0 47.5 %collective-permute-start.22 = (bf16[512,2048]{1,0:T(8,128)(2,1)}, bf16[512,2048]{1,0:T(8,128)(2,1)}, u32[]{:S(2)}, u32[]{:S(2)}) collective-permute-start(bf16[512,2048]{1,0:T(8,128)(2,1)} %add_convert_fusion.2), channel_id=1, source_target_pairs={{0,1},{1,0},{2,3},{3,2},{4,5},{5,4},{6,7},{7,6},{8,9},{9,8},{10,11... | collective-permute-start | bytes 6291464 | tf_op jit(solution)/shard_map/ppermute | solution.py:811
  447.2 178.3 %reduce-scatter.11.cloned.1.call-start = ((), (), s32[]{:S(2)}) async-start(), calls=%async_computation.13 | async-start | bytes 3604480 | tf_op jit(solution)/shard_map/reduce_scatter | solution.py:712
  498.7 6.4 collective-permute-start.23
  498.7 48.4 %collective-permute-start.21 = (bf16[512,2048]{1,0:T(8,128)(2,1)}, bf16[512,2048]{1,0:T(8,128)(2,1)}, u32[]{:S(2)}, u32[]{:S(2)}) collective-permute-start(bf16[512,2048]{1,0:T(8,128)(2,1)} %shard_map.272), channel_id=1, source_target_pairs={{0,4},{4,0},{1,5},{5,1},{2,6},{6,2},{3,7},{7,3},{8,12},{12,8},{9,1... | collective-permute-start | bytes 6291464 | tf_op jit(solution)/shard_map/ppermute | solution.py:715
  504.8 249.9 %reduce-scatter.13.cloned.1.call-start = ((), (), s32[]{:S(2)}) async-start(), calls=%async_computation.14 | async-start | bytes 1966080 | tf_op jit(solution)/shard_map/reduce_scatter | solution.py:712
  550.7 5.6 collective-permute-start.27
  552.2 47.2 %collective-permute-start.28 = (bf16[704,512]{1,0:T(8,128)(2,1)S(1)}, bf16[704,512]{1,0:T(8,128)(2,1)}, u32[]{:S(2)}, u32[]{:S(2)}) collective-permute-start(bf16[704,512]{1,0:T(8,128)(2,1)S(1)} %bitcast.103), channel_id=1, source_target_pairs={{0,4},{4,0},{1,5},{5,1},{2,6},{6,2},{3,7},{7,3},{8,12},{12,8},{9,1... | collective-permute-start | bytes 2162696 | tf_op jit(solution)/shard_map/ppermute | solution.py:101
  553.7 48.3 %collective-permute-start.29 = (bf16[704,512]{1,0:T(8,128)(2,1)S(1)}, bf16[704,512]{1,0:T(8,128)(2,1)}, u32[]{:S(2)}, u32[]{:S(2)}) collective-permute-start(bf16[704,512]{1,0:T(8,128)(2,1)S(1)} %bitcast.104), channel_id=1, source_target_pairs={{0,2},{2,0},{1,3},{3,1},{4,6},{6,4},{5,7},{7,5},{8,10},{10,8},{9,1... | collective-permute-start | bytes 2162696 | tf_op jit(solution)/shard_map/ppermute | solution.py:103
  553.7 20.4 %collective-permute-start.25 = (bf16[2,2,128,128]{3,2,1,0:T(8,128)(2,1)}, bf16[2,2,128,128]{3,2,1,0:T(8,128)(2,1)S(1)}, u32[]{:S(2)}, u32[]{:S(2)}) collective-permute-start(bf16[2,2,128,128]{3,2,1,0:T(8,128)(2,1)} %get-tuple-element.383), channel_id=1, source_target_pairs={{4,0},{5,1},{6,2},{7,3},{12,8},{13,9},{14,10},{15,11},{20,16},{21,... | collective-permute-start | bytes 393224 | tf_op jit(solution)/shard_map/ppermute | solution.py:875
  555.0 22.0 %collective-permute-start.26 = (bf16[2,2,128,128]{3,2,1,0:T(8,128)(2,1)S(1)}, bf16[2,2,128,128]{3,2,1,0:T(8,128)(2,1)}, u32[]{:S(2)}, u32[]{:S(2)}) collective-permute-start(bf16[2,2,128,128]{3,2,1,0:T(8,128)(2,1)S(1)} %get-tuple-element.375), channel_id=1, source_target_pairs={{4,0},{5,1},{6,2},{7,3},{12,8},{13,9},{14,10},{15,11},{20,16},{21,... | collective-permute-start | bytes 393224 | tf_op jit(solution)/shard_map/ppermute | solution.py:873
  556.3 69.2 %collective-permute-start.31 = (bf16[2048,256]{1,0:T(8,128)(2,1)}, bf16[2048,256]{1,0:T(8,128)(2,1)}, u32[]{:S(2)}, u32[]{:S(2)}) collective-permute-start(bf16[2048,256]{1,0:T(8,128)(2,1)} %shard_map.276), channel_id=1, source_target_pairs={{0,4},{4,0},{1,5},{5,1},{2,6},{6,2},{3,7},{7,3},{8,12},{12,8},{9,1... | collective-permute-start | bytes 3145736 | tf_op jit(solution)/shard_map/ppermute | solution.py:715
  601.4 48.4 %collective-permute-start.24 = (bf16[512,2048]{1,0:T(8,128)(2,1)}, bf16[512,2048]{1,0:T(8,128)(2,1)}, u32[]{:S(2)}, u32[]{:S(2)}) collective-permute-start(bf16[512,2048]{1,0:T(8,128)(2,1)} %add_convert_fusion.1), channel_id=1, source_target_pairs={{0,1},{1,0},{2,3},{3,2},{4,5},{5,4},{6,7},{7,6},{8,9},{9,8},{10,11... | collective-permute-start | bytes 6291464 | tf_op jit(solution)/shard_map/ppermute | solution.py:811
  608.7 46.9 %collective-permute-start.32 = (bf16[2,16,768]{2,1,0:T(8,128)(2,1)S(1)}, bf16[2,16,768]{2,1,0:T(8,128)(2,1)S(1)}, u32[]{:S(2)}, u32[]{:S(2)}) collective-permute-start(bf16[2,16,768]{2,1,0:T(8,128)(2,1)S(1)} %get-tuple-element.413), channel_id=1, source_target_pairs={{4,0},{5,1},{6,2},{7,3},{12,8},{13,9},{14,10},{15,11},{20,16},{21,... | collective-permute-start | bytes 147464 | tf_op jit(solution)/shard_map/ppermute | solution.py:896
  616.5 38.2 %collective-permute-start.33 = (bf16[2048,384]{1,0:T(8,128)(2,1)}, bf16[2048,384]{1,0:T(8,128)(2,1)}, u32[]{:S(2)}, u32[]{:S(2)}) collective-permute-start(bf16[2048,384]{1,0:T(8,128)(2,1)} %shard_map.279), channel_id=1, source_target_pairs={{0,4},{4,0},{1,5},{5,1},{2,6},{6,2},{3,7},{7,3},{8,12},{12,8},{9,1... | collective-permute-start | bytes 4718600 | tf_op jit(solution)/shard_map/ppermute | solution.py:715
  648.5 7.7 collective-permute-start.34
  689.8 76.8 %reduce-scatter.17.cloned.1.call-start = ((), (), s32[]{:S(2)}) async-start(), calls=%async_computation.16 | async-start | bytes 1310720 | tf_op jit(solution)/shard_map/reduce_scatter | solution.py:712
  690.4 102.6 %reduce-scatter.15.cloned.1.call-start = ((), (), s32[]{:S(2)}) async-start(), calls=%async_computation.15 | async-start | bytes 1966080 | tf_op jit(solution)/shard_map/reduce_scatter | solution.py:712
  690.4 71.0 %collective-permute-start.36 = (bf16[512,2048]{1,0:T(8,128)(2,1)S(1)}, bf16[512,2048]{1,0:T(8,128)(2,1)}, u32[]{:S(2)}, u32[]{:S(2)}) collective-permute-start(bf16[512,2048]{1,0:T(8,128)(2,1)S(1)} %shard_map.283), channel_id=1, source_target_pairs={{0,1},{1,0},{2,3},{3,2},{4,5},{5,4},{6,7},{7,6},{8,9},{9,8},{10,11... | collective-permute-start | bytes 6291464 | tf_op jit(solution)/shard_map/ppermute | solution.py:811
  692.0 54.7 %collective-permute-start.40 = (bf16[2048,384]{1,0:T(8,128)(2,1)}, bf16[2048,384]{1,0:T(8,128)(2,1)}, u32[]{:S(2)}, u32[]{:S(2)}) collective-permute-start(bf16[2048,384]{1,0:T(8,128)(2,1)} %copy-done.36), channel_id=1, source_target_pairs={{0,4},{4,0},{1,5},{5,1},{2,6},{6,2},{3,7},{7,3},{8,12},{12,8},{9,1... | collective-permute-start | bytes 4718600 | tf_op jit(solution)/shard_map/ppermute | solution.py:715
  694.6 50.2 %collective-permute-start.37 = (bf16[704,512]{1,0:T(8,128)(2,1)}, bf16[704,512]{1,0:T(8,128)(2,1)}, u32[]{:S(2)}, u32[]{:S(2)}) collective-permute-start(bf16[704,512]{1,0:T(8,128)(2,1)} %bitcast.100), channel_id=1, source_target_pairs={{0,4},{4,0},{1,5},{5,1},{2,6},{6,2},{3,7},{7,3},{8,12},{12,8},{9,1... | collective-permute-start | bytes 2162696 | tf_op jit(solution)/shard_map/ppermute | solution.py:101
  694.7 60.0 %collective-permute-start.38 = (bf16[704,512]{1,0:T(8,128)(2,1)}, bf16[704,512]{1,0:T(8,128)(2,1)}, u32[]{:S(2)}, u32[]{:S(2)}) collective-permute-start(bf16[704,512]{1,0:T(8,128)(2,1)} %bitcast.101), channel_id=1, source_target_pairs={{0,2},{2,0},{1,3},{3,1},{4,6},{6,4},{5,7},{7,5},{8,10},{10,8},{9,1... | collective-permute-start | bytes 2162696 | tf_op jit(solution)/shard_map/ppermute | solution.py:103
  744.8 9.9 %collective-permute-start.39 = (bf16[704,512]{1,0:T(8,128)(2,1)}, bf16[704,512]{1,0:T(8,128)(2,1)}, u32[]{:S(2)}, u32[]{:S(2)}) collective-permute-start(bf16[704,512]{1,0:T(8,128)(2,1)} %collective-permute-done.37.b), channel_id=1, source_target_pairs={{0,2},{2,0},{1,3},{3,1},{4,6},{6,4},{5,7},{7,5},{8,10},{10,8},{9,1... | collective-permute-start | bytes 2162696 | tf_op jit(solution)/shard_map/ppermute | solution.py:103
  744.8 31.1 %collective-permute-start.56 = (bf16[704,512]{1,0:T(8,128)(2,1)}, bf16[704,512]{1,0:T(8,128)(2,1)}, u32[]{:S(2)}, u32[]{:S(2)}) collective-permute-start(bf16[704,512]{1,0:T(8,128)(2,1)} %bitcast.40.a), channel_id=1, source_target_pairs={{0,4},{4,0},{1,5},{5,1},{2,6},{6,2},{3,7},{7,3},{8,12},{12,8},{9,1... | collective-permute-start | bytes 2162696 | tf_op jit(solution)/shard_map/ppermute | solution.py:101
  766.6 9.3 %collective-permute-start.53 = (bf16[512,256]{1,0:T(8,128)(2,1)}, bf16[512,256]{1,0:T(8,128)(2,1)}, u32[]{:S(2)}, u32[]{:S(2)}) collective-permute-start(bf16[512,256]{1,0:T(8,128)(2,1)} %reduce-scatter.17.cloned.1.call-done.a), channel_id=1, source_target_pairs={{0,4},{4,0},{1,5},{5,1},{2,6},{6,2},{3,7},{7,3},{8,12},{12,8},{9,1... | collective-permute-start | bytes 786440 | tf_op jit(solution)/shard_map/ppermute | solution.py:101
  767.1 9.1 %collective-permute-start.42 = (bf16[18560]{0:T(1024)(128)(2,1)S(1)}, bf16[18560]{0:T(1024)(128)(2,1)S(1)}, u32[]{:S(2)}, u32[]{:S(2)}) collective-permute-start(bf16[18560]{0:T(1024)(128)(2,1)S(1)} %pad_maximum_fusion.5), channel_id=1, source_target_pairs={{0,4},{4,0},{1,5},{5,1},{2,6},{6,2},{3,7},{7,3},{8,12},{12,8},{9,1... | collective-permute-start | bytes 111368 | tf_op jit(solution)/shard_map/ppermute | solution.py:677
  768.8 40.5 %collective-permute-start.57 = (bf16[704,512]{1,0:T(8,128)(2,1)}, bf16[704,512]{1,0:T(8,128)(2,1)}, u32[]{:S(2)}, u32[]{:S(2)}) collective-permute-start(bf16[704,512]{1,0:T(8,128)(2,1)} %bitcast.40.a), channel_id=1, source_target_pairs={{0,2},{2,0},{1,3},{3,1},{4,6},{6,4},{5,7},{7,5},{8,10},{10,8},{9,1... | collective-permute-start | bytes 2162696 | tf_op jit(solution)/shard_map/ppermute | solution.py:103
  775.9 33.5 %collective-permute-start.58 = (bf16[704,512]{1,0:T(8,128)(2,1)}, bf16[704,512]{1,0:T(8,128)(2,1)}, u32[]{:S(2)}, u32[]{:S(2)}) collective-permute-start(bf16[704,512]{1,0:T(8,128)(2,1)} %collective-permute-done.56.b), channel_id=1, source_target_pairs={{0,2},{2,0},{1,3},{3,1},{4,6},{6,4},{5,7},{7,5},{8,10},{10,8},{9,1... | collective-permute-start | bytes 2162696 | tf_op jit(solution)/shard_map/ppermute | solution.py:103
  776.3 6.2 collective-permute-start.43
  782.5 12.0 %collective-permute-start.44 = (bf16[18560]{0:T(1024)(128)(2,1)S(1)}, bf16[18560]{0:T(1024)(128)(2,1)S(1)}, u32[]{:S(2)}, u32[]{:S(2)}) collective-permute-start(bf16[18560]{0:T(1024)(128)(2,1)S(1)} %add_convert_fusion.4), channel_id=1, source_target_pairs={{0,16},{8,24},{16,0},{24,8},{1,17},{9,25},{17,1},{25,9},{2,18},{10... | collective-permute-start | bytes 111368 | tf_op jit(solution)/shard_map/ppermute | solution.py:677
  789.4 19.4 %collective-permute-start.45 = (bf16[512,384]{1,0:T(8,128)(2,1)S(1)}, bf16[512,384]{1,0:T(8,128)(2,1)S(1)}, u32[]{:S(2)}, u32[]{:S(2)}) collective-permute-start(bf16[512,384]{1,0:T(8,128)(2,1)S(1)} %copy-done.77), channel_id=1, source_target_pairs={{0,4},{4,0},{1,5},{5,1},{2,6},{6,2},{3,7},{7,3},{8,12},{12,8},{9,1... | collective-permute-start | bytes 1179656 | tf_op jit(solution)/shard_map/ppermute | solution.py:101
  793.0 15.8 %collective-permute-start.48 = (bf16[512,384]{1,0:T(8,128)(2,1)}, bf16[512,384]{1,0:T(8,128)(2,1)S(1)}, u32[]{:S(2)}, u32[]{:S(2)}) collective-permute-start(bf16[512,384]{1,0:T(8,128)(2,1)} %reduce-scatter.15.cloned.1.call-done.refs_4_), channel_id=1, source_target_pairs={{0,4},{4,0},{1,5},{5,1},{2,6},{6,2},{3,7},{7,3},{8,12},{12,8},{9,1... | collective-permute-start | bytes 1179656 | tf_op jit(solution)/shard_map/ppermute | solution.py:101
  798.4 11.5 %collective-permute-start.54 = (bf16[512,256]{1,0:T(8,128)(2,1)S(1)}, bf16[512,256]{1,0:T(8,128)(2,1)S(1)}, u32[]{:S(2)}, u32[]{:S(2)}) collective-permute-start(bf16[512,256]{1,0:T(8,128)(2,1)S(1)} %copy-done.79), channel_id=1, source_target_pairs={{0,2},{2,0},{1,3},{3,1},{4,6},{6,4},{5,7},{7,5},{8,10},{10,8},{9,1... | collective-permute-start | bytes 786440 | tf_op jit(solution)/shard_map/ppermute | solution.py:103
  808.8 7.3 collective-permute-start.55
  808.8 10.9 %collective-permute-start.49 = (bf16[512,384]{1,0:T(8,128)(2,1)}, bf16[512,384]{1,0:T(8,128)(2,1)S(1)}, u32[]{:S(2)}, u32[]{:S(2)}) collective-permute-start(bf16[512,384]{1,0:T(8,128)(2,1)} %reduce-scatter.15.cloned.1.call-done.refs_4_), channel_id=1, source_target_pairs={{0,2},{2,0},{1,3},{3,1},{4,6},{6,4},{5,7},{7,5},{8,10},{10,8},{9,1... | collective-permute-start | bytes 1179656 | tf_op jit(solution)/shard_map/ppermute | solution.py:103
  809.3 10.4 %collective-permute-start.46 = (bf16[512,384]{1,0:T(8,128)(2,1)S(1)}, bf16[512,384]{1,0:T(8,128)(2,1)S(1)}, u32[]{:S(2)}, u32[]{:S(2)}) collective-permute-start(bf16[512,384]{1,0:T(8,128)(2,1)S(1)} %copy-done.77), channel_id=1, source_target_pairs={{0,2},{2,0},{1,3},{3,1},{4,6},{6,4},{5,7},{7,5},{8,10},{10,8},{9,1... | collective-permute-start | bytes 1179656 | tf_op jit(solution)/shard_map/ppermute | solution.py:103
  809.4 10.3 %collective-permute-start.50 = (bf16[512,384]{1,0:T(8,128)(2,1)S(1)}, bf16[512,384]{1,0:T(8,128)(2,1)S(1)}, u32[]{:S(2)}, u32[]{:S(2)}) collective-permute-start(bf16[512,384]{1,0:T(8,128)(2,1)S(1)} %collective-permute-done.48.refs_5_), channel_id=1, source_target_pairs={{0,2},{2,0},{1,3},{3,1},{4,6},{6,4},{5,7},{7,5},{8,10},{10,8},{9,1... | collective-permute-start | bytes 1179656 | tf_op jit(solution)/shard_map/ppermute | solution.py:103
  810.5 9.2 %collective-permute-start.47 = (bf16[512,384]{1,0:T(8,128)(2,1)S(1)}, bf16[512,384]{1,0:T(8,128)(2,1)S(1)}, u32[]{:S(2)}, u32[]{:S(2)}) collective-permute-start(bf16[512,384]{1,0:T(8,128)(2,1)S(1)} %collective-permute-done.45.refs_1_), channel_id=1, source_target_pairs={{0,2},{2,0},{1,3},{3,1},{4,6},{6,4},{5,7},{7,5},{8,10},{10,8},{9,1... | collective-permute-start | bytes 1179656 | tf_op jit(solution)/shard_map/ppermute | solution.py:103
  (138 other events, 1054.2 us)
Sparse Core Ops, SparseCore 0:
  13.1 66.6 all-gather.5
  81.9 26.2 all-gather.7
  110.4 63.0 all-gather.9
  175.4 62.1 all-gather.11
  239.0 62.1 all-gather.13
  390.6 54.8 reduce-scatter.6
  447.8 56.0 reduce-scatter.8
  506.1 56.0 reduce-scatter.10
  689.9 35.5 reduce-scatter.12
  728.2 26.1 reduce-scatter.16
  757.4 35.6 reduce-scatter.14

commit v5 on v4

--- a/solution.py
+++ b/solution.py
@@ -955,7 +955,7 @@
     grad_joint.append(over_shard(joint_total))
     steps.wait(grad_joint[0])
     out_gate = steps(
-        lambda pieces: lay_units(places, pieces, True, 1000), pieces_of(grad_gate.T, fourth_own[1])
+        lambda pieces: lay_units(places, pieces, True, 1000), pieces_of(grad_gate.T, joint_total)
     )
 
     def input_back(pair, d_resid, hidden):

time: 839 us -> 835 us (level)
    ppermute x6, waiting for transfers between devices: 65.5 us -> 17.4 us  [pieces_of(): across = lax.ppermute(own, 'cx', SWAP)]
    ppermute x9, waiting for transfers between devices: 85.5 us -> 119 us  [across(): return lax.ppermute(part, 'cx', SWAP)]
    unnamed x275 -> x279, local copies, waits for them, and re-layouts: 76.8 us -> 78.7 us
  transfers between devices with their start and end apart: 70 -> 70, of which waited for: 28 -> 30; matrix products, arithmetic and copies ran while one was open for 15% -> 15% of each run, Pallas kernels for 26% -> 26%
where the time goes in v5:
time: 835 us; the launch traced here: 825 us
  Pallas kernels  281 us (34%)
  waiting for transfers between devices  260 us (31%)
  local copies, waits for them, and re-layouts  114 us (14%)
  other arithmetic  64.6 us (8%)
  starting transfers between devices  56.3 us (7%)
  matrix products  19.7 us (2%)
  between operations  15.7 us (2%)
  blocking collectives  13.9 us (2%)
    ppermute x9, waiting for transfers between devices, across(): return lax.ppermute(part, 'cx', SWAP)  119 us
    unnamed x279, local copies, waits for them, and re-layouts  78.7 us
    pallas_call x12, Pallas kernels, rows_products(): pl.pallas_call(kernel, grid=(columns // tile,), in_specs=lefts + rights +...  69.1 us
    pallas_call x9, Pallas kernels, token_products(): pl.pallas_call(kernel, grid=(height // tile,), in_specs=lefts + rights +...  59.1 us
    ppermute x4, waiting for transfers between devices, with_tp(): return (part, lax.ppermute(part, 'tp', SWAP))  50.3 us
    pallas_call x2, Pallas kernels, one(): call(functools.partial(forward_one, size=size, own=own), grid, conv_specs...  37.7 us
    pallas_call x2, Pallas kernels, four(): call(functools.partial(backward_two, size=size, own=own), grid, conv_spec...  33 us
    pallas_call x2, Pallas kernels, feed_forward(): pl.pallas_call(kernel, grid=(tokens // tile,), in_specs=[token_spec] * 2...  30.8 us
  transfers between devices with their start and end apart: 70, of which 30 were waited for; matrix products, arithmetic and copies ran while one was open for 15% of the time, Pallas kernels for 26%

profile of v5, /device:TPU:0, one launch (start us, length us, event | category | flops | bytes accessed | tf_op | source)
XLA Modules:
  0.0 825.2 jit_solution(15164154218131446327)
XLA Ops:
  17.6 13.9 %all_gather.18 = bf16[4,80,128]{2,1,0:T(8,128)(2,1)S(1)} all-gather(bf16[1,80,128]{2,1,0:T(8,128)(2,1)S(1)} %pad_bitcast_fusion), channel_id=1, replica_groups=mesh['shard'=4,'cx'=2,'core'=2,'tp'=2] {'shard'}, dimensions={0}, use_global_device_ids=true | all-gather | bytes 102400 | tf_op jit(solution)/shard_map/all_gather | solution.py:737
  42.3 20.3 %collective-permute-done.4 = bf16[512,2048]{1,0:T(8,128)(2,1)} collective-permute-done((bf16[512,2048]{1,0:T(8,128)(2,1)}, bf16[512,2048]{1,0:T(8,128)(2,1)}, u32[]{:S(2)}, u32[]{:S(2)}) %collective-permute-start.4) | collective-permute-done | bytes 2097184 | tf_op jit(solution)/shard_map/ppermute | solution.py:715
  72.7 4.4 collective-permute-start.3
  91.3 6.8 convolution_convert_fusion.1.q0.k0.v0.q1.k1.v1.qh.kh.vh
  98.1 18.8 %shard_map.255 = (bf16[2,2,256,256]{3,2,1,0:T(8,128)(2,1)S(1)}, bf16[2,2,256,256]{3,2,1,0:T(8,128)(2,1)S(1)}, bf16[2,2,256,256]{3,2,1,0:T(8,128)(2,1)S(1)}, bf16...) custom-call(s32[2]{0:T(128)S(1)} %pad_add_fusion.1.where, ...), custom_call_target="tpu_custom_call" | custom-call | flops 1000 | bytes 1000 | tf_op jit(solution)/shard_map/pallas_call | solution.py:469
  121.7 34.1 %collective-permute-done.6.refs_4_ = bf16[2048,768]{1,0:T(8,128)(2,1)} collective-permute-done((bf16[2048,768]{1,0:T(8,128)(2,1)}, bf16[2048,768]{1,0:T(8,128)(2,1)}, u32[]{:S(2)}, u32[]{:S(2)}) %collective-permute-start.6) | collective-permute-done | bytes 3145760 | tf_op jit(solution)/shard_map/ppermute | solution.py:715
  158.3 6.7 convolution_convert_fusion.q0.k0.v0.q1.k1.v1.qh.kh.vh
  165.0 18.9 %shard_map.256 = (bf16[2,2,256,256]{3,2,1,0:T(8,128)(2,1)S(1)}, bf16[2,2,256,256]{3,2,1,0:T(8,128)(2,1)S(1)}, bf16[2,2,256,256]{3,2,1,0:T(8,128)(2,1)S(1)}, bf16...) custom-call(s32[2]{0:T(128)S(1)} %pad_add_fusion.1.where, ...), custom_call_target="tpu_custom_call" | custom-call | flops 1000 | bytes 1000 | tf_op jit(solution)/shard_map/pallas_call | solution.py:469
  193.7 6.1 shard_map.257
  205.2 6.1 shard_map.258
  215.0 5.9 collective-permute-done.10.refs_4_
  222.2 4.6 shard_map.260
  232.1 4.9 pad_maximum_fusion.2.grads_ref.refs_0_
  237.5 4.2 bitcast_convert_fusion
  241.7 33.2 %collective-permute-done.11 = bf16[512,2048]{1,0:T(8,128)(2,1)} collective-permute-done((bf16[512,2048]{1,0:T(8,128)(2,1)}, bf16[512,2048]{1,0:T(8,128)(2,1)}, u32[]{:S(2)}, u32[]{:S(2)}) %collective-permute-start.11) | collective-permute-done | bytes 2097184 | tf_op jit(solution)/shard_map/ppermute | solution.py:811
  274.9 4.4 multiply_reduce_fusion.6
  283.1 4.4 collective-permute-done.12
  287.4 4.2 pad_maximum_fusion.1.rows_ref.refs_0_
  291.6 9.6 %all-gather.14.cloned.1.call-done.downs_ref.refs_1_ = bf16[2048,704]{1,0:T(8,128)(2,1)} async-done(((bf16[512,704]{1,0:T(8,128)(2,1)}), bf16[2048,704]{1,0:T(8,128)(2,1)}) %all-gather.14.cloned.1.call-update) | async-done | bytes 2883600 | tf_op jit(solution)/shard_map/all_gather | solution.py:709
  301.2 15.4 %shard_map.261 = (bf16[1024,704]{1,0:T(8,128)(2,1)S(1)}, bf16[1024,704]{1,0:T(8,128)(2,1)S(1)}, bf16[1024,704]{1,0:T(8,128)(2,1)S(1)}) custom-call(bf16[1024,2048]{1,0:T(8,128)(2,1)} %pad_maximum_fusion.1.rows_ref.refs_0_, bf16[1024,2048]{1,0:T(8,128)(2,1)} %pad_maximum_fusion.2.grads_ref.refs_0_, ...), custom_call_target="tpu_custom_call" | custom-call | flops 1000 | bytes 1000 | tf_op jit(solution)/shard_map/pallas_call | solution.py:624
  316.7 7.1 shard_map.262
  325.1 4.2 shard_map.263
  340.2 15.4 %shard_map.264 = (bf16[1024,704]{1,0:T(8,128)(2,1)S(1)}, bf16[1024,704]{1,0:T(8,128)(2,1)S(1)}, bf16[1024,704]{1,0:T(8,128)(2,1)S(1)}) custom-call(bf16[1024,2048]{1,0:T(8,128)(2,1)} %copy-done.114, bf16[1024,2048]{1,0:T(8,128)(2,1)} %constant_dynamic-update-slice_fusion.grads_ref.refs_1_, bf16[2048,704]{1,0:T(8,128)(2,1)} %all-gather.12.cloned.1.call-done.gates_ref.refs_2_, ...), custom_call_target="tpu_custom_call" | custom-call | flops 1000 | bytes 1000 | tf_op jit(solution)/shard_map/pallas_call | solution.py:624
  355.7 7.1 shard_map.265
  363.0 4.0 collective-permute-done.18.refs_4_
  368.3 6.3 shard_map.266
  376.0 9.8 %shard_map.267 = bf16[2048,704]{1,0:T(8,128)(2,1)} custom-call(bf16[1024,2048]{1,0:T(8,128)(2,1)} %pad_maximum_fusion.2.grads_ref.refs_0_, bf16[1024,2048]{1,0:T(8,128)(2,1)} %constant_dynamic-update-slice_fusion.grads_ref.refs_1_, bf16[1024,704]{1,0:T(8,128)(2,1)S(1)} %get-tuple-element.356.refs_0_.refs_2_, ...), custom_call_target="tpu_custom_call" | custom-call | flops 1000 | bytes 1000 | tf_op jit(solution)/shard_map/pallas_call | solution.py:596
  385.8 4.7 copy.105
  398.1 7.4 shard_map.268
  405.5 5.3 shard_map.269
  411.0 10.0 %shard_map.270 = bf16[2048,704]{1,0:T(8,128)(2,1)} custom-call(bf16[1024,2048]{1,0:T(8,128)(2,1)} %pad_maximum_fusion.1.rows_ref.refs_0_, bf16[1024,2048]{1,0:T(8,128)(2,1)} %copy-done.114, bf16[1024,704]{1,0:T(8,128)(2,1)S(1)} %copy-done.15, bf16[1024,704]{1,0:T(8,128)(2,1)S(1)} %copy-done.10), custom_call_target="tpu_custom_call" | custom-call | flops 1000 | bytes 1000 | tf_op jit(solution)/shard_map/pallas_call | solution.py:596
  421.0 18.1 %collective-permute-done.20 = bf16[512,2048]{1,0:T(8,128)(2,1)S(1)} collective-permute-done((bf16[512,2048]{1,0:T(8,128)(2,1)}, bf16[512,2048]{1,0:T(8,128)(2,1)S(1)}, u32[]{:S(2)}, u32[]{:S(2)}) %collective-permute-start.20) | collective-permute-done | bytes 2097184 | tf_op jit(solution)/shard_map/ppermute | solution.py:715
  442.6 4.7 copy.108
  450.2 9.9 %shard_map.271 = bf16[2048,704]{1,0:T(8,128)(2,1)} custom-call(bf16[1024,2048]{1,0:T(8,128)(2,1)} %pad_maximum_fusion.1.rows_ref.refs_0_, bf16[1024,2048]{1,0:T(8,128)(2,1)} %copy-done.114, bf16[1024,704]{1,0:T(8,128)(2,1)S(1)} %copy-done.13, bf16[1024,704]{1,0:T(8,128)(2,1)S(1)} %copy-done.8), custom_call_target="tpu_custom_call" | custom-call | flops 1000 | bytes 1000 | tf_op jit(solution)/shard_map/pallas_call | solution.py:596
  460.1 5.7 shard_map.272
  465.8 5.7 shard_map.273
  471.5 17.1 %collective-permute-done.22 = bf16[512,2048]{1,0:T(8,128)(2,1)} collective-permute-done((bf16[512,2048]{1,0:T(8,128)(2,1)}, bf16[512,2048]{1,0:T(8,128)(2,1)}, u32[]{:S(2)}, u32[]{:S(2)}) %collective-permute-start.22) | collective-permute-done | bytes 2097184 | tf_op jit(solution)/shard_map/ppermute | solution.py:811
  489.0 4.2 multiply_reduce_fusion
  493.2 5.5 fusion.25
  500.2 4.6 copy.110
  516.3 7.1 shard_map.274
  524.3 7.8 shard_map.275
  536.1 11.0 %collective-permute-done.21 = bf16[512,2048]{1,0:T(8,128)(2,1)} collective-permute-done((bf16[512,2048]{1,0:T(8,128)(2,1)}, bf16[512,2048]{1,0:T(8,128)(2,1)}, u32[]{:S(2)}, u32[]{:S(2)}) %collective-permute-start.21) | collective-permute-done | bytes 2097184 | tf_op jit(solution)/shard_map/ppermute | solution.py:715
  560.2 14.0 %collective-permute-done.25.rest_8_ = bf16[2,2,128,128]{3,2,1,0:T(8,128)(2,1)S(1)} collective-permute-done((bf16[2,2,128,128]{3,2,1,0:T(8,128)(2,1)}, bf16[2,2,128,128]{3,2,1,0:T(8,128)(2,1)S(1)}, u32[]{:S(2)}, u32[]{:S(2)}) %collective-permute-start.25) | collective-permute-done | bytes 131104 | tf_op jit(solution)/shard_map/ppermute | solution.py:875
  582.3 16.4 %shard_map.277 = (bf16[2,2,256,768]{3,2,1,0:T(8,128)(2,1)}, bf16[2,16,768]{2,1,0:T(8,128)(2,1)S(1)}, f32[2,2,256,128]{3,2,1,0:T(8,128)S(1)}, f32[2,3,2,4,128]{4,3,2,1,0:T(4,128)S(1)}) custom-call(s32[2]{0:T(128)S(1)} %pad_add_fusion.1.where, bf16[1056,768]{1,0:T(8,128)(2,1)} %copy-done.3, bf16[1056,768]{1,0:T(8,128)(2,1)} %copy-done.3, ...), custom_call_target="tpu_custom_call" | custom-call | flops 28600000512 | bytes 1000 | tf_op jit(solution)/shard_map/pallas_call | solution.py:502
  604.0 4.6 shard_map.278
  610.5 6.0 shard_map.279
  619.3 5.1 shard_map.280
  632.0 16.6 %shard_map.281 = (bf16[2,2,256,768]{3,2,1,0:T(8,128)(2,1)}, bf16[2,16,768]{2,1,0:T(8,128)(2,1)S(1)}, f32[2,2,256,128]{3,2,1,0:T(8,128)S(1)}, f32[2,3,2,4,128]{4,3,2,1,0:T(4,128)S(1)}) custom-call(s32[2]{0:T(128)S(1)} %pad_add_fusion.1.where, bf16[1056,768]{1,0:T(8,128)(2,1)} %copy-done.2, bf16[1056,768]{1,0:T(8,128)(2,1)} %copy-done.2, ...), custom_call_target="tpu_custom_call" | custom-call | flops 28600000512 | bytes 1000 | tf_op jit(solution)/shard_map/pallas_call | solution.py:502
  649.9 4.8 add_convert_fusion
  656.4 6.9 shard_map.282
  663.4 4.1 collective-permute-done.35.refs_6_
  670.2 6.7 shard_map.283
  676.9 4.1 shard_map.284
  683.3 5.4 shard_map.285
  694.7 33.4 %collective-permute-done.39.refs_4_ = bf16[2048,384]{1,0:T(8,128)(2,1)} collective-permute-done((bf16[2048,384]{1,0:T(8,128)(2,1)}, bf16[2048,384]{1,0:T(8,128)(2,1)}, u32[]{:S(2)}, u32[]{:S(2)}) %collective-permute-start.39) | collective-permute-done | bytes 1572896 | tf_op jit(solution)/shard_map/ppermute | solution.py:715
  729.3 5.6 shard_map.286
  736.1 7.0 collective-permute-done.37.b
  748.6 5.4 shard_map.287
  761.3 7.2 collective-permute-done.53.b
  768.9 5.9 collective-permute-done.43
  775.0 6.8 fusion.5
  783.4 9.6 %reduce-scatter.15.cloned.1.call-done.refs_4_ = bf16[512,384]{1,0:T(8,128)(2,1)} async-done(((bf16[2048,384]{1,0:T(8,128)(2,1)}), bf16[512,384]{1,0:T(8,128)(2,1)}) %reduce-scatter.15.cloned.1.call-update) | async-done | bytes 393232 | tf_op jit(solution)/shard_map/reduce_scatter | solution.py:712
  805.7 5.5 shard_map.289
  (521 shorter events, 218.7 us)
Async XLA Ops:
  7.2 77.6 %all-gather.6.cloned.1.call-start = ((), (), s32[]{:S(2)}) async-start(), calls=%async_computation.6 | async-start | bytes 3932160 | tf_op jit(solution)/shard_map/all_gather | solution.py:709
  12.9 142.8 %all-gather.8.cloned.1.call-start = ((), (), s32[]{:S(2)}) async-start(), calls=%async_computation.7 | async-start | bytes 1310720 | tf_op jit(solution)/shard_map/all_gather | solution.py:709
  13.0 24.4 %collective-permute-start = (bf16[512,2048]{1,0:T(8,128)(2,1)S(1)}, bf16[512,2048]{1,0:T(8,128)(2,1)}, u32[]{:S(2)}, u32[]{:S(2)}) collective-permute-start(bf16[512,2048]{1,0:T(8,128)(2,1)S(1)} %bitcast.112), channel_id=1, source_target_pairs={{0,2},{2,0},{1,3},{3,1},{4,6},{6,4},{5,7},{7,5},{8,10},{10,8},{9,1... | collective-permute-start | bytes 6291464 | tf_op jit(solution)/shard_map/ppermute | solution.py:718
  13.5 49.1 %collective-permute-start.4 = (bf16[512,2048]{1,0:T(8,128)(2,1)}, bf16[512,2048]{1,0:T(8,128)(2,1)}, u32[]{:S(2)}, u32[]{:S(2)}) collective-permute-start(bf16[512,2048]{1,0:T(8,128)(2,1)} %bitcast.9), channel_id=1, source_target_pairs={{0,4},{4,0},{1,5},{5,1},{2,6},{6,2},{3,7},{7,3},{8,12},{12,8},{9,1... | collective-permute-start | bytes 6291464 | tf_op jit(solution)/shard_map/ppermute | solution.py:715
  17.0 224.7 %all-gather.10.cloned.1.call-start = ((), (), s32[]{:S(2)}) async-start(), calls=%async_computation.8 | async-start | bytes 3932160 | tf_op jit(solution)/shard_map/all_gather | solution.py:709
  39.3 25.3 %collective-permute-start.1 = (bf16[2,16,2048]{2,1,0:T(8,128)(2,1)S(1)}, bf16[2,16,2048]{2,1,0:T(8,128)(2,1)S(1)}, u32[]{:S(2)}, u32[]{:S(2)}) collective-permute-start(bf16[2,16,2048]{2,1,0:T(8,128)(2,1)S(1)} %slice.109), channel_id=1, source_target_pairs={{0,4},{1,5},{2,6},{3,7},{8,12},{9,13},{10,14},{11,15},{16,20},{17,... | collective-permute-start | bytes 393224 | tf_op jit(solution)/shard_map/ppermute | solution.py:759
  62.6 19.1 %collective-permute-start.5 = (bf16[512,2048]{1,0:T(8,128)(2,1)}, bf16[512,2048]{1,0:T(8,128)(2,1)}, u32[]{:S(2)}, u32[]{:S(2)}) collective-permute-start(bf16[512,2048]{1,0:T(8,128)(2,1)} %collective-permute-done.4), channel_id=1, source_target_pairs={{0,2},{2,0},{1,3},{3,1},{4,6},{6,4},{5,7},{7,5},{8,10},{10,8},{9,1... | collective-permute-start | bytes 6291464 | tf_op jit(solution)/shard_map/ppermute | solution.py:718
  71.4 220.2 %all-gather.12.cloned.1.call-start = ((), (), s32[]{:S(2)}) async-start(), calls=%async_computation.9 | async-start | bytes 3932160 | tf_op jit(solution)/shard_map/all_gather | solution.py:709
  72.7 5.7 collective-permute-start.3
  84.8 70.9 %collective-permute-start.6 = (bf16[2048,768]{1,0:T(8,128)(2,1)}, bf16[2048,768]{1,0:T(8,128)(2,1)}, u32[]{:S(2)}, u32[]{:S(2)}) collective-permute-start(bf16[2048,768]{1,0:T(8,128)(2,1)} %all-gather.6.cloned.1.call-done.refs_3_), channel_id=1, source_target_pairs={{0,4},{4,0},{1,5},{5,1},{2,6},{6,2},{3,7},{7,3},{8,12},{12,8},{9,1... | collective-permute-start | bytes 9437192 | tf_op jit(solution)/shard_map/ppermute | solution.py:715
  91.0 210.2 %all-gather.14.cloned.1.call-start = ((), (), s32[]{:S(2)}) async-start(), calls=%async_computation.10 | async-start | bytes 3932160 | tf_op jit(solution)/shard_map/all_gather | solution.py:709
  119.5 69.8 %collective-permute-start.8 = (bf16[2,2,128,128]{3,2,1,0:T(8,128)(2,1)S(1)}, bf16[2,2,128,128]{3,2,1,0:T(8,128)(2,1)S(1)}, u32[]{:S(2)}, u32[]{:S(2)}) collective-permute-start(bf16[2,2,128,128]{3,2,1,0:T(8,128)(2,1)S(1)} %get-tuple-element.256), channel_id=1, source_target_pairs={{0,4},{1,5},{2,6},{3,7},{8,12},{9,13},{10,14},{11,15},{16,20},{17,... | collective-permute-start | bytes 393224 | tf_op jit(solution)/shard_map/ppermute | solution.py:790
  155.8 56.6 %collective-permute-start.9 = (bf16[2048,256]{1,0:T(8,128)(2,1)}, bf16[2048,256]{1,0:T(8,128)(2,1)S(1)}, u32[]{:S(2)}, u32[]{:S(2)}) collective-permute-start(bf16[2048,256]{1,0:T(8,128)(2,1)} %all-gather.8.cloned.1.call-done.refs_2_), channel_id=1, source_target_pairs={{0,4},{4,0},{1,5},{5,1},{2,6},{6,2},{3,7},{7,3},{8,12},{12,8},{9,1... | collective-permute-start | bytes 3145736 | tf_op jit(solution)/shard_map/ppermute | solution.py:715
  187.3 14.3 %collective-permute-start.7 = (bf16[2,2,128,128]{3,2,1,0:T(8,128)(2,1)S(1)}, bf16[2,2,128,128]{3,2,1,0:T(8,128)(2,1)S(1)}, u32[]{:S(2)}, u32[]{:S(2)}) collective-permute-start(bf16[2,2,128,128]{3,2,1,0:T(8,128)(2,1)S(1)} %get-tuple-element.260), channel_id=1, source_target_pairs={{0,4},{1,5},{2,6},{3,7},{8,12},{9,13},{10,14},{11,15},{16,20},{17,... | collective-permute-start | bytes 393224 | tf_op jit(solution)/shard_map/ppermute | solution.py:791
  214.4 6.4 collective-permute-start.10
  214.5 17.6 %collective-permute-start.13 = (bf16[512,2048]{1,0:T(8,128)(2,1)}, bf16[512,2048]{1,0:T(8,128)(2,1)}, u32[]{:S(2)}, u32[]{:S(2)}) collective-permute-start(bf16[512,2048]{1,0:T(8,128)(2,1)} %bitcast.9), channel_id=1, source_target_pairs={{0,2},{2,0},{1,3},{3,1},{4,6},{6,4},{5,7},{7,5},{8,10},{10,8},{9,1... | collective-permute-start | bytes 6291464 | tf_op jit(solution)/shard_map/ppermute | solution.py:718
  226.9 48.1 %collective-permute-start.11 = (bf16[512,2048]{1,0:T(8,128)(2,1)}, bf16[512,2048]{1,0:T(8,128)(2,1)}, u32[]{:S(2)}, u32[]{:S(2)}) collective-permute-start(bf16[512,2048]{1,0:T(8,128)(2,1)} %shard_map.260), channel_id=1, source_target_pairs={{0,1},{1,0},{2,3},{3,2},{4,5},{5,4},{6,7},{7,6},{8,9},{9,8},{10,11... | collective-permute-start | bytes 6291464 | tf_op jit(solution)/shard_map/ppermute | solution.py:811
  237.0 276.0 %reduce-scatter.7.cloned.1.call-start = ((), (), s32[]{:S(2)}) async-start(), calls=%async_computation.11 | async-start | bytes 3604480 | tf_op jit(solution)/shard_map/reduce_scatter | solution.py:712
  283.0 4.4 collective-permute-start.12
  283.1 48.4 %collective-permute-start.15 = (bf16[512,2048]{1,0:T(8,128)(2,1)}, bf16[512,2048]{1,0:T(8,128)(2,1)}, u32[]{:S(2)}, u32[]{:S(2)}) collective-permute-start(bf16[512,2048]{1,0:T(8,128)(2,1)} %multiply_convert_fusion), channel_id=1, source_target_pairs={{0,4},{4,0},{1,5},{5,1},{2,6},{6,2},{3,7},{7,3},{8,12},{12,8},{9,1... | collective-permute-start | bytes 6291464 | tf_op jit(solution)/shard_map/ppermute | solution.py:715
  329.3 4.2 collective-permute-start.14
  333.6 4.4 collective-permute-start.16
  362.8 4.2 collective-permute-start.18
  390.5 169.7 %reduce-scatter.9.cloned.1.call-start = ((), (), s32[]{:S(2)}) async-start(), calls=%async_computation.12 | async-start | bytes 3604480 | tf_op jit(solution)/shard_map/reduce_scatter | solution.py:712
  390.7 4.4 collective-permute-start.17
  390.9 48.1 %collective-permute-start.20 = (bf16[512,2048]{1,0:T(8,128)(2,1)}, bf16[512,2048]{1,0:T(8,128)(2,1)S(1)}, u32[]{:S(2)}, u32[]{:S(2)}) collective-permute-start(bf16[512,2048]{1,0:T(8,128)(2,1)} %copy-done.35), channel_id=1, source_target_pairs={{0,4},{4,0},{1,5},{5,1},{2,6},{6,2},{3,7},{7,3},{8,12},{12,8},{9,1... | collective-permute-start | bytes 6291464 | tf_op jit(solution)/shard_map/ppermute | solution.py:715
  410.8 49.3 %collective-permute-start.19 = (bf16[512,2048]{1,0:T(8,128)(2,1)}, bf16[512,2048]{1,0:T(8,128)(2,1)}, u32[]{:S(2)}, u32[]{:S(2)}) collective-permute-start(bf16[512,2048]{1,0:T(8,128)(2,1)} %shard_map.269), channel_id=1, source_target_pairs={{0,2},{2,0},{1,3},{3,1},{4,6},{6,4},{5,7},{7,5},{8,10},{10,8},{9,1... | collective-permute-start | bytes 6291464 | tf_op jit(solution)/shard_map/ppermute | solution.py:718
  441.1 47.5 %collective-permute-start.22 = (bf16[512,2048]{1,0:T(8,128)(2,1)}, bf16[512,2048]{1,0:T(8,128)(2,1)}, u32[]{:S(2)}, u32[]{:S(2)}) collective-permute-start(bf16[512,2048]{1,0:T(8,128)(2,1)} %add_convert_fusion.2), channel_id=1, source_target_pairs={{0,1},{1,0},{2,3},{3,2},{4,5},{5,4},{6,7},{7,6},{8,9},{9,8},{10,11... | collective-permute-start | bytes 6291464 | tf_op jit(solution)/shard_map/ppermute | solution.py:811
  447.3 178.3 %reduce-scatter.11.cloned.1.call-start = ((), (), s32[]{:S(2)}) async-start(), calls=%async_computation.13 | async-start | bytes 3604480 | tf_op jit(solution)/shard_map/reduce_scatter | solution.py:712
  498.7 6.4 collective-permute-start.23
  498.7 48.4 %collective-permute-start.21 = (bf16[512,2048]{1,0:T(8,128)(2,1)}, bf16[512,2048]{1,0:T(8,128)(2,1)}, u32[]{:S(2)}, u32[]{:S(2)}) collective-permute-start(bf16[512,2048]{1,0:T(8,128)(2,1)} %shard_map.272), channel_id=1, source_target_pairs={{0,4},{4,0},{1,5},{5,1},{2,6},{6,2},{3,7},{7,3},{8,12},{12,8},{9,1... | collective-permute-start | bytes 6291464 | tf_op jit(solution)/shard_map/ppermute | solution.py:715
  504.9 241.5 %reduce-scatter.13.cloned.1.call-start = ((), (), s32[]{:S(2)}) async-start(), calls=%async_computation.14 | async-start | bytes 1966080 | tf_op jit(solution)/shard_map/reduce_scatter | solution.py:712
  550.7 5.6 collective-permute-start.27
  552.3 47.2 %collective-permute-start.28 = (bf16[704,512]{1,0:T(8,128)(2,1)S(1)}, bf16[704,512]{1,0:T(8,128)(2,1)}, u32[]{:S(2)}, u32[]{:S(2)}) collective-permute-start(bf16[704,512]{1,0:T(8,128)(2,1)S(1)} %bitcast.103), channel_id=1, source_target_pairs={{0,4},{4,0},{1,5},{5,1},{2,6},{6,2},{3,7},{7,3},{8,12},{12,8},{9,1... | collective-permute-start | bytes 2162696 | tf_op jit(solution)/shard_map/ppermute | solution.py:101
  553.8 48.3 %collective-permute-start.29 = (bf16[704,512]{1,0:T(8,128)(2,1)S(1)}, bf16[704,512]{1,0:T(8,128)(2,1)}, u32[]{:S(2)}, u32[]{:S(2)}) collective-permute-start(bf16[704,512]{1,0:T(8,128)(2,1)S(1)} %bitcast.104), channel_id=1, source_target_pairs={{0,2},{2,0},{1,3},{3,1},{4,6},{6,4},{5,7},{7,5},{8,10},{10,8},{9,1... | collective-permute-start | bytes 2162696 | tf_op jit(solution)/shard_map/ppermute | solution.py:103
  553.8 20.4 %collective-permute-start.25 = (bf16[2,2,128,128]{3,2,1,0:T(8,128)(2,1)}, bf16[2,2,128,128]{3,2,1,0:T(8,128)(2,1)S(1)}, u32[]{:S(2)}, u32[]{:S(2)}) collective-permute-start(bf16[2,2,128,128]{3,2,1,0:T(8,128)(2,1)} %get-tuple-element.383), channel_id=1, source_target_pairs={{4,0},{5,1},{6,2},{7,3},{12,8},{13,9},{14,10},{15,11},{20,16},{21,... | collective-permute-start | bytes 393224 | tf_op jit(solution)/shard_map/ppermute | solution.py:875
  555.0 22.0 %collective-permute-start.26 = (bf16[2,2,128,128]{3,2,1,0:T(8,128)(2,1)S(1)}, bf16[2,2,128,128]{3,2,1,0:T(8,128)(2,1)}, u32[]{:S(2)}, u32[]{:S(2)}) collective-permute-start(bf16[2,2,128,128]{3,2,1,0:T(8,128)(2,1)S(1)} %get-tuple-element.375), channel_id=1, source_target_pairs={{4,0},{5,1},{6,2},{7,3},{12,8},{13,9},{14,10},{15,11},{20,16},{21,... | collective-permute-start | bytes 393224 | tf_op jit(solution)/shard_map/ppermute | solution.py:873
  556.4 69.2 %collective-permute-start.31 = (bf16[2048,256]{1,0:T(8,128)(2,1)}, bf16[2048,256]{1,0:T(8,128)(2,1)}, u32[]{:S(2)}, u32[]{:S(2)}) collective-permute-start(bf16[2048,256]{1,0:T(8,128)(2,1)} %shard_map.276), channel_id=1, source_target_pairs={{0,4},{4,0},{1,5},{5,1},{2,6},{6,2},{3,7},{7,3},{8,12},{12,8},{9,1... | collective-permute-start | bytes 3145736 | tf_op jit(solution)/shard_map/ppermute | solution.py:715
  601.5 48.4 %collective-permute-start.24 = (bf16[512,2048]{1,0:T(8,128)(2,1)}, bf16[512,2048]{1,0:T(8,128)(2,1)}, u32[]{:S(2)}, u32[]{:S(2)}) collective-permute-start(bf16[512,2048]{1,0:T(8,128)(2,1)} %add_convert_fusion.1), channel_id=1, source_target_pairs={{0,1},{1,0},{2,3},{3,2},{4,5},{5,4},{6,7},{7,6},{8,9},{9,8},{10,11... | collective-permute-start | bytes 6291464 | tf_op jit(solution)/shard_map/ppermute | solution.py:811
  608.7 46.9 %collective-permute-start.32 = (bf16[2,16,768]{2,1,0:T(8,128)(2,1)S(1)}, bf16[2,16,768]{2,1,0:T(8,128)(2,1)S(1)}, u32[]{:S(2)}, u32[]{:S(2)}) collective-permute-start(bf16[2,16,768]{2,1,0:T(8,128)(2,1)S(1)} %get-tuple-element.413), channel_id=1, source_target_pairs={{4,0},{5,1},{6,2},{7,3},{12,8},{13,9},{14,10},{15,11},{20,16},{21,... | collective-permute-start | bytes 147464 | tf_op jit(solution)/shard_map/ppermute | solution.py:896
  616.6 38.2 %collective-permute-start.33 = (bf16[2048,384]{1,0:T(8,128)(2,1)}, bf16[2048,384]{1,0:T(8,128)(2,1)}, u32[]{:S(2)}, u32[]{:S(2)}) collective-permute-start(bf16[2048,384]{1,0:T(8,128)(2,1)} %shard_map.279), channel_id=1, source_target_pairs={{0,4},{4,0},{1,5},{5,1},{2,6},{6,2},{3,7},{7,3},{8,12},{12,8},{9,1... | collective-permute-start | bytes 4718600 | tf_op jit(solution)/shard_map/ppermute | solution.py:715
  648.6 7.7 collective-permute-start.34
  663.3 4.2 collective-permute-start.35
  689.9 69.2 %reduce-scatter.17.cloned.1.call-start = ((), (), s32[]{:S(2)}) async-start(), calls=%async_computation.16 | async-start | bytes 1310720 | tf_op jit(solution)/shard_map/reduce_scatter | solution.py:712
  689.9 38.2 %collective-permute-start.39 = (bf16[2048,384]{1,0:T(8,128)(2,1)}, bf16[2048,384]{1,0:T(8,128)(2,1)}, u32[]{:S(2)}, u32[]{:S(2)}) collective-permute-start(bf16[2048,384]{1,0:T(8,128)(2,1)} %copy-done.36), channel_id=1, source_target_pairs={{0,4},{4,0},{1,5},{5,1},{2,6},{6,2},{3,7},{7,3},{8,12},{12,8},{9,1... | collective-permute-start | bytes 4718600 | tf_op jit(solution)/shard_map/ppermute | solution.py:715
  692.6 100.4 %reduce-scatter.15.cloned.1.call-start = ((), (), s32[]{:S(2)}) async-start(), calls=%async_computation.15 | async-start | bytes 1966080 | tf_op jit(solution)/shard_map/reduce_scatter | solution.py:712
  692.7 61.3 %collective-permute-start.36 = (bf16[512,2048]{1,0:T(8,128)(2,1)S(1)}, bf16[512,2048]{1,0:T(8,128)(2,1)}, u32[]{:S(2)}, u32[]{:S(2)}) collective-permute-start(bf16[512,2048]{1,0:T(8,128)(2,1)S(1)} %shard_map.283), channel_id=1, source_target_pairs={{0,1},{1,0},{2,3},{3,2},{4,5},{5,4},{6,7},{7,6},{8,9},{9,8},{10,11... | collective-permute-start | bytes 6291464 | tf_op jit(solution)/shard_map/ppermute | solution.py:811
  694.2 48.9 %collective-permute-start.37 = (bf16[704,512]{1,0:T(8,128)(2,1)}, bf16[704,512]{1,0:T(8,128)(2,1)}, u32[]{:S(2)}, u32[]{:S(2)}) collective-permute-start(bf16[704,512]{1,0:T(8,128)(2,1)} %bitcast.100), channel_id=1, source_target_pairs={{0,4},{4,0},{1,5},{5,1},{2,6},{6,2},{3,7},{7,3},{8,12},{12,8},{9,1... | collective-permute-start | bytes 2162696 | tf_op jit(solution)/shard_map/ppermute | solution.py:101
  694.7 50.3 %collective-permute-start.38 = (bf16[704,512]{1,0:T(8,128)(2,1)}, bf16[704,512]{1,0:T(8,128)(2,1)}, u32[]{:S(2)}, u32[]{:S(2)}) collective-permute-start(bf16[704,512]{1,0:T(8,128)(2,1)} %bitcast.101), channel_id=1, source_target_pairs={{0,2},{2,0},{1,3},{3,1},{4,6},{6,4},{5,7},{7,5},{8,10},{10,8},{9,1... | collective-permute-start | bytes 2162696 | tf_op jit(solution)/shard_map/ppermute | solution.py:103
  743.1 25.3 %collective-permute-start.56 = (bf16[704,512]{1,0:T(8,128)(2,1)}, bf16[704,512]{1,0:T(8,128)(2,1)}, u32[]{:S(2)}, u32[]{:S(2)}) collective-permute-start(bf16[704,512]{1,0:T(8,128)(2,1)} %bitcast.40.a), channel_id=1, source_target_pairs={{0,4},{4,0},{1,5},{5,1},{2,6},{6,2},{3,7},{7,3},{8,12},{12,8},{9,1... | collective-permute-start | bytes 2162696 | tf_op jit(solution)/shard_map/ppermute | solution.py:101
  759.1 9.4 %collective-permute-start.53 = (bf16[512,256]{1,0:T(8,128)(2,1)}, bf16[512,256]{1,0:T(8,128)(2,1)}, u32[]{:S(2)}, u32[]{:S(2)}) collective-permute-start(bf16[512,256]{1,0:T(8,128)(2,1)} %reduce-scatter.17.cloned.1.call-done.a), channel_id=1, source_target_pairs={{0,4},{4,0},{1,5},{5,1},{2,6},{6,2},{3,7},{7,3},{8,12},{12,8},{9,1... | collective-permute-start | bytes 786440 | tf_op jit(solution)/shard_map/ppermute | solution.py:101
  760.9 7.8 collective-permute-start.42
  761.3 43.1 %collective-permute-start.57 = (bf16[704,512]{1,0:T(8,128)(2,1)}, bf16[704,512]{1,0:T(8,128)(2,1)}, u32[]{:S(2)}, u32[]{:S(2)}) collective-permute-start(bf16[704,512]{1,0:T(8,128)(2,1)} %bitcast.40.a), channel_id=1, source_target_pairs={{0,2},{2,0},{1,3},{3,1},{4,6},{6,4},{5,7},{7,5},{8,10},{10,8},{9,1... | collective-permute-start | bytes 2162696 | tf_op jit(solution)/shard_map/ppermute | solution.py:103
  768.5 36.0 %collective-permute-start.58 = (bf16[704,512]{1,0:T(8,128)(2,1)}, bf16[704,512]{1,0:T(8,128)(2,1)}, u32[]{:S(2)}, u32[]{:S(2)}) collective-permute-start(bf16[704,512]{1,0:T(8,128)(2,1)} %collective-permute-done.56.b), channel_id=1, source_target_pairs={{0,2},{2,0},{1,3},{3,1},{4,6},{6,4},{5,7},{7,5},{8,10},{10,8},{9,1... | collective-permute-start | bytes 2162696 | tf_op jit(solution)/shard_map/ppermute | solution.py:103
  768.8 6.0 collective-permute-start.43
  774.8 19.6 %collective-permute-start.44 = (bf16[18560]{0:T(1024)(128)(2,1)S(1)}, bf16[18560]{0:T(1024)(128)(2,1)S(1)}, u32[]{:S(2)}, u32[]{:S(2)}) collective-permute-start(bf16[18560]{0:T(1024)(128)(2,1)S(1)} %add_convert_fusion.4), channel_id=1, source_target_pairs={{0,16},{8,24},{16,0},{24,8},{1,17},{9,25},{17,1},{25,9},{2,18},{10... | collective-permute-start | bytes 111368 | tf_op jit(solution)/shard_map/ppermute | solution.py:677
  781.8 22.1 %collective-permute-start.45 = (bf16[512,384]{1,0:T(8,128)(2,1)S(1)}, bf16[512,384]{1,0:T(8,128)(2,1)S(1)}, u32[]{:S(2)}, u32[]{:S(2)}) collective-permute-start(bf16[512,384]{1,0:T(8,128)(2,1)S(1)} %copy-done.79), channel_id=1, source_target_pairs={{0,4},{4,0},{1,5},{5,1},{2,6},{6,2},{3,7},{7,3},{8,12},{12,8},{9,1... | collective-permute-start | bytes 1179656 | tf_op jit(solution)/shard_map/ppermute | solution.py:101
  793.0 10.9 %collective-permute-start.48 = (bf16[512,384]{1,0:T(8,128)(2,1)}, bf16[512,384]{1,0:T(8,128)(2,1)S(1)}, u32[]{:S(2)}, u32[]{:S(2)}) collective-permute-start(bf16[512,384]{1,0:T(8,128)(2,1)} %reduce-scatter.15.cloned.1.call-done.refs_4_), channel_id=1, source_target_pairs={{0,4},{4,0},{1,5},{5,1},{2,6},{6,2},{3,7},{7,3},{8,12},{12,8},{9,1... | collective-permute-start | bytes 1179656 | tf_op jit(solution)/shard_map/ppermute | solution.py:101
  798.3 6.6 collective-permute-start.54
  803.9 7.3 collective-permute-start.55
  803.9 10.9 %collective-permute-start.49 = (bf16[512,384]{1,0:T(8,128)(2,1)}, bf16[512,384]{1,0:T(8,128)(2,1)S(1)}, u32[]{:S(2)}, u32[]{:S(2)}) collective-permute-start(bf16[512,384]{1,0:T(8,128)(2,1)} %reduce-scatter.15.cloned.1.call-done.refs_4_), channel_id=1, source_target_pairs={{0,2},{2,0},{1,3},{3,1},{4,6},{6,4},{5,7},{7,5},{8,10},{10,8},{9,1... | collective-permute-start | bytes 1179656 | tf_op jit(solution)/shard_map/ppermute | solution.py:103
  804.4 10.4 %collective-permute-start.46 = (bf16[512,384]{1,0:T(8,128)(2,1)S(1)}, bf16[512,384]{1,0:T(8,128)(2,1)S(1)}, u32[]{:S(2)}, u32[]{:S(2)}) collective-permute-start(bf16[512,384]{1,0:T(8,128)(2,1)S(1)} %copy-done.79), channel_id=1, source_target_pairs={{0,2},{2,0},{1,3},{3,1},{4,6},{6,4},{5,7},{7,5},{8,10},{10,8},{9,1... | collective-permute-start | bytes 1179656 | tf_op jit(solution)/shard_map/ppermute | solution.py:103
  804.5 10.3 %collective-permute-start.50 = (bf16[512,384]{1,0:T(8,128)(2,1)S(1)}, bf16[512,384]{1,0:T(8,128)(2,1)S(1)}, u32[]{:S(2)}, u32[]{:S(2)}) collective-permute-start(bf16[512,384]{1,0:T(8,128)(2,1)S(1)} %collective-permute-done.48.refs_5_), channel_id=1, source_target_pairs={{0,2},{2,0},{1,3},{3,1},{4,6},{6,4},{5,7},{7,5},{8,10},{10,8},{9,1... | collective-permute-start | bytes 1179656 | tf_op jit(solution)/shard_map/ppermute | solution.py:103
  805.6 9.2 %collective-permute-start.47 = (bf16[512,384]{1,0:T(8,128)(2,1)S(1)}, bf16[512,384]{1,0:T(8,128)(2,1)S(1)}, u32[]{:S(2)}, u32[]{:S(2)}) collective-permute-start(bf16[512,384]{1,0:T(8,128)(2,1)S(1)} %collective-permute-done.45.refs_1_), channel_id=1, source_target_pairs={{0,2},{2,0},{1,3},{3,1},{4,6},{6,4},{5,7},{7,5},{8,10},{10,8},{9,1... | collective-permute-start | bytes 1179656 | tf_op jit(solution)/shard_map/ppermute | solution.py:103
  (140 other events, 1053.1 us)
Sparse Core Ops, SparseCore 0:
  13.1 66.6 all-gather.5
  81.9 26.2 all-gather.7
  110.4 63.0 all-gather.9
  175.4 62.1 all-gather.11
  239.0 62.1 all-gather.13
  390.6 54.8 reduce-scatter.6
  447.8 56.0 reduce-scatter.8
  506.2 56.0 reduce-scatter.10
  690.0 35.4 reduce-scatter.12
  728.2 26.0 reduce-scatter.16
  757.3 35.6 reduce-scatter.14

commit v6 on v5

--- a/solution.py
+++ b/solution.py
@@ -955,7 +955,7 @@
     grad_joint.append(over_shard(joint_total))
     steps.wait(grad_joint[0])
     out_gate = steps(
-        lambda pieces: lay_units(places, pieces, True, 1000), pieces_of(grad_gate.T, joint_total)
+        lambda pieces: lay_units(places, pieces, True, 1000), pieces_of(grad_gate.T, grad_joint[0])
     )
 
     def input_back(pair, d_resid, hidden):

time: 835 us -> 863 us (1.034)
  waiting for transfers between devices: 260 us -> 286 us
    ppermute x6, waiting for transfers between devices: 17.4 us -> 35 us  [pieces_of(): across = lax.ppermute(own, 'cx', SWAP)]
    reduce_scatter x6, waiting for transfers between devices: 9.57 us -> 20.4 us  [over_shard(): return lax.psum_scatter(total, 'shard', scatter_dimension=0, tiled=True)]
    unnamed x279 -> x273, local copies, waits for them, and re-layouts: 78.7 us -> 77.5 us
  transfers between devices with their start and end apart: 70 -> 70, of which waited for: 30 -> 29; matrix products, arithmetic and copies ran while one was open for 15% -> 14% of each run, Pallas kernels for 26% -> 25%
where the time goes in v6:
time: 863 us; the launch traced here: 854 us
  waiting for transfers between devices  286 us (33%)
  Pallas kernels  282 us (33%)
  local copies, waits for them, and re-layouts  113 us (13%)
  other arithmetic  64.5 us (7%)
  starting transfers between devices  58.8 us (7%)
  matrix products  20.3 us (2%)
  between operations  15.7 us (2%)
  blocking collectives  13.9 us (2%)
    ppermute x9, waiting for transfers between devices, across(): return lax.ppermute(part, 'cx', SWAP)  119 us
    unnamed x273, local copies, waits for them, and re-layouts  77.5 us
    pallas_call x12, Pallas kernels, rows_products(): pl.pallas_call(kernel, grid=(columns // tile,), in_specs=lefts + rights +...  69.1 us
    pallas_call x9, Pallas kernels, token_products(): pl.pallas_call(kernel, grid=(height // tile,), in_specs=lefts + rights +...  58.8 us
    ppermute x4, waiting for transfers between devices, with_tp(): return (part, lax.ppermute(part, 'tp', SWAP))  50.3 us
    pallas_call x2, Pallas kernels, one(): call(functools.partial(forward_one, size=size, own=own), grid, conv_specs...  37.7 us
    ppermute x6, waiting for transfers between devices, pieces_of(): across = lax.ppermute(own, 'cx', SWAP)  35 us
    pallas_call x2, Pallas kernels, four(): call(functools.partial(backward_two, size=size, own=own), grid, conv_spec...  33 us
  transfers between devices with their start and end apart: 70, of which 29 were waited for; matrix products, arithmetic and copies ran while one was open for 14% of the time, Pallas kernels for 25%

profile of v6, /device:TPU:0, one launch (start us, length us, event | category | flops | bytes accessed | tf_op | source)
XLA Modules:
  0.0 854.1 jit_solution(3053864214894390853)
XLA Ops:
  17.6 13.9 %all_gather.18 = bf16[4,80,128]{2,1,0:T(8,128)(2,1)S(1)} all-gather(bf16[1,80,128]{2,1,0:T(8,128)(2,1)S(1)} %pad_bitcast_fusion), channel_id=1, replica_groups=mesh['shard'=4,'cx'=2,'core'=2,'tp'=2] {'shard'}, dimensions={0}, use_global_device_ids=true | all-gather | bytes 102400 | tf_op jit(solution)/shard_map/all_gather | solution.py:737
  42.3 20.3 %collective-permute-done.4 = bf16[512,2048]{1,0:T(8,128)(2,1)} collective-permute-done((bf16[512,2048]{1,0:T(8,128)(2,1)}, bf16[512,2048]{1,0:T(8,128)(2,1)}, u32[]{:S(2)}, u32[]{:S(2)}) %collective-permute-start.4) | collective-permute-done | bytes 2097184 | tf_op jit(solution)/shard_map/ppermute | solution.py:715
  72.7 4.4 collective-permute-start.3
  91.3 6.8 convolution_convert_fusion.1.q0.k0.v0.q1.k1.v1.qh.kh.vh
  98.1 18.8 %shard_map.255 = (bf16[2,2,256,256]{3,2,1,0:T(8,128)(2,1)S(1)}, bf16[2,2,256,256]{3,2,1,0:T(8,128)(2,1)S(1)}, bf16[2,2,256,256]{3,2,1,0:T(8,128)(2,1)S(1)}, bf16...) custom-call(s32[2]{0:T(128)S(1)} %pad_add_fusion.1.where, ...), custom_call_target="tpu_custom_call" | custom-call | flops 1000 | bytes 1000 | tf_op jit(solution)/shard_map/pallas_call | solution.py:469
  121.8 34.0 %collective-permute-done.6.refs_4_ = bf16[2048,768]{1,0:T(8,128)(2,1)} collective-permute-done((bf16[2048,768]{1,0:T(8,128)(2,1)}, bf16[2048,768]{1,0:T(8,128)(2,1)}, u32[]{:S(2)}, u32[]{:S(2)}) %collective-permute-start.6) | collective-permute-done | bytes 3145760 | tf_op jit(solution)/shard_map/ppermute | solution.py:715
  158.3 6.7 convolution_convert_fusion.q0.k0.v0.q1.k1.v1.qh.kh.vh
  165.0 18.9 %shard_map.256 = (bf16[2,2,256,256]{3,2,1,0:T(8,128)(2,1)S(1)}, bf16[2,2,256,256]{3,2,1,0:T(8,128)(2,1)S(1)}, bf16[2,2,256,256]{3,2,1,0:T(8,128)(2,1)S(1)}, bf16...) custom-call(s32[2]{0:T(128)S(1)} %pad_add_fusion.1.where, ...), custom_call_target="tpu_custom_call" | custom-call | flops 1000 | bytes 1000 | tf_op jit(solution)/shard_map/pallas_call | solution.py:469
  193.8 6.1 shard_map.257
  205.3 6.1 shard_map.258
  215.1 5.9 collective-permute-done.10.refs_4_
  222.3 4.6 shard_map.260
  232.2 4.8 pad_maximum_fusion.2.grads_ref.refs_0_
  237.6 4.2 bitcast_convert_fusion
  241.7 33.2 %collective-permute-done.11 = bf16[512,2048]{1,0:T(8,128)(2,1)} collective-permute-done((bf16[512,2048]{1,0:T(8,128)(2,1)}, bf16[512,2048]{1,0:T(8,128)(2,1)}, u32[]{:S(2)}, u32[]{:S(2)}) %collective-permute-start.11) | collective-permute-done | bytes 2097184 | tf_op jit(solution)/shard_map/ppermute | solution.py:811
  275.0 4.4 multiply_reduce_fusion.6
  283.1 4.4 collective-permute-done.12
  287.5 4.2 pad_maximum_fusion.1.rows_ref.refs_0_
  291.7 9.5 %all-gather.14.cloned.1.call-done.downs_ref.refs_1_ = bf16[2048,704]{1,0:T(8,128)(2,1)} async-done(((bf16[512,704]{1,0:T(8,128)(2,1)}), bf16[2048,704]{1,0:T(8,128)(2,1)}) %all-gather.14.cloned.1.call-update) | async-done | bytes 2883600 | tf_op jit(solution)/shard_map/all_gather | solution.py:709
  301.2 15.4 %shard_map.261 = (bf16[1024,704]{1,0:T(8,128)(2,1)S(1)}, bf16[1024,704]{1,0:T(8,128)(2,1)S(1)}, bf16[1024,704]{1,0:T(8,128)(2,1)S(1)}) custom-call(bf16[1024,2048]{1,0:T(8,128)(2,1)} %pad_maximum_fusion.1.rows_ref.refs_0_, bf16[1024,2048]{1,0:T(8,128)(2,1)} %pad_maximum_fusion.2.grads_ref.refs_0_, ...), custom_call_target="tpu_custom_call" | custom-call | flops 1000 | bytes 1000 | tf_op jit(solution)/shard_map/pallas_call | solution.py:624
  316.6 7.1 shard_map.262
  325.0 4.2 shard_map.263
  340.2 15.4 %shard_map.264 = (bf16[1024,704]{1,0:T(8,128)(2,1)S(1)}, bf16[1024,704]{1,0:T(8,128)(2,1)S(1)}, bf16[1024,704]{1,0:T(8,128)(2,1)S(1)}) custom-call(bf16[1024,2048]{1,0:T(8,128)(2,1)} %copy-done.110, bf16[1024,2048]{1,0:T(8,128)(2,1)} %constant_dynamic-update-slice_fusion.grads_ref.refs_1_, bf16[2048,704]{1,0:T(8,128)(2,1)} %all-gather.12.cloned.1.call-done.gates_ref.refs_2_, ...), custom_call_target="tpu_custom_call" | custom-call | flops 1000 | bytes 1000 | tf_op jit(solution)/shard_map/pallas_call | solution.py:624
  355.6 7.1 shard_map.265
  368.3 6.3 shard_map.266
  376.0 9.8 %shard_map.267 = bf16[2048,704]{1,0:T(8,128)(2,1)} custom-call(bf16[1024,2048]{1,0:T(8,128)(2,1)} %pad_maximum_fusion.2.grads_ref.refs_0_, bf16[1024,2048]{1,0:T(8,128)(2,1)} %constant_dynamic-update-slice_fusion.grads_ref.refs_1_, bf16[1024,704]{1,0:T(8,128)(2,1)S(1)} %get-tuple-element.356.refs_0_.refs_2_, ...), custom_call_target="tpu_custom_call" | custom-call | flops 1000 | bytes 1000 | tf_op jit(solution)/shard_map/pallas_call | solution.py:596
  385.8 4.7 copy.105
  398.1 7.4 shard_map.268
  405.5 5.3 shard_map.269
  411.0 10.0 %shard_map.270 = bf16[2048,704]{1,0:T(8,128)(2,1)} custom-call(bf16[1024,2048]{1,0:T(8,128)(2,1)} %pad_maximum_fusion.1.rows_ref.refs_0_, bf16[1024,2048]{1,0:T(8,128)(2,1)} %copy-done.110, bf16[1024,704]{1,0:T(8,128)(2,1)S(1)} %copy-done.15, bf16[1024,704]{1,0:T(8,128)(2,1)S(1)} %copy-done.10), custom_call_target="tpu_custom_call" | custom-call | flops 1000 | bytes 1000 | tf_op jit(solution)/shard_map/pallas_call | solution.py:596
  420.9 18.1 %collective-permute-done.20 = bf16[512,2048]{1,0:T(8,128)(2,1)S(1)} collective-permute-done((bf16[512,2048]{1,0:T(8,128)(2,1)}, bf16[512,2048]{1,0:T(8,128)(2,1)S(1)}, u32[]{:S(2)}, u32[]{:S(2)}) %collective-permute-start.20) | collective-permute-done | bytes 2097184 | tf_op jit(solution)/shard_map/ppermute | solution.py:715
  442.5 4.7 copy.108
  450.1 10.0 %shard_map.271 = bf16[2048,704]{1,0:T(8,128)(2,1)} custom-call(bf16[1024,2048]{1,0:T(8,128)(2,1)} %pad_maximum_fusion.1.rows_ref.refs_0_, bf16[1024,2048]{1,0:T(8,128)(2,1)} %copy-done.110, bf16[1024,704]{1,0:T(8,128)(2,1)S(1)} %copy-done.13, bf16[1024,704]{1,0:T(8,128)(2,1)S(1)} %copy-done.8), custom_call_target="tpu_custom_call" | custom-call | flops 1000 | bytes 1000 | tf_op jit(solution)/shard_map/pallas_call | solution.py:596
  460.1 5.7 shard_map.272
  465.8 5.7 shard_map.273
  471.5 17.1 %collective-permute-done.22 = bf16[512,2048]{1,0:T(8,128)(2,1)} collective-permute-done((bf16[512,2048]{1,0:T(8,128)(2,1)}, bf16[512,2048]{1,0:T(8,128)(2,1)}, u32[]{:S(2)}, u32[]{:S(2)}) %collective-permute-start.22) | collective-permute-done | bytes 2097184 | tf_op jit(solution)/shard_map/ppermute | solution.py:811
  488.9 4.2 multiply_reduce_fusion
  493.1 5.5 fusion.25
  500.1 4.6 copy.110
  516.2 7.1 shard_map.274
  524.3 7.8 shard_map.275
  536.0 11.0 %collective-permute-done.21 = bf16[512,2048]{1,0:T(8,128)(2,1)} collective-permute-done((bf16[512,2048]{1,0:T(8,128)(2,1)}, bf16[512,2048]{1,0:T(8,128)(2,1)}, u32[]{:S(2)}, u32[]{:S(2)}) %collective-permute-start.21) | collective-permute-done | bytes 2097184 | tf_op jit(solution)/shard_map/ppermute | solution.py:715
  560.1 14.0 %collective-permute-done.25.rest_8_ = bf16[2,2,128,128]{3,2,1,0:T(8,128)(2,1)S(1)} collective-permute-done((bf16[2,2,128,128]{3,2,1,0:T(8,128)(2,1)}, bf16[2,2,128,128]{3,2,1,0:T(8,128)(2,1)S(1)}, u32[]{:S(2)}, u32[]{:S(2)}) %collective-permute-start.25) | collective-permute-done | bytes 131104 | tf_op jit(solution)/shard_map/ppermute | solution.py:875
  582.2 16.4 %shard_map.277 = (bf16[2,2,256,768]{3,2,1,0:T(8,128)(2,1)}, bf16[2,16,768]{2,1,0:T(8,128)(2,1)S(1)}, f32[2,2,256,128]{3,2,1,0:T(8,128)S(1)}, f32[2,3,2,4,128]{4,3,2,1,0:T(4,128)S(1)}) custom-call(s32[2]{0:T(128)S(1)} %pad_add_fusion.1.where, bf16[1056,768]{1,0:T(8,128)(2,1)} %copy-done.3, bf16[1056,768]{1,0:T(8,128)(2,1)} %copy-done.3, ...), custom_call_target="tpu_custom_call" | custom-call | flops 28600000512 | bytes 1000 | tf_op jit(solution)/shard_map/pallas_call | solution.py:502
  603.9 4.6 shard_map.278
  610.4 6.0 shard_map.279
  619.2 5.1 shard_map.280
  631.9 16.6 %shard_map.281 = (bf16[2,2,256,768]{3,2,1,0:T(8,128)(2,1)}, bf16[2,16,768]{2,1,0:T(8,128)(2,1)S(1)}, f32[2,2,256,128]{3,2,1,0:T(8,128)S(1)}, f32[2,3,2,4,128]{4,3,2,1,0:T(4,128)S(1)}) custom-call(s32[2]{0:T(128)S(1)} %pad_add_fusion.1.where, bf16[1056,768]{1,0:T(8,128)(2,1)} %copy-done.2, bf16[1056,768]{1,0:T(8,128)(2,1)} %copy-done.2, ...), custom_call_target="tpu_custom_call" | custom-call | flops 28600000512 | bytes 1000 | tf_op jit(solution)/shard_map/pallas_call | solution.py:502
  649.9 4.8 add_convert_fusion
  656.4 6.9 shard_map.282
  663.4 4.1 collective-permute-done.35.refs_6_
  670.3 6.7 shard_map.283
  677.0 4.1 shard_map.284
  683.3 5.4 shard_map.285
  694.9 33.4 %collective-permute-done.40.refs_4_ = bf16[2048,384]{1,0:T(8,128)(2,1)S(1)} collective-permute-done((bf16[2048,384]{1,0:T(8,128)(2,1)}, bf16[2048,384]{1,0:T(8,128)(2,1)S(1)}, u32[]{:S(2)}, u32[]{:S(2)}) %collective-permute-start.40) | collective-permute-done | bytes 1572896 | tf_op jit(solution)/shard_map/ppermute | solution.py:715
  729.5 5.2 shard_map.286
  737.8 16.1 %collective-permute-done.37.b = bf16[704,512]{1,0:T(8,128)(2,1)S(1)} collective-permute-done((bf16[704,512]{1,0:T(8,128)(2,1)}, bf16[704,512]{1,0:T(8,128)(2,1)S(1)}, u32[]{:S(2)}, u32[]{:S(2)}) %collective-permute-start.37) | collective-permute-done | bytes 720928 | tf_op jit(solution)/shard_map/ppermute | solution.py:101
  758.5 5.4 shard_map.287
  771.1 20.4 %reduce-scatter.15.cloned.1.call-done.refs_4_ = bf16[512,384]{1,0:T(8,128)(2,1)} async-done(((bf16[2048,384]{1,0:T(8,128)(2,1)}), bf16[512,384]{1,0:T(8,128)(2,1)}) %reduce-scatter.15.cloned.1.call-update) | async-done | bytes 393232 | tf_op jit(solution)/shard_map/reduce_scatter | solution.py:712
  795.0 8.7 %collective-permute-done.48.refs_5_ = bf16[512,384]{1,0:T(8,128)(2,1)} collective-permute-done((bf16[512,384]{1,0:T(8,128)(2,1)}, bf16[512,384]{1,0:T(8,128)(2,1)}, u32[]{:S(2)}, u32[]{:S(2)}) %collective-permute-start.48) | collective-permute-done | bytes 393248 | tf_op jit(solution)/shard_map/ppermute | solution.py:101
  808.6 10.1 %collective-permute-done.56.b = bf16[704,512]{1,0:T(8,128)(2,1)} collective-permute-done((bf16[704,512]{1,0:T(8,128)(2,1)}, bf16[704,512]{1,0:T(8,128)(2,1)}, u32[]{:S(2)}, u32[]{:S(2)}) %collective-permute-start.56) | collective-permute-done | bytes 720928 | tf_op jit(solution)/shard_map/ppermute | solution.py:101
  820.3 6.7 fusion.5
  828.1 4.6 shard_map.288
  838.4 5.3 shard_map.289
  (515 shorter events, 222.0 us)
Async XLA Ops:
  7.2 77.6 %all-gather.6.cloned.1.call-start = ((), (), s32[]{:S(2)}) async-start(), calls=%async_computation.6 | async-start | bytes 3932160 | tf_op jit(solution)/shard_map/all_gather | solution.py:709
  12.9 142.8 %all-gather.8.cloned.1.call-start = ((), (), s32[]{:S(2)}) async-start(), calls=%async_computation.7 | async-start | bytes 1310720 | tf_op jit(solution)/shard_map/all_gather | solution.py:709
  13.0 24.4 %collective-permute-start = (bf16[512,2048]{1,0:T(8,128)(2,1)S(1)}, bf16[512,2048]{1,0:T(8,128)(2,1)}, u32[]{:S(2)}, u32[]{:S(2)}) collective-permute-start(bf16[512,2048]{1,0:T(8,128)(2,1)S(1)} %bitcast.112), channel_id=1, source_target_pairs={{0,2},{2,0},{1,3},{3,1},{4,6},{6,4},{5,7},{7,5},{8,10},{10,8},{9,1... | collective-permute-start | bytes 6291464 | tf_op jit(solution)/shard_map/ppermute | solution.py:718
  13.5 49.1 %collective-permute-start.4 = (bf16[512,2048]{1,0:T(8,128)(2,1)}, bf16[512,2048]{1,0:T(8,128)(2,1)}, u32[]{:S(2)}, u32[]{:S(2)}) collective-permute-start(bf16[512,2048]{1,0:T(8,128)(2,1)} %bitcast.9), channel_id=1, source_target_pairs={{0,4},{4,0},{1,5},{5,1},{2,6},{6,2},{3,7},{7,3},{8,12},{12,8},{9,1... | collective-permute-start | bytes 6291464 | tf_op jit(solution)/shard_map/ppermute | solution.py:715
  17.0 224.8 %all-gather.10.cloned.1.call-start = ((), (), s32[]{:S(2)}) async-start(), calls=%async_computation.8 | async-start | bytes 3932160 | tf_op jit(solution)/shard_map/all_gather | solution.py:709
  39.3 25.3 %collective-permute-start.1 = (bf16[2,16,2048]{2,1,0:T(8,128)(2,1)S(1)}, bf16[2,16,2048]{2,1,0:T(8,128)(2,1)S(1)}, u32[]{:S(2)}, u32[]{:S(2)}) collective-permute-start(bf16[2,16,2048]{2,1,0:T(8,128)(2,1)S(1)} %slice.109), channel_id=1, source_target_pairs={{0,4},{1,5},{2,6},{3,7},{8,12},{9,13},{10,14},{11,15},{16,20},{17,... | collective-permute-start | bytes 393224 | tf_op jit(solution)/shard_map/ppermute | solution.py:759
  62.6 19.1 %collective-permute-start.5 = (bf16[512,2048]{1,0:T(8,128)(2,1)}, bf16[512,2048]{1,0:T(8,128)(2,1)}, u32[]{:S(2)}, u32[]{:S(2)}) collective-permute-start(bf16[512,2048]{1,0:T(8,128)(2,1)} %collective-permute-done.4), channel_id=1, source_target_pairs={{0,2},{2,0},{1,3},{3,1},{4,6},{6,4},{5,7},{7,5},{8,10},{10,8},{9,1... | collective-permute-start | bytes 6291464 | tf_op jit(solution)/shard_map/ppermute | solution.py:718
  71.4 220.3 %all-gather.12.cloned.1.call-start = ((), (), s32[]{:S(2)}) async-start(), calls=%async_computation.9 | async-start | bytes 3932160 | tf_op jit(solution)/shard_map/all_gather | solution.py:709
  72.7 5.7 collective-permute-start.3
  84.8 70.9 %collective-permute-start.6 = (bf16[2048,768]{1,0:T(8,128)(2,1)}, bf16[2048,768]{1,0:T(8,128)(2,1)}, u32[]{:S(2)}, u32[]{:S(2)}) collective-permute-start(bf16[2048,768]{1,0:T(8,128)(2,1)} %all-gather.6.cloned.1.call-done.refs_3_), channel_id=1, source_target_pairs={{0,4},{4,0},{1,5},{5,1},{2,6},{6,2},{3,7},{7,3},{8,12},{12,8},{9,1... | collective-permute-start | bytes 9437192 | tf_op jit(solution)/shard_map/ppermute | solution.py:715
  91.0 210.1 %all-gather.14.cloned.1.call-start = ((), (), s32[]{:S(2)}) async-start(), calls=%async_computation.10 | async-start | bytes 3932160 | tf_op jit(solution)/shard_map/all_gather | solution.py:709
  119.6 69.8 %collective-permute-start.8 = (bf16[2,2,128,128]{3,2,1,0:T(8,128)(2,1)S(1)}, bf16[2,2,128,128]{3,2,1,0:T(8,128)(2,1)S(1)}, u32[]{:S(2)}, u32[]{:S(2)}) collective-permute-start(bf16[2,2,128,128]{3,2,1,0:T(8,128)(2,1)S(1)} %get-tuple-element.256), channel_id=1, source_target_pairs={{0,4},{1,5},{2,6},{3,7},{8,12},{9,13},{10,14},{11,15},{16,20},{17,... | collective-permute-start | bytes 393224 | tf_op jit(solution)/shard_map/ppermute | solution.py:790
  155.8 56.7 %collective-permute-start.9 = (bf16[2048,256]{1,0:T(8,128)(2,1)}, bf16[2048,256]{1,0:T(8,128)(2,1)S(1)}, u32[]{:S(2)}, u32[]{:S(2)}) collective-permute-start(bf16[2048,256]{1,0:T(8,128)(2,1)} %all-gather.8.cloned.1.call-done.refs_2_), channel_id=1, source_target_pairs={{0,4},{4,0},{1,5},{5,1},{2,6},{6,2},{3,7},{7,3},{8,12},{12,8},{9,1... | collective-permute-start | bytes 3145736 | tf_op jit(solution)/shard_map/ppermute | solution.py:715
  187.3 14.3 %collective-permute-start.7 = (bf16[2,2,128,128]{3,2,1,0:T(8,128)(2,1)S(1)}, bf16[2,2,128,128]{3,2,1,0:T(8,128)(2,1)S(1)}, u32[]{:S(2)}, u32[]{:S(2)}) collective-permute-start(bf16[2,2,128,128]{3,2,1,0:T(8,128)(2,1)S(1)} %get-tuple-element.260), channel_id=1, source_target_pairs={{0,4},{1,5},{2,6},{3,7},{8,12},{9,13},{10,14},{11,15},{16,20},{17,... | collective-permute-start | bytes 393224 | tf_op jit(solution)/shard_map/ppermute | solution.py:791
  214.5 6.4 collective-permute-start.10
  214.6 17.6 %collective-permute-start.13 = (bf16[512,2048]{1,0:T(8,128)(2,1)}, bf16[512,2048]{1,0:T(8,128)(2,1)}, u32[]{:S(2)}, u32[]{:S(2)}) collective-permute-start(bf16[512,2048]{1,0:T(8,128)(2,1)} %bitcast.9), channel_id=1, source_target_pairs={{0,2},{2,0},{1,3},{3,1},{4,6},{6,4},{5,7},{7,5},{8,10},{10,8},{9,1... | collective-permute-start | bytes 6291464 | tf_op jit(solution)/shard_map/ppermute | solution.py:718
  226.9 48.1 %collective-permute-start.11 = (bf16[512,2048]{1,0:T(8,128)(2,1)}, bf16[512,2048]{1,0:T(8,128)(2,1)}, u32[]{:S(2)}, u32[]{:S(2)}) collective-permute-start(bf16[512,2048]{1,0:T(8,128)(2,1)} %shard_map.260), channel_id=1, source_target_pairs={{0,1},{1,0},{2,3},{3,2},{4,5},{5,4},{6,7},{7,6},{8,9},{9,8},{10,11... | collective-permute-start | bytes 6291464 | tf_op jit(solution)/shard_map/ppermute | solution.py:811
  237.0 275.9 %reduce-scatter.7.cloned.1.call-start = ((), (), s32[]{:S(2)}) async-start(), calls=%async_computation.11 | async-start | bytes 3604480 | tf_op jit(solution)/shard_map/reduce_scatter | solution.py:712
  283.1 4.4 collective-permute-start.12
  283.1 48.4 %collective-permute-start.15 = (bf16[512,2048]{1,0:T(8,128)(2,1)}, bf16[512,2048]{1,0:T(8,128)(2,1)}, u32[]{:S(2)}, u32[]{:S(2)}) collective-permute-start(bf16[512,2048]{1,0:T(8,128)(2,1)} %multiply_convert_fusion), channel_id=1, source_target_pairs={{0,4},{4,0},{1,5},{5,1},{2,6},{6,2},{3,7},{7,3},{8,12},{12,8},{9,1... | collective-permute-start | bytes 6291464 | tf_op jit(solution)/shard_map/ppermute | solution.py:715
  329.3 4.2 collective-permute-start.14
  333.5 4.4 collective-permute-start.16
  362.7 4.2 collective-permute-start.18
  390.5 169.6 %reduce-scatter.9.cloned.1.call-start = ((), (), s32[]{:S(2)}) async-start(), calls=%async_computation.12 | async-start | bytes 3604480 | tf_op jit(solution)/shard_map/reduce_scatter | solution.py:712
  390.7 4.4 collective-permute-start.17
  390.9 48.1 %collective-permute-start.20 = (bf16[512,2048]{1,0:T(8,128)(2,1)}, bf16[512,2048]{1,0:T(8,128)(2,1)S(1)}, u32[]{:S(2)}, u32[]{:S(2)}) collective-permute-start(bf16[512,2048]{1,0:T(8,128)(2,1)} %copy-done.35), channel_id=1, source_target_pairs={{0,4},{4,0},{1,5},{5,1},{2,6},{6,2},{3,7},{7,3},{8,12},{12,8},{9,1... | collective-permute-start | bytes 6291464 | tf_op jit(solution)/shard_map/ppermute | solution.py:715
  410.8 49.3 %collective-permute-start.19 = (bf16[512,2048]{1,0:T(8,128)(2,1)}, bf16[512,2048]{1,0:T(8,128)(2,1)}, u32[]{:S(2)}, u32[]{:S(2)}) collective-permute-start(bf16[512,2048]{1,0:T(8,128)(2,1)} %shard_map.269), channel_id=1, source_target_pairs={{0,2},{2,0},{1,3},{3,1},{4,6},{6,4},{5,7},{7,5},{8,10},{10,8},{9,1... | collective-permute-start | bytes 6291464 | tf_op jit(solution)/shard_map/ppermute | solution.py:718
  441.0 47.5 %collective-permute-start.22 = (bf16[512,2048]{1,0:T(8,128)(2,1)}, bf16[512,2048]{1,0:T(8,128)(2,1)}, u32[]{:S(2)}, u32[]{:S(2)}) collective-permute-start(bf16[512,2048]{1,0:T(8,128)(2,1)} %add_convert_fusion.2), channel_id=1, source_target_pairs={{0,1},{1,0},{2,3},{3,2},{4,5},{5,4},{6,7},{7,6},{8,9},{9,8},{10,11... | collective-permute-start | bytes 6291464 | tf_op jit(solution)/shard_map/ppermute | solution.py:811
  447.2 178.2 %reduce-scatter.11.cloned.1.call-start = ((), (), s32[]{:S(2)}) async-start(), calls=%async_computation.13 | async-start | bytes 3604480 | tf_op jit(solution)/shard_map/reduce_scatter | solution.py:712
  498.7 6.4 collective-permute-start.23
  498.7 48.4 %collective-permute-start.21 = (bf16[512,2048]{1,0:T(8,128)(2,1)}, bf16[512,2048]{1,0:T(8,128)(2,1)}, u32[]{:S(2)}, u32[]{:S(2)}) collective-permute-start(bf16[512,2048]{1,0:T(8,128)(2,1)} %shard_map.272), channel_id=1, source_target_pairs={{0,4},{4,0},{1,5},{5,1},{2,6},{6,2},{3,7},{7,3},{8,12},{12,8},{9,1... | collective-permute-start | bytes 6291464 | tf_op jit(solution)/shard_map/ppermute | solution.py:715
  504.8 249.1 %reduce-scatter.13.cloned.1.call-start = ((), (), s32[]{:S(2)}) async-start(), calls=%async_computation.14 | async-start | bytes 1966080 | tf_op jit(solution)/shard_map/reduce_scatter | solution.py:712
  550.7 5.6 collective-permute-start.27
  552.2 47.2 %collective-permute-start.28 = (bf16[704,512]{1,0:T(8,128)(2,1)S(1)}, bf16[704,512]{1,0:T(8,128)(2,1)}, u32[]{:S(2)}, u32[]{:S(2)}) collective-permute-start(bf16[704,512]{1,0:T(8,128)(2,1)S(1)} %bitcast.103), channel_id=1, source_target_pairs={{0,4},{4,0},{1,5},{5,1},{2,6},{6,2},{3,7},{7,3},{8,12},{12,8},{9,1... | collective-permute-start | bytes 2162696 | tf_op jit(solution)/shard_map/ppermute | solution.py:101
  553.7 48.3 %collective-permute-start.29 = (bf16[704,512]{1,0:T(8,128)(2,1)S(1)}, bf16[704,512]{1,0:T(8,128)(2,1)}, u32[]{:S(2)}, u32[]{:S(2)}) collective-permute-start(bf16[704,512]{1,0:T(8,128)(2,1)S(1)} %bitcast.104), channel_id=1, source_target_pairs={{0,2},{2,0},{1,3},{3,1},{4,6},{6,4},{5,7},{7,5},{8,10},{10,8},{9,1... | collective-permute-start | bytes 2162696 | tf_op jit(solution)/shard_map/ppermute | solution.py:103
  553.7 20.4 %collective-permute-start.25 = (bf16[2,2,128,128]{3,2,1,0:T(8,128)(2,1)}, bf16[2,2,128,128]{3,2,1,0:T(8,128)(2,1)S(1)}, u32[]{:S(2)}, u32[]{:S(2)}) collective-permute-start(bf16[2,2,128,128]{3,2,1,0:T(8,128)(2,1)} %get-tuple-element.383), channel_id=1, source_target_pairs={{4,0},{5,1},{6,2},{7,3},{12,8},{13,9},{14,10},{15,11},{20,16},{21,... | collective-permute-start | bytes 393224 | tf_op jit(solution)/shard_map/ppermute | solution.py:875
  555.0 22.0 %collective-permute-start.26 = (bf16[2,2,128,128]{3,2,1,0:T(8,128)(2,1)S(1)}, bf16[2,2,128,128]{3,2,1,0:T(8,128)(2,1)}, u32[]{:S(2)}, u32[]{:S(2)}) collective-permute-start(bf16[2,2,128,128]{3,2,1,0:T(8,128)(2,1)S(1)} %get-tuple-element.375), channel_id=1, source_target_pairs={{4,0},{5,1},{6,2},{7,3},{12,8},{13,9},{14,10},{15,11},{20,16},{21,... | collective-permute-start | bytes 393224 | tf_op jit(solution)/shard_map/ppermute | solution.py:873
  556.3 69.2 %collective-permute-start.31 = (bf16[2048,256]{1,0:T(8,128)(2,1)}, bf16[2048,256]{1,0:T(8,128)(2,1)}, u32[]{:S(2)}, u32[]{:S(2)}) collective-permute-start(bf16[2048,256]{1,0:T(8,128)(2,1)} %shard_map.276), channel_id=1, source_target_pairs={{0,4},{4,0},{1,5},{5,1},{2,6},{6,2},{3,7},{7,3},{8,12},{12,8},{9,1... | collective-permute-start | bytes 3145736 | tf_op jit(solution)/shard_map/ppermute | solution.py:715
  601.4 48.4 %collective-permute-start.24 = (bf16[512,2048]{1,0:T(8,128)(2,1)}, bf16[512,2048]{1,0:T(8,128)(2,1)}, u32[]{:S(2)}, u32[]{:S(2)}) collective-permute-start(bf16[512,2048]{1,0:T(8,128)(2,1)} %add_convert_fusion.1), channel_id=1, source_target_pairs={{0,1},{1,0},{2,3},{3,2},{4,5},{5,4},{6,7},{7,6},{8,9},{9,8},{10,11... | collective-permute-start | bytes 6291464 | tf_op jit(solution)/shard_map/ppermute | solution.py:811
  608.7 47.5 %collective-permute-start.32 = (bf16[2,16,768]{2,1,0:T(8,128)(2,1)S(1)}, bf16[2,16,768]{2,1,0:T(8,128)(2,1)S(1)}, u32[]{:S(2)}, u32[]{:S(2)}) collective-permute-start(bf16[2,16,768]{2,1,0:T(8,128)(2,1)S(1)} %get-tuple-element.413), channel_id=1, source_target_pairs={{4,0},{5,1},{6,2},{7,3},{12,8},{13,9},{14,10},{15,11},{20,16},{21,... | collective-permute-start | bytes 147464 | tf_op jit(solution)/shard_map/ppermute | solution.py:896
  616.5 38.2 %collective-permute-start.33 = (bf16[2048,384]{1,0:T(8,128)(2,1)}, bf16[2048,384]{1,0:T(8,128)(2,1)}, u32[]{:S(2)}, u32[]{:S(2)}) collective-permute-start(bf16[2048,384]{1,0:T(8,128)(2,1)} %shard_map.279), channel_id=1, source_target_pairs={{0,4},{4,0},{1,5},{5,1},{2,6},{6,2},{3,7},{7,3},{8,12},{12,8},{9,1... | collective-permute-start | bytes 4718600 | tf_op jit(solution)/shard_map/ppermute | solution.py:715
  648.5 7.8 collective-permute-start.34
  663.3 4.2 collective-permute-start.35
  689.9 79.1 %reduce-scatter.17.cloned.1.call-start = ((), (), s32[]{:S(2)}) async-start(), calls=%async_computation.16 | async-start | bytes 1310720 | tf_op jit(solution)/shard_map/reduce_scatter | solution.py:712
  690.5 101.0 %reduce-scatter.15.cloned.1.call-start = ((), (), s32[]{:S(2)}) async-start(), calls=%async_computation.15 | async-start | bytes 1966080 | tf_op jit(solution)/shard_map/reduce_scatter | solution.py:712
  690.7 37.6 %collective-permute-start.40 = (bf16[2048,384]{1,0:T(8,128)(2,1)}, bf16[2048,384]{1,0:T(8,128)(2,1)S(1)}, u32[]{:S(2)}, u32[]{:S(2)}) collective-permute-start(bf16[2048,384]{1,0:T(8,128)(2,1)} %copy-done.36), channel_id=1, source_target_pairs={{0,4},{4,0},{1,5},{5,1},{2,6},{6,2},{3,7},{7,3},{8,12},{12,8},{9,1... | collective-permute-start | bytes 4718600 | tf_op jit(solution)/shard_map/ppermute | solution.py:715
  693.4 70.4 %collective-permute-start.36 = (bf16[512,2048]{1,0:T(8,128)(2,1)S(1)}, bf16[512,2048]{1,0:T(8,128)(2,1)}, u32[]{:S(2)}, u32[]{:S(2)}) collective-permute-start(bf16[512,2048]{1,0:T(8,128)(2,1)S(1)} %shard_map.283), channel_id=1, source_target_pairs={{0,1},{1,0},{2,3},{3,2},{4,5},{5,4},{6,7},{7,6},{8,9},{9,8},{10,11... | collective-permute-start | bytes 6291464 | tf_op jit(solution)/shard_map/ppermute | solution.py:811
  736.0 18.0 %collective-permute-start.37 = (bf16[704,512]{1,0:T(8,128)(2,1)}, bf16[704,512]{1,0:T(8,128)(2,1)S(1)}, u32[]{:S(2)}, u32[]{:S(2)}) collective-permute-start(bf16[704,512]{1,0:T(8,128)(2,1)} %bitcast.100), channel_id=1, source_target_pairs={{0,4},{4,0},{1,5},{5,1},{2,6},{6,2},{3,7},{7,3},{8,12},{12,8},{9,1... | collective-permute-start | bytes 2162696 | tf_op jit(solution)/shard_map/ppermute | solution.py:101
  737.8 17.0 %collective-permute-start.38 = (bf16[704,512]{1,0:T(8,128)(2,1)}, bf16[704,512]{1,0:T(8,128)(2,1)}, u32[]{:S(2)}, u32[]{:S(2)}) collective-permute-start(bf16[704,512]{1,0:T(8,128)(2,1)} %bitcast.101), channel_id=1, source_target_pairs={{0,2},{2,0},{1,3},{3,1},{4,6},{6,4},{5,7},{7,5},{8,10},{10,8},{9,1... | collective-permute-start | bytes 2162696 | tf_op jit(solution)/shard_map/ppermute | solution.py:103
  767.6 25.3 %collective-permute-start.41 = (bf16[4224]{0:T(1024)(128)(2,1)S(1)}, bf16[4224]{0:T(1024)(128)(2,1)S(1)}, u32[]{:S(2)}, u32[]{:S(2)}) collective-permute-start(bf16[4224]{0:T(1024)(128)(2,1)S(1)} %pad_maximum_fusion.6), channel_id=1, source_target_pairs={{0,2},{2,0},{1,3},{3,1},{4,6},{6,4},{5,7},{7,5},{8,10},{10,8},{9,1... | collective-permute-start | bytes 25352 | tf_op jit(solution)/shard_map/ppermute | solution.py:677
  769.0 26.1 %collective-permute-start.53 = (bf16[512,256]{1,0:T(8,128)(2,1)}, bf16[512,256]{1,0:T(8,128)(2,1)}, u32[]{:S(2)}, u32[]{:S(2)}) collective-permute-start(bf16[512,256]{1,0:T(8,128)(2,1)} %reduce-scatter.17.cloned.1.call-done.a), channel_id=1, source_target_pairs={{0,4},{4,0},{1,5},{5,1},{2,6},{6,2},{3,7},{7,3},{8,12},{12,8},{9,1... | collective-permute-start | bytes 786440 | tf_op jit(solution)/shard_map/ppermute | solution.py:101
  770.5 33.3 %collective-permute-start.45 = (bf16[512,384]{1,0:T(8,128)(2,1)S(1)}, bf16[512,384]{1,0:T(8,128)(2,1)S(1)}, u32[]{:S(2)}, u32[]{:S(2)}) collective-permute-start(bf16[512,384]{1,0:T(8,128)(2,1)S(1)} %copy-done.79), channel_id=1, source_target_pairs={{0,4},{4,0},{1,5},{5,1},{2,6},{6,2},{3,7},{7,3},{8,12},{12,8},{9,1... | collective-permute-start | bytes 1179656 | tf_op jit(solution)/shard_map/ppermute | solution.py:101
  791.4 12.3 %collective-permute-start.48 = (bf16[512,384]{1,0:T(8,128)(2,1)}, bf16[512,384]{1,0:T(8,128)(2,1)}, u32[]{:S(2)}, u32[]{:S(2)}) collective-permute-start(bf16[512,384]{1,0:T(8,128)(2,1)} %reduce-scatter.15.cloned.1.call-done.refs_4_), channel_id=1, source_target_pairs={{0,4},{4,0},{1,5},{5,1},{2,6},{6,2},{3,7},{7,3},{8,12},{12,8},{9,1... | collective-permute-start | bytes 1179656 | tf_op jit(solution)/shard_map/ppermute | solution.py:101
  792.9 11.6 %collective-permute-start.42 = (bf16[18560]{0:T(1024)(128)(2,1)S(1)}, bf16[18560]{0:T(1024)(128)(2,1)S(1)}, u32[]{:S(2)}, u32[]{:S(2)}) collective-permute-start(bf16[18560]{0:T(1024)(128)(2,1)S(1)} %pad_maximum_fusion.5), channel_id=1, source_target_pairs={{0,4},{4,0},{1,5},{5,1},{2,6},{6,2},{3,7},{7,3},{8,12},{12,8},{9,1... | collective-permute-start | bytes 111368 | tf_op jit(solution)/shard_map/ppermute | solution.py:677
  793.6 25.2 %collective-permute-start.56 = (bf16[704,512]{1,0:T(8,128)(2,1)}, bf16[704,512]{1,0:T(8,128)(2,1)}, u32[]{:S(2)}, u32[]{:S(2)}) collective-permute-start(bf16[704,512]{1,0:T(8,128)(2,1)} %bitcast.40.a), channel_id=1, source_target_pairs={{0,4},{4,0},{1,5},{5,1},{2,6},{6,2},{3,7},{7,3},{8,12},{12,8},{9,1... | collective-permute-start | bytes 2162696 | tf_op jit(solution)/shard_map/ppermute | solution.py:101
  795.0 32.0 %collective-permute-start.49 = (bf16[512,384]{1,0:T(8,128)(2,1)}, bf16[512,384]{1,0:T(8,128)(2,1)S(1)}, u32[]{:S(2)}, u32[]{:S(2)}) collective-permute-start(bf16[512,384]{1,0:T(8,128)(2,1)} %reduce-scatter.15.cloned.1.call-done.refs_4_), channel_id=1, source_target_pairs={{0,2},{2,0},{1,3},{3,1},{4,6},{6,4},{5,7},{7,5},{8,10},{10,8},{9,1... | collective-permute-start | bytes 1179656 | tf_op jit(solution)/shard_map/ppermute | solution.py:103
  803.8 23.3 %collective-permute-start.46 = (bf16[512,384]{1,0:T(8,128)(2,1)S(1)}, bf16[512,384]{1,0:T(8,128)(2,1)S(1)}, u32[]{:S(2)}, u32[]{:S(2)}) collective-permute-start(bf16[512,384]{1,0:T(8,128)(2,1)S(1)} %copy-done.79), channel_id=1, source_target_pairs={{0,2},{2,0},{1,3},{3,1},{4,6},{6,4},{5,7},{7,5},{8,10},{10,8},{9,1... | collective-permute-start | bytes 1179656 | tf_op jit(solution)/shard_map/ppermute | solution.py:103
  803.8 23.8 %collective-permute-start.50 = (bf16[512,384]{1,0:T(8,128)(2,1)}, bf16[512,384]{1,0:T(8,128)(2,1)S(1)}, u32[]{:S(2)}, u32[]{:S(2)}) collective-permute-start(bf16[512,384]{1,0:T(8,128)(2,1)} %collective-permute-done.48.refs_5_), channel_id=1, source_target_pairs={{0,2},{2,0},{1,3},{3,1},{4,6},{6,4},{5,7},{7,5},{8,10},{10,8},{9,1... | collective-permute-start | bytes 1179656 | tf_op jit(solution)/shard_map/ppermute | solution.py:103
  808.6 19.0 %collective-permute-start.47 = (bf16[512,384]{1,0:T(8,128)(2,1)S(1)}, bf16[512,384]{1,0:T(8,128)(2,1)S(1)}, u32[]{:S(2)}, u32[]{:S(2)}) collective-permute-start(bf16[512,384]{1,0:T(8,128)(2,1)S(1)} %collective-permute-done.45.refs_1_), channel_id=1, source_target_pairs={{0,2},{2,0},{1,3},{3,1},{4,6},{6,4},{5,7},{7,5},{8,10},{10,8},{9,1... | collective-permute-start | bytes 1179656 | tf_op jit(solution)/shard_map/ppermute | solution.py:103
  818.7 14.0 %collective-permute-start.44 = (bf16[18560]{0:T(1024)(128)(2,1)S(1)}, bf16[18560]{0:T(1024)(128)(2,1)S(1)}, u32[]{:S(2)}, u32[]{:S(2)}) collective-permute-start(bf16[18560]{0:T(1024)(128)(2,1)S(1)} %add_convert_fusion.4), channel_id=1, source_target_pairs={{0,16},{8,24},{16,0},{24,8},{1,17},{9,25},{17,1},{25,9},{2,18},{10... | collective-permute-start | bytes 111368 | tf_op jit(solution)/shard_map/ppermute | solution.py:677
  827.0 11.3 %collective-permute-start.57 = (bf16[704,512]{1,0:T(8,128)(2,1)}, bf16[704,512]{1,0:T(8,128)(2,1)S(1)}, u32[]{:S(2)}, u32[]{:S(2)}) collective-permute-start(bf16[704,512]{1,0:T(8,128)(2,1)} %bitcast.40.a), channel_id=1, source_target_pairs={{0,2},{2,0},{1,3},{3,1},{4,6},{6,4},{5,7},{7,5},{8,10},{10,8},{9,1... | collective-permute-start | bytes 2162696 | tf_op jit(solution)/shard_map/ppermute | solution.py:103
  827.0 16.6 %collective-permute-start.54 = (bf16[512,256]{1,0:T(8,128)(2,1)}, bf16[512,256]{1,0:T(8,128)(2,1)S(1)}, u32[]{:S(2)}, u32[]{:S(2)}) collective-permute-start(bf16[512,256]{1,0:T(8,128)(2,1)} %reduce-scatter.17.cloned.1.call-done.a), channel_id=1, source_target_pairs={{0,2},{2,0},{1,3},{3,1},{4,6},{6,4},{5,7},{7,5},{8,10},{10,8},{9,1... | collective-permute-start | bytes 786440 | tf_op jit(solution)/shard_map/ppermute | solution.py:103
  827.5 16.1 %collective-permute-start.55 = (bf16[512,256]{1,0:T(8,128)(2,1)}, bf16[512,256]{1,0:T(8,128)(2,1)S(1)}, u32[]{:S(2)}, u32[]{:S(2)}) collective-permute-start(bf16[512,256]{1,0:T(8,128)(2,1)} %collective-permute-done.53.b), channel_id=1, source_target_pairs={{0,2},{2,0},{1,3},{3,1},{4,6},{6,4},{5,7},{7,5},{8,10},{10,8},{9,1... | collective-permute-start | bytes 786440 | tf_op jit(solution)/shard_map/ppermute | solution.py:103
  827.6 10.7 %collective-permute-start.58 = (bf16[704,512]{1,0:T(8,128)(2,1)}, bf16[704,512]{1,0:T(8,128)(2,1)S(1)}, u32[]{:S(2)}, u32[]{:S(2)}) collective-permute-start(bf16[704,512]{1,0:T(8,128)(2,1)} %collective-permute-done.56.b), channel_id=1, source_target_pairs={{0,2},{2,0},{1,3},{3,1},{4,6},{6,4},{5,7},{7,5},{8,10},{10,8},{9,1... | collective-permute-start | bytes 2162696 | tf_op jit(solution)/shard_map/ppermute | solution.py:103
  (137 other events, 1018.6 us)
Sparse Core Ops, SparseCore 0:
  13.1 66.6 all-gather.5
  81.9 26.2 all-gather.7
  110.4 63.0 all-gather.9
  175.4 62.1 all-gather.11
  239.0 62.1 all-gather.13
  390.6 54.8 reduce-scatter.6
  447.8 56.0 reduce-scatter.8
  506.1 56.0 reduce-scatter.10
  690.0 35.5 reduce-scatter.12
  728.3 26.1 reduce-scatter.16
  757.4 33.9 reduce-scatter.14
